TPU v7x, 128 devices: a whole 4x4x4 slice. The times are simulated.
128 devices in a mesh: grp: 4 (over z), tok: 32 (over y, x, core).
Axes of the slice: x: 4, y: 4, z: 4, core: 2. Of those that a mesh axis runs over, the one named last changes fastest.
Arguments:
- tokens: bfloat16 [32768, 1408], P(('grp', 'tok')), may hold values from -6 to 6
- seg_ids: int32 [32768], P(('grp', 'tok')), may hold values from 0 to 8191, as said below
- merge_index: int32 [32768], P(('grp', 'tok')), may hold values from 0 to 255, as said below
- owners: int32 [8192, 1], P(('grp', 'tok')), may hold values from 0 to 31; in each aligned block of 64 rows (0 to 63, 64 to 127, ...) at most 4 rows name the same one
- w_qkv: bfloat16 [1408, 2112], replicated, may hold values from -0.15625 to 0.15625
- w_attn_out: bfloat16 [704, 1408], replicated, may hold values from -1.75 to 1.75
- w_in: bfloat16 [6144, 1408], P('grp'), may hold values from -0.15625 to 0.15625
- in_bias: bfloat16 [6144], P('grp'), may hold values from -3 to 3
- w_out: bfloat16 [6144, 1408], P('grp'), may hold values from -0.078125 to 0.078125
- out_bias: float32 [1408], replicated, may hold values from -3 to 3
- merge_gain: float32 [1408], replicated, may hold values from 0.1 to 1.9
- w_merge: bfloat16 [5632, 2048], P(None, 'grp'), may hold values from -0.078125 to 0.078125
- merge_bias: float32 [2048], P('grp'), may hold values from -3 to 3
Outputs:
- embeds: bfloat16 [16384, 2048], P('tok', 'grp')
Inputs may be any that keep to these rules, and one draw needn't show every extreme that they name: `seg_ids`: never falling along the tokens; every segment starts at a multiple of 4 tokens, has a multiple of 4 tokens and lies within one aligned block of 8192 tokens. `merge_index`: in each aligned block of 256 entries the values are a permutation of 0 to 255, and each aligned group of 4 entries names rows of a single segment. `owners`: among the 64 merged tokens of one device no owner is named more than 4 times.
All inputs are finite; a program needn't handle non-finite values.
Results may differ from a plain program's by a relative error of at most 0.014.
Values may be sent and summed in bfloat16 or wider, within the bound.
No kernel may reach another device: no remote copies, remote signals or barrier semaphores. Data moves between devices by JAX's collectives and lax.ppermute only.
A program may use at most 320 MiB of HBM per device.

v0:
```python
import math

import jax
import jax.numpy as jnp
from jax import lax
from jax.sharding import PartitionSpec as P

HEADS = 8
HD = 88


NORM_EPS = 1e-06


def layer_norm(values):
    centred = values - jnp.mean(values, axis=-1, keepdims=True)
    return centred * lax.rsqrt(jnp.mean(centred * centred, axis=-1, keepdims=True) + NORM_EPS)


def head_norm(values):
    return values * lax.rsqrt(jnp.mean(values * values, axis=-1, keepdims=True) + NORM_EPS)


def local(
    tokens,
    seg_ids,
    merge_index,
    owners,
    w_qkv,
    w_attn_out,
    w_in,
    in_bias,
    w_out,
    out_bias,
    merge_gain,
    w_merge,
    merge_bias,
):
    tok_rows = tokens.shape[0]
    feat_width = tokens.shape[1]
    head_width = HEADS * HD
    normed = layer_norm(tokens.astype(jnp.float32)).astype(jnp.bfloat16)
    projected = jnp.dot(normed, w_qkv, preferred_element_type=jnp.float32).astype(jnp.bfloat16)
    queries = head_norm(
        projected[:, :head_width].astype(jnp.float32).reshape(tok_rows, HEADS, HD)
    ).astype(jnp.bfloat16)
    key_rows = head_norm(
        projected[:, head_width : 2 * head_width].astype(jnp.float32).reshape(tok_rows, HEADS, HD)
    ).astype(jnp.bfloat16)
    keys_values = jnp.concatenate(
        [key_rows.reshape(tok_rows, head_width), projected[:, 2 * head_width :]], axis=1
    )
    score_scale = 1.0 / math.sqrt(HD)
    piece_kv = lax.all_gather(keys_values, "tok", axis=0, tiled=True)
    piece_seg = lax.all_gather(seg_ids, "tok", axis=0, tiled=True)
    row_count = piece_kv.shape[0]
    piece_keys = piece_kv[:, :head_width].reshape(row_count, HEADS, HD)
    piece_values = piece_kv[:, head_width:].reshape(row_count, HEADS, HD)
    scores = (
        jnp.einsum("qhd,khd->hqk", queries, piece_keys, preferred_element_type=jnp.float32)
        * score_scale
    )
    same_segment = (seg_ids[:, None] == piece_seg[None, :])[None]
    weights = jnp.where(same_segment, jnp.exp(scores), 0.0)
    denominator = jnp.sum(weights, axis=-1)
    numerator = jnp.einsum(
        "hqk,khd->qhd",
        weights.astype(jnp.bfloat16),
        piece_values,
        preferred_element_type=jnp.float32,
    )
    numerator, denominator = (numerator, denominator)
    attended = (
        (numerator / jnp.transpose(denominator)[:, :, None])
        .astype(jnp.bfloat16)
        .reshape(tok_rows, head_width)
    )
    residual = (
        tokens.astype(jnp.float32)
        + jnp.dot(attended, w_attn_out, preferred_element_type=jnp.float32)
    ).astype(jnp.bfloat16)
    mlp_in = layer_norm(residual.astype(jnp.float32)).astype(jnp.bfloat16)
    pre_act = lax.dot_general(
        lax.all_gather(mlp_in, "grp", axis=0, tiled=True),
        w_in,
        (((1,), (1,)), ((), ())),
        preferred_element_type=jnp.float32,
    )
    hidden = jax.nn.gelu(pre_act + in_bias.astype(jnp.float32), approximate=False).astype(
        jnp.bfloat16
    )
    mlp_sum = lax.psum_scatter(
        jnp.dot(hidden, w_out, preferred_element_type=jnp.float32).astype(jnp.bfloat16),
        "grp",
        scatter_dimension=0,
        tiled=True,
    ).astype(jnp.float32)
    normed_out = (
        layer_norm(residual.astype(jnp.float32) + mlp_sum + out_bias) * merge_gain
    ).astype(jnp.bfloat16)
    merged_count = tok_rows // 4
    merged = jnp.take(normed_out, merge_index, axis=0).reshape(merged_count, 4 * feat_width)
    tok_devices = lax.axis_size("tok")
    grp_devices = lax.axis_size("grp")
    slot_cap = max(2, 2 * merged_count // tok_devices)
    owner_col = owners[:, 0]
    positions = jnp.arange(merged_count, dtype=jnp.int32)
    earlier = (owner_col[:, None] == owner_col[None, :]) & (positions[None, :] < positions[:, None])
    owner_rank = jnp.sum(earlier.astype(jnp.int32), axis=1)
    slot_index = owner_col * slot_cap + owner_rank
    merged_all, slots_all = (
        lax.all_gather(merged, "grp", axis=0, tiled=True),
        lax.all_gather(slot_index, "grp", axis=0, tiled=True),
    )
    embedded = (
        jnp.dot(merged_all, w_merge, preferred_element_type=jnp.float32) + merge_bias
    ).astype(jnp.bfloat16)
    out_cols = embedded.shape[1]
    slot_range = jnp.arange(tok_devices * slot_cap, dtype=jnp.int32)
    placement = (
        slots_all.reshape(grp_devices, 1, merged_count) == slot_range[None, :, None]
    ).astype(jnp.bfloat16)
    placement = placement.reshape(grp_devices, tok_devices, slot_cap, merged_count)
    outgoing = jnp.einsum(
        "gjrm,gmc->jgrc",
        placement,
        embedded.reshape(grp_devices, merged_count, out_cols),
        preferred_element_type=jnp.float32,
    ).astype(jnp.bfloat16)
    received = lax.all_to_all(outgoing, "tok", split_axis=0, concat_axis=2, tiled=True)
    return received.reshape(grp_devices * tok_devices * slot_cap, out_cols)


def solution(mesh):
    placed = (
        P(("grp", "tok"), None),
        P(("grp", "tok")),
        P(("grp", "tok")),
        P(("grp", "tok"), None),
        P(),
        P(),
        P("grp", None),
        P("grp"),
        P("grp", None),
        P(),
        P(),
        P(None, "grp"),
        P("grp"),
    )
    return jax.shard_map(
        local, mesh=mesh, in_specs=placed, out_specs=P("tok", "grp"), check_vma=False
    )
```

profile of v0, /device:TPU:1, one launch (start us, length us, event | category | flops | bytes accessed | tf_op | source)
XLA Modules:
  0.0 376.1 jit_solution(4948535860461258292)
XLA Ops:
  6.5 0.0 copy-start
  6.5 0.0 all-gather.5.cloned.1.call-start
  6.5 1.4 convert_reduce_fusion
  8.0 1.4 fusion.21
  9.4 0.0 copy-start.5
  9.4 4.9 %convolution_convert_fusion = bf16[256,2112]{0,1:T(8,128)(2,1)S(1)} fusion(bf16[1408,2112]{0,1:T(8,128)(2,1)} %param.17, bf16[256,1408]{1,0:T(8,128)(2,1)} %param.13, f32[256]{0:T(256)S(1)} %add_rsqrt_fusion.4, f32[256]{0:T(256)S(1)} %broadcast_multiply_fusion.2), kind=kOutput, calls=%fused_computation.28 | convolution fusion | flops 1524514816 | bytes 7751680 | tf_op jit(solution)/shard_map/dot_general | solution.py:43
  14.3 0.0 copy-start.2
  14.4 0.1 convert_multiply_fusion.3
  14.4 0.9 copy-done.2
  15.4 0.1 reduce_sum.92
  15.5 1.1 fusion.34
  16.5 0.9 pad_maximum_fusion
  17.4 0.0 all-gather.5.cloned.1.call-update
  17.5 0.0 all-gather.7.cloned.1.call-start
  17.5 0.0 copy-done.5
  17.5 26.0 %all-gather = s32[32,1,256]{2,1,0:T(1,128)S(1)} all-gather(s32[1,1,256]{2,1,0:T(1,128)S(1)} %bitcast.54), channel_id=1, replica_groups=mesh['grp'=4,'tok'=32] {'tok'}, dimensions={0}, use_global_device_ids=true | all-gather | bytes 33792 | tf_op jit(solution)/shard_map/all_gather | solution.py:55
  43.5 0.1 fusion.35
  43.6 2.5 broadcast_compare_fusion
  46.1 72.6 %all-gather.5.cloned.1.call-done = bf16[8192,1408]{0,1:T(8,128)(2,1)} async-done(((bf16[256,1408]{0,1:T(8,128)(2,1)}), bf16[8192,1408]{0,1:T(8,128)(2,1)}) %all-gather.5.cloned.1.call-update) | async-done | bytes 23068688 | tf_op jit(solution)/shard_map/all_gather | solution.py:54
  118.7 16.6 %fusion.80 = (bf16[8192,704]{0,1:T(8,128)(2,1)}, bf16[8192,704]{0,1:T(8,128)(2,1)}) fusion(bf16[8192,1408]{0,1:T(8,128)(2,1)} %all-gather.5.cloned.1.call-done), kind=kLoop, calls=%fused_computation.116 | loop fusion | bytes 46137344 | tf_op jit(solution)/shard_map/slice | solution.py:57
  135.3 32.1 %fusion = (f32[8,256]{1,0:T(8,128)S(1)}, f32[8,256,8192]{2,1,0:T(8,128)}) fusion(pred[256,8192]{1,0:T(8,128)(4,1)} %broadcast_compare_fusion, bf16[8192,8,88]{0,2,1:T(8,128)(2,1)} %bitcast.44, bf16[256,8,88]{0,2,1:T(8,128)(2,1)S(1)} %bitcast.50, f32[256,8]{0,1:T(8,128)S(1)} %add_rsqrt_fusion), kind=kOutput, calls=%fused_computation.2 | convolution fusion | flops 3003660288 | bytes 81117184 | tf_op jit(solution)/shard_map/qhd,khd->hqk/dot_general | solution.py:60
  167.4 28.2 %fusion.30 = bf16[256,8,88]{0,2,1:T(8,128)(2,1)} fusion(bf16[8192,8,88]{0,2,1:T(8,128)(2,1)} %bitcast.43, f32[8,256,8192]{2,1,0:T(8,128)} %get-tuple-element.10, pred[256,8192]{1,0:T(8,128)(4,1)} %broadcast_compare_fusion, f32[256,8]{0,1:T(8,128)S(1)} %bitcast.56), kind=kOutput, calls=%fused_computation.48 | convolution fusion | flops 3003482112 | bytes 81108992 | tf_op jit(solution)/shard_map/hqk,khd->qhd/dot_general | solution.py:66
  195.6 0.0 copy-done
  195.6 2.1 fusion.82
  197.7 0.3 multiply_reduce_fusion.1
  198.0 1.1 multiply_convert_fusion.1
  199.1 0.0 all-gather.7.cloned.1.call-update
  199.2 0.3 reduce-scatter.2.cloned.1.call-start
  199.4 0.0 copy-done.6
  199.5 0.0 copy-start.7
  199.5 0.0 copy-start.3
  199.5 37.7 %all-gather.7.cloned.1.call-done = bf16[1024,1408]{1,0:T(8,128)(2,1)} async-done(((bf16[256,1408]{1,0:T(8,128)(2,1)}), bf16[1024,1408]{1,0:T(8,128)(2,1)}) %all-gather.7.cloned.1.call-update) | async-done | bytes 2883600 | tf_op jit(solution)/shard_map/all_gather | solution.py:84
  237.2 25.3 %convolution_convert_fusion.1 = bf16[1024,1408]{1,0:T(8,128)(2,1)} fusion(bf16[1536,1408]{1,0:T(8,128)(2,1)} %param.21, bf16[1024,1408]{1,0:T(8,128)(2,1)} %all-gather.7.cloned.1.call-done, bf16[1536,1408]{1,0:T(8,128)(2,1)} %param.19, f32[1536]{0:T(1024)S(1)} %convert_element_type.76), kind=kOutput, calls=%fused_computation.29 | convolution fusion | flops 8963620864 | bytes 14424064 | tf_op jit(solution)/shard_map/dot_general | solution.py:93
  262.5 0.0 reduce-scatter.2.cloned.1.call-update
  262.6 0.3 all-gather.9.cloned.1.call-start
  262.9 0.0 copy-done.7
  262.9 0.1 broadcast_in_dim.25
  263.0 0.3 broadcast_in_dim.29
  263.3 0.2 copy.20
  263.5 35.6 %reduce-scatter.2.cloned.1.call-done = bf16[256,1408]{1,0:T(8,128)(2,1)} async-done(((bf16[1024,1408]{1,0:T(8,128)(2,1)}), bf16[256,1408]{1,0:T(8,128)(2,1)}) %reduce-scatter.2.cloned.1.call-update) | async-done | bytes 720912 | tf_op jit(solution)/shard_map/reduce_scatter | solution.py:92
  299.1 0.0 copy-done.3
  299.1 1.4 fusion.40
  300.5 1.5 multiply_reduce_fusion
  302.0 0.0 copy-done.4
  302.0 0.0 copy-start.10
  302.0 0.0 copy-start.8
  302.0 0.0 copy-start.9
  302.0 1.5 multiply_convert_fusion
  303.5 1.3 gather_fusion
  304.8 0.5 gather.7
  305.3 1.0 broadcast_select_fusion
  306.2 0.0 all-gather.9.cloned.1.call-update
  306.2 0.6 dynamic-slice
  307.5 0.2 convert_reduce_fusion.1
  307.7 0.1 add_dynamic-update-slice_fusion
  307.8 5.3 %all-reduce = s32[256]{0:T(256)S(1)} all-reduce(s32[256]{0:T(256)S(1)} %add_dynamic-update-slice_fusion), channel_id=1, replica_groups=mesh['grp'=4,'tok'=32] {'grp'}, use_global_device_ids=true, to_apply=%add | all-reduce | flops 256 | bytes 2048
  313.1 0.1 eq.58
  313.2 30.3 %all-gather.9.cloned.1.call-done = bf16[256,5632]{1,0:T(8,128)(2,1)} async-done(((bf16[64,5632]{1,0:T(8,128)(2,1)}), bf16[256,5632]{1,0:T(8,128)(2,1)}) %all-gather.9.cloned.1.call-update) | async-done | bytes 2883600 | tf_op jit(solution)/shard_map/all_gather | solution.py:112
  343.5 5.3 %fusion.33 = bf16[256,512]{1,0:T(8,128)(2,1)S(1)} fusion(bf16[256,5632]{1,0:T(8,128)(2,1)} %all-gather.9.cloned.1.call-done, bf16[5632,512]{1,0:T(8,128)(2,1)} %param.24, f32[512]{0:T(512)S(1)} %copy-done.9), kind=kOutput, calls=%fused_computation.50 | convolution fusion | flops 1476657152 | bytes 8914944 | tf_op jit(solution)/shard_map/dot_general | solution.py:116
  348.8 0.3 fusion.26
  349.2 0.4 copy.17
  349.6 18.9 %all_to_all.15 = bf16[32,4,4,512]{3,2,1,0:T(4,128)(2,1)S(1)} all-to-all(bf16[32,4,4,512]{3,2,1,0:T(4,128)(2,1)S(1)} %copy.17), channel_id=1, replica_groups=mesh['grp'=4,'tok'=32] {'tok'}, dimensions={0} | all-to-all | bytes 1048576 | tf_op jit(solution)/shard_map/all_to_all | solution.py:130
  368.5 0.2 copy.18
  368.7 0.9 reshape.131
  (22 shorter events, 0.1 us)
Async XLA Ops:
  6.5 189.1 %copy-start = (bf16[704,1408]{1,0:T(8,128)(2,1)S(1)}, bf16[704,1408]{1,0:T(8,128)(2,1)}, u32[]{:S(2)}) copy-start(bf16[704,1408]{1,0:T(8,128)(2,1)} %param.18) | copy-start | bytes 5947396
  6.5 112.2 %all-gather.5.cloned.1.call-start = ((), (), s32[]{:S(2)}) async-start(), calls=%async_computation.2 | async-start | bytes 23789568 | tf_op jit(solution)/shard_map/all_gather | solution.py:54
  9.4 8.1 %copy-start.5 = (s32[256]{0:T(256)S(1)}, s32[256]{0:T(256)}, u32[]{:S(2)}) copy-start(s32[256]{0:T(256)} %param.14) | copy-start | bytes 3076
  14.3 1.0 copy-start.2
  17.5 219.8 %all-gather.7.cloned.1.call-start = ((), (), s32[]{:S(2)}) async-start(), calls=%async_computation.3 | async-start | bytes 3604480 | tf_op jit(solution)/shard_map/all_gather | solution.py:84
  195.6 3.8 %copy-start.6 = (bf16[1536]{0:T(1024)(128)(2,1)S(1)}, bf16[1536]{0:T(1024)(128)(2,1)}, u32[]{:S(2)}) copy-start(bf16[1536]{0:T(1024)(128)(2,1)} %param.20) | copy-start | bytes 9220
  199.2 99.9 %reduce-scatter.2.cloned.1.call-start = ((), (), s32[]{:S(2)}) async-start(), calls=%async_computation.4 | async-start | bytes 3604480 | tf_op jit(solution)/shard_map/reduce_scatter | solution.py:92
  199.5 63.4 %copy-start.7 = (s32[256]{0:T(256)S(1)}, s32[256]{0:T(256)}, u32[]{:S(2)}) copy-start(s32[256]{0:T(256)} %param.15) | copy-start | bytes 3076
  199.5 99.6 %copy-start.3 = (f32[1408]{0:T(1024)S(1)}, f32[1408]{0:T(1024)}, u32[]{:S(2)}) copy-start(f32[1408]{0:T(1024)} %param.22) | copy-start | bytes 16900
  262.5 39.4 %copy-start.4 = (f32[1408]{0:T(1024)S(1)}, f32[1408]{0:T(1024)}, u32[]{:S(2)}) copy-start(f32[1408]{0:T(1024)} %param.23) | copy-start | bytes 16900
  262.6 81.0 %all-gather.9.cloned.1.call-start = ((), (), s32[]{:S(2)}) async-start(), calls=%async_computation.5 | async-start | bytes 3604480 | tf_op jit(solution)/shard_map/all_gather | solution.py:112
  302.0 4.3 %copy-start.10 = (u32[128]{0:T(128)S(1)}, u32[128]{0:T(128)}, u32[]{:S(2)}) copy-start(u32[128]{0:T(128)} %constant.101) | copy-start | bytes 1540
  302.0 5.5 %copy-start.8 = (s32[64,1]{0,1:T(1,128)S(1)}, s32[64,1]{0,1:T(1,128)}, u32[]{:S(2)}) copy-start(s32[64,1]{0,1:T(1,128)} %param.16) | copy-start | bytes 772
  302.0 41.5 %copy-start.9 = (f32[512]{0:T(512)S(1)}, f32[512]{0:T(512)}, u32[]{:S(2)}) copy-start(f32[512]{0:T(512)} %param.25) | copy-start | bytes 6148
  343.5 26.1 %copy-start.1 = (bf16[704,1408]{1,0:T(8,128)(2,1)S(1)}, bf16[704,1408]{1,0:T(8,128)(2,1)}, u32[]{:S(2)}) copy-start(bf16[704,1408]{1,0:T(8,128)(2,1)} %param.18) | copy-start | bytes 5947396
Sparse Core Ops, SparseCore 0:
  17.6 101.0 all-gather.4
  199.3 37.8 all-gather.6
  262.7 36.3 reduce-scatter.1
  306.3 37.1 all-gather.8
where the time goes:
time: 377 us; the launch traced here: 376 us
  waiting for transfers between devices  176 us (47%)
  matrix products  98.3 us (26%)
  blocking collectives  50.2 us (13%)
  local copies, waits for them, and re-layouts  22.1 us (6%)
  other arithmetic  14.6 us (4%)
  between operations  14.1 us (4%)
    all_gather x1, waiting for transfers between devices, local(): piece_kv = lax.all_gather(keys_values, 'tok', axis=0, tiled=True)  72.6 us
    all_gather x1, waiting for transfers between devices, local(): lax.all_gather(mlp_in, 'grp', axis=0, tiled=True)  37.7 us
    reduce_scatter x1, waiting for transfers between devices, local(): lax.psum_scatter(jnp.dot(hidden, w_out, preferred_element_type=jnp.float3...  35.6 us
    dot_general x1, matrix products, local(): jnp.einsum('qhd,khd->hqk', queries, piece_keys, preferred_element_type=jn...  32.1 us
    all_gather x1, waiting for transfers between devices, local(): lax.all_gather(merged, 'grp', axis=0, tiled=True)  30.3 us
    dot_general x1, matrix products, local(): jnp.einsum('hqk,khd->qhd', weights.astype(jnp.bfloat16), piece_values, pr...  28.2 us
    all_gather x1, blocking collectives, local(): piece_seg = lax.all_gather(seg_ids, 'tok', axis=0, tiled=True)  26 us
    dot_general x1, matrix products, local(): jnp.dot(hidden, w_out, preferred_element_type=jnp.float32)  25.3 us
  transfers between devices with their start and end apart: 4, of which 4 were waited for; matrix products, arithmetic and copies ran while one was open for 1% of the time, Pallas kernels for 0%

commit v1 on v0

v1 whole, which is shorter than its diff:
```python
import math

import jax
import jax.numpy as jnp
from jax import lax
from jax.experimental import pallas as pl
from jax.experimental.pallas import tpu as pltpu
from jax.sharding import Mesh
from jax.sharding import PartitionSpec as P

HEADS = 8
HD = 88
EXT = 8
NORM_EPS = 1e-06
LANES = 128
F32 = jnp.float32
BF16 = jnp.bfloat16
VMEM_LIMIT = 60 * 1024 * 1024


def cparams(*semantics):
    return pltpu.CompilerParams(
        dimension_semantics=semantics or None, vmem_limit_bytes=VMEM_LIMIT
    )


def layer_norm(values):
    centred = values - jnp.mean(values, axis=-1, keepdims=True)
    return centred * lax.rsqrt(jnp.mean(centred * centred, axis=-1, keepdims=True) + NORM_EPS)


def dot(a, b, dims=(((1,), (0,)), ((), ()))):
    return lax.dot_general(a, b, dims, preferred_element_type=F32)


NT = (((1,), (1,)), ((), ()))


def qkv_kernel(x_ref, seg_ref, w_hbm, out_ref, w_ref, acc_ref, sems, *, chunks):
    copies = []
    for number, (start, size) in enumerate(chunks):
        copy = pltpu.make_async_copy(
            w_hbm.at[pl.ds(start, size)], w_ref.at[pl.ds(start, size)], sems.at[number]
        )
        copy.start()
        copies.append(copy)
    normed = layer_norm(x_ref[...].astype(F32)).astype(BF16)
    for number, (start, size) in enumerate(chunks):
        copies[number].wait()
        part = dot(normed[:, start : start + size], w_ref[start : start + size, :])
        if number == 0:
            acc_ref[...] = part
        else:
            acc_ref[...] += part
    projected = acc_ref[...].astype(BF16).astype(F32).T
    width = HEADS * HD
    seg = seg_ref[...]
    high = seg // 64
    low = seg - high * 64
    tokens = seg.shape[1]
    row = lax.broadcasted_iota(jnp.int32, (EXT, tokens), 0)
    extra = jnp.where(row == 0, 1, jnp.where(row == 1, high, jnp.where(row == 2, low, 0)))
    extra = extra.astype(F32)
    scale = math.log2(math.e) / math.sqrt(HD)
    for head in range(HEADS):
        at = head * HD
        q = projected[at : at + HD]
        k = projected[width + at : width + at + HD]
        v = projected[2 * width + at : 2 * width + at + HD]
        q = q * (lax.rsqrt(jnp.mean(q * q, axis=0, keepdims=True) + NORM_EPS) * scale)
        k = k * lax.rsqrt(jnp.mean(k * k, axis=0, keepdims=True) + NORM_EPS)
        out_ref[head] = jnp.concatenate([q, k, v, extra], axis=0).astype(BF16)


def qkv(tokens, seg_ids, w_qkv):
    rows, width = tokens.shape
    edges = list(range(0, width, 3 * LANES)) + [width]
    chunks = tuple((a, b - a) for a, b in zip(edges[:-1], edges[1:]))
    return pl.pallas_call(
        lambda *refs: qkv_kernel(*refs, chunks=chunks),
        out_shape=jax.ShapeDtypeStruct((HEADS, 3 * HD + EXT, rows), BF16),
        in_specs=[
            pl.BlockSpec(memory_space=pltpu.VMEM),
            pl.BlockSpec(memory_space=pltpu.VMEM),
            pl.BlockSpec(memory_space=pl.ANY),
        ],
        out_specs=pl.BlockSpec(memory_space=pltpu.VMEM),
        scratch_shapes=[
            pltpu.VMEM(w_qkv.shape, BF16),
            pltpu.VMEM((rows, w_qkv.shape[1]), F32),
            pltpu.SemaphoreType.DMA((len(chunks),)),
        ],
        compiler_params=cparams(),
        name="qkv",
    )(tokens, seg_ids.reshape(1, rows), w_qkv)


def attend_kernel(*refs, first, last, key_block):
    if first:
        q_ref, kv_ref, out_ref, q_sc, segq_sc, k_sc, v_sc, segk_sc = refs
    else:
        q_ref, kv_ref, acc_ref, out_ref, q_sc, segq_sc, k_sc, v_sc, segk_sc = refs
    blocks, _, tokens = kv_ref.shape
    for j in range(blocks):
        at = pl.ds(j * tokens, tokens)
        kv = kv_ref[j].astype(F32)
        k_sc[:, j * tokens : (j + 1) * tokens] = jnp.concatenate(
            [kv[:HD], jnp.zeros((LANES - HD, tokens), F32)], axis=0
        ).astype(BF16)
        wide = jnp.concatenate(
            [kv[HD:], jnp.zeros((LANES - HD - EXT, tokens), F32)], axis=0
        )
        v_sc[at, :] = wide.T.astype(BF16)
        segk_sc[:, j * tokens : (j + 1) * tokens] = (
            kv[2 * HD + 1 : 2 * HD + 2] * 64.0 + kv[2 * HD + 2 : 2 * HD + 3]
        )
        q = q_ref[j].astype(F32)
        q_sc[at, :] = (
            jnp.concatenate([q[:HD], jnp.zeros((LANES - HD, tokens), F32)], axis=0)
            .T.astype(BF16)
        )
        seg = q[3 * HD + 1 : 3 * HD + 2] * 64.0 + q[3 * HD + 2 : 3 * HD + 3]
        segq_sc[at, :] = jnp.broadcast_to(seg, (LANES, tokens)).T

    def tile(step, carry):
        rows = pl.ds(pl.multiple_of(step * tokens, tokens), tokens)
        q = q_sc[rows, :]
        segq = segq_sc[rows, 0:1]
        total = None
        for start in range(0, blocks * tokens, key_block):
            scores = dot(q, k_sc[:, start : start + key_block])
            same = segq == segk_sc[:, start : start + key_block]
            weights = jnp.where(same, jnp.exp2(scores), 0.0).astype(BF16)
            part = dot(weights, v_sc[start : start + key_block, :])
            total = part if total is None else total + part
        if not first:
            total = total + acc_ref[rows, :]
        if last:
            total = total / total[:, HD : HD + 1]
            out_ref[step] = total.T[:HD].astype(BF16)
        else:
            out_ref[rows, :] = total
        return carry

    lax.fori_loop(0, blocks, tile, 0)


def attend(queries, kv, acc=None, last=False, key_block=1024):
    blocks, _, tokens = kv.shape
    total = blocks * tokens
    first = acc is None
    if last:
        shape = jax.ShapeDtypeStruct((blocks, HD, tokens), BF16)
    else:
        shape = jax.ShapeDtypeStruct((total, LANES), F32)
    operands = (queries, kv) if first else (queries, kv, acc)
    return pl.pallas_call(
        lambda *refs: attend_kernel(*refs, first=first, last=last, key_block=key_block),
        out_shape=shape,
        in_specs=[pl.BlockSpec(memory_space=pltpu.VMEM)] * len(operands),
        out_specs=pl.BlockSpec(memory_space=pltpu.VMEM),
        scratch_shapes=[
            pltpu.VMEM((total, LANES), BF16),
            pltpu.VMEM((total, LANES), F32),
            pltpu.VMEM((LANES, total), BF16),
            pltpu.VMEM((total, LANES), BF16),
            pltpu.VMEM((1, total), F32),
        ],
        compiler_params=cparams(),
        name="attend",
    )(*operands)


def project_kernel(att_ref, x_ref, w_ref, res_ref, in_ref):
    heads, _, tokens = att_ref.shape
    att = att_ref[...].astype(F32).reshape(heads * HD, tokens).T.astype(BF16)
    residual = (x_ref[...].astype(F32) + dot(att, w_ref[...])).astype(BF16)
    res_ref[...] = residual
    in_ref[...] = layer_norm(residual.astype(F32)).astype(BF16)


def project(attended, tokens, w_attn_out):
    shape = jax.ShapeDtypeStruct(tokens.shape, BF16)
    return pl.pallas_call(
        project_kernel,
        out_shape=(shape, shape),
        in_specs=[pl.BlockSpec(memory_space=pltpu.VMEM)] * 3,
        out_specs=(pl.BlockSpec(memory_space=pltpu.VMEM),) * 2,
        compiler_params=cparams(),
        name="project",
    )(attended, tokens, w_attn_out)


def mlp_kernel(*refs, pieces):
    x_refs = refs[:pieces]
    w_in_ref, bias_ref, w_out_ref, out_ref, x_sc, acc_ref = refs[pieces:]
    step = pl.program_id(0)

    @pl.when(step == 0)
    def _():
        at = 0
        for x_ref in x_refs:
            x_sc[at : at + x_ref.shape[0], :] = x_ref[...]
            at += x_ref.shape[0]

    pre = dot(x_sc[...], w_in_ref[...], NT) + bias_ref[...].astype(F32)
    hidden = (0.5 * pre * (1.0 + lax.erf(pre * math.sqrt(0.5)))).astype(BF16)
    part = dot(hidden, w_out_ref[...])

    @pl.when(step == 0)
    def _():
        acc_ref[...] = part

    @pl.when(step > 0)
    def _():
        acc_ref[...] += part

    @pl.when(step == pl.num_programs(0) - 1)
    def _():
        out_ref[...] = acc_ref[...].astype(BF16)


def mlp(pieces, w_in, in_bias, w_out, block=256):
    units, width = w_in.shape
    rows = sum(piece.shape[0] for piece in pieces)
    whole = lambda i: (0, 0)
    return pl.pallas_call(
        lambda *refs: mlp_kernel(*refs, pieces=len(pieces)),
        out_shape=jax.ShapeDtypeStruct((rows, width), BF16),
        grid=(units // block,),
        in_specs=[pl.BlockSpec(piece.shape, whole) for piece in pieces]
        + [
            pl.BlockSpec((block, width), lambda i: (i, 0)),
            pl.BlockSpec((1, block), lambda i: (0, i)),
            pl.BlockSpec((block, width), lambda i: (i, 0)),
        ],
        out_specs=pl.BlockSpec((rows, width), whole),
        scratch_shapes=[pltpu.VMEM((rows, width), BF16), pltpu.VMEM((rows, width), F32)],
        compiler_params=cparams("arbitrary"),
        name="mlp",
    )(*pieces, w_in, in_bias.reshape(1, units), w_out)


def merge_kernel(*refs, halves, cap):
    res_ref, bias_ref, gain_ref, index_ref, owner_ref = refs[:5]
    parts = refs[5 : 5 + 3 * halves]
    out_ref, sum_sc = refs[5 + 3 * halves :]
    rows, width = res_ref.shape
    half = rows // halves
    for h in range(halves):
        at = slice(h * half, (h + 1) * half)
        own, left, right = parts[3 * h : 3 * h + 3]
        total = own[...].astype(F32) + left[...].astype(F32) + right[...].astype(F32)
        total = res_ref[at, :].astype(F32) + total + bias_ref[...]
        sum_sc[at, :] = (layer_norm(total) * gain_ref[...]).astype(BF16)
    normed = sum_sc[...]
    count = rows // 4
    lane = lax.broadcasted_iota(jnp.int32, (count, rows), 1)
    for c in range(4):
        pick = (index_ref[:, c : c + 1] == lane).astype(BF16)
        out_ref[:, c * width : (c + 1) * width] = dot(pick, normed).astype(BF16)
    owner = owner_ref[...]
    r = lax.broadcasted_iota(jnp.int32, (count, count), 0)
    s = lax.broadcasted_iota(jnp.int32, (count, count), 1)
    across = jnp.sum(jnp.where(r == s, owner, 0), axis=0, keepdims=True)
    earlier = (across == owner) & (s < r)
    rank = jnp.sum(earlier.astype(jnp.int32), axis=1, keepdims=True)
    slot = (owner * cap + rank).astype(F32).astype(BF16)
    out_ref[:, 4 * width :] = jnp.broadcast_to(slot, (count, LANES))


def merge(residual, out_bias, merge_gain, merge_index, owners, parts, cap):
    rows, width = residual.shape
    operands = (
        residual,
        out_bias.reshape(1, width),
        merge_gain.reshape(1, width),
        merge_index.reshape(rows // 4, 4),
        owners,
        *parts,
    )
    return pl.pallas_call(
        lambda *refs: merge_kernel(*refs, halves=len(parts) // 3, cap=cap),
        out_shape=jax.ShapeDtypeStruct((rows // 4, 4 * width + LANES), BF16),
        in_specs=[pl.BlockSpec(memory_space=pltpu.VMEM)] * len(operands),
        out_specs=pl.BlockSpec(memory_space=pltpu.VMEM),
        scratch_shapes=[pltpu.VMEM((rows, width), BF16)],
        compiler_params=cparams(),
        name="merge",
    )(*operands)


def embed_kernel(group_ref, *refs, pieces, cap, slots):
    x_refs = refs[: len(pieces)]
    w_ref, bias_ref, out_ref, x_sc, acc_ref = refs[len(pieces) :]
    step = pl.program_id(0)
    steps = pl.num_programs(0)
    for (at, _), x_ref in zip(pieces, x_refs):
        x_sc[at : at + x_ref.shape[0], :] = x_ref[...]

    @pl.when(step < steps - 1)
    def _():
        part = dot(x_sc[...], w_ref[...])

        @pl.when(step == 0)
        def _():
            acc_ref[...] = part

        @pl.when(step > 0)
        def _():
            acc_ref[...] += part

    @pl.when(step == steps - 1)
    def _():
        embedded = (acc_ref[...] + bias_ref[...]).astype(BF16)
        total = x_sc.shape[0]
        count = total // 4
        slot = x_sc[:, 0:1].astype(F32).astype(jnp.int32)
        owner = slot // cap
        rank = slot - owner * cap
        shift = lax.broadcasted_iota(jnp.int32, (total, 1), 0) // count
        group = group_ref[0] + shift
        group = jnp.where(group >= 4, group - 4, group)
        target = owner * slots + group * cap + rank
        lane = lax.broadcasted_iota(jnp.int32, (total, out_ref.shape[0]), 1)
        place = (target == lane).astype(F32).T.astype(BF16)
        out_ref[...] = dot(place, embedded).astype(BF16)


def embed(group, pieces, w_merge, merge_bias, cap, slots, owners, block=1408):
    arrays = [array for _, array in pieces]
    rows = sum(array.shape[0] for array in arrays)
    depth, cols = w_merge.shape
    steps = depth // block
    places = tuple((at, array.shape[0]) for at, array in pieces)
    x_block = block

    def x_map(i, _):
        return (0, i)

    spec = lambda array: pl.BlockSpec((array.shape[0], x_block), x_map)
    return pl.pallas_call(
        lambda *refs: embed_kernel(*refs, pieces=places, cap=cap, slots=slots),
        out_shape=jax.ShapeDtypeStruct((owners * slots, cols), BF16),
        grid_spec=pltpu.PrefetchScalarGridSpec(
            num_scalar_prefetch=1,
            grid=(steps + 1,),
            in_specs=[spec(array) for array in arrays]
            + [
                pl.BlockSpec((block, cols), lambda i, _: (jnp.minimum(i, steps - 1), 0)),
                pl.BlockSpec((1, cols), lambda i, _: (0, 0)),
            ],
            out_specs=pl.BlockSpec((owners * slots, cols), lambda i, _: (0, 0)),
            scratch_shapes=[pltpu.VMEM((rows, block), BF16), pltpu.VMEM((rows, cols), F32)],
        ),
        compiler_params=cparams("arbitrary"),
        name="embed",
    )(group, *arrays, w_merge, merge_bias.reshape(1, cols))


def flip(value, axis):
    return lax.ppermute(value, axis, [(0, 1), (1, 0)])


def turn(value, axis, by):
    size = lax.axis_size(axis)
    return lax.ppermute(value, axis, [(i, (i + by) % size) for i in range(size)])


def ring_gather(value, axis):
    before = turn(value, axis, 1)
    after = turn(value, axis, -1)
    half = value.shape[0] // 2
    return before, after, turn(before[:half], axis, 1), turn(after[half:], axis, -1)


def ring_scatter(own, before, after, opposite, axis):
    half = own.shape[0] // 2
    one = turn(opposite[:half], axis, 1)
    two = turn(opposite[half:], axis, -1)
    to_next = jnp.concatenate([(after[:half].astype(F32) + one.astype(F32)).astype(BF16), after[half:]])
    to_last = jnp.concatenate([before[:half], (before[half:].astype(F32) + two.astype(F32)).astype(BF16)])
    return own, turn(to_next, axis, 1), turn(to_last, axis, -1)


HALVES = 2


def local(
    tokens,
    seg_ids,
    merge_index,
    owners,
    w_qkv,
    w_attn_out,
    w_in,
    in_bias,
    w_out,
    out_bias,
    merge_gain,
    w_merge,
    merge_bias,
):
    rows = tokens.shape[0]
    heads = qkv(tokens, seg_ids, w_qkv)
    mine = lax.all_to_all(heads, ("y", "xh"), 0, 0, tiled=True)
    kv = mine[:, HD:]
    kv_c = flip(kv, "c")
    kv_x = flip(kv, "xl")
    kv_xc = flip(kv_x, "c")
    acc = attend(mine, kv)
    acc = attend(mine, kv_c, acc)
    acc = attend(mine, kv_x, acc)
    done = attend(mine, kv_xc, acc, last=True)
    attended = lax.all_to_all(done, ("y", "xh"), 0, 0, tiled=True)
    residual, mlp_in = project(attended, tokens, w_attn_out)
    half = rows // HALVES
    parts = []
    for h in range(HALVES):
        own = mlp_in[h * half : (h + 1) * half]
        before, after, far_a, far_b = ring_gather(own, "grp")
        out = mlp([own, before, after, far_a, far_b], w_in, in_bias, w_out)
        blocks = [out[i * half : (i + 1) * half] for i in range(4)]
        parts.extend(ring_scatter(*blocks, "grp"))
    owner_count = 32
    cap = 4
    merged = merge(residual, out_bias, merge_gain, merge_index, owners, parts, cap)
    count = merged.shape[0]
    before, after, far_a, far_b = ring_gather(merged, "grp")
    pieces = [
        (0, merged),
        (count, after),
        (2 * count, far_a),
        (2 * count + count // 2, far_b),
        (3 * count, before),
    ]
    group = lax.axis_index("grp").reshape(1).astype(jnp.int32)
    slots = 4 * cap
    outgoing = embed(group, pieces, w_merge, merge_bias, cap, slots, owner_count)
    cols = outgoing.shape[1]
    outgoing = outgoing.reshape(owner_count, 4, cap, cols)
    received = lax.all_to_all(
        outgoing, ("y", "xh", "xl", "c"), split_axis=0, concat_axis=2, tiled=True
    )
    return received.reshape(4 * owner_count * cap, cols)


def solution(mesh):
    inner = Mesh(mesh.devices.reshape(4, 4, 2, 2, 2), ("grp", "y", "xh", "xl", "c"))
    every = ("grp", "y", "xh", "xl", "c")
    tok = ("y", "xh", "xl", "c")
    placed = (
        P(every, None),
        P(every),
        P(every),
        P(every, None),
        P(),
        P(),
        P("grp", None),
        P("grp"),
        P("grp", None),
        P(),
        P(),
        P(None, "grp"),
        P("grp"),
    )
    return jax.shard_map(
        local, mesh=inner, in_specs=placed, out_specs=P(tok, "grp"), check_vma=False
    )
```

time: 377 us -> 260 us (0.69)
  waiting for transfers between devices: 176 us -> 48.4 us
  matrix products: 98.3 us -> 0 us
  Pallas kernels: 0 us -> 89.8 us
  starting transfers between devices: 0.61 us -> 33.2 us
  between operations: 14.1 us -> 0.31 us
  other arithmetic: 14.6 us -> 3.47 us
  blocking collectives: 50.2 us -> 59.1 us
    all_gather x3 -> x0, waiting for transfers between devices: 141 us -> none  [the longest x1 72.6 us: local(): piece_kv = lax.all_gather(keys_values, 'tok', axis=0, tiled=True)]
    dot_general x7 -> x0, matrix products: 98.3 us -> none  [the longest x1 32.1 us: local(): jnp.einsum('qhd,khd->hqk', queries, piece_keys, preferred_element_type=jn...]
    pallas_call x0 -> x10, Pallas kernels: none -> 89.8 us  [the longest x4 36.7 us: attend(): pl.pallas_call(lambda *refs: attend_kernel(*refs, first=first, last=last,...]
    ppermute x0 -> x23, waiting for transfers between devices: none -> 48.4 us  [the longest x20 35.2 us: turn(): lax.ppermute(value, axis, [(i, (i + by) % size) for i in range(size)])]
    all_to_all x1 -> x3, blocking collectives: 18.9 us -> 59.1 us  [the longest x1 24.2 us: local(): mine = lax.all_to_all(heads, ('y', 'xh'), 0, 0, tiled=True)]
    reduce_scatter x1 -> x0, waiting for transfers between devices: 35.6 us -> none  [local(): lax.psum_scatter(jnp.dot(hidden, w_out, preferred_element_type=jnp.float3...]
    ppermute x0 -> x23, starting transfers between devices: none -> 33.2 us  [the longest x20 27 us: turn(): lax.ppermute(value, axis, [(i, (i + by) % size) for i in range(size)])]
    all_gather x1 -> x0, blocking collectives: 26 us -> none  [local(): piece_seg = lax.all_gather(seg_ids, 'tok', axis=0, tiled=True)]
  transfers between devices with their start and end apart: 4 -> 23, of which waited for: 4 -> 9; matrix products, arithmetic and copies ran while one was open for 1% -> 4% of each run, Pallas kernels for 0% -> 22%
where the time goes in v1:
time: 260 us; the launch traced here: 259 us
  Pallas kernels  89.8 us (35%)
  blocking collectives  59.1 us (23%)
  waiting for transfers between devices  48.4 us (19%)
  starting transfers between devices  33.2 us (13%)
  local copies, waits for them, and re-layouts  25.1 us (10%)
  other arithmetic  3.47 us (1%)
    pallas_call x4, Pallas kernels, attend(): pl.pallas_call(lambda *refs: attend_kernel(*refs, first=first, last=last,...  36.7 us
    ppermute x20, waiting for transfers between devices, turn(): lax.ppermute(value, axis, [(i, (i + by) % size) for i in range(size)])  35.2 us
    pallas_call x2, Pallas kernels, mlp(): pl.pallas_call(lambda *refs: mlp_kernel(*refs, pieces=len(pieces)), out_s...  31.4 us
    ppermute x20, starting transfers between devices, turn(): lax.ppermute(value, axis, [(i, (i + by) % size) for i in range(size)])  27 us
    all_to_all x1, blocking collectives, local(): mine = lax.all_to_all(heads, ('y', 'xh'), 0, 0, tiled=True)  24.2 us
    all_to_all x1, blocking collectives, local(): lax.all_to_all(outgoing, ('y', 'xh', 'xl', 'c'), split_axis=0, concat_axi...  21.1 us
    unnamed x54, local copies, waits for them, and re-layouts  14.9 us
    all_to_all x1, blocking collectives, local(): attended = lax.all_to_all(done, ('y', 'xh'), 0, 0, tiled=True)  13.7 us
  transfers between devices with their start and end apart: 23, of which 9 were waited for; matrix products, arithmetic and copies ran while one was open for 4% of the time, Pallas kernels for 22%

profile of v1, /device:TPU:1, one launch (start us, length us, event | category | flops | bytes accessed | tf_op | source)
XLA Modules:
  0.0 259.3 jit_solution(4942084578204510727)
XLA Ops:
  0.0 8.9 %copy.17.refs_2_ = bf16[1408,2112]{1,0:T(8,128)(2,1)} copy(bf16[1408,2112]{0,1:T(8,128)(2,1)} %param.17) | data formatting | bytes 11894784 | tf_op args[4]
  8.9 6.8 %qkv.1 = bf16[8,272,256]{2,1,0:T(8,128)(2,1)} custom-call(bf16[256,1408]{1,0:T(8,128)(2,1)} %x_ref.1, s32[1,256]{1,0:T(1,128)} %bitcast.8, bf16[1408,2112]{1,0:T(8,128)(2,1)} %copy.17.refs_2_), custom_call_target="tpu_custom_call" | custom-call | tf_op jit(solution)/shard_map/qkv/pallas_call | solution.py:79
  15.7 24.2 %all_to_all.25.refs_0_ = bf16[8,272,256]{2,1,0:T(8,128)(2,1)S(1)} all-to-all(bf16[8,272,256]{2,1,0:T(8,128)(2,1)} %qkv.1), channel_id=1, replica_groups=mesh['grp'=4,'y'=4,'xh'=2,'xl'=2,'c'=2] {'y','xh'}, dimensions={0} | all-to-all | bytes 2228224 | tf_op jit(solution)/shard_map/all_to_all | solution.py:406
  39.9 0.5 collective-permute-start
  40.4 2.5 collective-permute-start.2
  42.9 13.1 %collective-permute-done.refs_1_ = bf16[8,184,256]{2,1,0:T(8,128)(2,1)S(1)} collective-permute-done((bf16[8,184,256]{2,1,0:T(8,128)(2,1)S(1)}, bf16[8,184,256]{2,1,0:T(8,128)(2,1)S(1)}, u32[]{:S(2)}, u32[]{:S(2)}) %collective-permute-start) | collective-permute-done | bytes 753696 | tf_op jit(solution)/shard_map/ppermute | solution.py:362
  56.0 3.2 %collective-permute-start.1 = (bf16[8,184,256]{2,1,0:T(8,128)(2,1)S(1)}, bf16[8,184,256]{2,1,0:T(8,128)(2,1)S(1)}, u32[]{:S(2)}, u32[]{:S(2)}) collective-permute-start(bf16[8,184,256]{2,1,0:T(8,128)(2,1)S(1)} %collective-permute-done.refs_1_), channel_id=1, source_target_pairs={{0,1},{1,0},{2,3},{3,2},{4,5},{5,4},{6,7},{7,6},{8,9},{9,8},{10,11... | collective-permute-start | bytes 2261000 | tf_op jit(solution)/shard_map/ppermute | solution.py:362
  59.2 8.7 %attend.4.refs_2_ = f32[2048,128]{1,0:T(8,128)} custom-call(bf16[8,272,256]{2,1,0:T(8,128)(2,1)} %copy-done, bf16[8,184,256]{2,1,0:T(8,128)(2,1)} %copy-done.3), custom_call_target="tpu_custom_call" | custom-call | tf_op jit(solution)/shard_map/attend/pallas_call | solution.py:157
  67.9 0.9 copy-done.14
  68.8 9.1 %attend.5.refs_2_ = f32[2048,128]{1,0:T(8,128)} custom-call(bf16[8,272,256]{2,1,0:T(8,128)(2,1)} %copy-done, bf16[8,184,256]{2,1,0:T(8,128)(2,1)} %copy-done.14, f32[2048,128]{1,0:T(8,128)} %attend.4.refs_2_), custom_call_target="tpu_custom_call" | custom-call | tf_op jit(solution)/shard_map/attend/pallas_call | solution.py:157
  77.9 9.1 %attend.6.refs_2_ = f32[2048,128]{1,0:T(8,128)} custom-call(bf16[8,272,256]{2,1,0:T(8,128)(2,1)} %copy-done, bf16[8,184,256]{2,1,0:T(8,128)(2,1)} %copy-done.13, f32[2048,128]{1,0:T(8,128)} %attend.5.refs_2_), custom_call_target="tpu_custom_call" | custom-call | tf_op jit(solution)/shard_map/attend/pallas_call | solution.py:157
  87.0 0.9 copy-done.12
  87.8 9.9 %attend.7 = bf16[8,88,256]{2,1,0:T(8,128)(2,1)} custom-call(bf16[8,272,256]{2,1,0:T(8,128)(2,1)} %copy-done, bf16[8,184,256]{2,1,0:T(8,128)(2,1)} %copy-done.12, f32[2048,128]{1,0:T(8,128)} %attend.6.refs_2_), custom_call_target="tpu_custom_call" | custom-call | tf_op jit(solution)/shard_map/attend/pallas_call | solution.py:157
  97.7 13.7 %all_to_all.26.att_ref = bf16[8,88,256]{2,1,0:T(8,128)(2,1)} all-to-all(bf16[8,88,256]{2,1,0:T(8,128)(2,1)} %attend.7), channel_id=1, replica_groups=mesh['grp'=4,'y'=4,'xh'=2,'xl'=2,'c'=2] {'y','xh'}, dimensions={0} | all-to-all | bytes 720896 | tf_op jit(solution)/shard_map/all_to_all | solution.py:415
  111.4 3.9 %project.1 = (bf16[256,1408]{1,0:T(8,128)(2,1)}, bf16[256,1408]{1,0:T(8,128)(2,1)}) custom-call(bf16[8,88,256]{2,1,0:T(8,128)(2,1)} %all_to_all.26.att_ref, bf16[256,1408]{1,0:T(8,128)(2,1)} %x_ref.1, bf16[704,1408]{1,0:T(8,128)(2,1)} %w_ref.1), custom_call_target="tpu_custom_call" | custom-call | tf_op jit(solution)/shard_map/project/pallas_call | solution.py:184
  115.4 1.2 fusion.2
  116.6 1.7 collective-permute-start.11
  118.3 2.2 collective-permute-start.12
  120.5 2.7 %collective-permute-start.4 = (bf16[128,1408]{1,0:T(8,128)(2,1)S(1)}, bf16[128,1408]{1,0:T(8,128)(2,1)S(1)}, u32[]{:S(2)}, u32[]{:S(2)}) collective-permute-start(bf16[128,1408]{1,0:T(8,128)(2,1)S(1)} %get-tuple-element.22.refs_0_), channel_id=1, source_target_pairs={{0,96},{32,0},{64,32},{96,64},{1,97},{33,1},{65,33},{97,65},{2,98}... | collective-permute-start | bytes 1081352 | tf_op jit(solution)/shard_map/ppermute | solution.py:367
  123.2 4.7 %collective-permute-done.11.refs_1_ = bf16[128,1408]{1,0:T(8,128)(2,1)S(1)} collective-permute-done((bf16[128,1408]{1,0:T(8,128)(2,1)S(1)}, bf16[128,1408]{1,0:T(8,128)(2,1)S(1)}, u32[]{:S(2)}, u32[]{:S(2)}) %collective-permute-start.11) | collective-permute-done | bytes 360480 | tf_op jit(solution)/shard_map/ppermute | solution.py:367
  127.9 0.3 collective-permute-start.13
  128.2 2.7 %collective-permute-start.14 = (bf16[64,1408]{1,0:T(8,128)(2,1)S(1)}, bf16[64,1408]{1,0:T(8,128)(2,1)S(1)}, u32[]{:S(2)}, u32[]{:S(2)}) collective-permute-start(bf16[64,1408]{1,0:T(8,128)(2,1)S(1)} %slice.121), channel_id=1, source_target_pairs={{0,96},{32,0},{64,32},{96,64},{1,97},{33,1},{65,33},{97,65},{2,98}... | collective-permute-start | bytes 540680 | tf_op jit(solution)/shard_map/ppermute | solution.py:367
  130.9 0.6 reshape.34.refs_6_
  131.5 4.1 %collective-permute-done.3.refs_1_ = bf16[128,1408]{1,0:T(8,128)(2,1)S(1)} collective-permute-done((bf16[128,1408]{1,0:T(8,128)(2,1)S(1)}, bf16[128,1408]{1,0:T(8,128)(2,1)S(1)}, u32[]{:S(2)}, u32[]{:S(2)}) %collective-permute-start.3) | collective-permute-done | bytes 360480 | tf_op jit(solution)/shard_map/ppermute | solution.py:367
  135.8 2.7 %collective-permute-start.6 = (bf16[64,1408]{1,0:T(8,128)(2,1)S(1)}, bf16[64,1408]{1,0:T(8,128)(2,1)S(1)}, u32[]{:S(2)}, u32[]{:S(2)}) collective-permute-start(bf16[64,1408]{1,0:T(8,128)(2,1)S(1)} %slice.112), channel_id=1, source_target_pairs={{0,96},{32,0},{64,32},{96,64},{1,97},{33,1},{65,33},{97,65},{2,98}... | collective-permute-start | bytes 540680 | tf_op jit(solution)/shard_map/ppermute | solution.py:367
  138.5 1.0 collective-permute-done.13.refs_3_
  139.5 0.7 copy-done.19
  140.2 0.6 copy-done.20
  140.8 15.7 %mlp.3 = bf16[512,1408]{1,0:T(8,128)(2,1)} custom-call(bf16[128,1408]{1,0:T(8,128)(2,1)} %copy-done.7, bf16[128,1408]{1,0:T(8,128)(2,1)} %copy-done.10, bf16[128,1408]{1,0:T(8,128)(2,1)} %copy-done.11, bf16[64,1408]{1,0:T(8,128)(2,1)} %copy-done.19, bf16[64,1408]{1,0:T(8,128)(2,1)} %copy-done.20, bf16[1536,1408]{1,0:T(8,128)(2,1)} %refs_5_.3, ...), custom_call_target="tpu_custom_call" | custom-call | tf_op jit(solution)/shard_map/mlp/pallas_call | solution.py:227
  156.6 1.2 fusion
  157.9 2.7 %collective-permute-start.17 = (bf16[64,1408]{1,0:T(8,128)(2,1)S(1)}, bf16[64,1408]{1,0:T(8,128)(2,1)}, u32[]{:S(2)}, u32[]{:S(2)}) collective-permute-start(bf16[64,1408]{1,0:T(8,128)(2,1)S(1)} %get-tuple-element.10), channel_id=1, source_target_pairs={{0,96},{32,0},{64,32},{96,64},{1,97},{33,1},{65,33},{97,65},{2,98}... | collective-permute-start | bytes 540680 | tf_op jit(solution)/shard_map/ppermute | solution.py:367
  160.6 0.7 copy-done.17
  161.3 0.7 copy-done.18
  161.9 15.7 %mlp.2 = bf16[512,1408]{1,0:T(8,128)(2,1)} custom-call(bf16[128,1408]{1,0:T(8,128)(2,1)} %copy-done.6, bf16[128,1408]{1,0:T(8,128)(2,1)} %copy-done.8, bf16[128,1408]{1,0:T(8,128)(2,1)} %copy-done.9, bf16[64,1408]{1,0:T(8,128)(2,1)} %copy-done.17, bf16[64,1408]{1,0:T(8,128)(2,1)} %copy-done.18, bf16[1536,1408]{1,0:T(8,128)(2,1)} %refs_5_.3, ...), custom_call_target="tpu_custom_call" | custom-call | tf_op jit(solution)/shard_map/mlp/pallas_call | solution.py:227
  177.6 1.3 fusion.1
  179.1 2.7 %collective-permute-start.9 = (bf16[64,1408]{1,0:T(8,128)(2,1)S(1)}, bf16[64,1408]{1,0:T(8,128)(2,1)S(1)}, u32[]{:S(2)}, u32[]{:S(2)}) collective-permute-start(bf16[64,1408]{1,0:T(8,128)(2,1)S(1)} %get-tuple-element.16), channel_id=1, source_target_pairs={{0,96},{32,0},{64,32},{96,64},{1,97},{33,1},{65,33},{97,65},{2,98}... | collective-permute-start | bytes 540680 | tf_op jit(solution)/shard_map/ppermute | solution.py:367
  181.7 1.0 add_convert_fusion
  182.9 0.8 pad_maximum_fusion.2
  183.7 1.5 collective-permute-start.16
  185.2 0.1 add_convert_fusion.2
  185.3 0.8 pad_maximum_fusion.1
  186.1 2.1 collective-permute-start.10
  188.2 0.8 pad_maximum_fusion
  189.0 0.7 copy.18.refs_4_
  189.7 0.7 reshape.33.refs_3_
  190.4 0.6 reshape.31.refs_1_
  191.0 0.6 reshape.32.refs_2_
  191.6 0.8 slice.122.refs_8_
  192.4 0.8 slice.113.refs_5_
  193.1 0.2 collective-permute-done.16.refs_9_
  193.3 6.9 %collective-permute-done.10.refs_7_ = bf16[128,1408]{1,0:T(8,128)(2,1)} collective-permute-done((bf16[128,1408]{1,0:T(8,128)(2,1)}, bf16[128,1408]{1,0:T(8,128)(2,1)}, u32[]{:S(2)}, u32[]{:S(2)}) %collective-permute-start.10) | collective-permute-done | bytes 360480 | tf_op jit(solution)/shard_map/ppermute | solution.py:367
  200.2 0.3 collective-permute-done.8.refs_6_
  200.5 3.9 %merge.1.refs_1_ = bf16[64,5760]{1,0:T(8,128)(2,1)} custom-call(bf16[256,1408]{1,0:T(8,128)(2,1)} %get-tuple-element.7.refs_0_, f32[1,1408]{1,0:T(1,128)} %reshape.31.refs_1_, f32[1,1408]{1,0:T(1,128)} %reshape.32.refs_2_, s32[64,4]{1,0:T(8,128)} %reshape.33.refs_3_, s32[64,1]{1,0:T(8,128)} %copy.18.refs_4_, bf16[128,1408]{1,0:T(8,128)(2,1)} %slice.113.refs_5_, ...), custom_call_target="tpu_custom_call" | custom-call | tf_op jit(solution)/shard_map/merge/pallas_call | solution.py:282
  204.4 2.7 %collective-permute-start.19 = (bf16[64,5760]{1,0:T(8,128)(2,1)}, bf16[64,5760]{1,0:T(8,128)(2,1)S(1)}, u32[]{:S(2)}, u32[]{:S(2)}) collective-permute-start(bf16[64,5760]{1,0:T(8,128)(2,1)} %merge.1.refs_1_), channel_id=1, source_target_pairs={{0,96},{32,0},{64,32},{96,64},{1,97},{33,1},{65,33},{97,65},{2,98}... | collective-permute-start | bytes 2211848 | tf_op jit(solution)/shard_map/ppermute | solution.py:367
  207.1 11.9 %collective-permute-done.20.refs_5_ = bf16[64,5760]{1,0:T(8,128)(2,1)S(1)} collective-permute-done((bf16[64,5760]{1,0:T(8,128)(2,1)}, bf16[64,5760]{1,0:T(8,128)(2,1)S(1)}, u32[]{:S(2)}, u32[]{:S(2)}) %collective-permute-start.20) | collective-permute-done | bytes 737312 | tf_op jit(solution)/shard_map/ppermute | solution.py:367
  219.2 2.7 %collective-permute-start.22 = (bf16[32,5760]{1,0:T(8,128)(2,1)S(1)}, bf16[32,5760]{1,0:T(8,128)(2,1)S(1)}, u32[]{:S(2)}, u32[]{:S(2)}) collective-permute-start(bf16[32,5760]{1,0:T(8,128)(2,1)S(1)} %slice.130), channel_id=1, source_target_pairs={{0,96},{32,0},{64,32},{96,64},{1,97},{33,1},{65,33},{97,65},{2,98}... | collective-permute-start | bytes 1105928 | tf_op jit(solution)/shard_map/ppermute | solution.py:367
  221.9 6.1 %collective-permute-done.21.refs_3_ = bf16[32,5760]{1,0:T(8,128)(2,1)S(1)} collective-permute-done((bf16[32,5760]{1,0:T(8,128)(2,1)S(1)}, bf16[32,5760]{1,0:T(8,128)(2,1)S(1)}, u32[]{:S(2)}, u32[]{:S(2)}) %collective-permute-start.21) | collective-permute-done | bytes 368672 | tf_op jit(solution)/shard_map/ppermute | solution.py:367
  228.0 0.7 copy-done.15
  228.7 0.1 copy-done.16
  228.9 7.0 %embed.1 = bf16[512,512]{1,0:T(8,128)(2,1)} custom-call(s32[1]{0:T(128)} %bitcast.refs_0_, bf16[64,5760]{1,0:T(8,128)(2,1)} %merge.1.refs_1_, bf16[64,5760]{1,0:T(8,128)(2,1)} %copy-done.5, bf16[32,5760]{1,0:T(8,128)(2,1)} %copy-done.15, bf16[32,5760]{1,0:T(8,128)(2,1)} %copy-done.16, bf16[64,5760]{1,0:T(8,128)(2,1)} %copy-done.4, ...), custom_call_target="tpu_custom_call" | custom-call | tf_op jit(solution)/shard_map/embed/pallas_call | solution.py:342
  235.9 1.2 reshape.36
  237.1 21.1 %all_to_all.27 = bf16[32,4,4,512]{3,2,1,0:T(4,128)(2,1)S(1)} all-to-all(bf16[32,4,4,512]{3,2,1,0:T(4,128)(2,1)S(1)} %reshape.36), channel_id=1, replica_groups=mesh['grp'=4,'y'=4,'xh'=2,'xl'=2,'c'=2] {'y','xh','xl','c'}, dimensions={0} | all-to-all | bytes 1048576 | tf_op jit(solution)/shard_map/all_to_all | solution.py:442
  258.2 0.2 copy.19
  258.4 0.9 reshape.37
  (74 shorter events, 0.7 us)
Async XLA Ops:
  39.8 19.4 %copy-start = (bf16[8,272,256]{2,1,0:T(8,128)(2,1)}, bf16[8,272,256]{2,1,0:T(8,128)(2,1)S(1)}, u32[]{:S(2)}) copy-start(bf16[8,272,256]{2,1,0:T(8,128)(2,1)S(1)} %all_to_all.25.refs_0_) | copy-start | bytes 3342340
  39.9 19.4 %copy-start.3 = (bf16[8,184,256]{2,1,0:T(8,128)(2,1)}, bf16[8,184,256]{2,1,0:T(8,128)(2,1)S(1)}, u32[]{:S(2)}) copy-start(bf16[8,184,256]{2,1,0:T(8,128)(2,1)S(1)} %slice.110.refs_1_) | copy-start | bytes 2260996
  39.9 16.1 %collective-permute-start = (bf16[8,184,256]{2,1,0:T(8,128)(2,1)S(1)}, bf16[8,184,256]{2,1,0:T(8,128)(2,1)S(1)}, u32[]{:S(2)}, u32[]{:S(2)}) collective-permute-start(bf16[8,184,256]{2,1,0:T(8,128)(2,1)S(1)} %slice.110.refs_1_), channel_id=1, source_target_pairs={{0,2},{2,0},{1,3},{3,1},{4,6},{6,4},{5,7},{7,5},{8,10},{10,8},{9,1... | collective-permute-start | bytes 2261000 | tf_op jit(solution)/shard_map/ppermute | solution.py:362
  40.4 27.5 %collective-permute-start.2 = (bf16[8,184,256]{2,1,0:T(8,128)(2,1)S(1)}, bf16[8,184,256]{2,1,0:T(8,128)(2,1)S(1)}, u32[]{:S(2)}, u32[]{:S(2)}) collective-permute-start(bf16[8,184,256]{2,1,0:T(8,128)(2,1)S(1)} %slice.110.refs_1_), channel_id=1, source_target_pairs={{0,1},{1,0},{2,3},{3,2},{4,5},{5,4},{6,7},{7,6},{8,9},{9,8},{10,11... | collective-permute-start | bytes 2261000 | tf_op jit(solution)/shard_map/ppermute | solution.py:362
  56.0 11.9 %copy-start.13 = (bf16[8,184,256]{2,1,0:T(8,128)(2,1)}, bf16[8,184,256]{2,1,0:T(8,128)(2,1)S(1)}, u32[]{:S(2)}) copy-start(bf16[8,184,256]{2,1,0:T(8,128)(2,1)S(1)} %collective-permute-done.refs_1_) | copy-start | bytes 2260996
  56.0 30.9 %collective-permute-start.1 = (bf16[8,184,256]{2,1,0:T(8,128)(2,1)S(1)}, bf16[8,184,256]{2,1,0:T(8,128)(2,1)S(1)}, u32[]{:S(2)}, u32[]{:S(2)}) collective-permute-start(bf16[8,184,256]{2,1,0:T(8,128)(2,1)S(1)} %collective-permute-done.refs_1_), channel_id=1, source_target_pairs={{0,1},{1,0},{2,3},{3,2},{4,5},{5,4},{6,7},{7,6},{8,9},{9,8},{10,11... | collective-permute-start | bytes 2261000 | tf_op jit(solution)/shard_map/ppermute | solution.py:362
  67.9 0.9 copy-start.14
  86.9 0.9 copy-start.12
  115.4 15.6 %copy-start.23 = (bf16[1536]{0:T(1024)(128)(2,1)S(1)}, bf16[1536]{0:T(1024)(128)(2,1)}, u32[]{:S(2)}) copy-start(bf16[1536]{0:T(1024)(128)(2,1)} %param.20) | copy-start | bytes 9220
  116.5 23.0 %copy-start.7 = (bf16[128,1408]{1,0:T(8,128)(2,1)}, bf16[128,1408]{1,0:T(8,128)(2,1)S(1)}, u32[]{:S(2)}) copy-start(bf16[128,1408]{1,0:T(8,128)(2,1)S(1)} %get-tuple-element.21.refs_0_) | copy-start | bytes 1081348
  116.6 40.0 %copy-start.6 = (bf16[128,1408]{1,0:T(8,128)(2,1)}, bf16[128,1408]{1,0:T(8,128)(2,1)S(1)}, u32[]{:S(2)}) copy-start(bf16[128,1408]{1,0:T(8,128)(2,1)S(1)} %get-tuple-element.22.refs_0_) | copy-start | bytes 1081348
  116.6 11.3 %collective-permute-start.11 = (bf16[128,1408]{1,0:T(8,128)(2,1)S(1)}, bf16[128,1408]{1,0:T(8,128)(2,1)S(1)}, u32[]{:S(2)}, u32[]{:S(2)}) collective-permute-start(bf16[128,1408]{1,0:T(8,128)(2,1)S(1)} %get-tuple-element.21.refs_0_), channel_id=1, source_target_pairs={{0,32},{32,64},{64,96},{96,0},{1,33},{33,65},{65,97},{97,1},{2,34}... | collective-permute-start | bytes 1081352 | tf_op jit(solution)/shard_map/ppermute | solution.py:367
  118.3 9.9 %collective-permute-start.12 = (bf16[128,1408]{1,0:T(8,128)(2,1)S(1)}, bf16[128,1408]{1,0:T(8,128)(2,1)S(1)}, u32[]{:S(2)}, u32[]{:S(2)}) collective-permute-start(bf16[128,1408]{1,0:T(8,128)(2,1)S(1)} %get-tuple-element.21.refs_0_), channel_id=1, source_target_pairs={{0,96},{32,0},{64,32},{96,64},{1,97},{33,1},{65,33},{97,65},{2,98}... | collective-permute-start | bytes 1081352 | tf_op jit(solution)/shard_map/ppermute | solution.py:367
  120.5 15.1 %collective-permute-start.3 = (bf16[128,1408]{1,0:T(8,128)(2,1)S(1)}, bf16[128,1408]{1,0:T(8,128)(2,1)S(1)}, u32[]{:S(2)}, u32[]{:S(2)}) collective-permute-start(bf16[128,1408]{1,0:T(8,128)(2,1)S(1)} %get-tuple-element.22.refs_0_), channel_id=1, source_target_pairs={{0,32},{32,64},{64,96},{96,0},{1,33},{33,65},{65,97},{97,1},{2,34}... | collective-permute-start | bytes 1081352 | tf_op jit(solution)/shard_map/ppermute | solution.py:367
  120.5 15.2 %collective-permute-start.4 = (bf16[128,1408]{1,0:T(8,128)(2,1)S(1)}, bf16[128,1408]{1,0:T(8,128)(2,1)S(1)}, u32[]{:S(2)}, u32[]{:S(2)}) collective-permute-start(bf16[128,1408]{1,0:T(8,128)(2,1)S(1)} %get-tuple-element.22.refs_0_), channel_id=1, source_target_pairs={{0,96},{32,0},{64,32},{96,64},{1,97},{33,1},{65,33},{97,65},{2,98}... | collective-permute-start | bytes 1081352 | tf_op jit(solution)/shard_map/ppermute | solution.py:367
  127.9 11.6 %copy-start.10 = (bf16[128,1408]{1,0:T(8,128)(2,1)}, bf16[128,1408]{1,0:T(8,128)(2,1)S(1)}, u32[]{:S(2)}) copy-start(bf16[128,1408]{1,0:T(8,128)(2,1)S(1)} %collective-permute-done.11.refs_1_) | copy-start | bytes 1081348
  127.9 11.6 %collective-permute-start.13 = (bf16[64,1408]{1,0:T(8,128)(2,1)S(1)}, bf16[64,1408]{1,0:T(8,128)(2,1)S(1)}, u32[]{:S(2)}, u32[]{:S(2)}) collective-permute-start(bf16[64,1408]{1,0:T(8,128)(2,1)S(1)} %slice.120), channel_id=1, source_target_pairs={{0,32},{32,64},{64,96},{96,0},{1,33},{33,65},{65,97},{97,1},{2,34}... | collective-permute-start | bytes 540680 | tf_op jit(solution)/shard_map/ppermute | solution.py:367
  128.2 11.3 %copy-start.11 = (bf16[128,1408]{1,0:T(8,128)(2,1)}, bf16[128,1408]{1,0:T(8,128)(2,1)S(1)}, u32[]{:S(2)}) copy-start(bf16[128,1408]{1,0:T(8,128)(2,1)S(1)} %collective-permute-done.12.refs_2_) | copy-start | bytes 1081348
  128.2 11.3 %collective-permute-start.14 = (bf16[64,1408]{1,0:T(8,128)(2,1)S(1)}, bf16[64,1408]{1,0:T(8,128)(2,1)S(1)}, u32[]{:S(2)}, u32[]{:S(2)}) collective-permute-start(bf16[64,1408]{1,0:T(8,128)(2,1)S(1)} %slice.121), channel_id=1, source_target_pairs={{0,96},{32,0},{64,32},{96,64},{1,97},{33,1},{65,33},{97,65},{2,98}... | collective-permute-start | bytes 540680 | tf_op jit(solution)/shard_map/ppermute | solution.py:367
  135.6 20.9 %copy-start.8 = (bf16[128,1408]{1,0:T(8,128)(2,1)}, bf16[128,1408]{1,0:T(8,128)(2,1)S(1)}, u32[]{:S(2)}) copy-start(bf16[128,1408]{1,0:T(8,128)(2,1)S(1)} %collective-permute-done.3.refs_1_) | copy-start | bytes 1081348
  135.6 24.9 %collective-permute-start.5 = (bf16[64,1408]{1,0:T(8,128)(2,1)S(1)}, bf16[64,1408]{1,0:T(8,128)(2,1)S(1)}, u32[]{:S(2)}, u32[]{:S(2)}) collective-permute-start(bf16[64,1408]{1,0:T(8,128)(2,1)S(1)} %slice.111), channel_id=1, source_target_pairs={{0,32},{32,64},{64,96},{96,0},{1,33},{33,65},{65,97},{97,1},{2,34}... | collective-permute-start | bytes 540680 | tf_op jit(solution)/shard_map/ppermute | solution.py:367
  135.7 20.8 %copy-start.9 = (bf16[128,1408]{1,0:T(8,128)(2,1)}, bf16[128,1408]{1,0:T(8,128)(2,1)S(1)}, u32[]{:S(2)}) copy-start(bf16[128,1408]{1,0:T(8,128)(2,1)S(1)} %collective-permute-done.4.refs_2_) | copy-start | bytes 1081348
  135.8 24.8 %collective-permute-start.6 = (bf16[64,1408]{1,0:T(8,128)(2,1)S(1)}, bf16[64,1408]{1,0:T(8,128)(2,1)S(1)}, u32[]{:S(2)}, u32[]{:S(2)}) collective-permute-start(bf16[64,1408]{1,0:T(8,128)(2,1)S(1)} %slice.112), channel_id=1, source_target_pairs={{0,96},{32,0},{64,32},{96,64},{1,97},{33,1},{65,33},{97,65},{2,98}... | collective-permute-start | bytes 540680 | tf_op jit(solution)/shard_map/ppermute | solution.py:367
  139.5 0.7 copy-start.19
  140.2 0.7 copy-start.20
  157.8 23.9 %collective-permute-start.15 = (bf16[64,1408]{1,0:T(8,128)(2,1)S(1)}, bf16[64,1408]{1,0:T(8,128)(2,1)S(1)}, u32[]{:S(2)}, u32[]{:S(2)}) collective-permute-start(bf16[64,1408]{1,0:T(8,128)(2,1)S(1)} %get-tuple-element.12), channel_id=1, source_target_pairs={{0,32},{32,64},{64,96},{96,0},{1,33},{33,65},{65,97},{97,1},{2,34}... | collective-permute-start | bytes 540680 | tf_op jit(solution)/shard_map/ppermute | solution.py:367
  157.9 23.8 %collective-permute-start.17 = (bf16[64,1408]{1,0:T(8,128)(2,1)S(1)}, bf16[64,1408]{1,0:T(8,128)(2,1)}, u32[]{:S(2)}, u32[]{:S(2)}) collective-permute-start(bf16[64,1408]{1,0:T(8,128)(2,1)S(1)} %get-tuple-element.10), channel_id=1, source_target_pairs={{0,96},{32,0},{64,32},{96,64},{1,97},{33,1},{65,33},{97,65},{2,98}... | collective-permute-start | bytes 540680 | tf_op jit(solution)/shard_map/ppermute | solution.py:367
  160.6 0.7 copy-start.17
  161.3 0.7 copy-start.18
  177.6 4.1 %copy-start.1 = (bf16[512,1408]{1,0:T(8,128)(2,1)S(1)}, bf16[512,1408]{1,0:T(8,128)(2,1)}, u32[]{:S(2)}) copy-start(bf16[512,1408]{1,0:T(8,128)(2,1)} %mlp.3) | copy-start | bytes 4325380
  179.0 6.2 %copy-start.2 = (bf16[512,1408]{1,0:T(8,128)(2,1)S(1)}, bf16[512,1408]{1,0:T(8,128)(2,1)}, u32[]{:S(2)}) copy-start(bf16[512,1408]{1,0:T(8,128)(2,1)} %mlp.2) | copy-start | bytes 4325380
  179.0 6.2 %collective-permute-start.7 = (bf16[64,1408]{1,0:T(8,128)(2,1)S(1)}, bf16[64,1408]{1,0:T(8,128)(2,1)S(1)}, u32[]{:S(2)}, u32[]{:S(2)}) collective-permute-start(bf16[64,1408]{1,0:T(8,128)(2,1)S(1)} %get-tuple-element.18), channel_id=1, source_target_pairs={{0,32},{32,64},{64,96},{96,0},{1,33},{33,65},{65,97},{97,1},{2,34}... | collective-permute-start | bytes 540680 | tf_op jit(solution)/shard_map/ppermute | solution.py:367
  179.1 6.1 %collective-permute-start.9 = (bf16[64,1408]{1,0:T(8,128)(2,1)S(1)}, bf16[64,1408]{1,0:T(8,128)(2,1)S(1)}, u32[]{:S(2)}, u32[]{:S(2)}) collective-permute-start(bf16[64,1408]{1,0:T(8,128)(2,1)S(1)} %get-tuple-element.16), channel_id=1, source_target_pairs={{0,96},{32,0},{64,32},{96,64},{1,97},{33,1},{65,33},{97,65},{2,98}... | collective-permute-start | bytes 540680 | tf_op jit(solution)/shard_map/ppermute | solution.py:367
  182.8 10.3 %collective-permute-start.18 = (bf16[128,1408]{1,0:T(8,128)(2,1)S(1)}, bf16[128,1408]{1,0:T(8,128)(2,1)}, u32[]{:S(2)}, u32[]{:S(2)}) collective-permute-start(bf16[128,1408]{1,0:T(8,128)(2,1)S(1)} %pad_maximum_fusion.3), channel_id=1, source_target_pairs={{0,96},{32,0},{64,32},{96,64},{1,97},{33,1},{65,33},{97,65},{2,98}... | collective-permute-start | bytes 1081352 | tf_op jit(solution)/shard_map/ppermute | solution.py:367
  183.7 5.3 %copy-start.25 = (s32[64,1]{0,1:T(1,128)S(1)}, s32[64,1]{0,1:T(1,128)}, u32[]{:S(2)}) copy-start(s32[64,1]{0,1:T(1,128)} %param.16) | copy-start | bytes 772
  183.7 6.0 %copy-start.24 = (s32[256]{0:T(256)S(1)}, s32[256]{0:T(256)}, u32[]{:S(2)}) copy-start(s32[256]{0:T(256)} %param.15) | copy-start | bytes 3076
  183.7 6.7 %copy-start.21 = (f32[1408]{0:T(1024)S(1)}, f32[1408]{0:T(1024)}, u32[]{:S(2)}) copy-start(f32[1408]{0:T(1024)} %param.22) | copy-start | bytes 16900
  183.7 7.3 %copy-start.22 = (f32[1408]{0:T(1024)S(1)}, f32[1408]{0:T(1024)}, u32[]{:S(2)}) copy-start(f32[1408]{0:T(1024)} %param.23) | copy-start | bytes 16900
  183.7 9.6 %collective-permute-start.16 = (bf16[128,1408]{1,0:T(8,128)(2,1)}, bf16[128,1408]{1,0:T(8,128)(2,1)}, u32[]{:S(2)}, u32[]{:S(2)}) collective-permute-start(bf16[128,1408]{1,0:T(8,128)(2,1)} %pad_maximum_fusion.2), channel_id=1, source_target_pairs={{0,32},{32,64},{64,96},{96,0},{1,33},{33,65},{65,97},{97,1},{2,34}... | collective-permute-start | bytes 1081352 | tf_op jit(solution)/shard_map/ppermute | solution.py:367
  186.1 14.1 %collective-permute-start.10 = (bf16[128,1408]{1,0:T(8,128)(2,1)}, bf16[128,1408]{1,0:T(8,128)(2,1)}, u32[]{:S(2)}, u32[]{:S(2)}) collective-permute-start(bf16[128,1408]{1,0:T(8,128)(2,1)} %pad_maximum_fusion.1), channel_id=1, source_target_pairs={{0,96},{32,0},{64,32},{96,64},{1,97},{33,1},{65,33},{97,65},{2,98}... | collective-permute-start | bytes 1081352 | tf_op jit(solution)/shard_map/ppermute | solution.py:367
  189.0 11.5 %collective-permute-start.8 = (bf16[128,1408]{1,0:T(8,128)(2,1)}, bf16[128,1408]{1,0:T(8,128)(2,1)}, u32[]{:S(2)}, u32[]{:S(2)}) collective-permute-start(bf16[128,1408]{1,0:T(8,128)(2,1)} %pad_maximum_fusion), channel_id=1, source_target_pairs={{0,32},{32,64},{64,96},{96,0},{1,33},{33,65},{65,97},{97,1},{2,34}... | collective-permute-start | bytes 1081352 | tf_op jit(solution)/shard_map/ppermute | solution.py:367
  204.4 14.6 %collective-permute-start.20 = (bf16[64,5760]{1,0:T(8,128)(2,1)}, bf16[64,5760]{1,0:T(8,128)(2,1)S(1)}, u32[]{:S(2)}, u32[]{:S(2)}) collective-permute-start(bf16[64,5760]{1,0:T(8,128)(2,1)} %merge.1.refs_1_), channel_id=1, source_target_pairs={{0,32},{32,64},{64,96},{96,0},{1,33},{33,65},{65,97},{97,1},{2,34}... | collective-permute-start | bytes 2211848 | tf_op jit(solution)/shard_map/ppermute | solution.py:367
  204.4 14.7 %collective-permute-start.19 = (bf16[64,5760]{1,0:T(8,128)(2,1)}, bf16[64,5760]{1,0:T(8,128)(2,1)S(1)}, u32[]{:S(2)}, u32[]{:S(2)}) collective-permute-start(bf16[64,5760]{1,0:T(8,128)(2,1)} %merge.1.refs_1_), channel_id=1, source_target_pairs={{0,96},{32,0},{64,32},{96,64},{1,97},{33,1},{65,33},{97,65},{2,98}... | collective-permute-start | bytes 2211848 | tf_op jit(solution)/shard_map/ppermute | solution.py:367
  219.0 9.0 %copy-start.4 = (bf16[64,5760]{1,0:T(8,128)(2,1)}, bf16[64,5760]{1,0:T(8,128)(2,1)S(1)}, u32[]{:S(2)}) copy-start(bf16[64,5760]{1,0:T(8,128)(2,1)S(1)} %collective-permute-done.20.refs_5_) | copy-start | bytes 2211844
  219.0 9.0 %collective-permute-start.21 = (bf16[32,5760]{1,0:T(8,128)(2,1)S(1)}, bf16[32,5760]{1,0:T(8,128)(2,1)S(1)}, u32[]{:S(2)}, u32[]{:S(2)}) collective-permute-start(bf16[32,5760]{1,0:T(8,128)(2,1)S(1)} %slice.129), channel_id=1, source_target_pairs={{0,32},{32,64},{64,96},{96,0},{1,33},{33,65},{65,97},{97,1},{2,34}... | collective-permute-start | bytes 1105928 | tf_op jit(solution)/shard_map/ppermute | solution.py:367
  219.1 8.9 %copy-start.5 = (bf16[64,5760]{1,0:T(8,128)(2,1)}, bf16[64,5760]{1,0:T(8,128)(2,1)S(1)}, u32[]{:S(2)}) copy-start(bf16[64,5760]{1,0:T(8,128)(2,1)S(1)} %collective-permute-done.19.refs_2_) | copy-start | bytes 2211844
  219.2 8.9 %collective-permute-start.22 = (bf16[32,5760]{1,0:T(8,128)(2,1)S(1)}, bf16[32,5760]{1,0:T(8,128)(2,1)S(1)}, u32[]{:S(2)}, u32[]{:S(2)}) collective-permute-start(bf16[32,5760]{1,0:T(8,128)(2,1)S(1)} %slice.130), channel_id=1, source_target_pairs={{0,96},{32,0},{64,32},{96,64},{1,97},{33,1},{65,33},{97,65},{2,98}... | collective-permute-start | bytes 1105928 | tf_op jit(solution)/shard_map/ppermute | solution.py:367
  228.0 0.7 copy-start.15
  228.0 0.9 copy-start.16

commit v2 on v1

v2 whole, which is shorter than its diff:
```python
import math

import jax
import jax.numpy as jnp
from jax import lax
from jax.experimental import pallas as pl
from jax.experimental.pallas import tpu as pltpu
from jax.sharding import Mesh
from jax.sharding import PartitionSpec as P

HEADS = 8
HD = 88
EXT = 8
NORM_EPS = 1e-06
LANES = 128
PAD = 16
F32 = jnp.float32
BF16 = jnp.bfloat16
VMEM_LIMIT = 60 * 1024 * 1024


def cparams(*semantics):
    return pltpu.CompilerParams(
        dimension_semantics=semantics or None, vmem_limit_bytes=VMEM_LIMIT
    )


def layer_norm(values):
    centred = values - jnp.mean(values, axis=-1, keepdims=True)
    return centred * lax.rsqrt(jnp.mean(centred * centred, axis=-1, keepdims=True) + NORM_EPS)


def dot(a, b, dims=(((1,), (0,)), ((), ()))):
    return lax.dot_general(a, b, dims, preferred_element_type=F32)


NT = (((1,), (1,)), ((), ()))


def cost(flops, size, transcendentals=0):
    return pl.CostEstimate(flops=flops, bytes_accessed=size, transcendentals=transcendentals)


def qkv_kernel(x_ref, seg_ref, w_hbm, out_ref, w_ref, sems):
    group = HEADS // 2 * HD
    count = w_ref.shape[0] // group
    copies = []
    for number in range(count):
        at = pl.ds(number * group, group)
        copies.append(pltpu.make_async_copy(w_hbm.at[at], w_ref.at[at], sems.at[number]))
        copies[-1].start()
    normed = layer_norm(x_ref[...].astype(F32)).astype(BF16)
    seg = seg_ref[...]
    high = seg // 64
    low = seg - high * 64
    tokens = seg.shape[1]
    row = lax.broadcasted_iota(jnp.int32, (EXT, tokens), 0)
    extra = jnp.where(row == 0, 1, jnp.where(row == 1, high, jnp.where(row == 2, low, 0)))
    extra = extra.astype(F32)
    scale = math.log2(math.e) / math.sqrt(HD)
    for number in range(count):
        copies[number].wait()
        part = dot(w_ref[number * group : (number + 1) * group, :], normed, NT)
        part = part.astype(BF16).astype(F32)
        kind = number // 2
        for i in range(HEADS // 2):
            head = number % 2 * (HEADS // 2) + i
            rows = part[i * HD : (i + 1) * HD]
            if kind == 2:
                out_ref[head, : HD + EXT] = jnp.concatenate([rows, extra], axis=0).astype(BF16)
                continue
            norm = lax.rsqrt(jnp.mean(rows * rows, axis=0, keepdims=True) + NORM_EPS)
            if kind == 0:
                out_ref[head, 2 * HD + EXT :] = (rows * (norm * scale)).astype(BF16)
            else:
                out_ref[head, HD + EXT : 2 * HD + EXT] = (rows * norm).astype(BF16)


def qkv(tokens, seg_ids, w_qkv):
    rows, width = tokens.shape
    return pl.pallas_call(
        qkv_kernel,
        out_shape=jax.ShapeDtypeStruct((HEADS, 3 * HD + EXT, rows), BF16),
        in_specs=[
            pl.BlockSpec(memory_space=pltpu.VMEM),
            pl.BlockSpec(memory_space=pltpu.VMEM),
            pl.BlockSpec(memory_space=pl.ANY),
        ],
        out_specs=pl.BlockSpec(memory_space=pltpu.VMEM),
        scratch_shapes=[
            pltpu.VMEM((w_qkv.shape[1], width), BF16),
            pltpu.SemaphoreType.DMA((6,)),
        ],
        compiler_params=cparams(),
        cost_estimate=cost(2 * rows * width * w_qkv.shape[1], 8 << 20),
        name="qkv",
    )(tokens, seg_ids.reshape(1, rows), w_qkv.T)


def attend_kernel(*refs, sets, first, last, key_block):
    q_ref = refs[0]
    kv_refs = refs[1 : 1 + sets]
    rest = refs[1 + sets :]
    if not first:
        acc_ref, rest = rest[0], rest[1:]
    out_ref, k_sc, v_sc, seg_sc = rest
    blocks, _, tokens = kv_refs[0].shape
    top = HD + EXT
    width = LANES - HD

    @pl.when(pl.program_id(0) == 0)
    def _():
        for number, kv_ref in enumerate(kv_refs):
            for j in range(blocks):
                start = (number * blocks + j) * tokens
                digits = kv_ref[j, :top].astype(F32)
                seg = digits[HD + 1 : HD + 2] * 64.0 + digits[HD + 2 : HD + 3]
                keys = kv_ref[j, top : top + HD].astype(F32)
                both = jnp.concatenate([keys, jnp.broadcast_to(seg, (width, tokens))], axis=0).T
                v_sc[:, start : start + tokens] = kv_ref[j, :top]
                k_sc[start : start + tokens, :] = both.astype(BF16)
                seg_sc[start : start + tokens, :] = jnp.broadcast_to(
                    both[:, HD : HD + 1], (tokens, LANES)
                )

    mine = q_ref[0].astype(F32)
    q = jnp.concatenate([mine[top + HD :], jnp.zeros((width, tokens), F32)], axis=0)
    q = q.astype(BF16)
    seg = mine[HD + 1 : HD + 2] * 64.0 + mine[HD + 2 : HD + 3]
    total = None if first else acc_ref[...]
    for start in range(0, sets * blocks * tokens, key_block):
        at = slice(start, start + key_block)
        scores = dot(k_sc[at, :], q)
        of_key = seg_sc[at, :]
        of_key = jnp.concatenate([of_key] * (tokens // LANES), axis=1)
        weights = jnp.where(of_key == seg, jnp.exp2(scores), 0.0).astype(BF16)
        part = dot(v_sc[:, at], weights)
        total = part if total is None else total + part
    if last:
        out_ref[0] = (total[:HD] / total[HD : HD + 1]).astype(BF16)
    else:
        out_ref[...] = total


def attend(queries, sets, acc=None, last=False, key_block=512):
    blocks, depth, tokens = queries.shape
    total = blocks * tokens
    keys = total * len(sets)
    first = acc is None
    top = HD + EXT
    block = pl.BlockSpec((top, tokens), lambda i: (0, i))
    if last:
        shape = jax.ShapeDtypeStruct((blocks, HD, tokens), BF16)
        out_spec = pl.BlockSpec((1, HD, tokens), lambda i: (i, 0, 0))
    else:
        shape = jax.ShapeDtypeStruct((top, total), F32)
        out_spec = block
    in_specs = [pl.BlockSpec((1, depth, tokens), lambda i: (i, 0, 0))]
    in_specs += [pl.BlockSpec(kv.shape, lambda i: (0, 0, 0)) for kv in sets]
    operands = [queries, *sets]
    if not first:
        in_specs.append(block)
        operands.append(acc)
    return pl.pallas_call(
        lambda *refs: attend_kernel(
            *refs, sets=len(sets), first=first, last=last, key_block=key_block
        ),
        out_shape=shape,
        grid=(blocks,),
        in_specs=in_specs,
        out_specs=out_spec,
        scratch_shapes=[
            pltpu.VMEM((keys, LANES), BF16),
            pltpu.VMEM((top, keys), BF16),
            pltpu.VMEM((keys, LANES), F32),
        ],
        compiler_params=cparams("arbitrary"),
        cost_estimate=cost(4 * total * keys * LANES, 3 << 20, total * keys),
        name="attend",
    )(*operands)


def project_kernel(att_ref, x_ref, w_ref, res_ref, in_ref):
    heads, _, tokens = att_ref.shape
    att = att_ref[...].astype(F32).reshape(heads * HD, tokens).T.astype(BF16)
    residual = (x_ref[...].astype(F32) + dot(att, w_ref[...])).astype(BF16)
    res_ref[...] = residual
    in_ref[...] = layer_norm(residual.astype(F32)).astype(BF16)


def project(attended, tokens, w_attn_out):
    shape = jax.ShapeDtypeStruct(tokens.shape, BF16)
    return pl.pallas_call(
        project_kernel,
        out_shape=(shape, shape),
        in_specs=[pl.BlockSpec(memory_space=pltpu.VMEM)] * 3,
        out_specs=(pl.BlockSpec(memory_space=pltpu.VMEM),) * 2,
        compiler_params=cparams(),
        cost_estimate=cost(2 * tokens.shape[0] * w_attn_out.shape[0] * w_attn_out.shape[1], 4 << 20),
        name="project",
    )(attended, tokens, w_attn_out)


def mlp_kernel(x_ref, pair_ref, *refs):
    packs = refs[:4]
    own_ref, other_ref, near, far, sems = refs[4:]
    rows = x_ref.shape[0]
    copies = []
    for number in range(3):
        copies.append(pltpu.make_async_copy(packs[number], near.at[number], sems.at[number]))
    copies.append(pltpu.make_async_copy(packs[3], far, sems.at[3]))
    for copy in copies:
        copy.start()
    units = (near.shape[1] - PAD) // 2
    shards = far.shape[0]
    piece = (far.shape[1] - EXT) // 2
    x = x_ref[...], pair_ref[...]
    total = [None, None]
    for number in range(4):
        copies[number].wait()
        if number < 3:
            into = near[number, :units]
            out_of = near[number, units : 2 * units]
            bias = near[number, 2 * units : 2 * units + 1, :units].astype(F32)
        else:
            into = far[:, :piece].reshape(shards * piece, -1)
            out_of = far[:, piece : 2 * piece].reshape(shards * piece, -1)
            bias = jnp.concatenate(
                [far[i, 2 * piece : 2 * piece + 1, :piece].astype(F32) for i in range(shards)],
                axis=1,
            )
        before = [dot(part, into, NT) + bias for part in x]
        for i in range(2):
            pre = before[i]
            hidden = (0.5 * pre * (1.0 + lax.erf(pre * math.sqrt(0.5)))).astype(BF16)
            part = dot(hidden, out_of)
            total[i] = part if total[i] is None else total[i] + part
    own_ref[...] = total[0].astype(BF16)
    other_ref[...] = total[1].astype(BF16)


def mlp(x, pair, packs):
    rows, width = x.shape
    shape = jax.ShapeDtypeStruct((rows, width), BF16)
    vmem = pl.BlockSpec(memory_space=pltpu.VMEM)
    units = (packs[0].shape[0] - PAD) // 2
    return pl.pallas_call(
        mlp_kernel,
        out_shape=(shape, shape),
        in_specs=[vmem, vmem] + [pl.BlockSpec(memory_space=pl.ANY)] * 4,
        out_specs=(vmem, vmem),
        scratch_shapes=[
            pltpu.VMEM((3,) + packs[0].shape, BF16),
            pltpu.VMEM(packs[3].shape, BF16),
            pltpu.SemaphoreType.DMA((4,)),
        ],
        compiler_params=cparams(),
        cost_estimate=cost(2 * rows * 4 * units * width * 4, 20 << 20),
        name="mlp",
    )(x, pair, *packs)


def merge_kernel(res_ref, bias_ref, gain_ref, index_ref, owner_ref, own_ref, other_ref, out_ref, *, cap):
    rows, width = res_ref.shape
    total = own_ref[...].astype(F32) + other_ref[...].astype(F32)
    total = res_ref[...].astype(F32) + total + bias_ref[...]
    normed = (layer_norm(total) * gain_ref[...]).astype(BF16)
    count = rows // 4
    r = lax.broadcasted_iota(jnp.int32, (rows, rows), 0)
    s = lax.broadcasted_iota(jnp.int32, (rows, rows), 1)
    named = (index_ref[...] == r).astype(F32).astype(BF16)
    order = (s == 4 * (r % count) + r // count).astype(F32).astype(BF16)
    pick = dot(order, named, NT).astype(BF16)
    merged = dot(pick, normed).astype(BF16)
    for c in range(4):
        out_ref[:, c * width : (c + 1) * width] = merged[c * count : (c + 1) * count]
    across = owner_ref[...]
    r = lax.broadcasted_iota(jnp.int32, (count, count), 0)
    s = lax.broadcasted_iota(jnp.int32, (count, count), 1)
    owner = jnp.sum(jnp.where(r == s, across, 0), axis=1, keepdims=True)
    earlier = (across == owner) & (s < r)
    rank = jnp.sum(earlier.astype(jnp.int32), axis=1, keepdims=True)
    slot = (owner * cap + rank).astype(F32).astype(BF16)
    out_ref[:, 4 * width :] = jnp.broadcast_to(slot, (count, LANES))


def merge(residual, out_bias, merge_gain, merge_index, owners, own, other, cap):
    rows, width = residual.shape
    operands = (
        residual,
        out_bias.reshape(1, width),
        merge_gain.reshape(1, width),
        merge_index.reshape(1, rows),
        owners.reshape(1, rows // 4),
        own,
        other,
    )
    return pl.pallas_call(
        lambda *refs: merge_kernel(*refs, cap=cap),
        out_shape=jax.ShapeDtypeStruct((rows // 4, 4 * width + LANES), BF16),
        in_specs=[pl.BlockSpec(memory_space=pltpu.VMEM)] * len(operands),
        out_specs=pl.BlockSpec(memory_space=pltpu.VMEM),
        compiler_params=cparams(),
        cost_estimate=cost(2 * rows * rows * width, 4 << 20),
        name="merge",
    )(*operands)


def embed_kernel(group_ref, *refs, pieces, cap, slots):
    x_refs = refs[: len(pieces)]
    w_ref, bias_ref, out_ref, x_sc, acc_ref = refs[len(pieces) :]
    step = pl.program_id(0)
    steps = pl.num_programs(0)
    for (at, _), x_ref in zip(pieces, x_refs):
        x_sc[at : at + x_ref.shape[0], :] = x_ref[...]

    @pl.when(step < steps - 1)
    def _():
        part = dot(x_sc[...], w_ref[...])

        @pl.when(step == 0)
        def _():
            acc_ref[...] = part

        @pl.when(step > 0)
        def _():
            acc_ref[...] += part

    @pl.when(step == steps - 1)
    def _():
        embedded = (acc_ref[...] + bias_ref[...]).astype(BF16)
        total = x_sc.shape[0]
        count = total // 4
        slot = x_sc[:, 0:1].astype(F32).astype(jnp.int32)
        owner = slot // cap
        rank = slot - owner * cap
        shift = lax.broadcasted_iota(jnp.int32, (total, 1), 0) // count
        group = group_ref[0] + shift
        group = jnp.where(group >= 4, group - 4, group)
        target = owner * slots + group * cap + rank
        lane = lax.broadcasted_iota(jnp.int32, (total, out_ref.shape[0]), 1)
        place = (target == lane).astype(F32).T.astype(BF16)
        out_ref[...] = dot(place, embedded).astype(BF16)


def embed(group, pieces, w_merge, merge_bias, cap, slots, owners, block=1408):
    arrays = [array for _, array in pieces]
    rows = sum(array.shape[0] for array in arrays)
    depth, cols = w_merge.shape
    steps = depth // block
    places = tuple((at, array.shape[0]) for at, array in pieces)
    x_block = block

    def x_map(i, _):
        return (0, i)

    spec = lambda array: pl.BlockSpec((array.shape[0], x_block), x_map)
    return pl.pallas_call(
        lambda *refs: embed_kernel(*refs, pieces=places, cap=cap, slots=slots),
        out_shape=jax.ShapeDtypeStruct((owners * slots, cols), BF16),
        grid_spec=pltpu.PrefetchScalarGridSpec(
            num_scalar_prefetch=1,
            grid=(steps + 1,),
            in_specs=[spec(array) for array in arrays]
            + [
                pl.BlockSpec((block, cols), lambda i, _: (jnp.minimum(i, steps - 1), 0)),
                pl.BlockSpec((1, cols), lambda i, _: (0, 0)),
            ],
            out_specs=pl.BlockSpec((owners * slots, cols), lambda i, _: (0, 0)),
            scratch_shapes=[pltpu.VMEM((rows, block), BF16), pltpu.VMEM((rows, cols), F32)],
        ),
        compiler_params=cparams("arbitrary"),
        cost_estimate=cost(2 * rows * depth * cols, 10 << 20),
        name="embed",
    )(group, *arrays, w_merge, merge_bias.reshape(1, cols))


def flip(value, axis):
    return lax.ppermute(value, axis, [(0, 1), (1, 0)])


def turn(value, axis, by):
    size = lax.axis_size(axis)
    return lax.ppermute(value, axis, [(i, (i + by) % size) for i in range(size)])


def ring_gather(value, axis):
    before = turn(value, axis, 1)
    after = turn(value, axis, -1)
    half = value.shape[0] // 2
    return before, after, turn(before[:half], axis, 1), turn(after[half:], axis, -1)


def pack(w_in, in_bias, w_out, start, count, extra):
    width = w_in.shape[1]
    bias = lax.dynamic_slice_in_dim(in_bias, start, count)
    bias = jnp.pad(bias.reshape(1, count), ((0, extra - 1), (0, width - count)))
    return jnp.concatenate(
        [
            lax.dynamic_slice_in_dim(w_in, start, count),
            lax.dynamic_slice_in_dim(w_out, start, count),
            bias,
        ]
    )


def spread_weights(w_in, in_bias, w_out):
    half = w_in.shape[0] // 2
    core = lax.axis_index("c") * half
    chips = ("y", "xh", "xl")
    share = half // lax.axis_size(chips)
    start = core + lax.axis_index(chips) * share
    far = turn(pack(w_in, in_bias, w_out, start, share, EXT), "grp", 2)
    own = pack(w_in, in_bias, w_out, core, half, PAD)
    far = lax.all_gather(far, chips)
    return own, turn(own, "grp", 1), turn(own, "grp", -1), far


def local(
    tokens,
    seg_ids,
    merge_index,
    owners,
    w_qkv,
    w_attn_out,
    w_in,
    in_bias,
    w_out,
    out_bias,
    merge_gain,
    w_merge,
    merge_bias,
):
    packs = spread_weights(w_in, in_bias, w_out)
    heads = qkv(tokens, seg_ids, w_qkv)
    mine = lax.all_to_all(heads, ("y", "xh"), 0, 0, tiled=True)
    kv = mine[:, : 2 * HD + EXT]
    kv_x = flip(kv, "xl")
    kv_c = flip(kv, "c")
    kv_xc = flip(kv_x, "c")
    acc = attend(mine, [kv])
    acc = attend(mine, [kv_c], acc)
    done = attend(mine, [kv_x, kv_xc], acc, last=True)
    attended = lax.all_to_all(done, ("y", "xh"), 0, 0, tiled=True)
    residual, mlp_in = project(attended, tokens, w_attn_out)
    own, other = mlp(mlp_in, flip(mlp_in, "c"), packs)
    owner_count = lax.axis_size(("y", "xh", "xl", "c"))
    cap = 4
    merged = merge(
        residual, out_bias, merge_gain, merge_index, owners, own, flip(other, "c"), cap
    )
    count = merged.shape[0]
    before, after, far_a, far_b = ring_gather(merged, "grp")
    pieces = [
        (0, merged),
        (count, after),
        (2 * count, far_a),
        (2 * count + count // 2, far_b),
        (3 * count, before),
    ]
    group = lax.axis_index("grp").reshape(1).astype(jnp.int32)
    slots = 4 * cap
    outgoing = embed(group, pieces, w_merge, merge_bias, cap, slots, owner_count)
    cols = outgoing.shape[1]
    outgoing = outgoing.reshape(owner_count, 4, cap, cols)
    received = lax.all_to_all(
        outgoing, ("y", "xh", "xl", "c"), split_axis=0, concat_axis=2, tiled=True
    )
    return received.reshape(4 * owner_count * cap, cols)


def solution(mesh):
    inner = Mesh(mesh.devices.reshape(4, 4, 2, 2, 2), ("grp", "y", "xh", "xl", "c"))
    every = ("grp", "y", "xh", "xl", "c")
    tok = ("y", "xh", "xl", "c")
    placed = (
        P(every, None),
        P(every),
        P(every),
        P(every, None),
        P(),
        P(),
        P("grp", None),
        P("grp"),
        P("grp", None),
        P(),
        P(),
        P(None, "grp"),
        P("grp"),
    )
    return jax.shard_map(
        local, mesh=inner, in_specs=placed, out_specs=P(tok, "grp"), check_vma=False
    )
```

time: 260 us -> 245 us (0.942)
  Pallas kernels: 89.8 us -> 71 us
  between operations: 0.31 us -> 13.5 us
  local copies, waits for them, and re-layouts: 25.1 us -> 13.8 us
  other arithmetic: 3.47 us -> 8.66 us
  starting transfers between devices: 33.2 us -> 29.6 us
    pallas_call x8 -> x6, Pallas kernels: 78.8 us -> 60.1 us  [the longest x3 33.3 us: attend(): pl.pallas_call(lambda *refs: attend_kernel(*refs, sets=len(sets), first=f...]
    ppermute x20 -> x7, starting transfers between devices: 27 us -> 12.8 us  [turn(): lax.ppermute(value, axis, [(i, (i + by) % size) for i in range(size)])]
    ppermute x3 -> x5, starting transfers between devices: 6.21 us -> 16.9 us  [flip(): return lax.ppermute(value, axis, [(0, 1), (1, 0)])]
    unnamed x54 -> x28, local copies, waits for them, and re-layouts: 14.9 us -> 5.11 us
    concatenate x4 -> x2, other arithmetic: 2.37 us -> 8.66 us  [pack(): jnp.concatenate([lax.dynamic_slice_in_dim(w_in, start, count), lax.dynami...]
    slice x6 -> x1, local copies, waits for them, and re-layouts: 5.34 us -> 0.05 us  [local(): kv = mine[:, :2 * HD + EXT]]
    ppermute x20 -> x7, waiting for transfers between devices: 35.2 us -> 30.5 us  [turn(): lax.ppermute(value, axis, [(i, (i + by) % size) for i in range(size)])]
    all_to_all x1, blocking collectives: 21.1 us -> 16.4 us  [local(): lax.all_to_all(outgoing, ('y', 'xh', 'xl', 'c'), split_axis=0, concat_axi...]
  transfers between devices with their start and end apart: 23 -> 13, of which waited for: 9 -> 6; matrix products, arithmetic and copies ran while one was open for 4% -> 5% of each run, Pallas kernels for 22% -> 18%
where the time goes in v2:
time: 245 us; the launch traced here: 244 us
  Pallas kernels  71 us (29%)
  blocking collectives  61.1 us (25%)
  waiting for transfers between devices  46.2 us (19%)
  starting transfers between devices  29.6 us (12%)
  local copies, waits for them, and re-layouts  13.8 us (6%)
  between operations  13.5 us (6%)
  other arithmetic  8.66 us (4%)
    pallas_call x3, Pallas kernels, attend(): pl.pallas_call(lambda *refs: attend_kernel(*refs, sets=len(sets), first=f...  33.3 us
    ppermute x7, waiting for transfers between devices, turn(): lax.ppermute(value, axis, [(i, (i + by) % size) for i in range(size)])  30.5 us
    all_to_all x1, blocking collectives, local(): mine = lax.all_to_all(heads, ('y', 'xh'), 0, 0, tiled=True)  28.1 us
    ppermute x5, starting transfers between devices, flip(): return lax.ppermute(value, axis, [(0, 1), (1, 0)])  16.9 us
    all_to_all x1, blocking collectives, local(): attended = lax.all_to_all(done, ('y', 'xh'), 0, 0, tiled=True)  16.6 us
    all_to_all x1, blocking collectives, local(): lax.all_to_all(outgoing, ('y', 'xh', 'xl', 'c'), split_axis=0, concat_axi...  16.4 us
    ppermute x5, waiting for transfers between devices, flip(): return lax.ppermute(value, axis, [(0, 1), (1, 0)])  15.7 us
    pallas_call x1, Pallas kernels, mlp(): pl.pallas_call(mlp_kernel, out_shape=(shape, shape), in_specs=[vmem, vmem...  15.3 us
  transfers between devices with their start and end apart: 13, of which 6 were waited for; matrix products, arithmetic and copies ran while one was open for 5% of the time, Pallas kernels for 18%

profile of v2, /device:TPU:1, one launch (start us, length us, event | category | flops | bytes accessed | tf_op | source)
XLA Modules:
  0.0 243.9 jit_solution(9235405620397167700)
XLA Ops:
  6.5 0.0 all-gather.3.cloned.1.call-start
  6.5 0.8 dynamic-slice_bitcast_fusion
  7.3 1.0 constant_dynamic-slice_fusion
  8.3 4.5 %collective-permute-start.6 = (bf16[104,1408]{1,0:T(8,128)(2,1)S(1)}, bf16[104,1408]{1,0:T(8,128)(2,1)S(1)}, u32[]{:S(2)}, u32[]{:S(2)}) collective-permute-start(bf16[104,1408]{1,0:T(8,128)(2,1)S(1)} %fusion.3), channel_id=1, source_target_pairs={{0,64},{32,96},{64,0},{96,32},{1,65},{33,97},{65,1},{97,33},{2,66}... | collective-permute-start | bytes 878600 | tf_op jit(solution)/shard_map/ppermute | solution.py:384
  12.8 6.7 %collective-permute-done.6 = bf16[104,1408]{1,0:T(8,128)(2,1)S(1)} collective-permute-done((bf16[104,1408]{1,0:T(8,128)(2,1)S(1)}, bf16[104,1408]{1,0:T(8,128)(2,1)S(1)}, u32[]{:S(2)}, u32[]{:S(2)}) %collective-permute-start.6) | collective-permute-done | bytes 292896 | tf_op jit(solution)/shard_map/ppermute | solution.py:384
  19.5 0.7 copy-done.7
  20.2 0.0 all-gather.3.cloned.1.call-update
  20.3 0.8 dynamic_slice.20
  21.1 2.6 %constant_dynamic-slice_fusion.2 = (bf16[768,1408]{1,0:T(8,128)(2,1)S(1)}, bf16[768,1408]{1,0:T(8,128)(2,1)S(1)}) fusion(bf16[1536,1408]{1,0:T(8,128)(2,1)} %param.21, s32[]{:T(128)S(6)} %select_n.4, bf16[1536,1408]{1,0:T(8,128)(2,1)} %param.19), kind=kLoop, calls=%fused_computation.8 | loop fusion | bytes 8650756 | tf_op jit(solution)/shard_map/dynamic_slice | solution.py:401
  23.6 8.6 %fusion.1.refs_0_ = bf16[1552,1408]{1,0:T(8,128)(2,1)} fusion(bf16[1,768]{1,0:T(2,128)(2,1)S(1)} %reshape.40, bf16[768,1408]{1,0:T(8,128)(2,1)S(1)} %get-tuple-element.13, bf16[768,1408]{1,0:T(8,128)(2,1)S(1)} %get-tuple-element.14), kind=kLoop, calls=%fused_computation.2 | loop fusion | flops 17481728 | bytes 8697344 | tf_op jit(solution)/shard_map/concatenate | solution.py:398
  32.3 2.8 %collective-permute-start.5 = (bf16[1552,1408]{1,0:T(8,128)(2,1)}, bf16[1552,1408]{1,0:T(8,128)(2,1)}, u32[]{:S(2)}, u32[]{:S(2)}) collective-permute-start(bf16[1552,1408]{1,0:T(8,128)(2,1)} %fusion.1.refs_0_), channel_id=1, source_target_pairs={{0,96},{32,0},{64,32},{96,64},{1,97},{33,1},{65,33},{97,65},{2,98}... | collective-permute-start | bytes 13111304 | tf_op jit(solution)/shard_map/ppermute | solution.py:384
  35.1 0.0 collective-permute-start.4
  35.1 7.9 %qkv.1 = bf16[8,272,256]{2,1,0:T(8,128)(2,1)} custom-call(bf16[256,1408]{1,0:T(8,128)(2,1)} %x_ref.3, s32[1,256]{1,0:T(1,128)} %bitcast.15, bf16[2112,1408]{1,0:T(8,128)(2,1)} %bitcast.12), custom_call_target="tpu_custom_call" | custom-call | flops 1522532352 | bytes 8388608 | tf_op jit(solution)/shard_map/qkv/pallas_call | solution.py:81
  43.0 28.1 %all_to_all.25.refs_0_ = bf16[8,272,256]{2,1,0:T(8,128)(2,1)S(1)} all-to-all(bf16[8,272,256]{2,1,0:T(8,128)(2,1)} %qkv.1), channel_id=1, replica_groups=mesh['grp'=4,'y'=4,'xh'=2,'xl'=2,'c'=2] {'y','xh'}, dimensions={0} | all-to-all | bytes 2228224 | tf_op jit(solution)/shard_map/all_to_all | solution.py:436
  71.1 0.0 copy-start.3
  71.1 0.4 collective-permute-start
  71.6 10.4 %collective-permute-start.2 = (bf16[8,184,256]{2,1,0:T(8,128)(2,1)S(1)}, bf16[8,184,256]{2,1,0:T(8,128)(2,1)S(1)}, u32[]{:S(2)}, u32[]{:S(2)}) collective-permute-start(bf16[8,184,256]{2,1,0:T(8,128)(2,1)S(1)} %slice.12.refs_1_), channel_id=1, source_target_pairs={{0,1},{1,0},{2,3},{3,2},{4,5},{5,4},{6,7},{7,6},{8,9},{9,8},{10,11... | collective-permute-start | bytes 2261000 | tf_op jit(solution)/shard_map/ppermute | solution.py:379
  82.0 12.9 %collective-permute-done.refs_1_ = bf16[8,184,256]{2,1,0:T(8,128)(2,1)S(1)} collective-permute-done((bf16[8,184,256]{2,1,0:T(8,128)(2,1)S(1)}, bf16[8,184,256]{2,1,0:T(8,128)(2,1)S(1)}, u32[]{:S(2)}, u32[]{:S(2)}) %collective-permute-start) | collective-permute-done | bytes 753696 | tf_op jit(solution)/shard_map/ppermute | solution.py:379
  94.8 3.9 %collective-permute-start.1 = (bf16[8,184,256]{2,1,0:T(8,128)(2,1)S(1)}, bf16[8,184,256]{2,1,0:T(8,128)(2,1)S(1)}, u32[]{:S(2)}, u32[]{:S(2)}) collective-permute-start(bf16[8,184,256]{2,1,0:T(8,128)(2,1)S(1)} %collective-permute-done.refs_1_), channel_id=1, source_target_pairs={{0,1},{1,0},{2,3},{3,2},{4,5},{5,4},{6,7},{7,6},{8,9},{9,8},{10,11... | collective-permute-start | bytes 2261000 | tf_op jit(solution)/shard_map/ppermute | solution.py:379
  98.7 0.0 copy-done
  98.7 0.0 copy-done.3
  98.7 9.0 %attend.3.refs_2_ = f32[96,2048]{1,0:T(8,128)} custom-call(bf16[8,272,256]{2,1,0:T(8,128)(2,1)} %copy-done, bf16[8,184,256]{2,1,0:T(8,128)(2,1)} %copy-done.3), custom_call_target="tpu_custom_call" | custom-call | flops 2147483648 | bytes 3145728 | tf_op jit(solution)/shard_map/attend/pallas_call | solution.py:164
  107.7 0.0 collective-permute-done.2.refs_1_
  107.7 0.9 copy-done.12
  108.6 9.9 %attend.4.refs_3_ = f32[96,2048]{1,0:T(8,128)} custom-call(bf16[8,272,256]{2,1,0:T(8,128)(2,1)} %copy-done, bf16[8,184,256]{2,1,0:T(8,128)(2,1)} %copy-done.12, f32[96,2048]{1,0:T(8,128)} %attend.3.refs_2_), custom_call_target="tpu_custom_call" | custom-call | flops 2147483648 | bytes 3145728 | tf_op jit(solution)/shard_map/attend/pallas_call | solution.py:164
  118.5 0.0 copy-done.10
  118.5 0.0 collective-permute-done.1.refs_2_
  118.5 0.0 copy-start.11
  118.5 0.9 copy-done.11
  119.4 14.4 %attend.5 = bf16[8,88,256]{2,1,0:T(8,128)(2,1)} custom-call(bf16[8,272,256]{2,1,0:T(8,128)(2,1)} %copy-done, bf16[8,184,256]{2,1,0:T(8,128)(2,1)} %copy-done.10, bf16[8,184,256]{2,1,0:T(8,128)(2,1)} %copy-done.11, f32[96,2048]{1,0:T(8,128)} %attend.4.refs_3_), custom_call_target="tpu_custom_call" | custom-call | flops 4294967296 | bytes 3145728 | tf_op jit(solution)/shard_map/attend/pallas_call | solution.py:164
  133.8 16.6 %all_to_all.26.att_ref = bf16[8,88,256]{2,1,0:T(8,128)(2,1)} all-to-all(bf16[8,88,256]{2,1,0:T(8,128)(2,1)} %attend.5), channel_id=1, replica_groups=mesh['grp'=4,'y'=4,'xh'=2,'xl'=2,'c'=2] {'y','xh'}, dimensions={0} | all-to-all | bytes 720896 | tf_op jit(solution)/shard_map/all_to_all | solution.py:444
  150.4 3.9 %project.1 = (bf16[256,1408]{1,0:T(8,128)(2,1)}, bf16[256,1408]{1,0:T(8,128)(2,1)}) custom-call(bf16[8,88,256]{2,1,0:T(8,128)(2,1)} %all_to_all.26.att_ref, bf16[256,1408]{1,0:T(8,128)(2,1)} %x_ref.3, bf16[704,1408]{1,0:T(8,128)(2,1)} %w_ref.1), custom_call_target="tpu_custom_call" | custom-call | flops 507510784 | bytes 4194304 | tf_op jit(solution)/shard_map/project/pallas_call | solution.py:193
  154.3 1.7 collective-permute-start.3
  156.0 2.0 collective-permute-done.3.pair_ref
  158.0 0.0 collective-permute-done.5.refs_2_
  158.0 0.0 collective-permute-done.4.refs_1_
  158.0 0.0 all-gather.3.cloned.1.call-done
  158.1 0.8 copy-done.13
  158.9 15.3 %mlp.1 = (bf16[256,1408]{1,0:T(8,128)(2,1)}, bf16[256,1408]{1,0:T(8,128)(2,1)}) custom-call(bf16[256,1408]{1,0:T(8,128)(2,1)} %get-tuple-element.10.x_ref, bf16[256,1408]{1,0:T(8,128)(2,1)} %copy-done.13, bf16[1552,1408]{1,0:T(8,128)(2,1)} %fusion.1.refs_0_, bf16[1552,1408]{1,0:T(8,128)(2,1)} %collective-permute-done.4.refs_1_, ...), custom_call_target="tpu_custom_call" | custom-call | flops 8858370048 | bytes 20971520 | tf_op jit(solution)/shard_map/mlp/pallas_call | solution.py:247
  174.2 0.5 collective-permute-start.7
  174.7 0.0 copy-done.8
  174.7 0.6 reshape.36.refs_1_
  175.3 0.0 copy-done.9
  175.3 0.6 reshape.37.refs_2_
  175.9 0.8 collective-permute-done.7.refs_6_
  176.7 0.9 copy-done.4
  177.6 3.5 %merge.1.refs_1_ = bf16[64,5760]{1,0:T(8,128)(2,1)} custom-call(bf16[256,1408]{1,0:T(8,128)(2,1)} %get-tuple-element.9.refs_0_, f32[1,1408]{1,0:T(1,128)} %reshape.36.refs_1_, f32[1,1408]{1,0:T(1,128)} %reshape.37.refs_2_, s32[1,256]{1,0:T(1,128)} %bitcast.16, s32[1,64]{1,0:T(1,128)} %bitcast.17, bf16[256,1408]{1,0:T(8,128)(2,1)} %get-tuple-element.11.refs_5_, ...), custom_call_target="tpu_custom_call" | custom-call | flops 184549376 | bytes 4194304 | tf_op jit(solution)/shard_map/merge/pallas_call | solution.py:298
  181.2 0.0 collective-permute-start.9
  181.2 2.7 %collective-permute-start.8 = (bf16[64,5760]{1,0:T(8,128)(2,1)}, bf16[64,5760]{1,0:T(8,128)(2,1)S(1)}, u32[]{:S(2)}, u32[]{:S(2)}) collective-permute-start(bf16[64,5760]{1,0:T(8,128)(2,1)} %merge.1.refs_1_), channel_id=1, source_target_pairs={{0,96},{32,0},{64,32},{96,64},{1,97},{33,1},{65,33},{97,65},{2,98}... | collective-permute-start | bytes 2211848 | tf_op jit(solution)/shard_map/ppermute | solution.py:384
  183.8 16.4 %collective-permute-done.9.refs_5_ = bf16[64,5760]{1,0:T(8,128)(2,1)S(1)} collective-permute-done((bf16[64,5760]{1,0:T(8,128)(2,1)}, bf16[64,5760]{1,0:T(8,128)(2,1)S(1)}, u32[]{:S(2)}, u32[]{:S(2)}) %collective-permute-start.9) | collective-permute-done | bytes 737312 | tf_op jit(solution)/shard_map/ppermute | solution.py:384
  200.3 0.1 collective-permute-start.10
  200.4 0.0 collective-permute-done.8.refs_2_
  200.4 0.0 copy-start.2
  200.5 2.7 %collective-permute-start.11 = (bf16[32,5760]{1,0:T(8,128)(2,1)S(1)}, bf16[32,5760]{1,0:T(8,128)(2,1)S(1)}, u32[]{:S(2)}, u32[]{:S(2)}) collective-permute-start(bf16[32,5760]{1,0:T(8,128)(2,1)S(1)} %slice.14), channel_id=1, source_target_pairs={{0,96},{32,0},{64,32},{96,64},{1,97},{33,1},{65,33},{97,65},{2,98}... | collective-permute-start | bytes 1105928 | tf_op jit(solution)/shard_map/ppermute | solution.py:384
  203.2 7.3 %collective-permute-done.10.refs_3_ = bf16[32,5760]{1,0:T(8,128)(2,1)S(1)} collective-permute-done((bf16[32,5760]{1,0:T(8,128)(2,1)S(1)}, bf16[32,5760]{1,0:T(8,128)(2,1)S(1)}, u32[]{:S(2)}, u32[]{:S(2)}) %collective-permute-start.10) | collective-permute-done | bytes 368672 | tf_op jit(solution)/shard_map/ppermute | solution.py:384
  210.5 0.0 collective-permute-done.11.refs_4_
  210.5 0.0 copy-done.2
  210.5 0.7 copy-done.5
  211.2 0.1 copy-done.6
  211.4 7.0 %embed.1 = bf16[512,512]{1,0:T(8,128)(2,1)} custom-call(s32[1]{0:T(128)} %bitcast.refs_0_, bf16[64,5760]{1,0:T(8,128)(2,1)} %merge.1.refs_1_, bf16[64,5760]{1,0:T(8,128)(2,1)} %copy-done.2, bf16[32,5760]{1,0:T(8,128)(2,1)} %copy-done.5, bf16[32,5760]{1,0:T(8,128)(2,1)} %copy-done.6, bf16[64,5760]{1,0:T(8,128)(2,1)} %copy-done.1, bf16[5632,512]{1,0:T(8,128)(2,1)} %refs_6_.1, ...), custom_call_target="tpu_custom_call" | custom-call | flops 1476395008 | bytes 10485760 | tf_op jit(solution)/shard_map/embed/pallas_call | solution.py:358
  218.4 1.2 reshape.43
  219.5 16.4 %all_to_all.27 = bf16[32,4,4,512]{3,2,1,0:T(4,128)(2,1)S(1)} all-to-all(bf16[32,4,4,512]{3,2,1,0:T(4,128)(2,1)S(1)} %reshape.43), channel_id=1, replica_groups=mesh['grp'=4,'y'=4,'xh'=2,'xl'=2,'c'=2] {'y','xh','xl','c'}, dimensions={0} | all-to-all | bytes 1048576 | tf_op jit(solution)/shard_map/all_to_all | solution.py:466
  236.0 0.2 copy.14
  236.2 0.9 reshape.44
  (17 shorter events, 0.2 us)
Async XLA Ops:
  6.5 151.5 %all-gather.3.cloned.1.call-start = ((), (), s32[]{:S(2)}) async-start(), calls=%async_computation.3 | async-start | bytes 4978688 | tf_op jit(solution)/shard_map/all_gather | solution.py:415
  8.3 11.2 %collective-permute-start.6 = (bf16[104,1408]{1,0:T(8,128)(2,1)S(1)}, bf16[104,1408]{1,0:T(8,128)(2,1)S(1)}, u32[]{:S(2)}, u32[]{:S(2)}) collective-permute-start(bf16[104,1408]{1,0:T(8,128)(2,1)S(1)} %fusion.3), channel_id=1, source_target_pairs={{0,64},{32,96},{64,0},{96,32},{1,65},{33,97},{65,1},{97,33},{2,66}... | collective-permute-start | bytes 878600 | tf_op jit(solution)/shard_map/ppermute | solution.py:384
  19.5 0.7 copy-start.7
  32.3 125.8 %collective-permute-start.5 = (bf16[1552,1408]{1,0:T(8,128)(2,1)}, bf16[1552,1408]{1,0:T(8,128)(2,1)}, u32[]{:S(2)}, u32[]{:S(2)}) collective-permute-start(bf16[1552,1408]{1,0:T(8,128)(2,1)} %fusion.1.refs_0_), channel_id=1, source_target_pairs={{0,96},{32,0},{64,32},{96,64},{1,97},{33,1},{65,33},{97,65},{2,98}... | collective-permute-start | bytes 13111304 | tf_op jit(solution)/shard_map/ppermute | solution.py:384
  35.1 123.0 %collective-permute-start.4 = (bf16[1552,1408]{1,0:T(8,128)(2,1)}, bf16[1552,1408]{1,0:T(8,128)(2,1)}, u32[]{:S(2)}, u32[]{:S(2)}) collective-permute-start(bf16[1552,1408]{1,0:T(8,128)(2,1)} %fusion.1.refs_0_), channel_id=1, source_target_pairs={{0,32},{32,64},{64,96},{96,0},{1,33},{33,65},{65,97},{97,1},{2,34}... | collective-permute-start | bytes 13111304 | tf_op jit(solution)/shard_map/ppermute | solution.py:384
  71.1 27.6 %copy-start = (bf16[8,272,256]{2,1,0:T(8,128)(2,1)}, bf16[8,272,256]{2,1,0:T(8,128)(2,1)S(1)}, u32[]{:S(2)}) copy-start(bf16[8,272,256]{2,1,0:T(8,128)(2,1)S(1)} %all_to_all.25.refs_0_) | copy-start | bytes 3342340
  71.1 27.6 %copy-start.3 = (bf16[8,184,256]{2,1,0:T(8,128)(2,1)}, bf16[8,184,256]{2,1,0:T(8,128)(2,1)S(1)}, u32[]{:S(2)}) copy-start(bf16[8,184,256]{2,1,0:T(8,128)(2,1)S(1)} %slice.12.refs_1_) | copy-start | bytes 2260996
  71.1 23.7 %collective-permute-start = (bf16[8,184,256]{2,1,0:T(8,128)(2,1)S(1)}, bf16[8,184,256]{2,1,0:T(8,128)(2,1)S(1)}, u32[]{:S(2)}, u32[]{:S(2)}) collective-permute-start(bf16[8,184,256]{2,1,0:T(8,128)(2,1)S(1)} %slice.12.refs_1_), channel_id=1, source_target_pairs={{0,2},{2,0},{1,3},{3,1},{4,6},{6,4},{5,7},{7,5},{8,10},{10,8},{9,1... | collective-permute-start | bytes 2261000 | tf_op jit(solution)/shard_map/ppermute | solution.py:379
  71.6 36.1 %collective-permute-start.2 = (bf16[8,184,256]{2,1,0:T(8,128)(2,1)S(1)}, bf16[8,184,256]{2,1,0:T(8,128)(2,1)S(1)}, u32[]{:S(2)}, u32[]{:S(2)}) collective-permute-start(bf16[8,184,256]{2,1,0:T(8,128)(2,1)S(1)} %slice.12.refs_1_), channel_id=1, source_target_pairs={{0,1},{1,0},{2,3},{3,2},{4,5},{5,4},{6,7},{7,6},{8,9},{9,8},{10,11... | collective-permute-start | bytes 2261000 | tf_op jit(solution)/shard_map/ppermute | solution.py:379
  94.8 23.7 %copy-start.10 = (bf16[8,184,256]{2,1,0:T(8,128)(2,1)}, bf16[8,184,256]{2,1,0:T(8,128)(2,1)S(1)}, u32[]{:S(2)}) copy-start(bf16[8,184,256]{2,1,0:T(8,128)(2,1)S(1)} %collective-permute-done.refs_1_) | copy-start | bytes 2260996
  94.8 23.7 %collective-permute-start.1 = (bf16[8,184,256]{2,1,0:T(8,128)(2,1)S(1)}, bf16[8,184,256]{2,1,0:T(8,128)(2,1)S(1)}, u32[]{:S(2)}, u32[]{:S(2)}) collective-permute-start(bf16[8,184,256]{2,1,0:T(8,128)(2,1)S(1)} %collective-permute-done.refs_1_), channel_id=1, source_target_pairs={{0,1},{1,0},{2,3},{3,2},{4,5},{5,4},{6,7},{7,6},{8,9},{9,8},{10,11... | collective-permute-start | bytes 2261000 | tf_op jit(solution)/shard_map/ppermute | solution.py:379
  107.7 0.9 copy-start.12
  118.5 0.9 copy-start.11
  154.3 3.7 %collective-permute-start.3 = (bf16[256,1408]{1,0:T(8,128)(2,1)}, bf16[256,1408]{1,0:T(8,128)(2,1)S(1)}, u32[]{:S(2)}, u32[]{:S(2)}) collective-permute-start(bf16[256,1408]{1,0:T(8,128)(2,1)} %get-tuple-element.10.x_ref), channel_id=1, source_target_pairs={{0,1},{1,0},{2,3},{3,2},{4,5},{5,4},{6,7},{7,6},{8,9},{9,8},{10,11... | collective-permute-start | bytes 2162696 | tf_op jit(solution)/shard_map/ppermute | solution.py:379
  158.0 0.9 copy-start.13
  158.9 15.8 %copy-start.8 = (f32[1408]{0:T(1024)S(1)}, f32[1408]{0:T(1024)}, u32[]{:S(2)}) copy-start(f32[1408]{0:T(1024)} %param.22) | copy-start | bytes 16900
  158.9 16.4 %copy-start.9 = (f32[1408]{0:T(1024)S(1)}, f32[1408]{0:T(1024)}, u32[]{:S(2)}) copy-start(f32[1408]{0:T(1024)} %param.23) | copy-start | bytes 16900
  174.2 2.5 %collective-permute-start.7 = (bf16[256,1408]{1,0:T(8,128)(2,1)}, bf16[256,1408]{1,0:T(8,128)(2,1)S(1)}, u32[]{:S(2)}, u32[]{:S(2)}) collective-permute-start(bf16[256,1408]{1,0:T(8,128)(2,1)} %get-tuple-element.12), channel_id=1, source_target_pairs={{0,1},{1,0},{2,3},{3,2},{4,5},{5,4},{6,7},{7,6},{8,9},{9,8},{10,11... | collective-permute-start | bytes 2162696 | tf_op jit(solution)/shard_map/ppermute | solution.py:379
  176.7 0.9 copy-start.4
  181.2 19.1 %collective-permute-start.9 = (bf16[64,5760]{1,0:T(8,128)(2,1)}, bf16[64,5760]{1,0:T(8,128)(2,1)S(1)}, u32[]{:S(2)}, u32[]{:S(2)}) collective-permute-start(bf16[64,5760]{1,0:T(8,128)(2,1)} %merge.1.refs_1_), channel_id=1, source_target_pairs={{0,32},{32,64},{64,96},{96,0},{1,33},{33,65},{65,97},{97,1},{2,34}... | collective-permute-start | bytes 2211848 | tf_op jit(solution)/shard_map/ppermute | solution.py:384
  181.2 19.2 %collective-permute-start.8 = (bf16[64,5760]{1,0:T(8,128)(2,1)}, bf16[64,5760]{1,0:T(8,128)(2,1)S(1)}, u32[]{:S(2)}, u32[]{:S(2)}) collective-permute-start(bf16[64,5760]{1,0:T(8,128)(2,1)} %merge.1.refs_1_), channel_id=1, source_target_pairs={{0,96},{32,0},{64,32},{96,64},{1,97},{33,1},{65,33},{97,65},{2,98}... | collective-permute-start | bytes 2211848 | tf_op jit(solution)/shard_map/ppermute | solution.py:384
  200.3 10.2 %copy-start.1 = (bf16[64,5760]{1,0:T(8,128)(2,1)}, bf16[64,5760]{1,0:T(8,128)(2,1)S(1)}, u32[]{:S(2)}) copy-start(bf16[64,5760]{1,0:T(8,128)(2,1)S(1)} %collective-permute-done.9.refs_5_) | copy-start | bytes 2211844
  200.3 10.2 %collective-permute-start.10 = (bf16[32,5760]{1,0:T(8,128)(2,1)S(1)}, bf16[32,5760]{1,0:T(8,128)(2,1)S(1)}, u32[]{:S(2)}, u32[]{:S(2)}) collective-permute-start(bf16[32,5760]{1,0:T(8,128)(2,1)S(1)} %slice.13), channel_id=1, source_target_pairs={{0,32},{32,64},{64,96},{96,0},{1,33},{33,65},{65,97},{97,1},{2,34}... | collective-permute-start | bytes 1105928 | tf_op jit(solution)/shard_map/ppermute | solution.py:384
  200.4 10.1 %copy-start.2 = (bf16[64,5760]{1,0:T(8,128)(2,1)}, bf16[64,5760]{1,0:T(8,128)(2,1)S(1)}, u32[]{:S(2)}) copy-start(bf16[64,5760]{1,0:T(8,128)(2,1)S(1)} %collective-permute-done.8.refs_2_) | copy-start | bytes 2211844
  200.5 10.0 %collective-permute-start.11 = (bf16[32,5760]{1,0:T(8,128)(2,1)S(1)}, bf16[32,5760]{1,0:T(8,128)(2,1)S(1)}, u32[]{:S(2)}, u32[]{:S(2)}) collective-permute-start(bf16[32,5760]{1,0:T(8,128)(2,1)S(1)} %slice.14), channel_id=1, source_target_pairs={{0,96},{32,0},{64,32},{96,64},{1,97},{33,1},{65,33},{97,65},{2,98}... | collective-permute-start | bytes 1105928 | tf_op jit(solution)/shard_map/ppermute | solution.py:384
  210.5 0.7 copy-start.5
  210.5 0.9 copy-start.6
Sparse Core Ops, SparseCore 0:
  20.4 66.8 all-gather.2

commit v3 on v2

--- a/solution.py
+++ b/solution.py
@@ -97,84 +97,84 @@
     )(tokens, seg_ids.reshape(1, rows), w_qkv.T)
 
 
-def attend_kernel(*refs, sets, first, last, key_block):
+def attend_kernel(*refs, sets, first, last, key_block, unroll):
     q_ref = refs[0]
     kv_refs = refs[1 : 1 + sets]
     rest = refs[1 + sets :]
     if not first:
         acc_ref, rest = rest[0], rest[1:]
     out_ref, k_sc, v_sc, seg_sc = rest
-    blocks, _, tokens = kv_refs[0].shape
+    blocks, _, tokens = q_ref.shape
     top = HD + EXT
     width = LANES - HD
-
-    @pl.when(pl.program_id(0) == 0)
-    def _():
-        for number, kv_ref in enumerate(kv_refs):
-            for j in range(blocks):
-                start = (number * blocks + j) * tokens
-                digits = kv_ref[j, :top].astype(F32)
-                seg = digits[HD + 1 : HD + 2] * 64.0 + digits[HD + 2 : HD + 3]
-                keys = kv_ref[j, top : top + HD].astype(F32)
-                both = jnp.concatenate([keys, jnp.broadcast_to(seg, (width, tokens))], axis=0).T
-                v_sc[:, start : start + tokens] = kv_ref[j, :top]
-                k_sc[start : start + tokens, :] = both.astype(BF16)
-                seg_sc[start : start + tokens, :] = jnp.broadcast_to(
-                    both[:, HD : HD + 1], (tokens, LANES)
-                )
-
-    mine = q_ref[0].astype(F32)
-    q = jnp.concatenate([mine[top + HD :], jnp.zeros((width, tokens), F32)], axis=0)
-    q = q.astype(BF16)
-    seg = mine[HD + 1 : HD + 2] * 64.0 + mine[HD + 2 : HD + 3]
-    total = None if first else acc_ref[...]
-    for start in range(0, sets * blocks * tokens, key_block):
-        at = slice(start, start + key_block)
-        scores = dot(k_sc[at, :], q)
-        of_key = seg_sc[at, :]
-        of_key = jnp.concatenate([of_key] * (tokens // LANES), axis=1)
-        weights = jnp.where(of_key == seg, jnp.exp2(scores), 0.0).astype(BF16)
-        part = dot(v_sc[:, at], weights)
-        total = part if total is None else total + part
-    if last:
-        out_ref[0] = (total[:HD] / total[HD : HD + 1]).astype(BF16)
-    else:
-        out_ref[...] = total
-
-
-def attend(queries, sets, acc=None, last=False, key_block=512):
+    for number, kv_ref in enumerate(kv_refs):
+        for j in range(blocks):
+            start = (number * blocks + j) * tokens
+            digits = kv_ref[j, :top].astype(F32)
+            seg = digits[HD + 1 : HD + 2] * 64.0 + digits[HD + 2 : HD + 3]
+            keys = kv_ref[j, top : top + HD].astype(F32)
+            both = jnp.concatenate([keys, jnp.broadcast_to(seg, (width, tokens))], axis=0).T
+            v_sc[:, start : start + tokens] = kv_ref[j, :top]
+            k_sc[start : start + tokens, :] = both.astype(BF16)
+            seg_sc[start : start + tokens, :] = jnp.broadcast_to(
+                both[:, HD : HD + 1], (tokens, LANES)
+            )
+    def tile(i):
+        at_q = pl.ds(pl.multiple_of(i * tokens, tokens), tokens)
+        mine = q_ref[i].astype(F32)
+        q = jnp.concatenate([mine[top + HD :], jnp.zeros((width, tokens), F32)], axis=0)
+        q = q.astype(BF16)
+        seg = mine[HD + 1 : HD + 2] * 64.0 + mine[HD + 2 : HD + 3]
+        total = None
+        for start in range(0, sets * blocks * tokens, key_block):
+            at = slice(start, start + key_block)
+            scores = dot(k_sc[at, :], q)
+            of_key = seg_sc[at, :]
+            of_key = jnp.concatenate([of_key] * (tokens // LANES), axis=1)
+            weights = jnp.where(of_key == seg, jnp.exp2(scores), 0.0).astype(BF16)
+            part = dot(v_sc[:, at], weights)
+            total = part if total is None else total + part
+        if not first:
+            total = total + acc_ref[:, at_q]
+        if last:
+            out_ref[i] = (total[:HD] / total[HD : HD + 1]).astype(BF16)
+        else:
+            out_ref[:, at_q] = total
+
+    def step(i, carry):
+        for j in range(unroll):
+            tile(i * unroll + j)
+        return carry
+
+    lax.fori_loop(0, blocks // unroll, step, 0)
+
+
+def attend(queries, sets, acc=None, last=False, key_block=512, unroll=4):
     blocks, depth, tokens = queries.shape
     total = blocks * tokens
     keys = total * len(sets)
     first = acc is None
     top = HD + EXT
-    block = pl.BlockSpec((top, tokens), lambda i: (0, i))
     if last:
         shape = jax.ShapeDtypeStruct((blocks, HD, tokens), BF16)
-        out_spec = pl.BlockSpec((1, HD, tokens), lambda i: (i, 0, 0))
     else:
         shape = jax.ShapeDtypeStruct((top, total), F32)
-        out_spec = block
-    in_specs = [pl.BlockSpec((1, depth, tokens), lambda i: (i, 0, 0))]
-    in_specs += [pl.BlockSpec(kv.shape, lambda i: (0, 0, 0)) for kv in sets]
     operands = [queries, *sets]
     if not first:
-        in_specs.append(block)
         operands.append(acc)
     return pl.pallas_call(
         lambda *refs: attend_kernel(
-            *refs, sets=len(sets), first=first, last=last, key_block=key_block
+            *refs, sets=len(sets), first=first, last=last, key_block=key_block, unroll=unroll
         ),
         out_shape=shape,
-        grid=(blocks,),
-        in_specs=in_specs,
-        out_specs=out_spec,
+        in_specs=[pl.BlockSpec(memory_space=pltpu.VMEM)] * len(operands),
+        out_specs=pl.BlockSpec(memory_space=pltpu.VMEM),
         scratch_shapes=[
             pltpu.VMEM((keys, LANES), BF16),
             pltpu.VMEM((top, keys), BF16),
             pltpu.VMEM((keys, LANES), F32),
         ],
-        compiler_params=cparams("arbitrary"),
+        compiler_params=cparams(),
         cost_estimate=cost(4 * total * keys * LANES, 3 << 20, total * keys),
         name="attend",
     )(*operands)
@@ -225,10 +225,7 @@
         else:
             into = far[:, :piece].reshape(shards * piece, -1)
             out_of = far[:, piece : 2 * piece].reshape(shards * piece, -1)
-            bias = jnp.concatenate(
-                [far[i, 2 * piece : 2 * piece + 1, :piece].astype(F32) for i in range(shards)],
-                axis=1,
-            )
+            bias = far[0, 2 * piece : 2 * piece + 1, :units].astype(F32)
         before = [dot(part, into, NT) + bias for part in x]
         for i in range(2):
             pre = before[i]
@@ -391,29 +388,57 @@
     return before, after, turn(before[:half], axis, 1), turn(after[half:], axis, -1)
 
 
-def pack(w_in, in_bias, w_out, start, count, extra):
-    width = w_in.shape[1]
-    bias = lax.dynamic_slice_in_dim(in_bias, start, count)
-    bias = jnp.pad(bias.reshape(1, count), ((0, extra - 1), (0, width - count)))
-    return jnp.concatenate(
-        [
-            lax.dynamic_slice_in_dim(w_in, start, count),
-            lax.dynamic_slice_in_dim(w_out, start, count),
-            bias,
-        ]
-    )
-
-
-def spread_weights(w_in, in_bias, w_out):
-    half = w_in.shape[0] // 2
-    core = lax.axis_index("c") * half
-    chips = ("y", "xh", "xl")
-    share = half // lax.axis_size(chips)
-    start = core + lax.axis_index(chips) * share
-    far = turn(pack(w_in, in_bias, w_out, start, share, EXT), "grp", 2)
-    own = pack(w_in, in_bias, w_out, core, half, PAD)
-    far = lax.all_gather(far, chips)
-    return own, turn(own, "grp", 1), turn(own, "grp", -1), far
+def pack_kernel(place_ref, in_ref, bias_ref, out_ref, near_ref, far_ref, row_sc, sems):
+    half = (near_ref.shape[0] - PAD) // 2
+    share = (far_ref.shape[0] - EXT) // 2
+    core = place_ref[0]
+    first = pl.multiple_of(core * half, half)
+    at = pl.multiple_of(first + place_ref[1] * share, 16)
+    width = in_ref.shape[1]
+    bias = bias_ref[...].astype(F32)
+    bias = jnp.where(core == 0, bias[:, :half], bias[:, half:])
+    bias = jnp.concatenate([bias, jnp.zeros((1, width - half), F32)], axis=1)
+    row_sc[...] = jnp.broadcast_to(bias, row_sc.shape).astype(BF16)
+    moves = [
+        (in_ref.at[pl.ds(first, half)], near_ref.at[pl.ds(0, half)]),
+        (out_ref.at[pl.ds(first, half)], near_ref.at[pl.ds(half, half)]),
+        (in_ref.at[pl.ds(at, share)], far_ref.at[pl.ds(0, share)]),
+        (out_ref.at[pl.ds(at, share)], far_ref.at[pl.ds(share, share)]),
+        (row_sc, near_ref.at[pl.ds(2 * half, PAD)]),
+        (row_sc.at[pl.ds(0, EXT)], far_ref.at[pl.ds(2 * share, EXT)]),
+    ]
+    copies = [
+        pltpu.make_async_copy(source, target, sems.at[i])
+        for i, (source, target) in enumerate(moves)
+    ]
+    for copy in copies:
+        copy.start()
+    for copy in copies:
+        copy.wait()
+
+
+def pack(place, w_in, in_bias, w_out, shares):
+    units, width = w_in.shape
+    half = units // 2
+    any_space = pl.BlockSpec(memory_space=pl.ANY)
+    return pl.pallas_call(
+        pack_kernel,
+        out_shape=(
+            jax.ShapeDtypeStruct((2 * half + PAD, width), BF16),
+            jax.ShapeDtypeStruct((2 * half // shares + EXT, width), BF16),
+        ),
+        in_specs=[
+            pl.BlockSpec(memory_space=pltpu.SMEM),
+            any_space,
+            pl.BlockSpec(memory_space=pltpu.VMEM),
+            any_space,
+        ],
+        out_specs=(any_space, any_space),
+        scratch_shapes=[pltpu.VMEM((PAD, width), BF16), pltpu.SemaphoreType.DMA((6,))],
+        compiler_params=cparams(),
+        cost_estimate=cost(0, 9 << 20),
+        name="pack",
+    )(place, w_in, in_bias.reshape(1, units), w_out)
 
 
 def local(
@@ -431,19 +456,28 @@
     w_merge,
     merge_bias,
 ):
-    packs = spread_weights(w_in, in_bias, w_out)
+    chips = ("y", "xh", "xl")
+    place = jnp.stack([lax.axis_index("c"), lax.axis_index(chips)]).astype(jnp.int32)
+    near, far = pack(place, w_in, in_bias, w_out, lax.axis_size(chips))
+    far = turn(far, "grp", 2)
+    one, two = turn(near, "grp", 1), turn(near, "grp", -1)
     heads = qkv(tokens, seg_ids, w_qkv)
+    far, heads = lax.optimization_barrier((far, heads))
+    far = lax.all_gather(far, chips)
     mine = lax.all_to_all(heads, ("y", "xh"), 0, 0, tiled=True)
     kv = mine[:, : 2 * HD + EXT]
     kv_x = flip(kv, "xl")
     kv_c = flip(kv, "c")
+    acc = attend(mine, [mine])
+    kv_c, acc = lax.optimization_barrier((kv_c, acc))
+    acc = attend(mine, [kv_c], acc)
+    kv_x, acc = lax.optimization_barrier((kv_x, acc))
     kv_xc = flip(kv_x, "c")
-    acc = attend(mine, [kv])
-    acc = attend(mine, [kv_c], acc)
-    done = attend(mine, [kv_x, kv_xc], acc, last=True)
+    acc = attend(mine, [kv_x], acc)
+    done = attend(mine, [kv_xc], acc, last=True)
     attended = lax.all_to_all(done, ("y", "xh"), 0, 0, tiled=True)
     residual, mlp_in = project(attended, tokens, w_attn_out)
-    own, other = mlp(mlp_in, flip(mlp_in, "c"), packs)
+    own, other = mlp(mlp_in, flip(mlp_in, "c"), (near, one, two, far))
     owner_count = lax.axis_size(("y", "xh", "xl", "c"))
     cap = 4
     merged = merge(

time: 245 us -> 352 us (1.44)
  Pallas kernels: 71 us -> 208 us
  starting transfers between devices: 29.6 us -> 20.4 us
  other arithmetic: 8.66 us -> 0.67 us
  blocking collectives: 61.1 us -> 56.6 us
  waiting for transfers between devices: 46.2 us -> 42.1 us
  local copies, waits for them, and re-layouts: 13.8 us -> 9.89 us
    pallas_call x0 -> x1, Pallas kernels: none -> 141 us  [pack(): pl.pallas_call(pack_kernel, out_shape=(jax.ShapeDtypeStruct((2 * half + P...]
    ppermute x5, starting transfers between devices: 16.9 us -> 7.73 us  [flip(): return lax.ppermute(value, axis, [(0, 1), (1, 0)])]
    concatenate x2 -> x0, other arithmetic: 8.66 us -> none  [pack(): jnp.concatenate([lax.dynamic_slice_in_dim(w_in, start, count), lax.dynami...]
    ppermute x7, waiting for transfers between devices: 30.5 us -> 23.8 us  [turn(): lax.ppermute(value, axis, [(i, (i + by) % size) for i in range(size)])]
    dynamic_slice x3 -> x0, local copies, waits for them, and re-layouts: 4.34 us -> none  [the longest x2 3.57 us: pack(): lax.dynamic_slice_in_dim(w_out, start, count)]
    pallas_call x3 -> x4, Pallas kernels: 33.3 us -> 28.9 us  [attend(): pl.pallas_call(lambda *refs: attend_kernel(*refs, sets=len(sets), first=f...]
  transfers between devices with their start and end apart: 13 -> 13, of which waited for: 6 -> 5; matrix products, arithmetic and copies ran while one was open for 5% -> 0% of each run, Pallas kernels for 18% -> 12%
where the time goes in v3:
time: 352 us; the launch traced here: 351 us
  Pallas kernels  208 us (59%)
  blocking collectives  56.6 us (16%)
  waiting for transfers between devices  42.1 us (12%)
  starting transfers between devices  20.4 us (6%)
  between operations  13.5 us (4%)
  local copies, waits for them, and re-layouts  9.89 us (3%)
    pallas_call x1, Pallas kernels, pack(): pl.pallas_call(pack_kernel, out_shape=(jax.ShapeDtypeStruct((2 * half + P...  141 us
    pallas_call x4, Pallas kernels, attend(): pl.pallas_call(lambda *refs: attend_kernel(*refs, sets=len(sets), first=f...  28.9 us
    all_to_all x1, blocking collectives, local(): mine = lax.all_to_all(heads, ('y', 'xh'), 0, 0, tiled=True)  27.1 us
    ppermute x7, waiting for transfers between devices, turn(): lax.ppermute(value, axis, [(i, (i + by) % size) for i in range(size)])  23.8 us
    ppermute x5, waiting for transfers between devices, flip(): return lax.ppermute(value, axis, [(0, 1), (1, 0)])  18.3 us
    all_to_all x1, blocking collectives, local(): lax.all_to_all(outgoing, ('y', 'xh', 'xl', 'c'), split_axis=0, concat_axi...  16.4 us
    pallas_call x1, Pallas kernels, mlp(): pl.pallas_call(mlp_kernel, out_shape=(shape, shape), in_specs=[vmem, vmem...  15.3 us
    all_to_all x1, blocking collectives, local(): attended = lax.all_to_all(done, ('y', 'xh'), 0, 0, tiled=True)  13.1 us
  transfers between devices with their start and end apart: 13, of which 5 were waited for; matrix products, arithmetic and copies ran while one was open for 0% of the time, Pallas kernels for 12%

profile of v3, /device:TPU:1, one launch (start us, length us, event | category | flops | bytes accessed | tf_op | source)
XLA Modules:
  0.0 350.9 jit_solution(11993907592127497183)
XLA Ops:
  6.5 0.0 all-gather.3.cloned.1.call-start
  6.5 1.3 reshape.32.bias_ref
  7.8 0.7 pad_add_fusion.place_ref
  8.5 141.1 %pack.1 = (bf16[1552,1408]{1,0:T(8,128)(2,1)}, bf16[104,1408]{1,0:T(8,128)(2,1)}) custom-call(s32[2]{0:T(128)} %pad_add_fusion.place_ref, bf16[1536,1408]{1,0:T(8,128)(2,1)} %in_ref.1, bf16[1,1536]{1,0:T(2,128)(2,1)} %reshape.32.bias_ref, bf16[1536,1408]{1,0:T(8,128)(2,1)} %out_ref.1), custom_call_target="tpu_custom_call" | custom-call | bytes 9437184 | tf_op jit(solution)/shard_map/pack/pallas_call | solution.py:424
  149.6 4.5 %collective-permute-start = (bf16[104,1408]{1,0:T(8,128)(2,1)}, bf16[104,1408]{1,0:T(8,128)(2,1)S(1)}, u32[]{:S(2)}, u32[]{:S(2)}) collective-permute-start(bf16[104,1408]{1,0:T(8,128)(2,1)} %get-tuple-element.17), channel_id=1, source_target_pairs={{0,64},{32,96},{64,0},{96,32},{1,65},{33,97},{65,1},{97,33},{2,66}... | collective-permute-start | bytes 878600 | tf_op jit(solution)/shard_map/ppermute | solution.py:381
  154.1 7.9 %qkv.1 = bf16[8,272,256]{2,1,0:T(8,128)(2,1)} custom-call(bf16[256,1408]{1,0:T(8,128)(2,1)} %x_ref.3, s32[1,256]{1,0:T(1,128)} %bitcast.15, bf16[2112,1408]{1,0:T(8,128)(2,1)} %bitcast.12), custom_call_target="tpu_custom_call" | custom-call | flops 1522532352 | bytes 8388608 | tf_op jit(solution)/shard_map/qkv/pallas_call | solution.py:81
  162.0 0.0 collective-permute-done
  162.0 0.0 copy-start.6
  162.0 0.7 copy-done.6
  162.7 0.0 all-gather.3.cloned.1.call-update
  162.7 0.8 collective-permute-start.5
  163.6 1.9 collective-permute-start.6
  165.5 27.1 %all_to_all.25.refs_0_.refs_1_ = bf16[8,272,256]{2,1,0:T(8,128)(2,1)S(1)} all-to-all(bf16[8,272,256]{2,1,0:T(8,128)(2,1)} %qkv.1), channel_id=1, replica_groups=mesh['grp'=4,'y'=4,'xh'=2,'xl'=2,'c'=2] {'y','xh'}, dimensions={0} | all-to-all | bytes 2228224 | tf_op jit(solution)/shard_map/all_to_all | solution.py:467
  192.6 0.0 copy-start
  192.6 3.4 collective-permute-start.2
  196.0 0.3 collective-permute-start.1
  196.3 0.0 copy-done
  196.3 7.2 %attend.4.refs_2_ = f32[96,2048]{1,0:T(8,128)} custom-call(bf16[8,272,256]{2,1,0:T(8,128)(2,1)} %copy-done, bf16[8,272,256]{2,1,0:T(8,128)(2,1)} %copy-done), custom_call_target="tpu_custom_call" | custom-call | flops 2147483648 | bytes 3145728 | tf_op jit(solution)/shard_map/attend/pallas_call | solution.py:165
  203.5 0.0 collective-permute-done.2.refs_1_
  203.5 0.0 copy-start.10
  203.5 0.9 copy-done.10
  204.3 7.3 %attend.5.refs_2_ = f32[96,2048]{1,0:T(8,128)} custom-call(bf16[8,272,256]{2,1,0:T(8,128)(2,1)} %copy-done, bf16[8,184,256]{2,1,0:T(8,128)(2,1)} %copy-done.10, f32[96,2048]{1,0:T(8,128)} %attend.4.refs_2_), custom_call_target="tpu_custom_call" | custom-call | flops 2147483648 | bytes 3145728 | tf_op jit(solution)/shard_map/attend/pallas_call | solution.py:165
  211.7 15.4 %collective-permute-done.1.refs_1_ = bf16[8,184,256]{2,1,0:T(8,128)(2,1)S(1)} collective-permute-done((bf16[8,184,256]{2,1,0:T(8,128)(2,1)S(1)}, bf16[8,184,256]{2,1,0:T(8,128)(2,1)S(1)}, u32[]{:S(2)}, u32[]{:S(2)}) %collective-permute-start.1) | collective-permute-done | bytes 753696 | tf_op jit(solution)/shard_map/ppermute | solution.py:376
  227.1 1.7 collective-permute-start.3
  228.8 0.0 copy-done.9
  228.8 7.3 %attend.6.refs_2_ = f32[96,2048]{1,0:T(8,128)} custom-call(bf16[8,272,256]{2,1,0:T(8,128)(2,1)} %copy-done, bf16[8,184,256]{2,1,0:T(8,128)(2,1)} %copy-done.9, f32[96,2048]{1,0:T(8,128)} %attend.5.refs_2_), custom_call_target="tpu_custom_call" | custom-call | flops 2147483648 | bytes 3145728 | tf_op jit(solution)/shard_map/attend/pallas_call | solution.py:165
  236.1 0.0 collective-permute-done.3.refs_1_
  236.1 0.9 copy-done.11
  237.0 7.2 %attend.7 = bf16[8,88,256]{2,1,0:T(8,128)(2,1)} custom-call(bf16[8,272,256]{2,1,0:T(8,128)(2,1)} %copy-done, bf16[8,184,256]{2,1,0:T(8,128)(2,1)} %copy-done.11, f32[96,2048]{1,0:T(8,128)} %attend.6.refs_2_), custom_call_target="tpu_custom_call" | custom-call | flops 2147483648 | bytes 3145728 | tf_op jit(solution)/shard_map/attend/pallas_call | solution.py:165
  244.1 13.1 %all_to_all.26.att_ref = bf16[8,88,256]{2,1,0:T(8,128)(2,1)} all-to-all(bf16[8,88,256]{2,1,0:T(8,128)(2,1)} %attend.7), channel_id=1, replica_groups=mesh['grp'=4,'y'=4,'xh'=2,'xl'=2,'c'=2] {'y','xh'}, dimensions={0} | all-to-all | bytes 720896 | tf_op jit(solution)/shard_map/all_to_all | solution.py:478
  257.2 3.9 %project.1 = (bf16[256,1408]{1,0:T(8,128)(2,1)}, bf16[256,1408]{1,0:T(8,128)(2,1)}) custom-call(bf16[8,88,256]{2,1,0:T(8,128)(2,1)} %all_to_all.26.att_ref, bf16[256,1408]{1,0:T(8,128)(2,1)} %x_ref.3, bf16[704,1408]{1,0:T(8,128)(2,1)} %w_ref.1), custom_call_target="tpu_custom_call" | custom-call | flops 507510784 | bytes 4194304 | tf_op jit(solution)/shard_map/project/pallas_call | solution.py:193
  261.1 1.9 collective-permute-start.4
  263.1 2.0 collective-permute-done.4.pair_ref
  265.1 0.0 collective-permute-done.5.refs_1_
  265.1 0.0 collective-permute-done.6.refs_2_
  265.1 0.0 all-gather.3.cloned.1.call-done
  265.1 0.8 copy-done.12
  265.9 15.3 %mlp.1 = (bf16[256,1408]{1,0:T(8,128)(2,1)}, bf16[256,1408]{1,0:T(8,128)(2,1)}) custom-call(bf16[256,1408]{1,0:T(8,128)(2,1)} %get-tuple-element.24.x_ref, bf16[256,1408]{1,0:T(8,128)(2,1)} %copy-done.12, bf16[1552,1408]{1,0:T(8,128)(2,1)} %get-tuple-element.25.refs_0_, bf16[1552,1408]{1,0:T(8,128)(2,1)} %collective-permute-done.5.refs_1_, ...), custom_call_target="tpu_custom_call" | custom-call | flops 8858370048 | bytes 20971520 | tf_op jit(solution)/shard_map/mlp/pallas_call | solution.py:244
  281.3 0.5 collective-permute-start.7
  281.7 0.0 copy-done.7
  281.7 0.6 reshape.34.refs_1_
  282.3 0.0 copy-done.8
  282.3 0.6 reshape.35.refs_2_
  282.9 0.8 collective-permute-done.7.refs_6_
  283.8 0.9 copy-done.3
  284.7 3.5 %merge.1.refs_1_ = bf16[64,5760]{1,0:T(8,128)(2,1)} custom-call(bf16[256,1408]{1,0:T(8,128)(2,1)} %get-tuple-element.23.refs_0_, f32[1,1408]{1,0:T(1,128)} %reshape.34.refs_1_, f32[1,1408]{1,0:T(1,128)} %reshape.35.refs_2_, s32[1,256]{1,0:T(1,128)} %bitcast.16, s32[1,64]{1,0:T(1,128)} %bitcast.17, bf16[256,1408]{1,0:T(8,128)(2,1)} %get-tuple-element.27.refs_5_, ...), custom_call_target="tpu_custom_call" | custom-call | flops 184549376 | bytes 4194304 | tf_op jit(solution)/shard_map/merge/pallas_call | solution.py:295
  288.2 0.0 collective-permute-start.9
  288.2 2.7 collective-permute-start.8
  290.9 16.4 %collective-permute-done.9.refs_5_ = bf16[64,5760]{1,0:T(8,128)(2,1)S(1)} collective-permute-done((bf16[64,5760]{1,0:T(8,128)(2,1)}, bf16[64,5760]{1,0:T(8,128)(2,1)S(1)}, u32[]{:S(2)}, u32[]{:S(2)}) %collective-permute-start.9) | collective-permute-done | bytes 737312 | tf_op jit(solution)/shard_map/ppermute | solution.py:381
  307.3 0.1 collective-permute-start.10
  307.4 0.0 collective-permute-done.8.refs_2_
  307.4 0.0 copy-start.2
  307.5 2.7 collective-permute-start.11
  310.2 7.3 %collective-permute-done.10.refs_3_ = bf16[32,5760]{1,0:T(8,128)(2,1)S(1)} collective-permute-done((bf16[32,5760]{1,0:T(8,128)(2,1)S(1)}, bf16[32,5760]{1,0:T(8,128)(2,1)S(1)}, u32[]{:S(2)}, u32[]{:S(2)}) %collective-permute-start.10) | collective-permute-done | bytes 368672 | tf_op jit(solution)/shard_map/ppermute | solution.py:381
  317.5 0.0 collective-permute-done.11.refs_4_
  317.5 0.0 copy-done.1
  317.5 0.0 copy-done.2
  317.5 0.7 copy-done.4
  318.3 0.1 copy-done.5
  318.4 7.0 %embed.1 = bf16[512,512]{1,0:T(8,128)(2,1)} custom-call(s32[1]{0:T(128)} %bitcast.refs_0_, bf16[64,5760]{1,0:T(8,128)(2,1)} %merge.1.refs_1_, bf16[64,5760]{1,0:T(8,128)(2,1)} %copy-done.2, bf16[32,5760]{1,0:T(8,128)(2,1)} %copy-done.4, bf16[32,5760]{1,0:T(8,128)(2,1)} %copy-done.5, bf16[64,5760]{1,0:T(8,128)(2,1)} %copy-done.1, bf16[5632,512]{1,0:T(8,128)(2,1)} %refs_6_.1, ...), custom_call_target="tpu_custom_call" | custom-call | flops 1476395008 | bytes 10485760 | tf_op jit(solution)/shard_map/embed/pallas_call | solution.py:355
  325.4 1.2 reshape.39
  326.6 16.4 %all_to_all.27 = bf16[32,4,4,512]{3,2,1,0:T(4,128)(2,1)S(1)} all-to-all(bf16[32,4,4,512]{3,2,1,0:T(4,128)(2,1)S(1)} %reshape.39), channel_id=1, replica_groups=mesh['grp'=4,'y'=4,'xh'=2,'xl'=2,'c'=2] {'y','xh','xl','c'}, dimensions={0} | all-to-all | bytes 1048576 | tf_op jit(solution)/shard_map/all_to_all | solution.py:500
  343.0 0.2 copy.14
  343.2 0.9 reshape.40
  (12 shorter events, 0.1 us)
Async XLA Ops:
  6.5 258.6 %all-gather.3.cloned.1.call-start = ((), (), s32[]{:S(2)}) async-start(), calls=%async_computation.3 | async-start | bytes 4978688 | tf_op jit(solution)/shard_map/all_gather | solution.py:466
  149.6 12.4 %collective-permute-start = (bf16[104,1408]{1,0:T(8,128)(2,1)}, bf16[104,1408]{1,0:T(8,128)(2,1)S(1)}, u32[]{:S(2)}, u32[]{:S(2)}) collective-permute-start(bf16[104,1408]{1,0:T(8,128)(2,1)} %get-tuple-element.17), channel_id=1, source_target_pairs={{0,64},{32,96},{64,0},{96,32},{1,65},{33,97},{65,1},{97,33},{2,66}... | collective-permute-start | bytes 878600 | tf_op jit(solution)/shard_map/ppermute | solution.py:381
  162.0 0.7 copy-start.6
  162.7 102.3 %collective-permute-start.5 = (bf16[1552,1408]{1,0:T(8,128)(2,1)}, bf16[1552,1408]{1,0:T(8,128)(2,1)}, u32[]{:S(2)}, u32[]{:S(2)}) collective-permute-start(bf16[1552,1408]{1,0:T(8,128)(2,1)} %get-tuple-element.25.refs_0_), channel_id=1, source_target_pairs={{0,32},{32,64},{64,96},{96,0},{1,33},{33,65},{65,97},{97,1},{2,34}... | collective-permute-start | bytes 13111304 | tf_op jit(solution)/shard_map/ppermute | solution.py:381
  163.6 101.5 %collective-permute-start.6 = (bf16[1552,1408]{1,0:T(8,128)(2,1)}, bf16[1552,1408]{1,0:T(8,128)(2,1)}, u32[]{:S(2)}, u32[]{:S(2)}) collective-permute-start(bf16[1552,1408]{1,0:T(8,128)(2,1)} %get-tuple-element.25.refs_0_), channel_id=1, source_target_pairs={{0,96},{32,0},{64,32},{96,64},{1,97},{33,1},{65,33},{97,65},{2,98}... | collective-permute-start | bytes 13111304 | tf_op jit(solution)/shard_map/ppermute | solution.py:381
  192.6 3.7 %copy-start = (bf16[8,272,256]{2,1,0:T(8,128)(2,1)}, bf16[8,272,256]{2,1,0:T(8,128)(2,1)S(1)}, u32[]{:S(2)}) copy-start(bf16[8,272,256]{2,1,0:T(8,128)(2,1)S(1)} %all_to_all.25.refs_0_.refs_1_) | copy-start | bytes 3342340
  192.6 10.8 %collective-permute-start.2 = (bf16[8,184,256]{2,1,0:T(8,128)(2,1)S(1)}, bf16[8,184,256]{2,1,0:T(8,128)(2,1)S(1)}, u32[]{:S(2)}, u32[]{:S(2)}) collective-permute-start(bf16[8,184,256]{2,1,0:T(8,128)(2,1)S(1)} %slice.12), channel_id=1, source_target_pairs={{0,1},{1,0},{2,3},{3,2},{4,5},{5,4},{6,7},{7,6},{8,9},{9,8},{10,11... | collective-permute-start | bytes 2261000 | tf_op jit(solution)/shard_map/ppermute | solution.py:376
  196.0 31.1 %collective-permute-start.1 = (bf16[8,184,256]{2,1,0:T(8,128)(2,1)S(1)}, bf16[8,184,256]{2,1,0:T(8,128)(2,1)S(1)}, u32[]{:S(2)}, u32[]{:S(2)}) collective-permute-start(bf16[8,184,256]{2,1,0:T(8,128)(2,1)S(1)} %slice.12), channel_id=1, source_target_pairs={{0,2},{2,0},{1,3},{3,1},{4,6},{6,4},{5,7},{7,5},{8,10},{10,8},{9,1... | collective-permute-start | bytes 2261000 | tf_op jit(solution)/shard_map/ppermute | solution.py:376
  203.5 0.9 copy-start.10
  227.1 1.7 copy-start.9
  227.1 9.0 %collective-permute-start.3 = (bf16[8,184,256]{2,1,0:T(8,128)(2,1)S(1)}, bf16[8,184,256]{2,1,0:T(8,128)(2,1)S(1)}, u32[]{:S(2)}, u32[]{:S(2)}) collective-permute-start(bf16[8,184,256]{2,1,0:T(8,128)(2,1)S(1)} %collective-permute-done.1.refs_1_), channel_id=1, source_target_pairs={{0,1},{1,0},{2,3},{3,2},{4,5},{5,4},{6,7},{7,6},{8,9},{9,8},{10,11... | collective-permute-start | bytes 2261000 | tf_op jit(solution)/shard_map/ppermute | solution.py:376
  236.1 0.9 copy-start.11
  261.1 3.9 %collective-permute-start.4 = (bf16[256,1408]{1,0:T(8,128)(2,1)}, bf16[256,1408]{1,0:T(8,128)(2,1)S(1)}, u32[]{:S(2)}, u32[]{:S(2)}) collective-permute-start(bf16[256,1408]{1,0:T(8,128)(2,1)} %get-tuple-element.24.x_ref), channel_id=1, source_target_pairs={{0,1},{1,0},{2,3},{3,2},{4,5},{5,4},{6,7},{7,6},{8,9},{9,8},{10,11... | collective-permute-start | bytes 2162696 | tf_op jit(solution)/shard_map/ppermute | solution.py:376
  265.1 0.9 copy-start.12
  265.9 15.8 %copy-start.7 = (f32[1408]{0:T(1024)S(1)}, f32[1408]{0:T(1024)}, u32[]{:S(2)}) copy-start(f32[1408]{0:T(1024)} %param.22) | copy-start | bytes 16900
  265.9 16.4 %copy-start.8 = (f32[1408]{0:T(1024)S(1)}, f32[1408]{0:T(1024)}, u32[]{:S(2)}) copy-start(f32[1408]{0:T(1024)} %param.23) | copy-start | bytes 16900
  281.3 2.5 collective-permute-start.7
  283.8 0.9 copy-start.3
  288.2 19.1 %collective-permute-start.9 = (bf16[64,5760]{1,0:T(8,128)(2,1)}, bf16[64,5760]{1,0:T(8,128)(2,1)S(1)}, u32[]{:S(2)}, u32[]{:S(2)}) collective-permute-start(bf16[64,5760]{1,0:T(8,128)(2,1)} %merge.1.refs_1_), channel_id=1, source_target_pairs={{0,32},{32,64},{64,96},{96,0},{1,33},{33,65},{65,97},{97,1},{2,34}... | collective-permute-start | bytes 2211848 | tf_op jit(solution)/shard_map/ppermute | solution.py:381
  288.2 19.2 %collective-permute-start.8 = (bf16[64,5760]{1,0:T(8,128)(2,1)}, bf16[64,5760]{1,0:T(8,128)(2,1)S(1)}, u32[]{:S(2)}, u32[]{:S(2)}) collective-permute-start(bf16[64,5760]{1,0:T(8,128)(2,1)} %merge.1.refs_1_), channel_id=1, source_target_pairs={{0,96},{32,0},{64,32},{96,64},{1,97},{33,1},{65,33},{97,65},{2,98}... | collective-permute-start | bytes 2211848 | tf_op jit(solution)/shard_map/ppermute | solution.py:381
  307.3 10.2 %copy-start.1 = (bf16[64,5760]{1,0:T(8,128)(2,1)}, bf16[64,5760]{1,0:T(8,128)(2,1)S(1)}, u32[]{:S(2)}) copy-start(bf16[64,5760]{1,0:T(8,128)(2,1)S(1)} %collective-permute-done.9.refs_5_) | copy-start | bytes 2211844
  307.3 10.2 %collective-permute-start.10 = (bf16[32,5760]{1,0:T(8,128)(2,1)S(1)}, bf16[32,5760]{1,0:T(8,128)(2,1)S(1)}, u32[]{:S(2)}, u32[]{:S(2)}) collective-permute-start(bf16[32,5760]{1,0:T(8,128)(2,1)S(1)} %slice.13), channel_id=1, source_target_pairs={{0,32},{32,64},{64,96},{96,0},{1,33},{33,65},{65,97},{97,1},{2,34}... | collective-permute-start | bytes 1105928 | tf_op jit(solution)/shard_map/ppermute | solution.py:381
  307.4 10.1 %copy-start.2 = (bf16[64,5760]{1,0:T(8,128)(2,1)}, bf16[64,5760]{1,0:T(8,128)(2,1)S(1)}, u32[]{:S(2)}) copy-start(bf16[64,5760]{1,0:T(8,128)(2,1)S(1)} %collective-permute-done.8.refs_2_) | copy-start | bytes 2211844
  307.5 10.0 %collective-permute-start.11 = (bf16[32,5760]{1,0:T(8,128)(2,1)S(1)}, bf16[32,5760]{1,0:T(8,128)(2,1)S(1)}, u32[]{:S(2)}, u32[]{:S(2)}) collective-permute-start(bf16[32,5760]{1,0:T(8,128)(2,1)S(1)} %slice.14), channel_id=1, source_target_pairs={{0,96},{32,0},{64,32},{96,64},{1,97},{33,1},{65,33},{97,65},{2,98}... | collective-permute-start | bytes 1105928 | tf_op jit(solution)/shard_map/ppermute | solution.py:381
  317.5 0.8 copy-start.4
  317.5 0.9 copy-start.5
Sparse Core Ops, SparseCore 0:
  162.9 71.2 all-gather.2

commit v4 on v3

--- a/solution.py
+++ b/solution.py
@@ -67,13 +67,15 @@
             head = number % 2 * (HEADS // 2) + i
             rows = part[i * HD : (i + 1) * HD]
             if kind == 2:
-                out_ref[head, : HD + EXT] = jnp.concatenate([rows, extra], axis=0).astype(BF16)
+                out_ref[head, HD : 2 * HD + EXT] = jnp.concatenate([extra, rows], axis=0).astype(
+                    BF16
+                )
                 continue
             norm = lax.rsqrt(jnp.mean(rows * rows, axis=0, keepdims=True) + NORM_EPS)
             if kind == 0:
-                out_ref[head, 2 * HD + EXT :] = (rows * (norm * scale)).astype(BF16)
+                out_ref[head, :HD] = (rows * (norm * scale)).astype(BF16)
             else:
-                out_ref[head, HD + EXT : 2 * HD + EXT] = (rows * norm).astype(BF16)
+                out_ref[head, 2 * HD + EXT :] = (rows * norm).astype(BF16)
 
 
 def qkv(tokens, seg_ids, w_qkv):
@@ -97,33 +99,32 @@
     )(tokens, seg_ids.reshape(1, rows), w_qkv.T)
 
 
-def attend_kernel(*refs, sets, first, last, key_block, unroll):
+def attend_kernel(*refs, sets, first, send, key_block, unroll):
     q_ref = refs[0]
     kv_refs = refs[1 : 1 + sets]
     rest = refs[1 + sets :]
     if not first:
         acc_ref, rest = rest[0], rest[1:]
     out_ref, k_sc, v_sc, seg_sc = rest
-    blocks, _, tokens = q_ref.shape
-    top = HD + EXT
+    blocks, top, tokens = q_ref.shape
     width = LANES - HD
     for number, kv_ref in enumerate(kv_refs):
         for j in range(blocks):
             start = (number * blocks + j) * tokens
-            digits = kv_ref[j, :top].astype(F32)
-            seg = digits[HD + 1 : HD + 2] * 64.0 + digits[HD + 2 : HD + 3]
-            keys = kv_ref[j, top : top + HD].astype(F32)
+            digits = kv_ref[j, : 2 * EXT].astype(F32)
+            seg = digits[1:2] * 64.0 + digits[2:3]
+            keys = kv_ref[j, top:].astype(F32)
             both = jnp.concatenate([keys, jnp.broadcast_to(seg, (width, tokens))], axis=0).T
             v_sc[:, start : start + tokens] = kv_ref[j, :top]
             k_sc[start : start + tokens, :] = both.astype(BF16)
             seg_sc[start : start + tokens, :] = jnp.broadcast_to(
                 both[:, HD : HD + 1], (tokens, LANES)
             )
+
     def tile(i):
         at_q = pl.ds(pl.multiple_of(i * tokens, tokens), tokens)
         mine = q_ref[i].astype(F32)
-        q = jnp.concatenate([mine[top + HD :], jnp.zeros((width, tokens), F32)], axis=0)
-        q = q.astype(BF16)
+        q = jnp.concatenate([mine[:HD], jnp.zeros((width, tokens), F32)], axis=0).astype(BF16)
         seg = mine[HD + 1 : HD + 2] * 64.0 + mine[HD + 2 : HD + 3]
         total = None
         for start in range(0, sets * blocks * tokens, key_block):
@@ -136,8 +137,10 @@
             total = part if total is None else total + part
         if not first:
             total = total + acc_ref[:, at_q]
-        if last:
-            out_ref[i] = (total[:HD] / total[HD : HD + 1]).astype(BF16)
+        if send:
+            near = total[:1].astype(BF16).astype(F32)
+            rows = [near, total[:1] - near, jnp.zeros((EXT - 2, tokens), F32), total[EXT:]]
+            out_ref[i] = jnp.concatenate(rows, axis=0).astype(BF16)
         else:
             out_ref[:, at_q] = total
 
@@ -149,14 +152,13 @@
     lax.fori_loop(0, blocks // unroll, step, 0)
 
 
-def attend(queries, sets, acc=None, last=False, key_block=512, unroll=4):
-    blocks, depth, tokens = queries.shape
+def attend(queries, sets, acc=None, send=False, key_block=512, unroll=4):
+    blocks, top, tokens = queries.shape
     total = blocks * tokens
     keys = total * len(sets)
     first = acc is None
-    top = HD + EXT
-    if last:
-        shape = jax.ShapeDtypeStruct((blocks, HD, tokens), BF16)
+    if send:
+        shape = jax.ShapeDtypeStruct(queries.shape, BF16)
     else:
         shape = jax.ShapeDtypeStruct((top, total), F32)
     operands = [queries, *sets]
@@ -164,7 +166,7 @@
         operands.append(acc)
     return pl.pallas_call(
         lambda *refs: attend_kernel(
-            *refs, sets=len(sets), first=first, last=last, key_block=key_block, unroll=unroll
+            *refs, sets=len(sets), first=first, send=send, key_block=key_block, unroll=unroll
         ),
         out_shape=shape,
         in_specs=[pl.BlockSpec(memory_space=pltpu.VMEM)] * len(operands),
@@ -178,6 +180,28 @@
         cost_estimate=cost(4 * total * keys * LANES, 3 << 20, total * keys),
         name="attend",
     )(*operands)
+
+
+def combine_kernel(acc_ref, sent_ref, out_ref):
+    blocks, _, tokens = sent_ref.shape
+    for i in range(blocks):
+        acc = acc_ref[:, i * tokens : (i + 1) * tokens]
+        sent = sent_ref[i].astype(F32)
+        weight = acc[:1] + (sent[:1] + sent[1:2])
+        out_ref[i] = ((acc[EXT:] + sent[EXT:]) / weight).astype(BF16)
+
+
+def combine(acc, sent):
+    blocks, top, tokens = sent.shape
+    return pl.pallas_call(
+        combine_kernel,
+        out_shape=jax.ShapeDtypeStruct((blocks, top - EXT, tokens), BF16),
+        in_specs=[pl.BlockSpec(memory_space=pltpu.VMEM)] * 2,
+        out_specs=pl.BlockSpec(memory_space=pltpu.VMEM),
+        compiler_params=cparams(),
+        cost_estimate=cost(0, 2 << 20),
+        name="combine",
+    )(acc, sent)
 
 
 def project_kernel(att_ref, x_ref, w_ref, res_ref, in_ref):
@@ -388,7 +412,7 @@
     return before, after, turn(before[:half], axis, 1), turn(after[half:], axis, -1)
 
 
-def pack_kernel(place_ref, in_ref, bias_ref, out_ref, near_ref, far_ref, row_sc, sems):
+def pack_kernel(place_ref, in_ref, bias_ref, out_ref, near_ref, far_ref, row_sc, near_sc, far_sc, sems):
     half = (near_ref.shape[0] - PAD) // 2
     share = (far_ref.shape[0] - EXT) // 2
     core = place_ref[0]
@@ -399,21 +423,36 @@
     bias = jnp.where(core == 0, bias[:, :half], bias[:, half:])
     bias = jnp.concatenate([bias, jnp.zeros((1, width - half), F32)], axis=1)
     row_sc[...] = jnp.broadcast_to(bias, row_sc.shape).astype(BF16)
-    moves = [
-        (in_ref.at[pl.ds(first, half)], near_ref.at[pl.ds(0, half)]),
-        (out_ref.at[pl.ds(first, half)], near_ref.at[pl.ds(half, half)]),
-        (in_ref.at[pl.ds(at, share)], far_ref.at[pl.ds(0, share)]),
-        (out_ref.at[pl.ds(at, share)], far_ref.at[pl.ds(share, share)]),
-        (row_sc, near_ref.at[pl.ds(2 * half, PAD)]),
-        (row_sc.at[pl.ds(0, EXT)], far_ref.at[pl.ds(2 * share, EXT)]),
+    pieces = [
+        (in_ref, first, 0, half, near_ref, near_sc),
+        (out_ref, first, half, half, near_ref, near_sc),
+        (in_ref, at, 0, share, far_ref, far_sc),
+        (out_ref, at, share, share, far_ref, far_sc),
     ]
-    copies = [
-        pltpu.make_async_copy(source, target, sems.at[i])
-        for i, (source, target) in enumerate(moves)
+    inward = []
+    for i, (source, begin, to, size, _, buffer) in enumerate(pieces):
+        copy = pltpu.make_async_copy(
+            source.at[pl.ds(begin, size)], buffer.at[pl.ds(to, size)], sems.at[i]
+        )
+        copy.start()
+        inward.append(copy)
+    outward = [
+        pltpu.make_async_copy(row_sc, near_ref.at[pl.ds(2 * half, PAD)], sems.at[8]),
+        pltpu.make_async_copy(
+            row_sc.at[pl.ds(0, EXT)], far_ref.at[pl.ds(2 * share, EXT)], sems.at[9]
+        ),
     ]
-    for copy in copies:
+    outward[0].start()
+    outward[1].start()
+    for i in (2, 3, 0, 1):
+        _, _, to, size, target, buffer = pieces[i]
+        inward[i].wait()
+        copy = pltpu.make_async_copy(
+            buffer.at[pl.ds(to, size)], target.at[pl.ds(to, size)], sems.at[4 + i]
+        )
         copy.start()
-    for copy in copies:
+        outward.append(copy)
+    for copy in outward:
         copy.wait()
 
 
@@ -434,7 +473,12 @@
             any_space,
         ],
         out_specs=(any_space, any_space),
-        scratch_shapes=[pltpu.VMEM((PAD, width), BF16), pltpu.SemaphoreType.DMA((6,))],
+        scratch_shapes=[
+            pltpu.VMEM((PAD, width), BF16),
+            pltpu.VMEM((2 * half, width), BF16),
+            pltpu.VMEM((2 * half // shares, width), BF16),
+            pltpu.SemaphoreType.DMA((10,)),
+        ],
         compiler_params=cparams(),
         cost_estimate=cost(0, 9 << 20),
         name="pack",
@@ -465,16 +509,15 @@
     far, heads = lax.optimization_barrier((far, heads))
     far = lax.all_gather(far, chips)
     mine = lax.all_to_all(heads, ("y", "xh"), 0, 0, tiled=True)
-    kv = mine[:, : 2 * HD + EXT]
-    kv_x = flip(kv, "xl")
+    queries, kv = mine[:, : HD + EXT], mine[:, HD:]
+    away = flip(queries, "xl")
     kv_c = flip(kv, "c")
-    acc = attend(mine, [mine])
-    kv_c, acc = lax.optimization_barrier((kv_c, acc))
-    acc = attend(mine, [kv_c], acc)
-    kv_x, acc = lax.optimization_barrier((kv_x, acc))
-    kv_xc = flip(kv_x, "c")
-    acc = attend(mine, [kv_x], acc)
-    done = attend(mine, [kv_xc], acc, last=True)
+    acc = attend(queries, [kv])
+    away, kv_c, acc = lax.optimization_barrier((away, kv_c, acc))
+    sent = flip(attend(away, [kv, kv_c], send=True), "xl")
+    acc = attend(queries, [kv_c], acc)
+    sent, acc = lax.optimization_barrier((sent, acc))
+    done = combine(acc, sent)
     attended = lax.all_to_all(done, ("y", "xh"), 0, 0, tiled=True)
     residual, mlp_in = project(attended, tokens, w_attn_out)
     own, other = mlp(mlp_in, flip(mlp_in, "c"), (near, one, two, far))

time: 352 us -> 215 us (0.61)
  Pallas kernels: 208 us -> 71 us
  waiting for transfers between devices: 42.1 us -> 37.1 us
    pallas_call x1, Pallas kernels: 141 us -> 5.22 us  [pack(): pl.pallas_call(pack_kernel, out_shape=(jax.ShapeDtypeStruct((2 * half + P...]
    ppermute x5, waiting for transfers between devices: 18.3 us -> 13.3 us  [flip(): return lax.ppermute(value, axis, [(0, 1), (1, 0)])]
    all_to_all x1, blocking collectives: 16.4 us -> 20.5 us  [local(): lax.all_to_all(outgoing, ('y', 'xh', 'xl', 'c'), split_axis=0, concat_axi...]
    pallas_call x4 -> x3, Pallas kernels: 28.9 us -> 26 us  [attend(): pl.pallas_call(lambda *refs: attend_kernel(*refs, sets=len(sets), first=f...]
  transfers between devices with their start and end apart: 13 -> 13, of which waited for: 5 -> 6; matrix products, arithmetic and copies ran while one was open for 0% -> 1% of each run, Pallas kernels for 12% -> 19%
where the time goes in v4:
time: 215 us; the launch traced here: 214 us
  Pallas kernels  71 us (33%)
  blocking collectives  59.9 us (28%)
  waiting for transfers between devices  37.1 us (17%)
  starting transfers between devices  20.8 us (10%)
  between operations  13.5 us (6%)
  local copies, waits for them, and re-layouts  10.9 us (5%)
    all_to_all x1, blocking collectives, local(): mine = lax.all_to_all(heads, ('y', 'xh'), 0, 0, tiled=True)  27 us
    pallas_call x3, Pallas kernels, attend(): pl.pallas_call(lambda *refs: attend_kernel(*refs, sets=len(sets), first=f...  26 us
    ppermute x7, waiting for transfers between devices, turn(): lax.ppermute(value, axis, [(i, (i + by) % size) for i in range(size)])  23.8 us
    all_to_all x1, blocking collectives, local(): lax.all_to_all(outgoing, ('y', 'xh', 'xl', 'c'), split_axis=0, concat_axi...  20.5 us
    pallas_call x1, Pallas kernels, mlp(): pl.pallas_call(mlp_kernel, out_shape=(shape, shape), in_specs=[vmem, vmem...  15.3 us
    ppermute x5, waiting for transfers between devices, flip(): return lax.ppermute(value, axis, [(0, 1), (1, 0)])  13.3 us
    ppermute x7, starting transfers between devices, turn(): lax.ppermute(value, axis, [(i, (i + by) % size) for i in range(size)])  12.7 us
    all_to_all x1, blocking collectives, local(): attended = lax.all_to_all(done, ('y', 'xh'), 0, 0, tiled=True)  12.4 us
  transfers between devices with their start and end apart: 13, of which 6 were waited for; matrix products, arithmetic and copies ran while one was open for 1% of the time, Pallas kernels for 19%

profile of v4, /device:TPU:1, one launch (start us, length us, event | category | flops | bytes accessed | tf_op | source)
XLA Modules:
  0.0 213.9 jit_solution(14502908940625373459)
XLA Ops:
  6.5 0.0 all-gather.3.cloned.1.call-start
  6.5 1.3 reshape.32.bias_ref
  7.8 0.6 pad_add_fusion.place_ref
  8.4 5.2 %pack.1 = (bf16[1552,1408]{1,0:T(8,128)(2,1)}, bf16[104,1408]{1,0:T(8,128)(2,1)}) custom-call(s32[2]{0:T(128)} %pad_add_fusion.place_ref, bf16[1536,1408]{1,0:T(8,128)(2,1)} %in_ref.1, bf16[1,1536]{1,0:T(2,128)(2,1)} %reshape.32.bias_ref, bf16[1536,1408]{1,0:T(8,128)(2,1)} %out_ref.1), custom_call_target="tpu_custom_call" | custom-call | bytes 9437184 | tf_op jit(solution)/shard_map/pack/pallas_call | solution.py:463
  13.6 4.5 %collective-permute-start = (bf16[104,1408]{1,0:T(8,128)(2,1)}, bf16[104,1408]{1,0:T(8,128)(2,1)S(1)}, u32[]{:S(2)}, u32[]{:S(2)}) collective-permute-start(bf16[104,1408]{1,0:T(8,128)(2,1)} %get-tuple-element.18), channel_id=1, source_target_pairs={{0,64},{32,96},{64,0},{96,32},{1,65},{33,97},{65,1},{97,33},{2,66}... | collective-permute-start | bytes 878600 | tf_op jit(solution)/shard_map/ppermute | solution.py:405
  18.1 7.9 %qkv.1 = bf16[8,272,256]{2,1,0:T(8,128)(2,1)} custom-call(bf16[256,1408]{1,0:T(8,128)(2,1)} %x_ref.3, s32[1,256]{1,0:T(1,128)} %bitcast.15, bf16[2112,1408]{1,0:T(8,128)(2,1)} %bitcast.12), custom_call_target="tpu_custom_call" | custom-call | flops 1522532352 | bytes 8388608 | tf_op jit(solution)/shard_map/qkv/pallas_call | solution.py:83
  26.0 0.0 collective-permute-done
  26.0 0.0 copy-start.8
  26.1 0.7 copy-done.8
  26.8 0.0 all-gather.3.cloned.1.call-update
  26.8 0.8 collective-permute-start.5
  27.6 1.9 collective-permute-start.6
  29.5 27.0 %all_to_all.25 = bf16[8,272,256]{2,1,0:T(8,128)(2,1)S(1)} all-to-all(bf16[8,272,256]{2,1,0:T(8,128)(2,1)} %qkv.1), channel_id=1, replica_groups=mesh['grp'=4,'y'=4,'xh'=2,'xl'=2,'c'=2] {'y','xh'}, dimensions={0} | all-to-all | bytes 2228224 | tf_op jit(solution)/shard_map/all_to_all | solution.py:511
  56.6 0.0 copy-start.2
  56.7 3.4 %collective-permute-start.2 = (bf16[8,184,256]{2,1,0:T(8,128)(2,1)S(1)}, bf16[8,184,256]{2,1,0:T(8,128)(2,1)S(1)}, u32[]{:S(2)}, u32[]{:S(2)}) collective-permute-start(bf16[8,184,256]{2,1,0:T(8,128)(2,1)S(1)} %slice.17.refs_1_), channel_id=1, source_target_pairs={{0,1},{1,0},{2,3},{3,2},{4,5},{5,4},{6,7},{7,6},{8,9},{9,8},{10,11... | collective-permute-start | bytes 2261000 | tf_op jit(solution)/shard_map/ppermute | solution.py:400
  60.1 0.0 copy-start.4
  60.1 0.4 collective-permute-start.1
  60.4 0.0 copy-done.2
  60.5 0.4 copy-done.4
  60.8 6.8 %attend.3.refs_2_ = f32[96,2048]{1,0:T(8,128)} custom-call(bf16[8,96,256]{2,1,0:T(8,128)(2,1)} %copy-done.4, bf16[8,184,256]{2,1,0:T(8,128)(2,1)} %copy-done.2), custom_call_target="tpu_custom_call" | custom-call | flops 2147483648 | bytes 3145728 | tf_op jit(solution)/shard_map/attend/pallas_call | solution.py:167
  67.6 8.6 %collective-permute-done.1.refs_0_ = bf16[8,96,256]{2,1,0:T(8,128)(2,1)S(1)} collective-permute-done((bf16[8,96,256]{2,1,0:T(8,128)(2,1)S(1)}, bf16[8,96,256]{2,1,0:T(8,128)(2,1)S(1)}, u32[]{:S(2)}, u32[]{:S(2)}) %collective-permute-start.1) | collective-permute-done | bytes 393248 | tf_op jit(solution)/shard_map/ppermute | solution.py:400
  76.2 0.0 collective-permute-done.2.refs_2_.refs_1_
  76.2 0.7 copy-done.13
  77.0 0.9 copy-done.11
  77.8 12.2 %attend.4 = bf16[8,96,256]{2,1,0:T(8,128)(2,1)} custom-call(bf16[8,96,256]{2,1,0:T(8,128)(2,1)} %copy-done.13, bf16[8,184,256]{2,1,0:T(8,128)(2,1)} %copy-done.2, bf16[8,184,256]{2,1,0:T(8,128)(2,1)} %copy-done.11), custom_call_target="tpu_custom_call" | custom-call | flops 4294967296 | bytes 3145728 | tf_op jit(solution)/shard_map/attend/pallas_call | solution.py:167
  90.0 0.5 collective-permute-start.3
  90.5 7.1 %attend.5.acc_ref = f32[96,2048]{1,0:T(8,128)} custom-call(bf16[8,96,256]{2,1,0:T(8,128)(2,1)} %copy-done.4, bf16[8,184,256]{2,1,0:T(8,128)(2,1)} %copy-done.11, f32[96,2048]{1,0:T(8,128)} %attend.3.refs_2_), custom_call_target="tpu_custom_call" | custom-call | flops 2147483648 | bytes 3145728 | tf_op jit(solution)/shard_map/attend/pallas_call | solution.py:167
  97.6 1.9 collective-permute-done.3.sent_ref
  99.5 0.7 copy-done.5
  100.2 2.1 combine.1
  102.3 12.4 %all_to_all.26.att_ref = bf16[8,88,256]{2,1,0:T(8,128)(2,1)} all-to-all(bf16[8,88,256]{2,1,0:T(8,128)(2,1)} %combine.1), channel_id=1, replica_groups=mesh['grp'=4,'y'=4,'xh'=2,'xl'=2,'c'=2] {'y','xh'}, dimensions={0} | all-to-all | bytes 720896 | tf_op jit(solution)/shard_map/all_to_all | solution.py:521
  114.7 3.9 %project.1 = (bf16[256,1408]{1,0:T(8,128)(2,1)}, bf16[256,1408]{1,0:T(8,128)(2,1)}) custom-call(bf16[8,88,256]{2,1,0:T(8,128)(2,1)} %all_to_all.26.att_ref, bf16[256,1408]{1,0:T(8,128)(2,1)} %x_ref.3, bf16[704,1408]{1,0:T(8,128)(2,1)} %w_ref.1), custom_call_target="tpu_custom_call" | custom-call | flops 507510784 | bytes 4194304 | tf_op jit(solution)/shard_map/project/pallas_call | solution.py:217
  118.6 3.4 %collective-permute-start.4 = (bf16[256,1408]{1,0:T(8,128)(2,1)}, bf16[256,1408]{1,0:T(8,128)(2,1)S(1)}, u32[]{:S(2)}, u32[]{:S(2)}) collective-permute-start(bf16[256,1408]{1,0:T(8,128)(2,1)} %get-tuple-element.26.x_ref), channel_id=1, source_target_pairs={{0,1},{1,0},{2,3},{3,2},{4,5},{5,4},{6,7},{7,6},{8,9},{9,8},{10,11... | collective-permute-start | bytes 2162696 | tf_op jit(solution)/shard_map/ppermute | solution.py:400
  122.0 2.0 collective-permute-done.4.pair_ref
  124.0 0.0 collective-permute-done.5.refs_1_
  124.0 0.0 collective-permute-done.6.refs_2_
  124.0 0.0 all-gather.3.cloned.1.call-done
  124.1 0.8 copy-done.12
  124.9 15.3 %mlp.1 = (bf16[256,1408]{1,0:T(8,128)(2,1)}, bf16[256,1408]{1,0:T(8,128)(2,1)}) custom-call(bf16[256,1408]{1,0:T(8,128)(2,1)} %get-tuple-element.26.x_ref, bf16[256,1408]{1,0:T(8,128)(2,1)} %copy-done.12, bf16[1552,1408]{1,0:T(8,128)(2,1)} %get-tuple-element.27.refs_0_, bf16[1552,1408]{1,0:T(8,128)(2,1)} %collective-permute-done.5.refs_1_, ...), custom_call_target="tpu_custom_call" | custom-call | flops 8858370048 | bytes 20971520 | tf_op jit(solution)/shard_map/mlp/pallas_call | solution.py:268
  140.2 0.5 collective-permute-start.7
  140.7 0.0 copy-done.9
  140.7 0.6 reshape.34.refs_1_
  141.3 0.0 copy-done.10
  141.3 0.6 reshape.35.refs_2_
  141.9 0.8 collective-permute-done.7.refs_6_
  142.7 0.9 copy-done.3
  143.6 3.5 %merge.1.refs_1_ = bf16[64,5760]{1,0:T(8,128)(2,1)} custom-call(bf16[256,1408]{1,0:T(8,128)(2,1)} %get-tuple-element.25.refs_0_, f32[1,1408]{1,0:T(1,128)} %reshape.34.refs_1_, f32[1,1408]{1,0:T(1,128)} %reshape.35.refs_2_, s32[1,256]{1,0:T(1,128)} %bitcast.16, s32[1,64]{1,0:T(1,128)} %bitcast.17, bf16[256,1408]{1,0:T(8,128)(2,1)} %get-tuple-element.29.refs_5_, ...), custom_call_target="tpu_custom_call" | custom-call | flops 184549376 | bytes 4194304 | tf_op jit(solution)/shard_map/merge/pallas_call | solution.py:319
  147.1 0.0 collective-permute-start.9
  147.1 2.7 %collective-permute-start.8 = (bf16[64,5760]{1,0:T(8,128)(2,1)}, bf16[64,5760]{1,0:T(8,128)(2,1)S(1)}, u32[]{:S(2)}, u32[]{:S(2)}) collective-permute-start(bf16[64,5760]{1,0:T(8,128)(2,1)} %merge.1.refs_1_), channel_id=1, source_target_pairs={{0,96},{32,0},{64,32},{96,64},{1,97},{33,1},{65,33},{97,65},{2,98}... | collective-permute-start | bytes 2211848 | tf_op jit(solution)/shard_map/ppermute | solution.py:405
  149.8 16.4 %collective-permute-done.9.refs_5_ = bf16[64,5760]{1,0:T(8,128)(2,1)S(1)} collective-permute-done((bf16[64,5760]{1,0:T(8,128)(2,1)}, bf16[64,5760]{1,0:T(8,128)(2,1)S(1)}, u32[]{:S(2)}, u32[]{:S(2)}) %collective-permute-start.9) | collective-permute-done | bytes 737312 | tf_op jit(solution)/shard_map/ppermute | solution.py:405
  166.3 0.1 collective-permute-start.10
  166.4 0.0 collective-permute-done.8.refs_2_
  166.4 0.0 copy-start.1
  166.4 2.7 %collective-permute-start.11 = (bf16[32,5760]{1,0:T(8,128)(2,1)S(1)}, bf16[32,5760]{1,0:T(8,128)(2,1)S(1)}, u32[]{:S(2)}, u32[]{:S(2)}) collective-permute-start(bf16[32,5760]{1,0:T(8,128)(2,1)S(1)} %slice.19), channel_id=1, source_target_pairs={{0,96},{32,0},{64,32},{96,64},{1,97},{33,1},{65,33},{97,65},{2,98}... | collective-permute-start | bytes 1105928 | tf_op jit(solution)/shard_map/ppermute | solution.py:405
  169.1 7.3 %collective-permute-done.10.refs_3_ = bf16[32,5760]{1,0:T(8,128)(2,1)S(1)} collective-permute-done((bf16[32,5760]{1,0:T(8,128)(2,1)S(1)}, bf16[32,5760]{1,0:T(8,128)(2,1)S(1)}, u32[]{:S(2)}, u32[]{:S(2)}) %collective-permute-start.10) | collective-permute-done | bytes 368672 | tf_op jit(solution)/shard_map/ppermute | solution.py:405
  176.4 0.0 collective-permute-done.11.refs_4_
  176.5 0.0 copy-done.1
  176.5 0.7 copy-done.6
  177.2 0.1 copy-done.7
  177.3 7.0 %embed.1 = bf16[512,512]{1,0:T(8,128)(2,1)} custom-call(s32[1]{0:T(128)} %bitcast.refs_0_, bf16[64,5760]{1,0:T(8,128)(2,1)} %merge.1.refs_1_, bf16[64,5760]{1,0:T(8,128)(2,1)} %copy-done.1, bf16[32,5760]{1,0:T(8,128)(2,1)} %copy-done.6, bf16[32,5760]{1,0:T(8,128)(2,1)} %copy-done.7, bf16[64,5760]{1,0:T(8,128)(2,1)} %copy-done, bf16[5632,512]{1,0:T(8,128)(2,1)} %refs_6_.1, ...), custom_call_target="tpu_custom_call" | custom-call | flops 1476395008 | bytes 10485760 | tf_op jit(solution)/shard_map/embed/pallas_call | solution.py:379
  184.3 1.2 reshape.39
  185.5 20.5 %all_to_all.27 = bf16[32,4,4,512]{3,2,1,0:T(4,128)(2,1)S(1)} all-to-all(bf16[32,4,4,512]{3,2,1,0:T(4,128)(2,1)S(1)} %reshape.39), channel_id=1, replica_groups=mesh['grp'=4,'y'=4,'xh'=2,'xl'=2,'c'=2] {'y','xh','xl','c'}, dimensions={0} | all-to-all | bytes 1048576 | tf_op jit(solution)/shard_map/all_to_all | solution.py:543
  206.0 0.2 copy.14
  206.2 0.9 reshape.40
  (15 shorter events, 0.1 us)
Async XLA Ops:
  6.5 117.5 %all-gather.3.cloned.1.call-start = ((), (), s32[]{:S(2)}) async-start(), calls=%async_computation.3 | async-start | bytes 4978688 | tf_op jit(solution)/shard_map/all_gather | solution.py:510
  13.6 12.4 %collective-permute-start = (bf16[104,1408]{1,0:T(8,128)(2,1)}, bf16[104,1408]{1,0:T(8,128)(2,1)S(1)}, u32[]{:S(2)}, u32[]{:S(2)}) collective-permute-start(bf16[104,1408]{1,0:T(8,128)(2,1)} %get-tuple-element.18), channel_id=1, source_target_pairs={{0,64},{32,96},{64,0},{96,32},{1,65},{33,97},{65,1},{97,33},{2,66}... | collective-permute-start | bytes 878600 | tf_op jit(solution)/shard_map/ppermute | solution.py:405
  26.0 0.7 copy-start.8
  26.8 97.2 %collective-permute-start.5 = (bf16[1552,1408]{1,0:T(8,128)(2,1)}, bf16[1552,1408]{1,0:T(8,128)(2,1)}, u32[]{:S(2)}, u32[]{:S(2)}) collective-permute-start(bf16[1552,1408]{1,0:T(8,128)(2,1)} %get-tuple-element.27.refs_0_), channel_id=1, source_target_pairs={{0,32},{32,64},{64,96},{96,0},{1,33},{33,65},{65,97},{97,1},{2,34}... | collective-permute-start | bytes 13111304 | tf_op jit(solution)/shard_map/ppermute | solution.py:405
  27.6 96.4 %collective-permute-start.6 = (bf16[1552,1408]{1,0:T(8,128)(2,1)}, bf16[1552,1408]{1,0:T(8,128)(2,1)}, u32[]{:S(2)}, u32[]{:S(2)}) collective-permute-start(bf16[1552,1408]{1,0:T(8,128)(2,1)} %get-tuple-element.27.refs_0_), channel_id=1, source_target_pairs={{0,96},{32,0},{64,32},{96,64},{1,97},{33,1},{65,33},{97,65},{2,98}... | collective-permute-start | bytes 13111304 | tf_op jit(solution)/shard_map/ppermute | solution.py:405
  56.6 3.8 %copy-start.2 = (bf16[8,184,256]{2,1,0:T(8,128)(2,1)}, bf16[8,184,256]{2,1,0:T(8,128)(2,1)S(1)}, u32[]{:S(2)}) copy-start(bf16[8,184,256]{2,1,0:T(8,128)(2,1)S(1)} %slice.17.refs_1_) | copy-start | bytes 2260996
  56.7 19.6 %collective-permute-start.2 = (bf16[8,184,256]{2,1,0:T(8,128)(2,1)S(1)}, bf16[8,184,256]{2,1,0:T(8,128)(2,1)S(1)}, u32[]{:S(2)}, u32[]{:S(2)}) collective-permute-start(bf16[8,184,256]{2,1,0:T(8,128)(2,1)S(1)} %slice.17.refs_1_), channel_id=1, source_target_pairs={{0,1},{1,0},{2,3},{3,2},{4,5},{5,4},{6,7},{7,6},{8,9},{9,8},{10,11... | collective-permute-start | bytes 2261000 | tf_op jit(solution)/shard_map/ppermute | solution.py:400
  60.1 0.7 copy-start.4
  60.1 16.1 %collective-permute-start.1 = (bf16[8,96,256]{2,1,0:T(8,128)(2,1)S(1)}, bf16[8,96,256]{2,1,0:T(8,128)(2,1)S(1)}, u32[]{:S(2)}, u32[]{:S(2)}) collective-permute-start(bf16[8,96,256]{2,1,0:T(8,128)(2,1)S(1)} %slice.16.refs_0_), channel_id=1, source_target_pairs={{0,2},{2,0},{1,3},{3,1},{4,6},{6,4},{5,7},{7,5},{8,10},{10,8},{9,1... | collective-permute-start | bytes 1179656 | tf_op jit(solution)/shard_map/ppermute | solution.py:400
  76.2 0.7 copy-start.13
  77.0 0.9 copy-start.11
  90.0 9.5 %collective-permute-start.3 = (bf16[8,96,256]{2,1,0:T(8,128)(2,1)}, bf16[8,96,256]{2,1,0:T(8,128)(2,1)S(1)}, u32[]{:S(2)}, u32[]{:S(2)}) collective-permute-start(bf16[8,96,256]{2,1,0:T(8,128)(2,1)} %attend.4), channel_id=1, source_target_pairs={{0,2},{2,0},{1,3},{3,1},{4,6},{6,4},{5,7},{7,5},{8,10},{10,8},{9,1... | collective-permute-start | bytes 1179656 | tf_op jit(solution)/shard_map/ppermute | solution.py:400
  99.5 0.7 copy-start.5
  118.6 5.4 %collective-permute-start.4 = (bf16[256,1408]{1,0:T(8,128)(2,1)}, bf16[256,1408]{1,0:T(8,128)(2,1)S(1)}, u32[]{:S(2)}, u32[]{:S(2)}) collective-permute-start(bf16[256,1408]{1,0:T(8,128)(2,1)} %get-tuple-element.26.x_ref), channel_id=1, source_target_pairs={{0,1},{1,0},{2,3},{3,2},{4,5},{5,4},{6,7},{7,6},{8,9},{9,8},{10,11... | collective-permute-start | bytes 2162696 | tf_op jit(solution)/shard_map/ppermute | solution.py:400
  124.0 0.9 copy-start.12
  124.9 15.8 %copy-start.9 = (f32[1408]{0:T(1024)S(1)}, f32[1408]{0:T(1024)}, u32[]{:S(2)}) copy-start(f32[1408]{0:T(1024)} %param.22) | copy-start | bytes 16900
  124.9 16.4 %copy-start.10 = (f32[1408]{0:T(1024)S(1)}, f32[1408]{0:T(1024)}, u32[]{:S(2)}) copy-start(f32[1408]{0:T(1024)} %param.23) | copy-start | bytes 16900
  140.2 2.5 %collective-permute-start.7 = (bf16[256,1408]{1,0:T(8,128)(2,1)}, bf16[256,1408]{1,0:T(8,128)(2,1)S(1)}, u32[]{:S(2)}, u32[]{:S(2)}) collective-permute-start(bf16[256,1408]{1,0:T(8,128)(2,1)} %get-tuple-element.30), channel_id=1, source_target_pairs={{0,1},{1,0},{2,3},{3,2},{4,5},{5,4},{6,7},{7,6},{8,9},{9,8},{10,11... | collective-permute-start | bytes 2162696 | tf_op jit(solution)/shard_map/ppermute | solution.py:400
  142.7 0.9 copy-start.3
  147.1 19.1 %collective-permute-start.9 = (bf16[64,5760]{1,0:T(8,128)(2,1)}, bf16[64,5760]{1,0:T(8,128)(2,1)S(1)}, u32[]{:S(2)}, u32[]{:S(2)}) collective-permute-start(bf16[64,5760]{1,0:T(8,128)(2,1)} %merge.1.refs_1_), channel_id=1, source_target_pairs={{0,32},{32,64},{64,96},{96,0},{1,33},{33,65},{65,97},{97,1},{2,34}... | collective-permute-start | bytes 2211848 | tf_op jit(solution)/shard_map/ppermute | solution.py:405
  147.1 19.2 %collective-permute-start.8 = (bf16[64,5760]{1,0:T(8,128)(2,1)}, bf16[64,5760]{1,0:T(8,128)(2,1)S(1)}, u32[]{:S(2)}, u32[]{:S(2)}) collective-permute-start(bf16[64,5760]{1,0:T(8,128)(2,1)} %merge.1.refs_1_), channel_id=1, source_target_pairs={{0,96},{32,0},{64,32},{96,64},{1,97},{33,1},{65,33},{97,65},{2,98}... | collective-permute-start | bytes 2211848 | tf_op jit(solution)/shard_map/ppermute | solution.py:405
  166.3 10.2 %copy-start = (bf16[64,5760]{1,0:T(8,128)(2,1)}, bf16[64,5760]{1,0:T(8,128)(2,1)S(1)}, u32[]{:S(2)}) copy-start(bf16[64,5760]{1,0:T(8,128)(2,1)S(1)} %collective-permute-done.9.refs_5_) | copy-start | bytes 2211844
  166.3 10.2 %collective-permute-start.10 = (bf16[32,5760]{1,0:T(8,128)(2,1)S(1)}, bf16[32,5760]{1,0:T(8,128)(2,1)S(1)}, u32[]{:S(2)}, u32[]{:S(2)}) collective-permute-start(bf16[32,5760]{1,0:T(8,128)(2,1)S(1)} %slice.18), channel_id=1, source_target_pairs={{0,32},{32,64},{64,96},{96,0},{1,33},{33,65},{65,97},{97,1},{2,34}... | collective-permute-start | bytes 1105928 | tf_op jit(solution)/shard_map/ppermute | solution.py:405
  166.4 10.1 %copy-start.1 = (bf16[64,5760]{1,0:T(8,128)(2,1)}, bf16[64,5760]{1,0:T(8,128)(2,1)S(1)}, u32[]{:S(2)}) copy-start(bf16[64,5760]{1,0:T(8,128)(2,1)S(1)} %collective-permute-done.8.refs_2_) | copy-start | bytes 2211844
  166.4 10.0 %collective-permute-start.11 = (bf16[32,5760]{1,0:T(8,128)(2,1)S(1)}, bf16[32,5760]{1,0:T(8,128)(2,1)S(1)}, u32[]{:S(2)}, u32[]{:S(2)}) collective-permute-start(bf16[32,5760]{1,0:T(8,128)(2,1)S(1)} %slice.19), channel_id=1, source_target_pairs={{0,96},{32,0},{64,32},{96,64},{1,97},{33,1},{65,33},{97,65},{2,98}... | collective-permute-start | bytes 1105928 | tf_op jit(solution)/shard_map/ppermute | solution.py:405
  176.4 0.7 copy-start.6
  176.4 0.9 copy-start.7
Sparse Core Ops, SparseCore 0:
  26.9 63.5 all-gather.2

commit v5 on v4

--- a/solution.py
+++ b/solution.py
@@ -14,6 +14,7 @@
 NORM_EPS = 1e-06
 LANES = 128
 PAD = 16
+CHIPS = ("y", "xh", "xl")
 F32 = jnp.float32
 BF16 = jnp.bfloat16
 VMEM_LIMIT = 60 * 1024 * 1024
@@ -225,31 +226,41 @@
     )(attended, tokens, w_attn_out)
 
 
-def mlp_kernel(x_ref, pair_ref, *refs):
-    packs = refs[:4]
-    own_ref, other_ref, near, far, sems = refs[4:]
-    rows = x_ref.shape[0]
+def mlp_kernel(x_ref, pair_ref, *refs, near_count, far_count):
+    near_refs, far_refs = refs[:near_count], refs[near_count : near_count + far_count]
+    rest = refs[near_count + far_count :]
+    own_ref, other_ref, near = rest[:3]
+    far, sems = (rest[3], rest[4]) if far_count else (None, rest[3])
     copies = []
-    for number in range(3):
-        copies.append(pltpu.make_async_copy(packs[number], near.at[number], sems.at[number]))
-    copies.append(pltpu.make_async_copy(packs[3], far, sems.at[3]))
+    for number, ref in enumerate(near_refs):
+        copies.append(pltpu.make_async_copy(ref, near.at[number], sems.at[number]))
+    at = 0
+    for number, ref in enumerate(far_refs):
+        target = far.at[pl.ds(at, ref.shape[0])]
+        copies.append(pltpu.make_async_copy(ref, target, sems.at[near_count + number]))
+        at += ref.shape[0]
     for copy in copies:
         copy.start()
     units = (near.shape[1] - PAD) // 2
-    shards = far.shape[0]
-    piece = (far.shape[1] - EXT) // 2
     x = x_ref[...], pair_ref[...]
     total = [None, None]
-    for number in range(4):
-        copies[number].wait()
-        if number < 3:
+    for number in range(near_count + (1 if far_count else 0)):
+        if number < near_count:
+            copies[number].wait()
             into = near[number, :units]
             out_of = near[number, units : 2 * units]
             bias = near[number, 2 * units : 2 * units + 1, :units].astype(F32)
         else:
+            for copy in copies[near_count:]:
+                copy.wait()
+            shards = far.shape[0]
+            piece = (far.shape[1] - EXT) // 2
             into = far[:, :piece].reshape(shards * piece, -1)
             out_of = far[:, piece : 2 * piece].reshape(shards * piece, -1)
-            bias = far[0, 2 * piece : 2 * piece + 1, :units].astype(F32)
+            bias = jnp.concatenate(
+                [far[i, 2 * piece : 2 * piece + 1, :piece].astype(F32) for i in range(shards)],
+                axis=1,
+            )
         before = [dot(part, into, NT) + bias for part in x]
         for i in range(2):
             pre = before[i]
@@ -260,32 +271,36 @@
     other_ref[...] = total[1].astype(BF16)
 
 
-def mlp(x, pair, packs):
+def mlp(x, pair, near, far=()):
     rows, width = x.shape
     shape = jax.ShapeDtypeStruct((rows, width), BF16)
     vmem = pl.BlockSpec(memory_space=pltpu.VMEM)
-    units = (packs[0].shape[0] - PAD) // 2
-    return pl.pallas_call(
-        mlp_kernel,
+    units = (near[0].shape[0] - PAD) // 2
+    groups = len(near) + (1 if far else 0)
+    scratch = [pltpu.VMEM((len(near),) + near[0].shape, BF16)]
+    if far:
+        shards = sum(array.shape[0] for array in far)
+        scratch.append(pltpu.VMEM((shards,) + far[0].shape[1:], BF16))
+    scratch.append(pltpu.SemaphoreType.DMA((len(near) + len(far),)))
+    return pl.pallas_call(
+        lambda *refs: mlp_kernel(*refs, near_count=len(near), far_count=len(far)),
         out_shape=(shape, shape),
-        in_specs=[vmem, vmem] + [pl.BlockSpec(memory_space=pl.ANY)] * 4,
+        in_specs=[vmem, vmem] + [pl.BlockSpec(memory_space=pl.ANY)] * (len(near) + len(far)),
         out_specs=(vmem, vmem),
-        scratch_shapes=[
-            pltpu.VMEM((3,) + packs[0].shape, BF16),
-            pltpu.VMEM(packs[3].shape, BF16),
-            pltpu.SemaphoreType.DMA((4,)),
-        ],
-        compiler_params=cparams(),
-        cost_estimate=cost(2 * rows * 4 * units * width * 4, 20 << 20),
+        scratch_shapes=scratch,
+        compiler_params=cparams(),
+        cost_estimate=cost(8 * rows * groups * units * width, groups * (5 << 20)),
         name="mlp",
-    )(x, pair, *packs)
-
-
-def merge_kernel(res_ref, bias_ref, gain_ref, index_ref, owner_ref, own_ref, other_ref, out_ref, *, cap):
+    )(x, pair, *near, *far)
+
+
+def merge_kernel(res_ref, bias_ref, gain_ref, index_ref, owner_ref, *refs, cap):
+    parts, out_ref = refs[:-1], refs[-1]
     rows, width = res_ref.shape
-    total = own_ref[...].astype(F32) + other_ref[...].astype(F32)
-    total = res_ref[...].astype(F32) + total + bias_ref[...]
-    normed = (layer_norm(total) * gain_ref[...]).astype(BF16)
+    total = res_ref[...].astype(F32) + bias_ref[...].reshape(1, width)
+    for part in parts:
+        total = total + part[...].astype(F32)
+    normed = (layer_norm(total) * gain_ref[...].reshape(1, width)).astype(BF16)
     count = rows // 4
     r = lax.broadcasted_iota(jnp.int32, (rows, rows), 0)
     s = lax.broadcasted_iota(jnp.int32, (rows, rows), 1)
@@ -305,16 +320,15 @@
     out_ref[:, 4 * width :] = jnp.broadcast_to(slot, (count, LANES))
 
 
-def merge(residual, out_bias, merge_gain, merge_index, owners, own, other, cap):
+def merge(residual, out_bias, merge_gain, merge_index, owners, parts, cap):
     rows, width = residual.shape
     operands = (
         residual,
-        out_bias.reshape(1, width),
-        merge_gain.reshape(1, width),
+        out_bias,
+        merge_gain,
         merge_index.reshape(1, rows),
         owners.reshape(1, rows // 4),
-        own,
-        other,
+        *parts,
     )
     return pl.pallas_call(
         lambda *refs: merge_kernel(*refs, cap=cap),
@@ -412,17 +426,21 @@
     return before, after, turn(before[:half], axis, 1), turn(after[half:], axis, -1)
 
 
-def pack_kernel(place_ref, in_ref, bias_ref, out_ref, near_ref, far_ref, row_sc, near_sc, far_sc, sems):
+def pack_kernel(in_ref, bias_ref, out_ref, near_ref, far_ref, row_sc, near_sc, far_sc, sems):
     half = (near_ref.shape[0] - PAD) // 2
     share = (far_ref.shape[0] - EXT) // 2
-    core = place_ref[0]
+    core = lax.axis_index("c")
     first = pl.multiple_of(core * half, half)
-    at = pl.multiple_of(first + place_ref[1] * share, 16)
+    chip = lax.axis_index(CHIPS)
+    at = pl.multiple_of(first + chip * share, 16)
     width = in_ref.shape[1]
-    bias = bias_ref[...].astype(F32)
+    bias = bias_ref[...].astype(F32).reshape(1, 2 * half)
     bias = jnp.where(core == 0, bias[:, :half], bias[:, half:])
-    bias = jnp.concatenate([bias, jnp.zeros((1, width - half), F32)], axis=1)
-    row_sc[...] = jnp.broadcast_to(bias, row_sc.shape).astype(BF16)
+    rest = jnp.zeros((PAD, width - half), F32)
+    bias = jnp.broadcast_to(bias, (PAD, half))
+    row_sc[0] = jnp.concatenate([bias, rest], axis=1).astype(BF16)
+    bias = pltpu.roll(bias, jnp.where(chip == 0, 0, half - chip * share), 1)
+    row_sc[1] = jnp.concatenate([bias, rest], axis=1).astype(BF16)
     pieces = [
         (in_ref, first, 0, half, near_ref, near_sc),
         (out_ref, first, half, half, near_ref, near_sc),
@@ -437,9 +455,9 @@
         copy.start()
         inward.append(copy)
     outward = [
-        pltpu.make_async_copy(row_sc, near_ref.at[pl.ds(2 * half, PAD)], sems.at[8]),
+        pltpu.make_async_copy(row_sc.at[0], near_ref.at[pl.ds(2 * half, PAD)], sems.at[8]),
         pltpu.make_async_copy(
-            row_sc.at[pl.ds(0, EXT)], far_ref.at[pl.ds(2 * share, EXT)], sems.at[9]
+            row_sc.at[1, pl.ds(0, EXT)], far_ref.at[pl.ds(2 * share, EXT)], sems.at[9]
         ),
     ]
     outward[0].start()
@@ -456,7 +474,7 @@
         copy.wait()
 
 
-def pack(place, w_in, in_bias, w_out, shares):
+def pack(w_in, in_bias, w_out, shares):
     units, width = w_in.shape
     half = units // 2
     any_space = pl.BlockSpec(memory_space=pl.ANY)
@@ -467,14 +485,13 @@
             jax.ShapeDtypeStruct((2 * half // shares + EXT, width), BF16),
         ),
         in_specs=[
-            pl.BlockSpec(memory_space=pltpu.SMEM),
             any_space,
             pl.BlockSpec(memory_space=pltpu.VMEM),
             any_space,
         ],
         out_specs=(any_space, any_space),
         scratch_shapes=[
-            pltpu.VMEM((PAD, width), BF16),
+            pltpu.VMEM((2, PAD, width), BF16),
             pltpu.VMEM((2 * half, width), BF16),
             pltpu.VMEM((2 * half // shares, width), BF16),
             pltpu.SemaphoreType.DMA((10,)),
@@ -482,7 +499,7 @@
         compiler_params=cparams(),
         cost_estimate=cost(0, 9 << 20),
         name="pack",
-    )(place, w_in, in_bias.reshape(1, units), w_out)
+    )(w_in, in_bias, w_out)
 
 
 def local(
@@ -500,32 +517,41 @@
     w_merge,
     merge_bias,
 ):
-    chips = ("y", "xh", "xl")
-    place = jnp.stack([lax.axis_index("c"), lax.axis_index(chips)]).astype(jnp.int32)
-    near, far = pack(place, w_in, in_bias, w_out, lax.axis_size(chips))
+    near, far = pack(w_in, in_bias, w_out, lax.axis_size(CHIPS))
     far = turn(far, "grp", 2)
     one, two = turn(near, "grp", 1), turn(near, "grp", -1)
     heads = qkv(tokens, seg_ids, w_qkv)
     far, heads = lax.optimization_barrier((far, heads))
-    far = lax.all_gather(far, chips)
+    row = [far] + [turn(far, ("xh", "xl"), by) for by in (1, 2, 3)]
     mine = lax.all_to_all(heads, ("y", "xh"), 0, 0, tiled=True)
+    row, mine = lax.optimization_barrier((row, mine))
+    row = jnp.stack(row)
+    below, above = turn(row, "y", 1), turn(row, "y", -1)
     queries, kv = mine[:, : HD + EXT], mine[:, HD:]
     away = flip(queries, "xl")
     kv_c = flip(kv, "c")
     acc = attend(queries, [kv])
     away, kv_c, acc = lax.optimization_barrier((away, kv_c, acc))
-    sent = flip(attend(away, [kv, kv_c], send=True), "xl")
+    sent = attend(away, [kv, kv_c], send=True)
+    below, above, sent = lax.optimization_barrier((below, above, sent))
+    sent = flip(sent, "xl")
+    far_a, far_b = turn(below[:2], "y", 1), turn(above[2:], "y", -1)
     acc = attend(queries, [kv_c], acc)
     sent, acc = lax.optimization_barrier((sent, acc))
     done = combine(acc, sent)
     attended = lax.all_to_all(done, ("y", "xh"), 0, 0, tiled=True)
+    far_a, far_b, attended = lax.optimization_barrier((far_a, far_b, attended))
+    far = [row, below, above, far_a, far_b]
     residual, mlp_in = project(attended, tokens, w_attn_out)
-    own, other = mlp(mlp_in, flip(mlp_in, "c"), (near, one, two, far))
+    pair = flip(mlp_in, "c")
+    own, other = mlp(mlp_in, pair, [near], far)
+    other = flip(other, "c")
+    one, two, own = lax.optimization_barrier((one, two, own))
+    own_b, other_b = mlp(mlp_in, pair, [one, two])
+    parts = [own, other, own_b, flip(other_b, "c")]
     owner_count = lax.axis_size(("y", "xh", "xl", "c"))
     cap = 4
-    merged = merge(
-        residual, out_bias, merge_gain, merge_index, owners, own, flip(other, "c"), cap
-    )
+    merged = merge(residual, out_bias, merge_gain, merge_index, owners, parts, cap)
     count = merged.shape[0]
     before, after, far_a, far_b = ring_gather(merged, "grp")
     pieces = [
@@ -539,11 +565,9 @@
     slots = 4 * cap
     outgoing = embed(group, pieces, w_merge, merge_bias, cap, slots, owner_count)
     cols = outgoing.shape[1]
-    outgoing = outgoing.reshape(owner_count, 4, cap, cols)
-    received = lax.all_to_all(
-        outgoing, ("y", "xh", "xl", "c"), split_axis=0, concat_axis=2, tiled=True
-    )
-    return received.reshape(4 * owner_count * cap, cols)
+    received = lax.all_to_all(outgoing, ("y", "xh", "xl", "c"), 0, 0, tiled=True)
+    received = received.reshape(owner_count, 4, cap, cols)
+    return received.transpose(1, 0, 2, 3).reshape(4 * owner_count * cap, cols)
 
 
 def solution(mesh):

time: 215 us -> 208 us (0.967)
  blocking collectives: 59.9 us -> 17.1 us
  waiting for transfers between devices: 37.1 us -> 61.2 us
  starting transfers between devices: 20.8 us -> 42.4 us
  between operations: 13.5 us -> 0.23 us
  Pallas kernels: 71 us -> 76.3 us
    all_to_all x3 -> x1, blocking collectives: 59.9 us -> 17.1 us  [local(): lax.all_to_all(outgoing, ('y', 'xh', 'xl', 'c'), 0, 0, tiled=True)]
    ppermute x7 -> x14, waiting for transfers between devices: 23.8 us -> 43.7 us  [turn(): lax.ppermute(value, axis, [(i, (i + by) % size) for i in range(size)])]
    ppermute x7 -> x14, starting transfers between devices: 12.7 us -> 23.2 us  [turn(): lax.ppermute(value, axis, [(i, (i + by) % size) for i in range(size)])]
    all_to_all x0 -> x2, starting transfers between devices: none -> 10.3 us  [the longest x1 6.67 us: local(): mine = lax.all_to_all(heads, ('y', 'xh'), 0, 0, tiled=True)]
    all_to_all x0 -> x2, waiting for transfers between devices: none -> 8.14 us  [the longest x1 8.14 us: local(): attended = lax.all_to_all(done, ('y', 'xh'), 0, 0, tiled=True)]
    pallas_call x1 -> x2, Pallas kernels: 15.3 us -> 20.1 us  [mlp(): pl.pallas_call(lambda *refs: mlp_kernel(*refs, near_count=len(near), far_...]
    ppermute x5 -> x6, waiting for transfers between devices: 13.3 us -> 9.42 us  [flip(): return lax.ppermute(value, axis, [(0, 1), (1, 0)])]
    reshape x5 -> x3, local copies, waits for them, and re-layouts: 4.56 us -> 1.22 us  [the longest x1 0.92 us: local(): return received.transpose(1, 0, 2, 3).reshape(4 * owner_count * cap, cols)]
  transfers between devices with their start and end apart: 13 -> 22, of which waited for: 6 -> 8; matrix products, arithmetic and copies ran while one was open for 1% -> 1% of each run, Pallas kernels for 19% -> 29%
where the time goes in v5:
time: 208 us; the launch traced here: 207 us
  Pallas kernels  76.3 us (37%)
  waiting for transfers between devices  61.2 us (29%)
  starting transfers between devices  42.4 us (20%)
  blocking collectives  17.1 us (8%)
  local copies, waits for them, and re-layouts  9.31 us (4%)
    ppermute x14, waiting for transfers between devices, turn(): lax.ppermute(value, axis, [(i, (i + by) % size) for i in range(size)])  43.7 us
    pallas_call x3, Pallas kernels, attend(): pl.pallas_call(lambda *refs: attend_kernel(*refs, sets=len(sets), first=f...  26 us
    ppermute x14, starting transfers between devices, turn(): lax.ppermute(value, axis, [(i, (i + by) % size) for i in range(size)])  23.2 us
    pallas_call x2, Pallas kernels, mlp(): pl.pallas_call(lambda *refs: mlp_kernel(*refs, near_count=len(near), far_...  20.1 us
    all_to_all x1, blocking collectives, local(): lax.all_to_all(outgoing, ('y', 'xh', 'xl', 'c'), 0, 0, tiled=True)  17.1 us
    ppermute x6, waiting for transfers between devices, flip(): return lax.ppermute(value, axis, [(0, 1), (1, 0)])  9.42 us
    ppermute x6, starting transfers between devices, flip(): return lax.ppermute(value, axis, [(0, 1), (1, 0)])  8.86 us
    all_to_all x1, waiting for transfers between devices, local(): attended = lax.all_to_all(done, ('y', 'xh'), 0, 0, tiled=True)  8.14 us
  transfers between devices with their start and end apart: 22, of which 8 were waited for; matrix products, arithmetic and copies ran while one was open for 1% of the time, Pallas kernels for 29%

profile of v5, /device:TPU:1, one launch (start us, length us, event | category | flops | bytes accessed | tf_op | source)
XLA Modules:
  0.0 206.8 jit_solution(7765452504109344032)
XLA Ops:
  0.0 5.3 %pack.1 = (bf16[1552,1408]{1,0:T(8,128)(2,1)}, bf16[104,1408]{1,0:T(8,128)(2,1)}) custom-call(bf16[1536,1408]{1,0:T(8,128)(2,1)} %in_ref.1, bf16[1536]{0:T(1024)(128)(2,1)} %bias_ref.1, bf16[1536,1408]{1,0:T(8,128)(2,1)} %out_ref.1), custom_call_target="tpu_custom_call" | custom-call | bytes 9437184 | tf_op jit(solution)/shard_map/pack/pallas_call | solution.py:481
  5.3 4.5 %collective-permute-start = (bf16[104,1408]{1,0:T(8,128)(2,1)}, bf16[104,1408]{1,0:T(8,128)(2,1)S(1)}, u32[]{:S(2)}, u32[]{:S(2)}) collective-permute-start(bf16[104,1408]{1,0:T(8,128)(2,1)} %get-tuple-element.34), channel_id=1, source_target_pairs={{0,64},{32,96},{64,0},{96,32},{1,65},{33,97},{65,1},{97,33},{2,66}... | collective-permute-start | bytes 878600 | tf_op jit(solution)/shard_map/ppermute | solution.py:419
  9.8 7.9 %qkv.1 = bf16[8,272,256]{2,1,0:T(8,128)(2,1)} custom-call(bf16[256,1408]{1,0:T(8,128)(2,1)} %x_ref.3, s32[1,256]{1,0:T(1,128)} %bitcast.22, bf16[2112,1408]{1,0:T(8,128)(2,1)} %bitcast.14), custom_call_target="tpu_custom_call" | custom-call | flops 1522532352 | bytes 8388608 | tf_op jit(solution)/shard_map/qkv/pallas_call | solution.py:84
  17.7 0.0 collective-permute-done
  17.7 6.7 %all-to-all-start = ((bf16[8,272,256]{2,1,0:T(8,128)(2,1)}), bf16[8,272,256]{2,1,0:T(8,128)(2,1)S(1)}, u32[]{:S(2)}, u32[]{:S(2)}) async-start(bf16[8,272,256]{2,1,0:T(8,128)(2,1)} %qkv.1), calls=%async_computation | async-start | bytes 2228224 | tf_op jit(solution)/shard_map/all_to_all | solution.py:526
  24.4 0.7 collective-permute-start.11
  25.1 1.9 collective-permute-start.12
  27.0 0.3 collective-permute-start.1
  27.3 3.6 %collective-permute-start.2 = (bf16[104,1408]{1,0:T(8,128)(2,1)S(1)}, bf16[104,1408]{1,0:T(8,128)(2,1)S(1)}, u32[]{:S(2)}, u32[]{:S(2)}) collective-permute-start(bf16[104,1408]{1,0:T(8,128)(2,1)S(1)} %collective-permute-done), channel_id=1, source_target_pairs={{0,4},{2,6},{4,0},{6,2},{1,5},{3,7},{5,1},{7,3},{8,12},{10,14},{12... | collective-permute-start | bytes 878600 | tf_op jit(solution)/shard_map/ppermute | solution.py:419
  30.9 1.2 collective-permute-start.3
  32.1 16.6 %collective-permute-done.1 = bf16[104,1408]{1,0:T(8,128)(2,1)S(1)} collective-permute-done((bf16[104,1408]{1,0:T(8,128)(2,1)S(1)}, bf16[104,1408]{1,0:T(8,128)(2,1)S(1)}, u32[]{:S(2)}, u32[]{:S(2)}) %collective-permute-start.1) | collective-permute-done | bytes 292896 | tf_op jit(solution)/shard_map/ppermute | solution.py:419
  48.7 2.8 %collective-permute-done.2 = bf16[104,1408]{1,0:T(8,128)(2,1)S(1)} collective-permute-done((bf16[104,1408]{1,0:T(8,128)(2,1)S(1)}, bf16[104,1408]{1,0:T(8,128)(2,1)S(1)}, u32[]{:S(2)}, u32[]{:S(2)}) %collective-permute-start.2) | collective-permute-done | bytes 292896 | tf_op jit(solution)/shard_map/ppermute | solution.py:419
  51.5 0.0 collective-permute-done.3
  51.5 0.0 all-to-all-done
  51.5 0.0 copy-start.7
  51.5 2.2 %collective-permute-start.6 = (bf16[8,96,256]{2,1,0:T(8,128)(2,1)S(1)}, bf16[8,96,256]{2,1,0:T(8,128)(2,1)S(1)}, u32[]{:S(2)}, u32[]{:S(2)}) collective-permute-start(bf16[8,96,256]{2,1,0:T(8,128)(2,1)S(1)} %slice.18.refs_0_), channel_id=1, source_target_pairs={{0,2},{2,0},{1,3},{3,1},{4,6},{6,4},{5,7},{7,5},{8,10},{10,8},{9,1... | collective-permute-start | bytes 1179656 | tf_op jit(solution)/shard_map/ppermute | solution.py:414
  53.7 0.2 pad_maximum_fusion.refs_3_
  53.9 1.3 collective-permute-start.4
  55.2 1.5 collective-permute-start.5
  56.7 5.1 %collective-permute-done.6.refs_0_ = bf16[8,96,256]{2,1,0:T(8,128)(2,1)S(1)} collective-permute-done((bf16[8,96,256]{2,1,0:T(8,128)(2,1)S(1)}, bf16[8,96,256]{2,1,0:T(8,128)(2,1)S(1)}, u32[]{:S(2)}, u32[]{:S(2)}) %collective-permute-start.6) | collective-permute-done | bytes 393248 | tf_op jit(solution)/shard_map/ppermute | solution.py:414
  61.8 0.8 copy-done.15
  62.6 2.0 collective-permute-start.7
  64.5 6.8 %attend.3.refs_2_ = f32[96,2048]{1,0:T(8,128)} custom-call(bf16[8,96,256]{2,1,0:T(8,128)(2,1)} %copy-done.7, bf16[8,184,256]{2,1,0:T(8,128)(2,1)} %copy-done.4), custom_call_target="tpu_custom_call" | custom-call | flops 2147483648 | bytes 3145728 | tf_op jit(solution)/shard_map/attend/pallas_call | solution.py:168
  71.4 0.0 collective-permute-done.7.refs_2_.refs_1_
  71.4 0.9 copy-done.11
  72.3 12.1 %attend.4 = bf16[8,96,256]{2,1,0:T(8,128)(2,1)} custom-call(bf16[8,96,256]{2,1,0:T(8,128)(2,1)} %copy-done.15, bf16[8,184,256]{2,1,0:T(8,128)(2,1)} %copy-done.4, bf16[8,184,256]{2,1,0:T(8,128)(2,1)} %copy-done.11), custom_call_target="tpu_custom_call" | custom-call | flops 4294967296 | bytes 3145728 | tf_op jit(solution)/shard_map/attend/pallas_call | solution.py:168
  84.4 1.5 collective-permute-start.10
  85.8 1.1 slice.20
  86.9 1.3 collective-permute-start.8
  88.2 1.1 slice.21
  89.3 1.6 collective-permute-start.9
  90.9 7.1 %attend.5.acc_ref = f32[96,2048]{1,0:T(8,128)} custom-call(bf16[8,96,256]{2,1,0:T(8,128)(2,1)} %copy-done.7, bf16[8,184,256]{2,1,0:T(8,128)(2,1)} %copy-done.11, f32[96,2048]{1,0:T(8,128)} %attend.3.refs_2_), custom_call_target="tpu_custom_call" | custom-call | flops 2147483648 | bytes 3145728 | tf_op jit(solution)/shard_map/attend/pallas_call | solution.py:168
  97.9 0.7 copy-done.8
  98.7 2.1 combine.1
  100.7 3.7 %all-to-all-start.1 = ((bf16[8,88,256]{2,1,0:T(8,128)(2,1)}), bf16[8,88,256]{2,1,0:T(8,128)(2,1)S(1)}, u32[]{:S(2)}, u32[]{:S(2)}) async-start(bf16[8,88,256]{2,1,0:T(8,128)(2,1)} %combine.1), calls=%async_computation.1 | async-start | bytes 720896 | tf_op jit(solution)/shard_map/all_to_all | solution.py:542
  104.5 8.1 %all-to-all-done.1.att_ref = bf16[8,88,256]{2,1,0:T(8,128)(2,1)S(1)} async-done(((bf16[8,88,256]{2,1,0:T(8,128)(2,1)}), bf16[8,88,256]{2,1,0:T(8,128)(2,1)S(1)}, u32[]{:S(2)}, u32[]{:S(2)}) %all-to-all-start.1) | async-done | bytes 360480 | tf_op jit(solution)/shard_map/all_to_all | solution.py:542
  112.6 0.7 copy-done.2
  113.3 3.9 %project.1 = (bf16[256,1408]{1,0:T(8,128)(2,1)}, bf16[256,1408]{1,0:T(8,128)(2,1)}) custom-call(bf16[8,88,256]{2,1,0:T(8,128)(2,1)} %copy-done.2, bf16[256,1408]{1,0:T(8,128)(2,1)} %x_ref.3, bf16[704,1408]{1,0:T(8,128)(2,1)} %w_ref.1), custom_call_target="tpu_custom_call" | custom-call | flops 507510784 | bytes 4194304 | tf_op jit(solution)/shard_map/project/pallas_call | solution.py:218
  117.3 2.3 %collective-permute-start.13 = (bf16[256,1408]{1,0:T(8,128)(2,1)}, bf16[256,1408]{1,0:T(8,128)(2,1)S(1)}, u32[]{:S(2)}, u32[]{:S(2)}) collective-permute-start(bf16[256,1408]{1,0:T(8,128)(2,1)} %get-tuple-element.53.refs_0_), channel_id=1, source_target_pairs={{0,1},{1,0},{2,3},{3,2},{4,5},{5,4},{6,7},{7,6},{8,9},{9,8},{10,11... | collective-permute-start | bytes 2162696 | tf_op jit(solution)/shard_map/ppermute | solution.py:414
  119.6 2.0 collective-permute-done.13.refs_1_
  121.6 0.9 copy-done.12
  122.5 10.0 %mlp.2 = (bf16[256,1408]{1,0:T(8,128)(2,1)}, bf16[256,1408]{1,0:T(8,128)(2,1)}) custom-call(bf16[256,1408]{1,0:T(8,128)(2,1)} %get-tuple-element.53.refs_0_, bf16[256,1408]{1,0:T(8,128)(2,1)} %copy-done.12, bf16[1552,1408]{1,0:T(8,128)(2,1)} %get-tuple-element.52.refs_2_, bf16[4,104,1408]{2,1,0:T(8,128)(2,1)} %copy-done.3, ...), custom_call_target="tpu_custom_call" | custom-call | flops 4429185024 | bytes 10485760 | tf_op jit(solution)/shard_map/mlp/pallas_call | solution.py:285
  132.5 0.5 collective-permute-start.14
  133.0 0.0 collective-permute-done.11.refs_2_
  133.0 10.0 %mlp.3 = (bf16[256,1408]{1,0:T(8,128)(2,1)}, bf16[256,1408]{1,0:T(8,128)(2,1)}) custom-call(bf16[256,1408]{1,0:T(8,128)(2,1)} %get-tuple-element.53.refs_0_, bf16[256,1408]{1,0:T(8,128)(2,1)} %copy-done.12, bf16[1552,1408]{1,0:T(8,128)(2,1)} %collective-permute-done.11.refs_2_, bf16[1552,1408]{1,0:T(8,128)(2,1)} %collective-permute-done.12.refs_3_), custom_call_target="tpu_custom_call" | custom-call | flops 4429185024 | bytes 10485760 | tf_op jit(solution)/shard_map/mlp/pallas_call | solution.py:285
  143.0 0.5 collective-permute-start.15
  143.5 0.0 collective-permute-done.14.refs_6_
  143.5 2.3 %collective-permute-done.15.refs_8_ = bf16[256,1408]{1,0:T(8,128)(2,1)S(1)} collective-permute-done((bf16[256,1408]{1,0:T(8,128)(2,1)}, bf16[256,1408]{1,0:T(8,128)(2,1)S(1)}, u32[]{:S(2)}, u32[]{:S(2)}) %collective-permute-start.15) | collective-permute-done | bytes 720928 | tf_op jit(solution)/shard_map/ppermute | solution.py:414
  145.8 0.9 copy-done.6
  146.6 4.1 %merge.1.refs_1_ = bf16[64,5760]{1,0:T(8,128)(2,1)} custom-call(bf16[256,1408]{1,0:T(8,128)(2,1)} %get-tuple-element.51.refs_0_, f32[1408]{0:T(1024)} %refs_1_.1, f32[1408]{0:T(1024)} %refs_2_.1, s32[1,256]{1,0:T(1,128)} %bitcast.23, s32[1,64]{1,0:T(1,128)} %bitcast.24, bf16[256,1408]{1,0:T(8,128)(2,1)} %get-tuple-element.57.refs_5_, ...), custom_call_target="tpu_custom_call" | custom-call | flops 184549376 | bytes 4194304 | tf_op jit(solution)/shard_map/merge/pallas_call | solution.py:333
  150.8 0.7 collective-permute-start.17
  151.5 1.9 collective-permute-start.16
  153.5 16.7 %collective-permute-done.17.refs_5_ = bf16[64,5760]{1,0:T(8,128)(2,1)S(1)} collective-permute-done((bf16[64,5760]{1,0:T(8,128)(2,1)}, bf16[64,5760]{1,0:T(8,128)(2,1)S(1)}, u32[]{:S(2)}, u32[]{:S(2)}) %collective-permute-start.17) | collective-permute-done | bytes 737312 | tf_op jit(solution)/shard_map/ppermute | solution.py:419
  170.2 0.1 collective-permute-start.18
  170.3 2.7 %collective-permute-start.19 = (bf16[32,5760]{1,0:T(8,128)(2,1)S(1)}, bf16[32,5760]{1,0:T(8,128)(2,1)S(1)}, u32[]{:S(2)}, u32[]{:S(2)}) collective-permute-start(bf16[32,5760]{1,0:T(8,128)(2,1)S(1)} %slice.25), channel_id=1, source_target_pairs={{0,96},{32,0},{64,32},{96,64},{1,97},{33,1},{65,33},{97,65},{2,98}... | collective-permute-start | bytes 1105928 | tf_op jit(solution)/shard_map/ppermute | solution.py:419
  173.0 7.6 %collective-permute-done.18.refs_3_ = bf16[32,5760]{1,0:T(8,128)(2,1)S(1)} collective-permute-done((bf16[32,5760]{1,0:T(8,128)(2,1)S(1)}, bf16[32,5760]{1,0:T(8,128)(2,1)S(1)}, u32[]{:S(2)}, u32[]{:S(2)}) %collective-permute-start.18) | collective-permute-done | bytes 368672 | tf_op jit(solution)/shard_map/ppermute | solution.py:419
  180.6 0.0 collective-permute-done.19.refs_4_
  180.6 0.7 copy-done.9
  181.3 0.1 copy-done.10
  181.4 7.0 %embed.1 = bf16[512,512]{1,0:T(8,128)(2,1)} custom-call(s32[1]{0:T(128)} %bitcast.refs_0_, bf16[64,5760]{1,0:T(8,128)(2,1)} %merge.1.refs_1_, bf16[64,5760]{1,0:T(8,128)(2,1)} %copy-done.1, bf16[32,5760]{1,0:T(8,128)(2,1)} %copy-done.9, bf16[32,5760]{1,0:T(8,128)(2,1)} %copy-done.10, bf16[64,5760]{1,0:T(8,128)(2,1)} %copy-done, bf16[5632,512]{1,0:T(8,128)(2,1)} %refs_6_.1, ...), custom_call_target="tpu_custom_call" | custom-call | flops 1476395008 | bytes 10485760 | tf_op jit(solution)/shard_map/embed/pallas_call | solution.py:393
  188.5 17.1 %all_to_all.19 = bf16[32,16,512]{2,1,0:T(8,128)(2,1)S(1)} all-to-all(bf16[32,16,512]{2,1,0:T(8,128)(2,1)} %bitcast.16), channel_id=1, replica_groups=mesh['grp'=4,'y'=4,'xh'=2,'xl'=2,'c'=2] {'y','xh','xl','c'}, dimensions={0} | all-to-all | bytes 1048576 | tf_op jit(solution)/shard_map/all_to_all | solution.py:568
  205.5 0.1 reshape.29
  205.7 0.2 copy.16
  205.8 0.9 reshape.30
  (34 shorter events, 0.2 us)
Async XLA Ops:
  5.3 12.4 %collective-permute-start = (bf16[104,1408]{1,0:T(8,128)(2,1)}, bf16[104,1408]{1,0:T(8,128)(2,1)S(1)}, u32[]{:S(2)}, u32[]{:S(2)}) collective-permute-start(bf16[104,1408]{1,0:T(8,128)(2,1)} %get-tuple-element.34), channel_id=1, source_target_pairs={{0,64},{32,96},{64,0},{96,32},{1,65},{33,97},{65,1},{97,33},{2,66}... | collective-permute-start | bytes 878600 | tf_op jit(solution)/shard_map/ppermute | solution.py:419
  17.7 33.8 %all-to-all-start = ((bf16[8,272,256]{2,1,0:T(8,128)(2,1)}), bf16[8,272,256]{2,1,0:T(8,128)(2,1)S(1)}, u32[]{:S(2)}, u32[]{:S(2)}) async-start(bf16[8,272,256]{2,1,0:T(8,128)(2,1)} %qkv.1), calls=%async_computation | async-start | bytes 2228224 | tf_op jit(solution)/shard_map/all_to_all | solution.py:526
  24.4 108.6 %collective-permute-start.11 = (bf16[1552,1408]{1,0:T(8,128)(2,1)}, bf16[1552,1408]{1,0:T(8,128)(2,1)}, u32[]{:S(2)}, u32[]{:S(2)}) collective-permute-start(bf16[1552,1408]{1,0:T(8,128)(2,1)} %get-tuple-element.52.refs_2_), channel_id=1, source_target_pairs={{0,32},{32,64},{64,96},{96,0},{1,33},{33,65},{65,97},{97,1},{2,34}... | collective-permute-start | bytes 13111304 | tf_op jit(solution)/shard_map/ppermute | solution.py:419
  25.1 107.9 %collective-permute-start.12 = (bf16[1552,1408]{1,0:T(8,128)(2,1)}, bf16[1552,1408]{1,0:T(8,128)(2,1)}, u32[]{:S(2)}, u32[]{:S(2)}) collective-permute-start(bf16[1552,1408]{1,0:T(8,128)(2,1)} %get-tuple-element.52.refs_2_), channel_id=1, source_target_pairs={{0,96},{32,0},{64,32},{96,64},{1,97},{33,1},{65,33},{97,65},{2,98}... | collective-permute-start | bytes 13111304 | tf_op jit(solution)/shard_map/ppermute | solution.py:419
  27.0 21.7 %collective-permute-start.1 = (bf16[104,1408]{1,0:T(8,128)(2,1)S(1)}, bf16[104,1408]{1,0:T(8,128)(2,1)S(1)}, u32[]{:S(2)}, u32[]{:S(2)}) collective-permute-start(bf16[104,1408]{1,0:T(8,128)(2,1)S(1)} %collective-permute-done), channel_id=1, source_target_pairs={{0,2},{2,4},{4,6},{6,0},{1,3},{3,5},{5,7},{7,1},{8,10},{10,12},{12... | collective-permute-start | bytes 878600 | tf_op jit(solution)/shard_map/ppermute | solution.py:419
  27.3 24.1 %collective-permute-start.2 = (bf16[104,1408]{1,0:T(8,128)(2,1)S(1)}, bf16[104,1408]{1,0:T(8,128)(2,1)S(1)}, u32[]{:S(2)}, u32[]{:S(2)}) collective-permute-start(bf16[104,1408]{1,0:T(8,128)(2,1)S(1)} %collective-permute-done), channel_id=1, source_target_pairs={{0,4},{2,6},{4,0},{6,2},{1,5},{3,7},{5,1},{7,3},{8,12},{10,14},{12... | collective-permute-start | bytes 878600 | tf_op jit(solution)/shard_map/ppermute | solution.py:419
  30.9 20.5 %collective-permute-start.3 = (bf16[104,1408]{1,0:T(8,128)(2,1)S(1)}, bf16[104,1408]{1,0:T(8,128)(2,1)S(1)}, u32[]{:S(2)}, u32[]{:S(2)}) collective-permute-start(bf16[104,1408]{1,0:T(8,128)(2,1)S(1)} %collective-permute-done), channel_id=1, source_target_pairs={{0,6},{2,0},{4,2},{6,4},{1,7},{3,1},{5,3},{7,5},{8,14},{10,8},{12,... | collective-permute-start | bytes 878600 | tf_op jit(solution)/shard_map/ppermute | solution.py:419
  51.5 2.4 %copy-start.7 = (bf16[8,96,256]{2,1,0:T(8,128)(2,1)}, bf16[8,96,256]{2,1,0:T(8,128)(2,1)S(1)}, u32[]{:S(2)}) copy-start(bf16[8,96,256]{2,1,0:T(8,128)(2,1)S(1)} %slice.18.refs_0_) | copy-start | bytes 1179652
  51.5 10.3 %collective-permute-start.6 = (bf16[8,96,256]{2,1,0:T(8,128)(2,1)S(1)}, bf16[8,96,256]{2,1,0:T(8,128)(2,1)S(1)}, u32[]{:S(2)}, u32[]{:S(2)}) collective-permute-start(bf16[8,96,256]{2,1,0:T(8,128)(2,1)S(1)} %slice.18.refs_0_), channel_id=1, source_target_pairs={{0,2},{2,0},{1,3},{3,1},{4,6},{6,4},{5,7},{7,5},{8,10},{10,8},{9,1... | collective-permute-start | bytes 1179656 | tf_op jit(solution)/shard_map/ppermute | solution.py:414
  53.9 17.5 %copy-start.3 = (bf16[4,104,1408]{2,1,0:T(8,128)(2,1)}, bf16[4,104,1408]{2,1,0:T(8,128)(2,1)S(1)}, u32[]{:S(2)}) copy-start(bf16[4,104,1408]{2,1,0:T(8,128)(2,1)S(1)} %pad_maximum_fusion.refs_3_) | copy-start | bytes 3514372
  53.9 30.5 %collective-permute-start.4 = (bf16[4,104,1408]{2,1,0:T(8,128)(2,1)S(1)}, bf16[4,104,1408]{2,1,0:T(8,128)(2,1)}, u32[]{:S(2)}, u32[]{:S(2)}) collective-permute-start(bf16[4,104,1408]{2,1,0:T(8,128)(2,1)S(1)} %pad_maximum_fusion.refs_3_), channel_id=1, source_target_pairs={{0,8},{8,16},{16,24},{24,0},{1,9},{9,17},{17,25},{25,1},{2,10},{10... | collective-permute-start | bytes 3514376 | tf_op jit(solution)/shard_map/ppermute | solution.py:419
  55.2 29.2 %collective-permute-start.5 = (bf16[4,104,1408]{2,1,0:T(8,128)(2,1)S(1)}, bf16[4,104,1408]{2,1,0:T(8,128)(2,1)}, u32[]{:S(2)}, u32[]{:S(2)}) collective-permute-start(bf16[4,104,1408]{2,1,0:T(8,128)(2,1)S(1)} %pad_maximum_fusion.refs_3_), channel_id=1, source_target_pairs={{0,24},{8,0},{16,8},{24,16},{1,25},{9,1},{17,9},{25,17},{2,26},{10... | collective-permute-start | bytes 3514376 | tf_op jit(solution)/shard_map/ppermute | solution.py:419
  56.7 7.8 %copy-start.4 = (bf16[8,184,256]{2,1,0:T(8,128)(2,1)}, bf16[8,184,256]{2,1,0:T(8,128)(2,1)S(1)}, u32[]{:S(2)}) copy-start(bf16[8,184,256]{2,1,0:T(8,128)(2,1)S(1)} %slice.19.refs_1_) | copy-start | bytes 2260996
  61.8 0.8 copy-start.15
  62.6 8.8 %collective-permute-start.7 = (bf16[8,184,256]{2,1,0:T(8,128)(2,1)S(1)}, bf16[8,184,256]{2,1,0:T(8,128)(2,1)S(1)}, u32[]{:S(2)}, u32[]{:S(2)}) collective-permute-start(bf16[8,184,256]{2,1,0:T(8,128)(2,1)S(1)} %slice.19.refs_1_), channel_id=1, source_target_pairs={{0,1},{1,0},{2,3},{3,2},{4,5},{5,4},{6,7},{7,6},{8,9},{9,8},{10,11... | collective-permute-start | bytes 2261000 | tf_op jit(solution)/shard_map/ppermute | solution.py:414
  71.4 0.9 copy-start.11
  84.4 13.6 %collective-permute-start.10 = (bf16[8,96,256]{2,1,0:T(8,128)(2,1)}, bf16[8,96,256]{2,1,0:T(8,128)(2,1)S(1)}, u32[]{:S(2)}, u32[]{:S(2)}) collective-permute-start(bf16[8,96,256]{2,1,0:T(8,128)(2,1)} %attend.4), channel_id=1, source_target_pairs={{0,2},{2,0},{1,3},{3,1},{4,6},{6,4},{5,7},{7,5},{8,10},{10,8},{9,1... | collective-permute-start | bytes 1179656 | tf_op jit(solution)/shard_map/ppermute | solution.py:414
  86.9 17.5 %collective-permute-start.8 = (bf16[2,104,1408]{2,1,0:T(8,128)(2,1)S(1)}, bf16[2,104,1408]{2,1,0:T(8,128)(2,1)S(1)}, u32[]{:S(2)}, u32[]{:S(2)}) collective-permute-start(bf16[2,104,1408]{2,1,0:T(8,128)(2,1)S(1)} %slice.20), channel_id=1, source_target_pairs={{0,8},{8,16},{16,24},{24,0},{1,9},{9,17},{17,25},{25,1},{2,10},{10... | collective-permute-start | bytes 1757192 | tf_op jit(solution)/shard_map/ppermute | solution.py:419
  89.3 15.1 %collective-permute-start.9 = (bf16[2,104,1408]{2,1,0:T(8,128)(2,1)S(1)}, bf16[2,104,1408]{2,1,0:T(8,128)(2,1)S(1)}, u32[]{:S(2)}, u32[]{:S(2)}) collective-permute-start(bf16[2,104,1408]{2,1,0:T(8,128)(2,1)S(1)} %slice.21), channel_id=1, source_target_pairs={{0,24},{8,0},{16,8},{24,16},{1,25},{9,1},{17,9},{25,17},{2,26},{10... | collective-permute-start | bytes 1757192 | tf_op jit(solution)/shard_map/ppermute | solution.py:419
  97.9 0.7 copy-start.8
  100.7 11.9 %all-to-all-start.1 = ((bf16[8,88,256]{2,1,0:T(8,128)(2,1)}), bf16[8,88,256]{2,1,0:T(8,128)(2,1)S(1)}, u32[]{:S(2)}, u32[]{:S(2)}) async-start(bf16[8,88,256]{2,1,0:T(8,128)(2,1)} %combine.1), calls=%async_computation.1 | async-start | bytes 720896 | tf_op jit(solution)/shard_map/all_to_all | solution.py:542
  104.4 17.2 %copy-start.13 = (bf16[2,104,1408]{2,1,0:T(8,128)(2,1)}, bf16[2,104,1408]{2,1,0:T(8,128)(2,1)S(1)}, u32[]{:S(2)}) copy-start(bf16[2,104,1408]{2,1,0:T(8,128)(2,1)S(1)} %collective-permute-done.8.refs_6_) | copy-start | bytes 1757188
  104.4 17.2 %copy-start.14 = (bf16[2,104,1408]{2,1,0:T(8,128)(2,1)}, bf16[2,104,1408]{2,1,0:T(8,128)(2,1)S(1)}, u32[]{:S(2)}) copy-start(bf16[2,104,1408]{2,1,0:T(8,128)(2,1)S(1)} %collective-permute-done.9.refs_7_) | copy-start | bytes 1757188
  112.6 0.7 copy-start.2
  117.3 4.4 %collective-permute-start.13 = (bf16[256,1408]{1,0:T(8,128)(2,1)}, bf16[256,1408]{1,0:T(8,128)(2,1)S(1)}, u32[]{:S(2)}, u32[]{:S(2)}) collective-permute-start(bf16[256,1408]{1,0:T(8,128)(2,1)} %get-tuple-element.53.refs_0_), channel_id=1, source_target_pairs={{0,1},{1,0},{2,3},{3,2},{4,5},{5,4},{6,7},{7,6},{8,9},{9,8},{10,11... | collective-permute-start | bytes 2162696 | tf_op jit(solution)/shard_map/ppermute | solution.py:414
  121.6 0.9 copy-start.12
  132.5 10.9 %collective-permute-start.14 = (bf16[256,1408]{1,0:T(8,128)(2,1)}, bf16[256,1408]{1,0:T(8,128)(2,1)S(1)}, u32[]{:S(2)}, u32[]{:S(2)}) collective-permute-start(bf16[256,1408]{1,0:T(8,128)(2,1)} %get-tuple-element.58), channel_id=1, source_target_pairs={{0,1},{1,0},{2,3},{3,2},{4,5},{5,4},{6,7},{7,6},{8,9},{9,8},{10,11... | collective-permute-start | bytes 2162696 | tf_op jit(solution)/shard_map/ppermute | solution.py:414
  143.0 2.7 %collective-permute-start.15 = (bf16[256,1408]{1,0:T(8,128)(2,1)}, bf16[256,1408]{1,0:T(8,128)(2,1)S(1)}, u32[]{:S(2)}, u32[]{:S(2)}) collective-permute-start(bf16[256,1408]{1,0:T(8,128)(2,1)} %get-tuple-element.62), channel_id=1, source_target_pairs={{0,1},{1,0},{2,3},{3,2},{4,5},{5,4},{6,7},{7,6},{8,9},{9,8},{10,11... | collective-permute-start | bytes 2162696 | tf_op jit(solution)/shard_map/ppermute | solution.py:414
  143.5 2.3 %copy-start.5 = (bf16[256,1408]{1,0:T(8,128)(2,1)}, bf16[256,1408]{1,0:T(8,128)(2,1)S(1)}, u32[]{:S(2)}) copy-start(bf16[256,1408]{1,0:T(8,128)(2,1)S(1)} %collective-permute-done.14.refs_6_) | copy-start | bytes 2162692
  145.8 0.9 copy-start.6
  150.8 19.4 %collective-permute-start.17 = (bf16[64,5760]{1,0:T(8,128)(2,1)}, bf16[64,5760]{1,0:T(8,128)(2,1)S(1)}, u32[]{:S(2)}, u32[]{:S(2)}) collective-permute-start(bf16[64,5760]{1,0:T(8,128)(2,1)} %merge.1.refs_1_), channel_id=1, source_target_pairs={{0,32},{32,64},{64,96},{96,0},{1,33},{33,65},{65,97},{97,1},{2,34}... | collective-permute-start | bytes 2211848 | tf_op jit(solution)/shard_map/ppermute | solution.py:419
  151.5 18.7 %collective-permute-start.16 = (bf16[64,5760]{1,0:T(8,128)(2,1)}, bf16[64,5760]{1,0:T(8,128)(2,1)S(1)}, u32[]{:S(2)}, u32[]{:S(2)}) collective-permute-start(bf16[64,5760]{1,0:T(8,128)(2,1)} %merge.1.refs_1_), channel_id=1, source_target_pairs={{0,96},{32,0},{64,32},{96,64},{1,97},{33,1},{65,33},{97,65},{2,98}... | collective-permute-start | bytes 2211848 | tf_op jit(solution)/shard_map/ppermute | solution.py:419
  170.1 10.5 %copy-start = (bf16[64,5760]{1,0:T(8,128)(2,1)}, bf16[64,5760]{1,0:T(8,128)(2,1)S(1)}, u32[]{:S(2)}) copy-start(bf16[64,5760]{1,0:T(8,128)(2,1)S(1)} %collective-permute-done.17.refs_5_) | copy-start | bytes 2211844
  170.2 10.4 %collective-permute-start.18 = (bf16[32,5760]{1,0:T(8,128)(2,1)S(1)}, bf16[32,5760]{1,0:T(8,128)(2,1)S(1)}, u32[]{:S(2)}, u32[]{:S(2)}) collective-permute-start(bf16[32,5760]{1,0:T(8,128)(2,1)S(1)} %slice.24), channel_id=1, source_target_pairs={{0,32},{32,64},{64,96},{96,0},{1,33},{33,65},{65,97},{97,1},{2,34}... | collective-permute-start | bytes 1105928 | tf_op jit(solution)/shard_map/ppermute | solution.py:419
  170.3 10.3 %copy-start.1 = (bf16[64,5760]{1,0:T(8,128)(2,1)}, bf16[64,5760]{1,0:T(8,128)(2,1)S(1)}, u32[]{:S(2)}) copy-start(bf16[64,5760]{1,0:T(8,128)(2,1)S(1)} %collective-permute-done.16.refs_2_) | copy-start | bytes 2211844
  170.3 10.3 %collective-permute-start.19 = (bf16[32,5760]{1,0:T(8,128)(2,1)S(1)}, bf16[32,5760]{1,0:T(8,128)(2,1)S(1)}, u32[]{:S(2)}, u32[]{:S(2)}) collective-permute-start(bf16[32,5760]{1,0:T(8,128)(2,1)S(1)} %slice.25), channel_id=1, source_target_pairs={{0,96},{32,0},{64,32},{96,64},{1,97},{33,1},{65,33},{97,65},{2,98}... | collective-permute-start | bytes 1105928 | tf_op jit(solution)/shard_map/ppermute | solution.py:419
  180.6 0.8 copy-start.9
  180.6 0.9 copy-start.10

commit v6 on v5

--- a/solution.py
+++ b/solution.py
@@ -24,6 +24,10 @@
     return pltpu.CompilerParams(
         dimension_semantics=semantics or None, vmem_limit_bytes=VMEM_LIMIT
     )
+
+
+def in_vmem(value):
+    return pltpu.with_memory_space_constraint(value, pltpu.VMEM)
 
 
 def layer_norm(values):
@@ -162,9 +166,9 @@
         shape = jax.ShapeDtypeStruct(queries.shape, BF16)
     else:
         shape = jax.ShapeDtypeStruct((top, total), F32)
-    operands = [queries, *sets]
+    operands = [in_vmem(queries), *map(in_vmem, sets)]
     if not first:
-        operands.append(acc)
+        operands.append(in_vmem(acc))
     return pl.pallas_call(
         lambda *refs: attend_kernel(
             *refs, sets=len(sets), first=first, send=send, key_block=key_block, unroll=unroll
@@ -202,7 +206,7 @@
         compiler_params=cparams(),
         cost_estimate=cost(0, 2 << 20),
         name="combine",
-    )(acc, sent)
+    )(in_vmem(acc), in_vmem(sent))
 
 
 def project_kernel(att_ref, x_ref, w_ref, res_ref, in_ref):
@@ -223,7 +227,7 @@
         compiler_params=cparams(),
         cost_estimate=cost(2 * tokens.shape[0] * w_attn_out.shape[0] * w_attn_out.shape[1], 4 << 20),
         name="project",
-    )(attended, tokens, w_attn_out)
+    )(in_vmem(attended), tokens, w_attn_out)
 
 
 def mlp_kernel(x_ref, pair_ref, *refs, near_count, far_count):
@@ -291,7 +295,7 @@
         compiler_params=cparams(),
         cost_estimate=cost(8 * rows * groups * units * width, groups * (5 << 20)),
         name="mlp",
-    )(x, pair, *near, *far)
+    )(x, in_vmem(pair), *near, *far)
 
 
 def merge_kernel(res_ref, bias_ref, gain_ref, index_ref, owner_ref, *refs, cap):
@@ -328,7 +332,8 @@
         merge_gain,
         merge_index.reshape(1, rows),
         owners.reshape(1, rows // 4),
-        *parts,
+        parts[0],
+        *map(in_vmem, parts[1:]),
     )
     return pl.pallas_call(
         lambda *refs: merge_kernel(*refs, cap=cap),
@@ -341,73 +346,57 @@
     )(*operands)
 
 
-def embed_kernel(group_ref, *refs, pieces, cap, slots):
+def embed_kernel(*refs, pieces, cap, slots):
     x_refs = refs[: len(pieces)]
-    w_ref, bias_ref, out_ref, x_sc, acc_ref = refs[len(pieces) :]
-    step = pl.program_id(0)
-    steps = pl.num_programs(0)
-    for (at, _), x_ref in zip(pieces, x_refs):
+    w_hbm, bias_ref, out_ref, x_sc, w_sc, sems = refs[len(pieces) :]
+    depth, cols = w_hbm.shape
+    block = depth // 4
+    copies = []
+    for i in range(4):
+        at = pl.ds(i * block, block)
+        copies.append(pltpu.make_async_copy(w_hbm.at[at], w_sc.at[at], sems.at[i]))
+        copies[-1].start()
+    for at, x_ref in zip(pieces, x_refs):
         x_sc[at : at + x_ref.shape[0], :] = x_ref[...]
-
-    @pl.when(step < steps - 1)
-    def _():
-        part = dot(x_sc[...], w_ref[...])
-
-        @pl.when(step == 0)
-        def _():
-            acc_ref[...] = part
-
-        @pl.when(step > 0)
-        def _():
-            acc_ref[...] += part
-
-    @pl.when(step == steps - 1)
-    def _():
-        embedded = (acc_ref[...] + bias_ref[...]).astype(BF16)
-        total = x_sc.shape[0]
-        count = total // 4
-        slot = x_sc[:, 0:1].astype(F32).astype(jnp.int32)
-        owner = slot // cap
-        rank = slot - owner * cap
-        shift = lax.broadcasted_iota(jnp.int32, (total, 1), 0) // count
-        group = group_ref[0] + shift
-        group = jnp.where(group >= 4, group - 4, group)
-        target = owner * slots + group * cap + rank
-        lane = lax.broadcasted_iota(jnp.int32, (total, out_ref.shape[0]), 1)
-        place = (target == lane).astype(F32).T.astype(BF16)
-        out_ref[...] = dot(place, embedded).astype(BF16)
-
-
-def embed(group, pieces, w_merge, merge_bias, cap, slots, owners, block=1408):
-    arrays = [array for _, array in pieces]
+    embedded = jnp.broadcast_to(bias_ref[...].reshape(1, cols), (x_sc.shape[0], cols))
+    for i in range(4):
+        copies[i].wait()
+        at = slice(i * block, (i + 1) * block)
+        embedded = embedded + dot(x_sc[:, at], w_sc[at, :])
+    embedded = embedded.astype(BF16)
+    total = x_sc.shape[0]
+    count = total // 4
+    slot = x_sc[:, depth : depth + 1].astype(F32).astype(jnp.int32)
+    owner = slot // cap
+    rank = slot - owner * cap
+    group = lax.axis_index("grp") + lax.broadcasted_iota(jnp.int32, (total, 1), 0) // count
+    group = jnp.where(group >= 4, group - 4, group)
+    target = owner * slots + group * cap + rank
+    lane = lax.broadcasted_iota(jnp.int32, (total, out_ref.shape[0]), 1)
+    place = (target == lane).astype(F32).T.astype(BF16)
+    out_ref[...] = dot(place, embedded).astype(BF16)
+
+
+def embed(pieces, w_merge, merge_bias, cap, slots, owners):
+    arrays = [in_vmem(array) for _, array in pieces]
     rows = sum(array.shape[0] for array in arrays)
     depth, cols = w_merge.shape
-    steps = depth // block
-    places = tuple((at, array.shape[0]) for at, array in pieces)
-    x_block = block
-
-    def x_map(i, _):
-        return (0, i)
-
-    spec = lambda array: pl.BlockSpec((array.shape[0], x_block), x_map)
+    places = tuple(at for at, _ in pieces)
     return pl.pallas_call(
         lambda *refs: embed_kernel(*refs, pieces=places, cap=cap, slots=slots),
         out_shape=jax.ShapeDtypeStruct((owners * slots, cols), BF16),
-        grid_spec=pltpu.PrefetchScalarGridSpec(
-            num_scalar_prefetch=1,
-            grid=(steps + 1,),
-            in_specs=[spec(array) for array in arrays]
-            + [
-                pl.BlockSpec((block, cols), lambda i, _: (jnp.minimum(i, steps - 1), 0)),
-                pl.BlockSpec((1, cols), lambda i, _: (0, 0)),
-            ],
-            out_specs=pl.BlockSpec((owners * slots, cols), lambda i, _: (0, 0)),
-            scratch_shapes=[pltpu.VMEM((rows, block), BF16), pltpu.VMEM((rows, cols), F32)],
-        ),
-        compiler_params=cparams("arbitrary"),
+        in_specs=[pl.BlockSpec(memory_space=pltpu.VMEM)] * len(arrays)
+        + [pl.BlockSpec(memory_space=pl.ANY), pl.BlockSpec(memory_space=pltpu.VMEM)],
+        out_specs=pl.BlockSpec(memory_space=pltpu.VMEM),
+        scratch_shapes=[
+            pltpu.VMEM((rows, arrays[0].shape[1]), BF16),
+            pltpu.VMEM((depth, cols), BF16),
+            pltpu.SemaphoreType.DMA((4,)),
+        ],
+        compiler_params=cparams(),
         cost_estimate=cost(2 * rows * depth * cols, 10 << 20),
         name="embed",
-    )(group, *arrays, w_merge, merge_bias.reshape(1, cols))
+    )(*arrays, w_merge, merge_bias)
 
 
 def flip(value, axis):
@@ -426,78 +415,57 @@
     return before, after, turn(before[:half], axis, 1), turn(after[half:], axis, -1)
 
 
-def pack_kernel(in_ref, bias_ref, out_ref, near_ref, far_ref, row_sc, near_sc, far_sc, sems):
-    half = (near_ref.shape[0] - PAD) // 2
-    share = (far_ref.shape[0] - EXT) // 2
+def pack_kernel(in_ref, bias_ref, out_ref, pack_ref, row_sc, sc, sems, *, shares):
+    size = sc.shape[0] // 2
+    half = size * shares
+    tail = row_sc.shape[0]
     core = lax.axis_index("c")
     first = pl.multiple_of(core * half, half)
-    chip = lax.axis_index(CHIPS)
-    at = pl.multiple_of(first + chip * share, 16)
+    if shares > 1:
+        chip = lax.axis_index(CHIPS)
+        first = pl.multiple_of(first + chip * size, 16)
+    copies = []
+    for i, ref in enumerate((in_ref, out_ref)):
+        source = ref.at[pl.ds(first, size)]
+        copies.append(pltpu.make_async_copy(source, sc.at[pl.ds(i * size, size)], sems.at[i]))
+        copies[-1].start()
     width = in_ref.shape[1]
     bias = bias_ref[...].astype(F32).reshape(1, 2 * half)
     bias = jnp.where(core == 0, bias[:, :half], bias[:, half:])
-    rest = jnp.zeros((PAD, width - half), F32)
-    bias = jnp.broadcast_to(bias, (PAD, half))
-    row_sc[0] = jnp.concatenate([bias, rest], axis=1).astype(BF16)
-    bias = pltpu.roll(bias, jnp.where(chip == 0, 0, half - chip * share), 1)
-    row_sc[1] = jnp.concatenate([bias, rest], axis=1).astype(BF16)
-    pieces = [
-        (in_ref, first, 0, half, near_ref, near_sc),
-        (out_ref, first, half, half, near_ref, near_sc),
-        (in_ref, at, 0, share, far_ref, far_sc),
-        (out_ref, at, share, share, far_ref, far_sc),
-    ]
-    inward = []
-    for i, (source, begin, to, size, _, buffer) in enumerate(pieces):
-        copy = pltpu.make_async_copy(
-            source.at[pl.ds(begin, size)], buffer.at[pl.ds(to, size)], sems.at[i]
-        )
-        copy.start()
-        inward.append(copy)
-    outward = [
-        pltpu.make_async_copy(row_sc.at[0], near_ref.at[pl.ds(2 * half, PAD)], sems.at[8]),
-        pltpu.make_async_copy(
-            row_sc.at[1, pl.ds(0, EXT)], far_ref.at[pl.ds(2 * share, EXT)], sems.at[9]
-        ),
-    ]
-    outward[0].start()
-    outward[1].start()
-    for i in (2, 3, 0, 1):
-        _, _, to, size, target, buffer = pieces[i]
-        inward[i].wait()
-        copy = pltpu.make_async_copy(
-            buffer.at[pl.ds(to, size)], target.at[pl.ds(to, size)], sems.at[4 + i]
-        )
-        copy.start()
-        outward.append(copy)
-    for copy in outward:
+    bias = jnp.broadcast_to(bias, (tail, half))
+    if shares > 1:
+        bias = pltpu.roll(bias, jnp.where(chip == 0, 0, half - chip * size), 1)
+    rest = jnp.zeros((tail, width - half), F32)
+    row_sc[...] = jnp.concatenate([bias, rest], axis=1).astype(BF16)
+    copies.append(
+        pltpu.make_async_copy(row_sc, pack_ref.at[pl.ds(2 * size, tail)], sems.at[2])
+    )
+    copies[-1].start()
+    for i in range(2):
+        at = pl.ds(i * size, size)
+        copies[i].wait()
+        copies.append(pltpu.make_async_copy(sc.at[at], pack_ref.at[at], sems.at[3 + i]))
+        copies[-1].start()
+    for copy in copies[2:]:
         copy.wait()
 
 
-def pack(w_in, in_bias, w_out, shares):
+def pack(w_in, in_bias, w_out, shares, tail):
     units, width = w_in.shape
-    half = units // 2
+    size = units // 2 // shares
     any_space = pl.BlockSpec(memory_space=pl.ANY)
     return pl.pallas_call(
-        pack_kernel,
-        out_shape=(
-            jax.ShapeDtypeStruct((2 * half + PAD, width), BF16),
-            jax.ShapeDtypeStruct((2 * half // shares + EXT, width), BF16),
-        ),
-        in_specs=[
-            any_space,
-            pl.BlockSpec(memory_space=pltpu.VMEM),
-            any_space,
+        lambda *refs: pack_kernel(*refs, shares=shares),
+        out_shape=jax.ShapeDtypeStruct((2 * size + tail, width), BF16),
+        in_specs=[any_space, pl.BlockSpec(memory_space=pltpu.VMEM), any_space],
+        out_specs=any_space,
+        scratch_shapes=[
+            pltpu.VMEM((tail, width), BF16),
+            pltpu.VMEM((2 * size, width), BF16),
+            pltpu.SemaphoreType.DMA((5,)),
         ],
-        out_specs=(any_space, any_space),
-        scratch_shapes=[
-            pltpu.VMEM((2, PAD, width), BF16),
-            pltpu.VMEM((2 * half, width), BF16),
-            pltpu.VMEM((2 * half // shares, width), BF16),
-            pltpu.SemaphoreType.DMA((10,)),
-        ],
-        compiler_params=cparams(),
-        cost_estimate=cost(0, 9 << 20),
+        compiler_params=cparams(),
+        cost_estimate=cost(0, 8 * size * width),
         name="pack",
     )(w_in, in_bias, w_out)
 
@@ -517,26 +485,26 @@
     w_merge,
     merge_bias,
 ):
-    near, far = pack(w_in, in_bias, w_out, lax.axis_size(CHIPS))
-    far = turn(far, "grp", 2)
+    far = turn(pack(w_in, in_bias, w_out, lax.axis_size(CHIPS), EXT), "grp", 2)
+    near = pack(w_in, in_bias, w_out, 1, PAD)
+    far, near = lax.optimization_barrier((far, near))
+    row = [far] + [turn(far, ("xh", "xl"), by) for by in (1, 2, 3)]
     one, two = turn(near, "grp", 1), turn(near, "grp", -1)
     heads = qkv(tokens, seg_ids, w_qkv)
-    far, heads = lax.optimization_barrier((far, heads))
-    row = [far] + [turn(far, ("xh", "xl"), by) for by in (1, 2, 3)]
+    row, heads = lax.optimization_barrier((row, heads))
     mine = lax.all_to_all(heads, ("y", "xh"), 0, 0, tiled=True)
-    row, mine = lax.optimization_barrier((row, mine))
-    row = jnp.stack(row)
+    row, mine = lax.optimization_barrier((jnp.stack(row), mine))
     below, above = turn(row, "y", 1), turn(row, "y", -1)
     queries, kv = mine[:, : HD + EXT], mine[:, HD:]
+    kv_c = flip(kv, "c")
+    queries, kv_c = lax.optimization_barrier((queries, kv_c))
     away = flip(queries, "xl")
-    kv_c = flip(kv, "c")
     acc = attend(queries, [kv])
-    away, kv_c, acc = lax.optimization_barrier((away, kv_c, acc))
-    sent = attend(away, [kv, kv_c], send=True)
-    below, above, sent = lax.optimization_barrier((below, above, sent))
-    sent = flip(sent, "xl")
+    away, acc = lax.optimization_barrier((away, acc))
+    sent = flip(attend(away, [kv, kv_c], send=True), "xl")
+    acc = attend(queries, [kv_c], acc)
+    below, above, acc = lax.optimization_barrier((below, above, acc))
     far_a, far_b = turn(below[:2], "y", 1), turn(above[2:], "y", -1)
-    acc = attend(queries, [kv_c], acc)
     sent, acc = lax.optimization_barrier((sent, acc))
     done = combine(acc, sent)
     attended = lax.all_to_all(done, ("y", "xh"), 0, 0, tiled=True)
@@ -544,11 +512,8 @@
     far = [row, below, above, far_a, far_b]
     residual, mlp_in = project(attended, tokens, w_attn_out)
     pair = flip(mlp_in, "c")
-    own, other = mlp(mlp_in, pair, [near], far)
-    other = flip(other, "c")
-    one, two, own = lax.optimization_barrier((one, two, own))
-    own_b, other_b = mlp(mlp_in, pair, [one, two])
-    parts = [own, other, own_b, flip(other_b, "c")]
+    own, other = mlp(mlp_in, pair, [near, one, two], far)
+    parts = [own, flip(other, "c")]
     owner_count = lax.axis_size(("y", "xh", "xl", "c"))
     cap = 4
     merged = merge(residual, out_bias, merge_gain, merge_index, owners, parts, cap)
@@ -561,9 +526,8 @@
         (2 * count + count // 2, far_b),
         (3 * count, before),
     ]
-    group = lax.axis_index("grp").reshape(1).astype(jnp.int32)
     slots = 4 * cap
-    outgoing = embed(group, pieces, w_merge, merge_bias, cap, slots, owner_count)
+    outgoing = embed(pieces, w_merge, merge_bias, cap, slots, owner_count)
     cols = outgoing.shape[1]
     received = lax.all_to_all(outgoing, ("y", "xh", "xl", "c"), 0, 0, tiled=True)
     received = received.reshape(owner_count, 4, cap, cols)

time: 208 us -> 196 us (0.942)
  Pallas kernels: 76.3 us -> 64.5 us
  waiting for transfers between devices: 61.2 us -> 69.5 us
  starting transfers between devices: 42.4 us -> 36.1 us
  local copies, waits for them, and re-layouts: 9.31 us -> 3.58 us
  blocking collectives: 17.1 us -> 20.1 us
    all_to_all x1, waiting for transfers between devices: 0.01 us -> 16.1 us  [local(): mine = lax.all_to_all(heads, ('y', 'xh'), 0, 0, tiled=True)]
    all_to_all x1, waiting for transfers between devices: 8.14 us -> 2.27 us  [local(): attended = lax.all_to_all(done, ('y', 'xh'), 0, 0, tiled=True)]
    unnamed x32 -> x10, local copies, waits for them, and re-layouts: 5.74 us -> 0.02 us
    pallas_call x2 -> x1, Pallas kernels: 20.1 us -> 15.2 us  [mlp(): pl.pallas_call(lambda *refs: mlp_kernel(*refs, near_count=len(near), far_...]
    pallas_call x3, Pallas kernels: 26 us -> 21.7 us  [attend(): pl.pallas_call(lambda *refs: attend_kernel(*refs, sets=len(sets), first=f...]
    ppermute x14, starting transfers between devices: 23.2 us -> 19.7 us  [turn(): lax.ppermute(value, axis, [(i, (i + by) % size) for i in range(size)])]
    all_to_all x1, blocking collectives: 17.1 us -> 20.1 us  [local(): lax.all_to_all(outgoing, ('y', 'xh', 'xl', 'c'), 0, 0, tiled=True)]
    all_to_all x1, starting transfers between devices: 6.67 us -> 4.43 us  [local(): mine = lax.all_to_all(heads, ('y', 'xh'), 0, 0, tiled=True)]
  transfers between devices with their start and end apart: 22 -> 21, of which waited for: 8 -> 13; matrix products, arithmetic and copies ran while one was open for 1% -> 2% of each run, Pallas kernels for 29% -> 20%
where the time goes in v6:
time: 196 us; the launch traced here: 195 us
  waiting for transfers between devices  69.5 us (35%)
  Pallas kernels  64.5 us (33%)
  starting transfers between devices  36.1 us (18%)
  blocking collectives  20.1 us (10%)
  local copies, waits for them, and re-layouts  3.58 us (2%)
    ppermute x14, waiting for transfers between devices, turn(): lax.ppermute(value, axis, [(i, (i + by) % size) for i in range(size)])  42 us
    pallas_call x3, Pallas kernels, attend(): pl.pallas_call(lambda *refs: attend_kernel(*refs, sets=len(sets), first=f...  21.7 us
    all_to_all x1, blocking collectives, local(): lax.all_to_all(outgoing, ('y', 'xh', 'xl', 'c'), 0, 0, tiled=True)  20.1 us
    ppermute x14, starting transfers between devices, turn(): lax.ppermute(value, axis, [(i, (i + by) % size) for i in range(size)])  19.7 us
    all_to_all x1, waiting for transfers between devices, local(): mine = lax.all_to_all(heads, ('y', 'xh'), 0, 0, tiled=True)  16.1 us
    pallas_call x1, Pallas kernels, mlp(): pl.pallas_call(lambda *refs: mlp_kernel(*refs, near_count=len(near), far_...  15.2 us
    ppermute x5, waiting for transfers between devices, flip(): return lax.ppermute(value, axis, [(0, 1), (1, 0)])  9.1 us
    ppermute x5, starting transfers between devices, flip(): return lax.ppermute(value, axis, [(0, 1), (1, 0)])  7.93 us
  transfers between devices with their start and end apart: 21, of which 13 were waited for; matrix products, arithmetic and copies ran while one was open for 2% of the time, Pallas kernels for 20%

profile of v6, /device:TPU:1, one launch (start us, length us, event | category | flops | bytes accessed | tf_op | source)
XLA Modules:
  0.0 195.1 jit_solution(17314868774202240538)
XLA Ops:
  0.0 2.4 %pack.2 = bf16[104,1408]{1,0:T(8,128)(2,1)} custom-call(bf16[1536,1408]{1,0:T(8,128)(2,1)} %refs_0_.3, bf16[1536]{0:T(1024)(128)(2,1)} %refs_1_.4, bf16[1536,1408]{1,0:T(8,128)(2,1)} %refs_2_.4), custom_call_target="tpu_custom_call" | custom-call | bytes 540672 | tf_op jit(solution)/shard_map/pack/pallas_call | solution.py:457
  2.4 4.5 %collective-permute-start = (bf16[104,1408]{1,0:T(8,128)(2,1)}, bf16[104,1408]{1,0:T(8,128)(2,1)S(1)}, u32[]{:S(2)}, u32[]{:S(2)}) collective-permute-start(bf16[104,1408]{1,0:T(8,128)(2,1)} %pack.2), channel_id=1, source_target_pairs={{0,64},{32,96},{64,0},{96,32},{1,65},{33,97},{65,1},{97,33},{2,66}... | collective-permute-start | bytes 878600 | tf_op jit(solution)/shard_map/ppermute | solution.py:408
  6.9 4.4 %pack.3.refs_2_ = bf16[1552,1408]{1,0:T(8,128)(2,1)} custom-call(bf16[1536,1408]{1,0:T(8,128)(2,1)} %refs_0_.3, bf16[1536]{0:T(1024)(128)(2,1)} %refs_1_.4, bf16[1536,1408]{1,0:T(8,128)(2,1)} %refs_2_.4), custom_call_target="tpu_custom_call" | custom-call | bytes 8650752 | tf_op jit(solution)/shard_map/pack/pallas_call | solution.py:457
  11.3 2.5 %collective-permute-done = bf16[104,1408]{1,0:T(8,128)(2,1)S(1)} collective-permute-done((bf16[104,1408]{1,0:T(8,128)(2,1)}, bf16[104,1408]{1,0:T(8,128)(2,1)S(1)}, u32[]{:S(2)}, u32[]{:S(2)}) %collective-permute-start) | collective-permute-done | bytes 292896 | tf_op jit(solution)/shard_map/ppermute | solution.py:408
  13.8 2.5 %collective-permute-start.3 = (bf16[104,1408]{1,0:T(8,128)(2,1)S(1)}, bf16[104,1408]{1,0:T(8,128)(2,1)S(1)}, u32[]{:S(2)}, u32[]{:S(2)}) collective-permute-start(bf16[104,1408]{1,0:T(8,128)(2,1)S(1)} %collective-permute-done), channel_id=1, source_target_pairs={{0,6},{2,0},{4,2},{6,4},{1,7},{3,1},{5,3},{7,5},{8,14},{10,8},{12,... | collective-permute-start | bytes 878600 | tf_op jit(solution)/shard_map/ppermute | solution.py:408
  16.3 0.5 collective-permute-start.2
  16.8 0.6 collective-permute-start.1
  17.4 2.8 %collective-permute-start.13 = (bf16[1552,1408]{1,0:T(8,128)(2,1)}, bf16[1552,1408]{1,0:T(8,128)(2,1)}, u32[]{:S(2)}, u32[]{:S(2)}) collective-permute-start(bf16[1552,1408]{1,0:T(8,128)(2,1)} %pack.3.refs_2_), channel_id=1, source_target_pairs={{0,96},{32,0},{64,32},{96,64},{1,97},{33,1},{65,33},{97,65},{2,98}... | collective-permute-start | bytes 13111304 | tf_op jit(solution)/shard_map/ppermute | solution.py:408
  20.2 0.0 collective-permute-start.12
  20.2 7.9 %qkv.1 = bf16[8,272,256]{2,1,0:T(8,128)(2,1)} custom-call(bf16[256,1408]{1,0:T(8,128)(2,1)} %x_ref.3, s32[1,256]{1,0:T(1,128)} %bitcast.19, bf16[2112,1408]{1,0:T(8,128)(2,1)} %bitcast.12), custom_call_target="tpu_custom_call" | custom-call | flops 1522532352 | bytes 8388608 | tf_op jit(solution)/shard_map/qkv/pallas_call | solution.py:88
  28.1 0.0 collective-permute-done.3
  28.1 0.0 collective-permute-done.2
  28.1 4.9 %collective-permute-done.1 = bf16[104,1408]{1,0:T(8,128)(2,1)S(1)} collective-permute-done((bf16[104,1408]{1,0:T(8,128)(2,1)S(1)}, bf16[104,1408]{1,0:T(8,128)(2,1)S(1)}, u32[]{:S(2)}, u32[]{:S(2)}) %collective-permute-start.1) | collective-permute-done | bytes 292896 | tf_op jit(solution)/shard_map/ppermute | solution.py:408
  33.0 4.4 %all-to-all-start = ((bf16[8,272,256]{2,1,0:T(8,128)(2,1)}), bf16[8,272,256]{2,1,0:T(8,128)(2,1)S(1)}, u32[]{:S(2)}, u32[]{:S(2)}) async-start(bf16[8,272,256]{2,1,0:T(8,128)(2,1)} %qkv.1), calls=%async_computation | async-start | bytes 2228224 | tf_op jit(solution)/shard_map/all_to_all | solution.py:495
  37.5 1.2 pad_maximum_fusion.refs_5_
  38.7 16.1 %all-to-all-done = bf16[8,272,256]{2,1,0:T(8,128)(2,1)S(1)} async-done(((bf16[8,272,256]{2,1,0:T(8,128)(2,1)}), bf16[8,272,256]{2,1,0:T(8,128)(2,1)S(1)}, u32[]{:S(2)}, u32[]{:S(2)}) %all-to-all-start) | async-done | bytes 1114144 | tf_op jit(solution)/shard_map/all_to_all | solution.py:495
  54.8 1.7 collective-permute-start.6
  56.5 0.5 collective-permute-start.5
  57.0 0.9 collective-permute-start.4
  58.0 0.4 collective-permute-done.6.refs_1_.refs_2_
  58.4 0.0 collective-permute-start.7
  58.4 5.5 %attend.3.refs_2_ = f32[96,2048]{1,0:T(8,128)} custom-call(bf16[8,96,256]{2,1,0:T(8,128)(2,1)S(1)} %slice.18.refs_0_, bf16[8,184,256]{2,1,0:T(8,128)(2,1)S(1)} %slice.19.refs_1_), custom_call_target="tpu_custom_call" | custom-call | flops 2147483648 | bytes 3145728 | tf_op jit(solution)/shard_map/attend/pallas_call | solution.py:172
  63.9 4.7 %collective-permute-done.7.refs_0_ = bf16[8,96,256]{2,1,0:T(8,128)(2,1)S(1)} collective-permute-done((bf16[8,96,256]{2,1,0:T(8,128)(2,1)S(1)}, bf16[8,96,256]{2,1,0:T(8,128)(2,1)S(1)}, u32[]{:S(2)}, u32[]{:S(2)}) %collective-permute-start.7) | collective-permute-done | bytes 393248 | tf_op jit(solution)/shard_map/ppermute | solution.py:403
  68.6 10.6 %attend.5 = bf16[8,96,256]{2,1,0:T(8,128)(2,1)} custom-call(bf16[8,96,256]{2,1,0:T(8,128)(2,1)S(1)} %collective-permute-done.7.refs_0_, bf16[8,184,256]{2,1,0:T(8,128)(2,1)S(1)} %slice.19.refs_1_, bf16[8,184,256]{2,1,0:T(8,128)(2,1)S(1)} %collective-permute-done.6.refs_1_.refs_2_), custom_call_target="tpu_custom_call" | custom-call | flops 4294967296 | bytes 3145728 | tf_op jit(solution)/shard_map/attend/pallas_call | solution.py:172
  79.2 0.3 collective-permute-start.10
  79.5 0.0 copy-done.2
  79.5 5.5 %attend.4.acc_ref = f32[96,2048]{1,0:T(8,128)} custom-call(bf16[8,96,256]{2,1,0:T(8,128)(2,1)S(1)} %slice.18.refs_0_, bf16[8,184,256]{2,1,0:T(8,128)(2,1)S(1)} %collective-permute-done.6.refs_1_.refs_2_, f32[96,2048]{1,0:T(8,128)S(1)} %copy-done.2), custom_call_target="tpu_custom_call" | custom-call | flops 2147483648 | bytes 3145728 | tf_op jit(solution)/shard_map/attend/pallas_call | solution.py:172
  85.1 0.0 collective-permute-done.5.refs_7_
  85.1 0.6 collective-permute-done.4.refs_6_
  85.6 1.1 slice.20
  86.7 1.1 slice.21
  87.8 1.2 collective-permute-start.9
  89.0 0.4 collective-permute-start.8
  89.4 0.0 collective-permute-done.10.sent_ref
  89.4 0.0 copy-done.1
  89.4 0.8 combine.1
  90.2 4.1 %all-to-all-start.1 = ((bf16[8,88,256]{2,1,0:T(8,128)(2,1)}), bf16[8,88,256]{2,1,0:T(8,128)(2,1)S(1)}, u32[]{:S(2)}, u32[]{:S(2)}) async-start(bf16[8,88,256]{2,1,0:T(8,128)(2,1)} %combine.1), calls=%async_computation.1 | async-start | bytes 720896 | tf_op jit(solution)/shard_map/all_to_all | solution.py:510
  94.3 8.2 %collective-permute-done.9.refs_9_ = bf16[2,104,1408]{2,1,0:T(8,128)(2,1)S(1)} collective-permute-done((bf16[2,104,1408]{2,1,0:T(8,128)(2,1)S(1)}, bf16[2,104,1408]{2,1,0:T(8,128)(2,1)S(1)}, u32[]{:S(2)}, u32[]{:S(2)}) %collective-permute-start.9) | collective-permute-done | bytes 585760 | tf_op jit(solution)/shard_map/ppermute | solution.py:408
  102.5 2.0 %collective-permute-done.8.refs_8_ = bf16[2,104,1408]{2,1,0:T(8,128)(2,1)S(1)} collective-permute-done((bf16[2,104,1408]{2,1,0:T(8,128)(2,1)S(1)}, bf16[2,104,1408]{2,1,0:T(8,128)(2,1)S(1)}, u32[]{:S(2)}, u32[]{:S(2)}) %collective-permute-start.8) | collective-permute-done | bytes 585760 | tf_op jit(solution)/shard_map/ppermute | solution.py:408
  104.5 2.3 %all-to-all-done.1.att_ref = bf16[8,88,256]{2,1,0:T(8,128)(2,1)S(1)} async-done(((bf16[8,88,256]{2,1,0:T(8,128)(2,1)}), bf16[8,88,256]{2,1,0:T(8,128)(2,1)S(1)}, u32[]{:S(2)}, u32[]{:S(2)}) %all-to-all-start.1) | async-done | bytes 360480 | tf_op jit(solution)/shard_map/all_to_all | solution.py:510
  106.8 3.8 %project.1 = (bf16[256,1408]{1,0:T(8,128)(2,1)}, bf16[256,1408]{1,0:T(8,128)(2,1)}) custom-call(bf16[8,88,256]{2,1,0:T(8,128)(2,1)S(1)} %all-to-all-done.1.att_ref, bf16[256,1408]{1,0:T(8,128)(2,1)} %x_ref.3, bf16[704,1408]{1,0:T(8,128)(2,1)} %w_ref.1), custom_call_target="tpu_custom_call" | custom-call | flops 507510784 | bytes 4194304 | tf_op jit(solution)/shard_map/project/pallas_call | solution.py:222
  110.6 0.0 copy-done.3
  110.6 0.0 copy-done.4
  110.6 2.9 %collective-permute-start.11 = (bf16[256,1408]{1,0:T(8,128)(2,1)}, bf16[256,1408]{1,0:T(8,128)(2,1)S(1)}, u32[]{:S(2)}, u32[]{:S(2)}) collective-permute-start(bf16[256,1408]{1,0:T(8,128)(2,1)} %get-tuple-element.49.refs_0_), channel_id=1, source_target_pairs={{0,1},{1,0},{2,3},{3,2},{4,5},{5,4},{6,7},{7,6},{8,9},{9,8},{10,11... | collective-permute-start | bytes 2162696 | tf_op jit(solution)/shard_map/ppermute | solution.py:403
  113.5 2.0 %collective-permute-done.11.refs_1_ = bf16[256,1408]{1,0:T(8,128)(2,1)S(1)} collective-permute-done((bf16[256,1408]{1,0:T(8,128)(2,1)}, bf16[256,1408]{1,0:T(8,128)(2,1)S(1)}, u32[]{:S(2)}, u32[]{:S(2)}) %collective-permute-start.11) | collective-permute-done | bytes 720928 | tf_op jit(solution)/shard_map/ppermute | solution.py:403
  115.6 0.0 collective-permute-done.13.refs_4_
  115.6 0.0 collective-permute-done.12.refs_3_
  115.6 15.2 %mlp.1 = (bf16[256,1408]{1,0:T(8,128)(2,1)}, bf16[256,1408]{1,0:T(8,128)(2,1)}) custom-call(bf16[256,1408]{1,0:T(8,128)(2,1)} %get-tuple-element.49.refs_0_, bf16[256,1408]{1,0:T(8,128)(2,1)S(1)} %collective-permute-done.11.refs_1_, bf16[1552,1408]{1,0:T(8,128)(2,1)} %pack.3.refs_2_, bf16[1552,1408]{1,0:T(8,128)(2,1)} %collective-permute-done.12.refs_3_, ...), custom_call_target="tpu_custom_call" | custom-call | flops 8858370048 | bytes 20971520 | tf_op jit(solution)/shard_map/mlp/pallas_call | solution.py:289
  130.7 3.0 %collective-permute-start.14 = (bf16[256,1408]{1,0:T(8,128)(2,1)}, bf16[256,1408]{1,0:T(8,128)(2,1)S(1)}, u32[]{:S(2)}, u32[]{:S(2)}) collective-permute-start(bf16[256,1408]{1,0:T(8,128)(2,1)} %get-tuple-element.54), channel_id=1, source_target_pairs={{0,1},{1,0},{2,3},{3,2},{4,5},{5,4},{6,7},{7,6},{8,9},{9,8},{10,11... | collective-permute-start | bytes 2162696 | tf_op jit(solution)/shard_map/ppermute | solution.py:403
  133.7 2.0 %collective-permute-done.14.refs_6_ = bf16[256,1408]{1,0:T(8,128)(2,1)S(1)} collective-permute-done((bf16[256,1408]{1,0:T(8,128)(2,1)}, bf16[256,1408]{1,0:T(8,128)(2,1)S(1)}, u32[]{:S(2)}, u32[]{:S(2)}) %collective-permute-start.14) | collective-permute-done | bytes 720928 | tf_op jit(solution)/shard_map/ppermute | solution.py:403
  135.8 3.3 %merge.1.refs_0_ = bf16[64,5760]{1,0:T(8,128)(2,1)} custom-call(bf16[256,1408]{1,0:T(8,128)(2,1)} %get-tuple-element.48.refs_0_, f32[1408]{0:T(1024)} %refs_1_.5, f32[1408]{0:T(1024)} %refs_2_.5, s32[1,256]{1,0:T(1,128)} %bitcast.20, s32[1,64]{1,0:T(1,128)} %bitcast.21, bf16[256,1408]{1,0:T(8,128)(2,1)} %get-tuple-element.53.refs_5_, ...), custom_call_target="tpu_custom_call" | custom-call | flops 184549376 | bytes 4194304 | tf_op jit(solution)/shard_map/merge/pallas_call | solution.py:338
  139.1 0.0 collective-permute-start.16
  139.1 2.7 %collective-permute-start.15 = (bf16[64,5760]{1,0:T(8,128)(2,1)}, bf16[64,5760]{1,0:T(8,128)(2,1)S(1)}, u32[]{:S(2)}, u32[]{:S(2)}) collective-permute-start(bf16[64,5760]{1,0:T(8,128)(2,1)} %merge.1.refs_0_), channel_id=1, source_target_pairs={{0,96},{32,0},{64,32},{96,64},{1,97},{33,1},{65,33},{97,65},{2,98}... | collective-permute-start | bytes 2211848 | tf_op jit(solution)/shard_map/ppermute | solution.py:408
  141.8 16.4 %collective-permute-done.16.refs_4_ = bf16[64,5760]{1,0:T(8,128)(2,1)S(1)} collective-permute-done((bf16[64,5760]{1,0:T(8,128)(2,1)}, bf16[64,5760]{1,0:T(8,128)(2,1)S(1)}, u32[]{:S(2)}, u32[]{:S(2)}) %collective-permute-start.16) | collective-permute-done | bytes 737312 | tf_op jit(solution)/shard_map/ppermute | solution.py:408
  158.2 0.3 collective-permute-start.17
  158.6 0.0 collective-permute-done.15.refs_1_
  158.6 2.7 %collective-permute-start.18 = (bf16[32,5760]{1,0:T(8,128)(2,1)S(1)}, bf16[32,5760]{1,0:T(8,128)(2,1)S(1)}, u32[]{:S(2)}, u32[]{:S(2)}) collective-permute-start(bf16[32,5760]{1,0:T(8,128)(2,1)S(1)} %slice.25), channel_id=1, source_target_pairs={{0,96},{32,0},{64,32},{96,64},{1,97},{33,1},{65,33},{97,65},{2,98}... | collective-permute-start | bytes 1105928 | tf_op jit(solution)/shard_map/ppermute | solution.py:408
  161.3 7.3 %collective-permute-done.17.refs_2_ = bf16[32,5760]{1,0:T(8,128)(2,1)S(1)} collective-permute-done((bf16[32,5760]{1,0:T(8,128)(2,1)S(1)}, bf16[32,5760]{1,0:T(8,128)(2,1)S(1)}, u32[]{:S(2)}, u32[]{:S(2)}) %collective-permute-start.17) | collective-permute-done | bytes 368672 | tf_op jit(solution)/shard_map/ppermute | solution.py:408
  168.7 0.0 collective-permute-done.18.refs_3_
  168.7 5.1 %embed.1 = bf16[512,512]{1,0:T(8,128)(2,1)} custom-call(bf16[64,5760]{1,0:T(8,128)(2,1)S(1)} %copy-done, bf16[64,5760]{1,0:T(8,128)(2,1)S(1)} %collective-permute-done.15.refs_1_, bf16[32,5760]{1,0:T(8,128)(2,1)S(1)} %collective-permute-done.17.refs_2_, bf16[32,5760]{1,0:T(8,128)(2,1)S(1)} %collective-permute-done.18.refs_3_, ...), custom_call_target="tpu_custom_call" | custom-call | flops 1476395008 | bytes 10485760 | tf_op jit(solution)/shard_map/embed/pallas_call | solution.py:385
  173.8 20.1 %all_to_all.19 = bf16[32,16,512]{2,1,0:T(8,128)(2,1)S(1)} all-to-all(bf16[32,16,512]{2,1,0:T(8,128)(2,1)} %bitcast.13), channel_id=1, replica_groups=mesh['grp'=4,'y'=4,'xh'=2,'xl'=2,'c'=2] {'y','xh','xl','c'}, dimensions={0} | all-to-all | bytes 1048576 | tf_op jit(solution)/shard_map/all_to_all | solution.py:532
  193.8 0.1 reshape.21
  194.0 0.2 copy.16
  194.2 0.9 reshape.22
  (10 shorter events, 0.1 us)
Async XLA Ops:
  2.4 11.4 %collective-permute-start = (bf16[104,1408]{1,0:T(8,128)(2,1)}, bf16[104,1408]{1,0:T(8,128)(2,1)S(1)}, u32[]{:S(2)}, u32[]{:S(2)}) collective-permute-start(bf16[104,1408]{1,0:T(8,128)(2,1)} %pack.2), channel_id=1, source_target_pairs={{0,64},{32,96},{64,0},{96,32},{1,65},{33,97},{65,1},{97,33},{2,66}... | collective-permute-start | bytes 878600 | tf_op jit(solution)/shard_map/ppermute | solution.py:408
  13.8 14.3 %collective-permute-start.3 = (bf16[104,1408]{1,0:T(8,128)(2,1)S(1)}, bf16[104,1408]{1,0:T(8,128)(2,1)S(1)}, u32[]{:S(2)}, u32[]{:S(2)}) collective-permute-start(bf16[104,1408]{1,0:T(8,128)(2,1)S(1)} %collective-permute-done), channel_id=1, source_target_pairs={{0,6},{2,0},{4,2},{6,4},{1,7},{3,1},{5,3},{7,5},{8,14},{10,8},{12,... | collective-permute-start | bytes 878600 | tf_op jit(solution)/shard_map/ppermute | solution.py:408
  16.3 11.9 %collective-permute-start.2 = (bf16[104,1408]{1,0:T(8,128)(2,1)S(1)}, bf16[104,1408]{1,0:T(8,128)(2,1)S(1)}, u32[]{:S(2)}, u32[]{:S(2)}) collective-permute-start(bf16[104,1408]{1,0:T(8,128)(2,1)S(1)} %collective-permute-done), channel_id=1, source_target_pairs={{0,4},{2,6},{4,0},{6,2},{1,5},{3,7},{5,1},{7,3},{8,12},{10,14},{12... | collective-permute-start | bytes 878600 | tf_op jit(solution)/shard_map/ppermute | solution.py:408
  16.8 16.3 %collective-permute-start.1 = (bf16[104,1408]{1,0:T(8,128)(2,1)S(1)}, bf16[104,1408]{1,0:T(8,128)(2,1)S(1)}, u32[]{:S(2)}, u32[]{:S(2)}) collective-permute-start(bf16[104,1408]{1,0:T(8,128)(2,1)S(1)} %collective-permute-done), channel_id=1, source_target_pairs={{0,2},{2,4},{4,6},{6,0},{1,3},{3,5},{5,7},{7,1},{8,10},{10,12},{12... | collective-permute-start | bytes 878600 | tf_op jit(solution)/shard_map/ppermute | solution.py:408
  17.4 98.2 %collective-permute-start.13 = (bf16[1552,1408]{1,0:T(8,128)(2,1)}, bf16[1552,1408]{1,0:T(8,128)(2,1)}, u32[]{:S(2)}, u32[]{:S(2)}) collective-permute-start(bf16[1552,1408]{1,0:T(8,128)(2,1)} %pack.3.refs_2_), channel_id=1, source_target_pairs={{0,96},{32,0},{64,32},{96,64},{1,97},{33,1},{65,33},{97,65},{2,98}... | collective-permute-start | bytes 13111304 | tf_op jit(solution)/shard_map/ppermute | solution.py:408
  20.2 95.4 %collective-permute-start.12 = (bf16[1552,1408]{1,0:T(8,128)(2,1)}, bf16[1552,1408]{1,0:T(8,128)(2,1)}, u32[]{:S(2)}, u32[]{:S(2)}) collective-permute-start(bf16[1552,1408]{1,0:T(8,128)(2,1)} %pack.3.refs_2_), channel_id=1, source_target_pairs={{0,32},{32,64},{64,96},{96,0},{1,33},{33,65},{65,97},{97,1},{2,34}... | collective-permute-start | bytes 13111304 | tf_op jit(solution)/shard_map/ppermute | solution.py:408
  33.0 21.7 %all-to-all-start = ((bf16[8,272,256]{2,1,0:T(8,128)(2,1)}), bf16[8,272,256]{2,1,0:T(8,128)(2,1)S(1)}, u32[]{:S(2)}, u32[]{:S(2)}) async-start(bf16[8,272,256]{2,1,0:T(8,128)(2,1)} %qkv.1), calls=%async_computation | async-start | bytes 2228224 | tf_op jit(solution)/shard_map/all_to_all | solution.py:495
  54.8 3.5 %collective-permute-start.6 = (bf16[8,184,256]{2,1,0:T(8,128)(2,1)S(1)}, bf16[8,184,256]{2,1,0:T(8,128)(2,1)S(1)}, u32[]{:S(2)}, u32[]{:S(2)}) collective-permute-start(bf16[8,184,256]{2,1,0:T(8,128)(2,1)S(1)} %slice.19.refs_1_), channel_id=1, source_target_pairs={{0,1},{1,0},{2,3},{3,2},{4,5},{5,4},{6,7},{7,6},{8,9},{9,8},{10,11... | collective-permute-start | bytes 2261000 | tf_op jit(solution)/shard_map/ppermute | solution.py:403
  56.5 28.6 %collective-permute-start.5 = (bf16[4,104,1408]{2,1,0:T(8,128)(2,1)}, bf16[4,104,1408]{2,1,0:T(8,128)(2,1)}, u32[]{:S(2)}, u32[]{:S(2)}) collective-permute-start(bf16[4,104,1408]{2,1,0:T(8,128)(2,1)} %pad_maximum_fusion.refs_5_), channel_id=1, source_target_pairs={{0,24},{8,0},{16,8},{24,16},{1,25},{9,1},{17,9},{25,17},{2,26},{10... | collective-permute-start | bytes 3514376 | tf_op jit(solution)/shard_map/ppermute | solution.py:408
  57.0 28.6 %collective-permute-start.4 = (bf16[4,104,1408]{2,1,0:T(8,128)(2,1)}, bf16[4,104,1408]{2,1,0:T(8,128)(2,1)}, u32[]{:S(2)}, u32[]{:S(2)}) collective-permute-start(bf16[4,104,1408]{2,1,0:T(8,128)(2,1)} %pad_maximum_fusion.refs_5_), channel_id=1, source_target_pairs={{0,8},{8,16},{16,24},{24,0},{1,9},{9,17},{17,25},{25,1},{2,10},{10... | collective-permute-start | bytes 3514376 | tf_op jit(solution)/shard_map/ppermute | solution.py:408
  58.4 10.2 %collective-permute-start.7 = (bf16[8,96,256]{2,1,0:T(8,128)(2,1)S(1)}, bf16[8,96,256]{2,1,0:T(8,128)(2,1)S(1)}, u32[]{:S(2)}, u32[]{:S(2)}) collective-permute-start(bf16[8,96,256]{2,1,0:T(8,128)(2,1)S(1)} %slice.18.refs_0_), channel_id=1, source_target_pairs={{0,2},{2,0},{1,3},{3,1},{4,6},{6,4},{5,7},{7,5},{8,10},{10,8},{9,1... | collective-permute-start | bytes 1179656 | tf_op jit(solution)/shard_map/ppermute | solution.py:403
  63.9 15.6 %copy-start.2 = (f32[96,2048]{1,0:T(8,128)S(1)}, f32[96,2048]{1,0:T(8,128)}, u32[]{:S(2)}) copy-start(f32[96,2048]{1,0:T(8,128)} %attend.3.refs_2_) | copy-start | bytes 2359300
  79.2 10.2 %collective-permute-start.10 = (bf16[8,96,256]{2,1,0:T(8,128)(2,1)}, bf16[8,96,256]{2,1,0:T(8,128)(2,1)S(1)}, u32[]{:S(2)}, u32[]{:S(2)}) collective-permute-start(bf16[8,96,256]{2,1,0:T(8,128)(2,1)} %attend.5), channel_id=1, source_target_pairs={{0,2},{2,0},{1,3},{3,1},{4,6},{6,4},{5,7},{7,5},{8,10},{10,8},{9,1... | collective-permute-start | bytes 1179656 | tf_op jit(solution)/shard_map/ppermute | solution.py:403
  85.0 4.3 %copy-start.1 = (f32[96,2048]{1,0:T(8,128)S(1)}, f32[96,2048]{1,0:T(8,128)}, u32[]{:S(2)}) copy-start(f32[96,2048]{1,0:T(8,128)} %attend.4.acc_ref) | copy-start | bytes 2359300
  87.8 14.7 %collective-permute-start.9 = (bf16[2,104,1408]{2,1,0:T(8,128)(2,1)S(1)}, bf16[2,104,1408]{2,1,0:T(8,128)(2,1)S(1)}, u32[]{:S(2)}, u32[]{:S(2)}) collective-permute-start(bf16[2,104,1408]{2,1,0:T(8,128)(2,1)S(1)} %slice.21), channel_id=1, source_target_pairs={{0,24},{8,0},{16,8},{24,16},{1,25},{9,1},{17,9},{25,17},{2,26},{10... | collective-permute-start | bytes 1757192 | tf_op jit(solution)/shard_map/ppermute | solution.py:408
  89.0 15.5 %collective-permute-start.8 = (bf16[2,104,1408]{2,1,0:T(8,128)(2,1)S(1)}, bf16[2,104,1408]{2,1,0:T(8,128)(2,1)S(1)}, u32[]{:S(2)}, u32[]{:S(2)}) collective-permute-start(bf16[2,104,1408]{2,1,0:T(8,128)(2,1)S(1)} %slice.20), channel_id=1, source_target_pairs={{0,8},{8,16},{16,24},{24,0},{1,9},{9,17},{17,25},{25,1},{2,10},{10... | collective-permute-start | bytes 1757192 | tf_op jit(solution)/shard_map/ppermute | solution.py:408
  90.2 16.6 %all-to-all-start.1 = ((bf16[8,88,256]{2,1,0:T(8,128)(2,1)}), bf16[8,88,256]{2,1,0:T(8,128)(2,1)S(1)}, u32[]{:S(2)}, u32[]{:S(2)}) async-start(bf16[8,88,256]{2,1,0:T(8,128)(2,1)} %combine.1), calls=%async_computation.1 | async-start | bytes 720896 | tf_op jit(solution)/shard_map/all_to_all | solution.py:510
  102.5 8.1 %copy-start.3 = (bf16[2,104,1408]{2,1,0:T(8,128)(2,1)}, bf16[2,104,1408]{2,1,0:T(8,128)(2,1)S(1)}, u32[]{:S(2)}) copy-start(bf16[2,104,1408]{2,1,0:T(8,128)(2,1)S(1)} %collective-permute-done.9.refs_9_) | copy-start | bytes 1757188
  104.5 6.1 %copy-start.4 = (bf16[2,104,1408]{2,1,0:T(8,128)(2,1)}, bf16[2,104,1408]{2,1,0:T(8,128)(2,1)S(1)}, u32[]{:S(2)}) copy-start(bf16[2,104,1408]{2,1,0:T(8,128)(2,1)S(1)} %collective-permute-done.8.refs_8_) | copy-start | bytes 1757188
  110.6 5.0 %collective-permute-start.11 = (bf16[256,1408]{1,0:T(8,128)(2,1)}, bf16[256,1408]{1,0:T(8,128)(2,1)S(1)}, u32[]{:S(2)}, u32[]{:S(2)}) collective-permute-start(bf16[256,1408]{1,0:T(8,128)(2,1)} %get-tuple-element.49.refs_0_), channel_id=1, source_target_pairs={{0,1},{1,0},{2,3},{3,2},{4,5},{5,4},{6,7},{7,6},{8,9},{9,8},{10,11... | collective-permute-start | bytes 2162696 | tf_op jit(solution)/shard_map/ppermute | solution.py:403
  130.7 5.0 %collective-permute-start.14 = (bf16[256,1408]{1,0:T(8,128)(2,1)}, bf16[256,1408]{1,0:T(8,128)(2,1)S(1)}, u32[]{:S(2)}, u32[]{:S(2)}) collective-permute-start(bf16[256,1408]{1,0:T(8,128)(2,1)} %get-tuple-element.54), channel_id=1, source_target_pairs={{0,1},{1,0},{2,3},{3,2},{4,5},{5,4},{6,7},{7,6},{8,9},{9,8},{10,11... | collective-permute-start | bytes 2162696 | tf_op jit(solution)/shard_map/ppermute | solution.py:403
  139.1 29.6 %copy-start = (bf16[64,5760]{1,0:T(8,128)(2,1)S(1)}, bf16[64,5760]{1,0:T(8,128)(2,1)}, u32[]{:S(2)}) copy-start(bf16[64,5760]{1,0:T(8,128)(2,1)} %merge.1.refs_0_) | copy-start | bytes 2211844
  139.1 19.1 %collective-permute-start.16 = (bf16[64,5760]{1,0:T(8,128)(2,1)}, bf16[64,5760]{1,0:T(8,128)(2,1)S(1)}, u32[]{:S(2)}, u32[]{:S(2)}) collective-permute-start(bf16[64,5760]{1,0:T(8,128)(2,1)} %merge.1.refs_0_), channel_id=1, source_target_pairs={{0,32},{32,64},{64,96},{96,0},{1,33},{33,65},{65,97},{97,1},{2,34}... | collective-permute-start | bytes 2211848 | tf_op jit(solution)/shard_map/ppermute | solution.py:408
  139.1 19.5 %collective-permute-start.15 = (bf16[64,5760]{1,0:T(8,128)(2,1)}, bf16[64,5760]{1,0:T(8,128)(2,1)S(1)}, u32[]{:S(2)}, u32[]{:S(2)}) collective-permute-start(bf16[64,5760]{1,0:T(8,128)(2,1)} %merge.1.refs_0_), channel_id=1, source_target_pairs={{0,96},{32,0},{64,32},{96,64},{1,97},{33,1},{65,33},{97,65},{2,98}... | collective-permute-start | bytes 2211848 | tf_op jit(solution)/shard_map/ppermute | solution.py:408
  158.2 10.4 %collective-permute-start.17 = (bf16[32,5760]{1,0:T(8,128)(2,1)S(1)}, bf16[32,5760]{1,0:T(8,128)(2,1)S(1)}, u32[]{:S(2)}, u32[]{:S(2)}) collective-permute-start(bf16[32,5760]{1,0:T(8,128)(2,1)S(1)} %slice.24), channel_id=1, source_target_pairs={{0,32},{32,64},{64,96},{96,0},{1,33},{33,65},{65,97},{97,1},{2,34}... | collective-permute-start | bytes 1105928 | tf_op jit(solution)/shard_map/ppermute | solution.py:408
  158.6 10.0 %collective-permute-start.18 = (bf16[32,5760]{1,0:T(8,128)(2,1)S(1)}, bf16[32,5760]{1,0:T(8,128)(2,1)S(1)}, u32[]{:S(2)}, u32[]{:S(2)}) collective-permute-start(bf16[32,5760]{1,0:T(8,128)(2,1)S(1)} %slice.25), channel_id=1, source_target_pairs={{0,96},{32,0},{64,32},{96,64},{1,97},{33,1},{65,33},{97,65},{2,98}... | collective-permute-start | bytes 1105928 | tf_op jit(solution)/shard_map/ppermute | solution.py:408

commit v7 on v6

--- a/solution.py
+++ b/solution.py
@@ -14,6 +14,7 @@
 NORM_EPS = 1e-06
 LANES = 128
 PAD = 16
+RINGS = 2
 CHIPS = ("y", "xh", "xl")
 F32 = jnp.float32
 BF16 = jnp.bfloat16
@@ -299,7 +300,7 @@
 
 
 def merge_kernel(res_ref, bias_ref, gain_ref, index_ref, owner_ref, *refs, cap):
-    parts, out_ref = refs[:-1], refs[-1]
+    parts, out_refs = refs[:-RINGS], refs[-RINGS:]
     rows, width = res_ref.shape
     total = res_ref[...].astype(F32) + bias_ref[...].reshape(1, width)
     for part in parts:
@@ -312,8 +313,11 @@
     order = (s == 4 * (r % count) + r // count).astype(F32).astype(BF16)
     pick = dot(order, named, NT).astype(BF16)
     merged = dot(pick, normed).astype(BF16)
+    size = count // RINGS
     for c in range(4):
-        out_ref[:, c * width : (c + 1) * width] = merged[c * count : (c + 1) * count]
+        for i, out_ref in enumerate(out_refs):
+            at = c * count + i * size
+            out_ref[:, c * width : (c + 1) * width] = merged[at : at + size]
     across = owner_ref[...]
     r = lax.broadcasted_iota(jnp.int32, (count, count), 0)
     s = lax.broadcasted_iota(jnp.int32, (count, count), 1)
@@ -321,7 +325,10 @@
     earlier = (across == owner) & (s < r)
     rank = jnp.sum(earlier.astype(jnp.int32), axis=1, keepdims=True)
     slot = (owner * cap + rank).astype(F32).astype(BF16)
-    out_ref[:, 4 * width :] = jnp.broadcast_to(slot, (count, LANES))
+    for i, out_ref in enumerate(out_refs):
+        out_ref[:, 4 * width :] = jnp.broadcast_to(
+            slot[i * size : (i + 1) * size], (size, LANES)
+        )
 
 
 def merge(residual, out_bias, merge_gain, merge_index, owners, parts, cap):
@@ -337,9 +344,9 @@
     )
     return pl.pallas_call(
         lambda *refs: merge_kernel(*refs, cap=cap),
-        out_shape=jax.ShapeDtypeStruct((rows // 4, 4 * width + LANES), BF16),
+        out_shape=(jax.ShapeDtypeStruct((rows // 4 // RINGS, 4 * width + LANES), BF16),) * RINGS,
         in_specs=[pl.BlockSpec(memory_space=pltpu.VMEM)] * len(operands),
-        out_specs=pl.BlockSpec(memory_space=pltpu.VMEM),
+        out_specs=(pl.BlockSpec(memory_space=pltpu.VMEM),) * RINGS,
         compiler_params=cparams(),
         cost_estimate=cost(2 * rows * rows * width, 4 << 20),
         name="merge",
@@ -517,15 +524,19 @@
     owner_count = lax.axis_size(("y", "xh", "xl", "c"))
     cap = 4
     merged = merge(residual, out_bias, merge_gain, merge_index, owners, parts, cap)
-    count = merged.shape[0]
-    before, after, far_a, far_b = ring_gather(merged, "grp")
-    pieces = [
-        (0, merged),
-        (count, after),
-        (2 * count, far_a),
-        (2 * count + count // 2, far_b),
-        (3 * count, before),
-    ]
+    size = merged[0].shape[0]
+    count = size * RINGS
+    pieces = []
+    for i, part in enumerate(merged):
+        before, after, far_a, far_b = ring_gather(part, "grp")
+        at = i * size
+        pieces += [
+            (at, part),
+            (count + at, after),
+            (2 * count + at, far_a),
+            (2 * count + at + size // 2, far_b),
+            (3 * count + at, before),
+        ]
     slots = 4 * cap
     outgoing = embed(pieces, w_merge, merge_bias, cap, slots, owner_count)
     cols = outgoing.shape[1]

time: 196 us -> 192 us (0.980)
  waiting for transfers between devices: 69.5 us -> 60.6 us
  starting transfers between devices: 36.1 us -> 41.3 us
    ppermute x14 -> x18, waiting for transfers between devices: 42 us -> 33.1 us  [turn(): lax.ppermute(value, axis, [(i, (i + by) % size) for i in range(size)])]
    ppermute x14 -> x18, starting transfers between devices: 19.7 us -> 24.9 us  [turn(): lax.ppermute(value, axis, [(i, (i + by) % size) for i in range(size)])]
  transfers between devices with their start and end apart: 21 -> 25, of which waited for: 13 -> 15; matrix products, arithmetic and copies ran while one was open for 2% -> 2% of each run, Pallas kernels for 20% -> 20%
where the time goes in v7:
time: 192 us
  Pallas kernels  64.6 us (34%)
  waiting for transfers between devices  60.6 us (32%)
  starting transfers between devices  41.3 us (22%)
  blocking collectives  20.1 us (10%)
  local copies, waits for them, and re-layouts  3.59 us (2%)
    ppermute x18, waiting for transfers between devices, turn(): lax.ppermute(value, axis, [(i, (i + by) % size) for i in range(size)])  33.1 us
    ppermute x18, starting transfers between devices, turn(): lax.ppermute(value, axis, [(i, (i + by) % size) for i in range(size)])  24.9 us
    pallas_call x3, Pallas kernels, attend(): pl.pallas_call(lambda *refs: attend_kernel(*refs, sets=len(sets), first=f...  21.7 us
    all_to_all x1, blocking collectives, local(): lax.all_to_all(outgoing, ('y', 'xh', 'xl', 'c'), 0, 0, tiled=True)  20.1 us
    all_to_all x1, waiting for transfers between devices, local(): mine = lax.all_to_all(heads, ('y', 'xh'), 0, 0, tiled=True)  16.1 us
    pallas_call x1, Pallas kernels, mlp(): pl.pallas_call(lambda *refs: mlp_kernel(*refs, near_count=len(near), far_...  15.2 us
    ppermute x5, waiting for transfers between devices, flip(): return lax.ppermute(value, axis, [(0, 1), (1, 0)])  9.09 us
    pallas_call x1, Pallas kernels, qkv(): pl.pallas_call(qkv_kernel, out_shape=jax.ShapeDtypeStruct((HEADS, 3 * HD...  7.92 us
  transfers between devices with their start and end apart: 25, of which 15 were waited for; matrix products, arithmetic and copies ran while one was open for 2% of the time, Pallas kernels for 20%

profile of v7, /device:TPU:1, one launch (start us, length us, event | category | flops | bytes accessed | tf_op | source)
XLA Modules:
  0.0 191.6 jit_solution(4715726192871594650)
XLA Ops:
  0.0 2.4 %pack.2 = bf16[104,1408]{1,0:T(8,128)(2,1)} custom-call(bf16[1536,1408]{1,0:T(8,128)(2,1)} %refs_0_.3, bf16[1536]{0:T(1024)(128)(2,1)} %refs_1_.4, bf16[1536,1408]{1,0:T(8,128)(2,1)} %refs_2_.4), custom_call_target="tpu_custom_call" | custom-call | bytes 540672 | tf_op jit(solution)/shard_map/pack/pallas_call | solution.py:464
  2.4 4.5 %collective-permute-start = (bf16[104,1408]{1,0:T(8,128)(2,1)}, bf16[104,1408]{1,0:T(8,128)(2,1)S(1)}, u32[]{:S(2)}, u32[]{:S(2)}) collective-permute-start(bf16[104,1408]{1,0:T(8,128)(2,1)} %pack.2), channel_id=1, source_target_pairs={{0,64},{32,96},{64,0},{96,32},{1,65},{33,97},{65,1},{97,33},{2,66}... | collective-permute-start | bytes 878600 | tf_op jit(solution)/shard_map/ppermute | solution.py:415
  6.9 4.4 %pack.3.refs_2_ = bf16[1552,1408]{1,0:T(8,128)(2,1)} custom-call(bf16[1536,1408]{1,0:T(8,128)(2,1)} %refs_0_.3, bf16[1536]{0:T(1024)(128)(2,1)} %refs_1_.4, bf16[1536,1408]{1,0:T(8,128)(2,1)} %refs_2_.4), custom_call_target="tpu_custom_call" | custom-call | bytes 8650752 | tf_op jit(solution)/shard_map/pack/pallas_call | solution.py:464
  11.3 2.5 %collective-permute-done = bf16[104,1408]{1,0:T(8,128)(2,1)S(1)} collective-permute-done((bf16[104,1408]{1,0:T(8,128)(2,1)}, bf16[104,1408]{1,0:T(8,128)(2,1)S(1)}, u32[]{:S(2)}, u32[]{:S(2)}) %collective-permute-start) | collective-permute-done | bytes 292896 | tf_op jit(solution)/shard_map/ppermute | solution.py:415
  13.8 2.5 %collective-permute-start.3 = (bf16[104,1408]{1,0:T(8,128)(2,1)S(1)}, bf16[104,1408]{1,0:T(8,128)(2,1)S(1)}, u32[]{:S(2)}, u32[]{:S(2)}) collective-permute-start(bf16[104,1408]{1,0:T(8,128)(2,1)S(1)} %collective-permute-done), channel_id=1, source_target_pairs={{0,6},{2,0},{4,2},{6,4},{1,7},{3,1},{5,3},{7,5},{8,14},{10,8},{12,... | collective-permute-start | bytes 878600 | tf_op jit(solution)/shard_map/ppermute | solution.py:415
  16.3 0.5 collective-permute-start.2
  16.8 0.6 collective-permute-start.1
  17.4 2.8 %collective-permute-start.13 = (bf16[1552,1408]{1,0:T(8,128)(2,1)}, bf16[1552,1408]{1,0:T(8,128)(2,1)}, u32[]{:S(2)}, u32[]{:S(2)}) collective-permute-start(bf16[1552,1408]{1,0:T(8,128)(2,1)} %pack.3.refs_2_), channel_id=1, source_target_pairs={{0,96},{32,0},{64,32},{96,64},{1,97},{33,1},{65,33},{97,65},{2,98}... | collective-permute-start | bytes 13111304 | tf_op jit(solution)/shard_map/ppermute | solution.py:415
  20.2 7.9 %qkv.1 = bf16[8,272,256]{2,1,0:T(8,128)(2,1)} custom-call(bf16[256,1408]{1,0:T(8,128)(2,1)} %x_ref.3, s32[1,256]{1,0:T(1,128)} %bitcast.19, bf16[2112,1408]{1,0:T(8,128)(2,1)} %bitcast.12), custom_call_target="tpu_custom_call" | custom-call | flops 1522532352 | bytes 8388608 | tf_op jit(solution)/shard_map/qkv/pallas_call | solution.py:89
  28.1 0.0 collective-permute-done.3
  28.1 0.0 collective-permute-done.2
  28.2 4.9 %collective-permute-done.1 = bf16[104,1408]{1,0:T(8,128)(2,1)S(1)} collective-permute-done((bf16[104,1408]{1,0:T(8,128)(2,1)S(1)}, bf16[104,1408]{1,0:T(8,128)(2,1)S(1)}, u32[]{:S(2)}, u32[]{:S(2)}) %collective-permute-start.1) | collective-permute-done | bytes 292896 | tf_op jit(solution)/shard_map/ppermute | solution.py:415
  33.0 4.4 %all-to-all-start = ((bf16[8,272,256]{2,1,0:T(8,128)(2,1)}), bf16[8,272,256]{2,1,0:T(8,128)(2,1)S(1)}, u32[]{:S(2)}, u32[]{:S(2)}) async-start(bf16[8,272,256]{2,1,0:T(8,128)(2,1)} %qkv.1), calls=%async_computation | async-start | bytes 2228224 | tf_op jit(solution)/shard_map/all_to_all | solution.py:502
  37.5 1.2 pad_maximum_fusion.refs_5_
  38.7 16.1 %all-to-all-done = bf16[8,272,256]{2,1,0:T(8,128)(2,1)S(1)} async-done(((bf16[8,272,256]{2,1,0:T(8,128)(2,1)}), bf16[8,272,256]{2,1,0:T(8,128)(2,1)S(1)}, u32[]{:S(2)}, u32[]{:S(2)}) %all-to-all-start) | async-done | bytes 1114144 | tf_op jit(solution)/shard_map/all_to_all | solution.py:502
  54.8 1.7 collective-permute-start.6
  56.5 0.5 collective-permute-start.5
  57.0 0.9 collective-permute-start.4
  58.0 0.4 collective-permute-done.6.refs_1_.refs_2_
  58.4 0.0 collective-permute-start.7
  58.4 5.6 %attend.3.refs_2_ = f32[96,2048]{1,0:T(8,128)} custom-call(bf16[8,96,256]{2,1,0:T(8,128)(2,1)S(1)} %slice.24.refs_0_, bf16[8,184,256]{2,1,0:T(8,128)(2,1)S(1)} %slice.25.refs_1_), custom_call_target="tpu_custom_call" | custom-call | flops 2147483648 | bytes 3145728 | tf_op jit(solution)/shard_map/attend/pallas_call | solution.py:173
  63.9 4.7 %collective-permute-done.7.refs_0_ = bf16[8,96,256]{2,1,0:T(8,128)(2,1)S(1)} collective-permute-done((bf16[8,96,256]{2,1,0:T(8,128)(2,1)S(1)}, bf16[8,96,256]{2,1,0:T(8,128)(2,1)S(1)}, u32[]{:S(2)}, u32[]{:S(2)}) %collective-permute-start.7) | collective-permute-done | bytes 393248 | tf_op jit(solution)/shard_map/ppermute | solution.py:410
  68.6 10.6 %attend.5 = bf16[8,96,256]{2,1,0:T(8,128)(2,1)} custom-call(bf16[8,96,256]{2,1,0:T(8,128)(2,1)S(1)} %collective-permute-done.7.refs_0_, bf16[8,184,256]{2,1,0:T(8,128)(2,1)S(1)} %slice.25.refs_1_, bf16[8,184,256]{2,1,0:T(8,128)(2,1)S(1)} %collective-permute-done.6.refs_1_.refs_2_), custom_call_target="tpu_custom_call" | custom-call | flops 4294967296 | bytes 3145728 | tf_op jit(solution)/shard_map/attend/pallas_call | solution.py:173
  79.2 0.3 collective-permute-start.10
  79.5 5.6 %attend.4.acc_ref = f32[96,2048]{1,0:T(8,128)} custom-call(bf16[8,96,256]{2,1,0:T(8,128)(2,1)S(1)} %slice.24.refs_0_, bf16[8,184,256]{2,1,0:T(8,128)(2,1)S(1)} %collective-permute-done.6.refs_1_.refs_2_, f32[96,2048]{1,0:T(8,128)S(1)} %copy-done.3), custom_call_target="tpu_custom_call" | custom-call | flops 2147483648 | bytes 3145728 | tf_op jit(solution)/shard_map/attend/pallas_call | solution.py:173
  85.1 0.0 collective-permute-done.5.refs_7_
  85.1 0.5 collective-permute-done.4.refs_6_
  85.6 1.1 slice.26
  86.7 1.1 slice.27
  87.8 1.2 collective-permute-start.9
  89.0 0.4 collective-permute-start.8
  89.4 0.0 collective-permute-done.10.sent_ref
  89.4 0.9 combine.1
  90.2 4.1 %all-to-all-start.1 = ((bf16[8,88,256]{2,1,0:T(8,128)(2,1)}), bf16[8,88,256]{2,1,0:T(8,128)(2,1)S(1)}, u32[]{:S(2)}, u32[]{:S(2)}) async-start(bf16[8,88,256]{2,1,0:T(8,128)(2,1)} %combine.1), calls=%async_computation.1 | async-start | bytes 720896 | tf_op jit(solution)/shard_map/all_to_all | solution.py:517
  94.3 8.2 %collective-permute-done.9.refs_9_ = bf16[2,104,1408]{2,1,0:T(8,128)(2,1)S(1)} collective-permute-done((bf16[2,104,1408]{2,1,0:T(8,128)(2,1)S(1)}, bf16[2,104,1408]{2,1,0:T(8,128)(2,1)S(1)}, u32[]{:S(2)}, u32[]{:S(2)}) %collective-permute-start.9) | collective-permute-done | bytes 585760 | tf_op jit(solution)/shard_map/ppermute | solution.py:415
  102.5 2.0 %collective-permute-done.8.refs_8_ = bf16[2,104,1408]{2,1,0:T(8,128)(2,1)S(1)} collective-permute-done((bf16[2,104,1408]{2,1,0:T(8,128)(2,1)S(1)}, bf16[2,104,1408]{2,1,0:T(8,128)(2,1)S(1)}, u32[]{:S(2)}, u32[]{:S(2)}) %collective-permute-start.8) | collective-permute-done | bytes 585760 | tf_op jit(solution)/shard_map/ppermute | solution.py:415
  104.5 2.3 %all-to-all-done.1.att_ref = bf16[8,88,256]{2,1,0:T(8,128)(2,1)S(1)} async-done(((bf16[8,88,256]{2,1,0:T(8,128)(2,1)}), bf16[8,88,256]{2,1,0:T(8,128)(2,1)S(1)}, u32[]{:S(2)}, u32[]{:S(2)}) %all-to-all-start.1) | async-done | bytes 360480 | tf_op jit(solution)/shard_map/all_to_all | solution.py:517
  106.8 3.8 %project.1 = (bf16[256,1408]{1,0:T(8,128)(2,1)}, bf16[256,1408]{1,0:T(8,128)(2,1)}) custom-call(bf16[8,88,256]{2,1,0:T(8,128)(2,1)S(1)} %all-to-all-done.1.att_ref, bf16[256,1408]{1,0:T(8,128)(2,1)} %x_ref.3, bf16[704,1408]{1,0:T(8,128)(2,1)} %w_ref.1), custom_call_target="tpu_custom_call" | custom-call | flops 507510784 | bytes 4194304 | tf_op jit(solution)/shard_map/project/pallas_call | solution.py:223
  110.6 2.9 %collective-permute-start.11 = (bf16[256,1408]{1,0:T(8,128)(2,1)}, bf16[256,1408]{1,0:T(8,128)(2,1)S(1)}, u32[]{:S(2)}, u32[]{:S(2)}) collective-permute-start(bf16[256,1408]{1,0:T(8,128)(2,1)} %get-tuple-element.51.refs_0_), channel_id=1, source_target_pairs={{0,1},{1,0},{2,3},{3,2},{4,5},{5,4},{6,7},{7,6},{8,9},{9,8},{10,11... | collective-permute-start | bytes 2162696 | tf_op jit(solution)/shard_map/ppermute | solution.py:410
  113.6 2.0 %collective-permute-done.11.refs_1_ = bf16[256,1408]{1,0:T(8,128)(2,1)S(1)} collective-permute-done((bf16[256,1408]{1,0:T(8,128)(2,1)}, bf16[256,1408]{1,0:T(8,128)(2,1)S(1)}, u32[]{:S(2)}, u32[]{:S(2)}) %collective-permute-start.11) | collective-permute-done | bytes 720928 | tf_op jit(solution)/shard_map/ppermute | solution.py:410
  115.6 0.0 collective-permute-done.13.refs_4_
  115.6 15.2 %mlp.1 = (bf16[256,1408]{1,0:T(8,128)(2,1)}, bf16[256,1408]{1,0:T(8,128)(2,1)}) custom-call(bf16[256,1408]{1,0:T(8,128)(2,1)} %get-tuple-element.51.refs_0_, bf16[256,1408]{1,0:T(8,128)(2,1)S(1)} %collective-permute-done.11.refs_1_, bf16[1552,1408]{1,0:T(8,128)(2,1)} %pack.3.refs_2_, bf16[1552,1408]{1,0:T(8,128)(2,1)} %collective-permute-done.12.refs_3_, ...), custom_call_target="tpu_custom_call" | custom-call | flops 8858370048 | bytes 20971520 | tf_op jit(solution)/shard_map/mlp/pallas_call | solution.py:290
  130.8 3.0 %collective-permute-start.14 = (bf16[256,1408]{1,0:T(8,128)(2,1)}, bf16[256,1408]{1,0:T(8,128)(2,1)S(1)}, u32[]{:S(2)}, u32[]{:S(2)}) collective-permute-start(bf16[256,1408]{1,0:T(8,128)(2,1)} %get-tuple-element.56), channel_id=1, source_target_pairs={{0,1},{1,0},{2,3},{3,2},{4,5},{5,4},{6,7},{7,6},{8,9},{9,8},{10,11... | collective-permute-start | bytes 2162696 | tf_op jit(solution)/shard_map/ppermute | solution.py:410
  133.7 2.0 %collective-permute-done.14.refs_6_ = bf16[256,1408]{1,0:T(8,128)(2,1)S(1)} collective-permute-done((bf16[256,1408]{1,0:T(8,128)(2,1)}, bf16[256,1408]{1,0:T(8,128)(2,1)S(1)}, u32[]{:S(2)}, u32[]{:S(2)}) %collective-permute-start.14) | collective-permute-done | bytes 720928 | tf_op jit(solution)/shard_map/ppermute | solution.py:410
  135.8 3.3 %merge.1 = (bf16[32,5760]{1,0:T(8,128)(2,1)}, bf16[32,5760]{1,0:T(8,128)(2,1)}) custom-call(bf16[256,1408]{1,0:T(8,128)(2,1)} %get-tuple-element.50.refs_0_, f32[1408]{0:T(1024)} %refs_1_.5, f32[1408]{0:T(1024)} %refs_2_.5, s32[1,256]{1,0:T(1,128)} %bitcast.20, s32[1,64]{1,0:T(1,128)} %bitcast.21, bf16[256,1408]{1,0:T(8,128)(2,1)} %get-tuple-element.55.refs_5_, ...), custom_call_target="tpu_custom_call" | custom-call | flops 184549376 | bytes 4194304 | tf_op jit(solution)/shard_map/merge/pallas_call | solution.py:345
  139.1 0.0 collective-permute-start.16
  139.1 2.7 %collective-permute-start.15 = (bf16[32,5760]{1,0:T(8,128)(2,1)}, bf16[32,5760]{1,0:T(8,128)(2,1)S(1)}, u32[]{:S(2)}, u32[]{:S(2)}) collective-permute-start(bf16[32,5760]{1,0:T(8,128)(2,1)} %get-tuple-element.57.refs_0_), channel_id=1, source_target_pairs={{0,96},{32,0},{64,32},{96,64},{1,97},{33,1},{65,33},{97,65},{2,98}... | collective-permute-start | bytes 1105928 | tf_op jit(solution)/shard_map/ppermute | solution.py:415
  141.7 0.0 collective-permute-start.20
  141.7 2.7 %collective-permute-start.19 = (bf16[32,5760]{1,0:T(8,128)(2,1)}, bf16[32,5760]{1,0:T(8,128)(2,1)S(1)}, u32[]{:S(2)}, u32[]{:S(2)}) collective-permute-start(bf16[32,5760]{1,0:T(8,128)(2,1)} %get-tuple-element.58.refs_5_), channel_id=1, source_target_pairs={{0,96},{32,0},{64,32},{96,64},{1,97},{33,1},{65,33},{97,65},{2,98}... | collective-permute-start | bytes 1105928 | tf_op jit(solution)/shard_map/ppermute | solution.py:415
  144.4 5.9 %collective-permute-done.16.refs_4_ = bf16[32,5760]{1,0:T(8,128)(2,1)S(1)} collective-permute-done((bf16[32,5760]{1,0:T(8,128)(2,1)}, bf16[32,5760]{1,0:T(8,128)(2,1)S(1)}, u32[]{:S(2)}, u32[]{:S(2)}) %collective-permute-start.16) | collective-permute-done | bytes 368672 | tf_op jit(solution)/shard_map/ppermute | solution.py:415
  150.3 0.1 collective-permute-start.17
  150.4 0.0 collective-permute-done.15.refs_1_
  150.4 2.7 %collective-permute-start.18 = (bf16[16,5760]{1,0:T(8,128)(2,1)S(1)}, bf16[16,5760]{1,0:T(8,128)(2,1)S(1)}, u32[]{:S(2)}, u32[]{:S(2)}) collective-permute-start(bf16[16,5760]{1,0:T(8,128)(2,1)S(1)} %slice.33), channel_id=1, source_target_pairs={{0,96},{32,0},{64,32},{96,64},{1,97},{33,1},{65,33},{97,65},{2,98}... | collective-permute-start | bytes 552968 | tf_op jit(solution)/shard_map/ppermute | solution.py:415
  153.1 5.0 %collective-permute-done.20.refs_9_ = bf16[32,5760]{1,0:T(8,128)(2,1)S(1)} collective-permute-done((bf16[32,5760]{1,0:T(8,128)(2,1)}, bf16[32,5760]{1,0:T(8,128)(2,1)S(1)}, u32[]{:S(2)}, u32[]{:S(2)}) %collective-permute-start.20) | collective-permute-done | bytes 368672 | tf_op jit(solution)/shard_map/ppermute | solution.py:415
  158.2 0.1 collective-permute-start.21
  158.3 0.0 collective-permute-done.19.refs_6_
  158.3 2.7 %collective-permute-start.22 = (bf16[16,5760]{1,0:T(8,128)(2,1)S(1)}, bf16[16,5760]{1,0:T(8,128)(2,1)S(1)}, u32[]{:S(2)}, u32[]{:S(2)}) collective-permute-start(bf16[16,5760]{1,0:T(8,128)(2,1)S(1)} %slice.35), channel_id=1, source_target_pairs={{0,96},{32,0},{64,32},{96,64},{1,97},{33,1},{65,33},{97,65},{2,98}... | collective-permute-start | bytes 552968 | tf_op jit(solution)/shard_map/ppermute | solution.py:415
  161.0 1.1 collective-permute-done.17.refs_2_
  162.1 3.0 %collective-permute-done.21.refs_7_ = bf16[16,5760]{1,0:T(8,128)(2,1)S(1)} collective-permute-done((bf16[16,5760]{1,0:T(8,128)(2,1)S(1)}, bf16[16,5760]{1,0:T(8,128)(2,1)S(1)}, u32[]{:S(2)}, u32[]{:S(2)}) %collective-permute-start.21) | collective-permute-done | bytes 184352 | tf_op jit(solution)/shard_map/ppermute | solution.py:415
  165.1 5.1 %embed.1 = bf16[512,512]{1,0:T(8,128)(2,1)} custom-call(bf16[32,5760]{1,0:T(8,128)(2,1)S(1)} %copy-done.1, bf16[32,5760]{1,0:T(8,128)(2,1)S(1)} %collective-permute-done.15.refs_1_, bf16[16,5760]{1,0:T(8,128)(2,1)S(1)} %collective-permute-done.17.refs_2_, bf16[16,5760]{1,0:T(8,128)(2,1)S(1)} %collective-permute-done.18.refs_3_, ...), custom_call_target="tpu_custom_call" | custom-call | flops 1476395008 | bytes 10485760 | tf_op jit(solution)/shard_map/embed/pallas_call | solution.py:392
  170.2 20.1 %all_to_all.19 = bf16[32,16,512]{2,1,0:T(8,128)(2,1)S(1)} all-to-all(bf16[32,16,512]{2,1,0:T(8,128)(2,1)} %bitcast.13), channel_id=1, replica_groups=mesh['grp'=4,'y'=4,'xh'=2,'xl'=2,'c'=2] {'y','xh','xl','c'}, dimensions={0} | all-to-all | bytes 1048576 | tf_op jit(solution)/shard_map/all_to_all | solution.py:543
  190.4 0.1 reshape.21
  190.5 0.2 copy.16
  190.7 0.9 reshape.22
  (22 shorter events, 0.2 us)
Async XLA Ops:
  2.4 11.4 %collective-permute-start = (bf16[104,1408]{1,0:T(8,128)(2,1)}, bf16[104,1408]{1,0:T(8,128)(2,1)S(1)}, u32[]{:S(2)}, u32[]{:S(2)}) collective-permute-start(bf16[104,1408]{1,0:T(8,128)(2,1)} %pack.2), channel_id=1, source_target_pairs={{0,64},{32,96},{64,0},{96,32},{1,65},{33,97},{65,1},{97,33},{2,66}... | collective-permute-start | bytes 878600 | tf_op jit(solution)/shard_map/ppermute | solution.py:415
  13.8 14.3 %collective-permute-start.3 = (bf16[104,1408]{1,0:T(8,128)(2,1)S(1)}, bf16[104,1408]{1,0:T(8,128)(2,1)S(1)}, u32[]{:S(2)}, u32[]{:S(2)}) collective-permute-start(bf16[104,1408]{1,0:T(8,128)(2,1)S(1)} %collective-permute-done), channel_id=1, source_target_pairs={{0,6},{2,0},{4,2},{6,4},{1,7},{3,1},{5,3},{7,5},{8,14},{10,8},{12,... | collective-permute-start | bytes 878600 | tf_op jit(solution)/shard_map/ppermute | solution.py:415
  16.3 11.9 %collective-permute-start.2 = (bf16[104,1408]{1,0:T(8,128)(2,1)S(1)}, bf16[104,1408]{1,0:T(8,128)(2,1)S(1)}, u32[]{:S(2)}, u32[]{:S(2)}) collective-permute-start(bf16[104,1408]{1,0:T(8,128)(2,1)S(1)} %collective-permute-done), channel_id=1, source_target_pairs={{0,4},{2,6},{4,0},{6,2},{1,5},{3,7},{5,1},{7,3},{8,12},{10,14},{12... | collective-permute-start | bytes 878600 | tf_op jit(solution)/shard_map/ppermute | solution.py:415
  16.8 16.3 %collective-permute-start.1 = (bf16[104,1408]{1,0:T(8,128)(2,1)S(1)}, bf16[104,1408]{1,0:T(8,128)(2,1)S(1)}, u32[]{:S(2)}, u32[]{:S(2)}) collective-permute-start(bf16[104,1408]{1,0:T(8,128)(2,1)S(1)} %collective-permute-done), channel_id=1, source_target_pairs={{0,2},{2,4},{4,6},{6,0},{1,3},{3,5},{5,7},{7,1},{8,10},{10,12},{12... | collective-permute-start | bytes 878600 | tf_op jit(solution)/shard_map/ppermute | solution.py:415
  17.4 98.2 %collective-permute-start.13 = (bf16[1552,1408]{1,0:T(8,128)(2,1)}, bf16[1552,1408]{1,0:T(8,128)(2,1)}, u32[]{:S(2)}, u32[]{:S(2)}) collective-permute-start(bf16[1552,1408]{1,0:T(8,128)(2,1)} %pack.3.refs_2_), channel_id=1, source_target_pairs={{0,96},{32,0},{64,32},{96,64},{1,97},{33,1},{65,33},{97,65},{2,98}... | collective-permute-start | bytes 13111304 | tf_op jit(solution)/shard_map/ppermute | solution.py:415
  20.2 95.4 %collective-permute-start.12 = (bf16[1552,1408]{1,0:T(8,128)(2,1)}, bf16[1552,1408]{1,0:T(8,128)(2,1)}, u32[]{:S(2)}, u32[]{:S(2)}) collective-permute-start(bf16[1552,1408]{1,0:T(8,128)(2,1)} %pack.3.refs_2_), channel_id=1, source_target_pairs={{0,32},{32,64},{64,96},{96,0},{1,33},{33,65},{65,97},{97,1},{2,34}... | collective-permute-start | bytes 13111304 | tf_op jit(solution)/shard_map/ppermute | solution.py:415
  33.0 21.7 %all-to-all-start = ((bf16[8,272,256]{2,1,0:T(8,128)(2,1)}), bf16[8,272,256]{2,1,0:T(8,128)(2,1)S(1)}, u32[]{:S(2)}, u32[]{:S(2)}) async-start(bf16[8,272,256]{2,1,0:T(8,128)(2,1)} %qkv.1), calls=%async_computation | async-start | bytes 2228224 | tf_op jit(solution)/shard_map/all_to_all | solution.py:502
  54.8 3.5 %collective-permute-start.6 = (bf16[8,184,256]{2,1,0:T(8,128)(2,1)S(1)}, bf16[8,184,256]{2,1,0:T(8,128)(2,1)S(1)}, u32[]{:S(2)}, u32[]{:S(2)}) collective-permute-start(bf16[8,184,256]{2,1,0:T(8,128)(2,1)S(1)} %slice.25.refs_1_), channel_id=1, source_target_pairs={{0,1},{1,0},{2,3},{3,2},{4,5},{5,4},{6,7},{7,6},{8,9},{9,8},{10,11... | collective-permute-start | bytes 2261000 | tf_op jit(solution)/shard_map/ppermute | solution.py:410
  56.5 28.6 %collective-permute-start.5 = (bf16[4,104,1408]{2,1,0:T(8,128)(2,1)}, bf16[4,104,1408]{2,1,0:T(8,128)(2,1)}, u32[]{:S(2)}, u32[]{:S(2)}) collective-permute-start(bf16[4,104,1408]{2,1,0:T(8,128)(2,1)} %pad_maximum_fusion.refs_5_), channel_id=1, source_target_pairs={{0,24},{8,0},{16,8},{24,16},{1,25},{9,1},{17,9},{25,17},{2,26},{10... | collective-permute-start | bytes 3514376 | tf_op jit(solution)/shard_map/ppermute | solution.py:415
  57.0 28.6 %collective-permute-start.4 = (bf16[4,104,1408]{2,1,0:T(8,128)(2,1)}, bf16[4,104,1408]{2,1,0:T(8,128)(2,1)}, u32[]{:S(2)}, u32[]{:S(2)}) collective-permute-start(bf16[4,104,1408]{2,1,0:T(8,128)(2,1)} %pad_maximum_fusion.refs_5_), channel_id=1, source_target_pairs={{0,8},{8,16},{16,24},{24,0},{1,9},{9,17},{17,25},{25,1},{2,10},{10... | collective-permute-start | bytes 3514376 | tf_op jit(solution)/shard_map/ppermute | solution.py:415
  58.4 10.2 %collective-permute-start.7 = (bf16[8,96,256]{2,1,0:T(8,128)(2,1)S(1)}, bf16[8,96,256]{2,1,0:T(8,128)(2,1)S(1)}, u32[]{:S(2)}, u32[]{:S(2)}) collective-permute-start(bf16[8,96,256]{2,1,0:T(8,128)(2,1)S(1)} %slice.24.refs_0_), channel_id=1, source_target_pairs={{0,2},{2,0},{1,3},{3,1},{4,6},{6,4},{5,7},{7,5},{8,10},{10,8},{9,1... | collective-permute-start | bytes 1179656 | tf_op jit(solution)/shard_map/ppermute | solution.py:410
  63.9 15.6 %copy-start.3 = (f32[96,2048]{1,0:T(8,128)S(1)}, f32[96,2048]{1,0:T(8,128)}, u32[]{:S(2)}) copy-start(f32[96,2048]{1,0:T(8,128)} %attend.3.refs_2_) | copy-start | bytes 2359300
  79.2 10.2 %collective-permute-start.10 = (bf16[8,96,256]{2,1,0:T(8,128)(2,1)}, bf16[8,96,256]{2,1,0:T(8,128)(2,1)S(1)}, u32[]{:S(2)}, u32[]{:S(2)}) collective-permute-start(bf16[8,96,256]{2,1,0:T(8,128)(2,1)} %attend.5), channel_id=1, source_target_pairs={{0,2},{2,0},{1,3},{3,1},{4,6},{6,4},{5,7},{7,5},{8,10},{10,8},{9,1... | collective-permute-start | bytes 1179656 | tf_op jit(solution)/shard_map/ppermute | solution.py:410
  85.1 4.3 %copy-start = (f32[96,2048]{1,0:T(8,128)S(1)}, f32[96,2048]{1,0:T(8,128)}, u32[]{:S(2)}) copy-start(f32[96,2048]{1,0:T(8,128)} %attend.4.acc_ref) | copy-start | bytes 2359300
  87.8 14.7 %collective-permute-start.9 = (bf16[2,104,1408]{2,1,0:T(8,128)(2,1)S(1)}, bf16[2,104,1408]{2,1,0:T(8,128)(2,1)S(1)}, u32[]{:S(2)}, u32[]{:S(2)}) collective-permute-start(bf16[2,104,1408]{2,1,0:T(8,128)(2,1)S(1)} %slice.27), channel_id=1, source_target_pairs={{0,24},{8,0},{16,8},{24,16},{1,25},{9,1},{17,9},{25,17},{2,26},{10... | collective-permute-start | bytes 1757192 | tf_op jit(solution)/shard_map/ppermute | solution.py:415
  89.0 15.5 %collective-permute-start.8 = (bf16[2,104,1408]{2,1,0:T(8,128)(2,1)S(1)}, bf16[2,104,1408]{2,1,0:T(8,128)(2,1)S(1)}, u32[]{:S(2)}, u32[]{:S(2)}) collective-permute-start(bf16[2,104,1408]{2,1,0:T(8,128)(2,1)S(1)} %slice.26), channel_id=1, source_target_pairs={{0,8},{8,16},{16,24},{24,0},{1,9},{9,17},{17,25},{25,1},{2,10},{10... | collective-permute-start | bytes 1757192 | tf_op jit(solution)/shard_map/ppermute | solution.py:415
  90.2 16.6 %all-to-all-start.1 = ((bf16[8,88,256]{2,1,0:T(8,128)(2,1)}), bf16[8,88,256]{2,1,0:T(8,128)(2,1)S(1)}, u32[]{:S(2)}, u32[]{:S(2)}) async-start(bf16[8,88,256]{2,1,0:T(8,128)(2,1)} %combine.1), calls=%async_computation.1 | async-start | bytes 720896 | tf_op jit(solution)/shard_map/all_to_all | solution.py:517
  102.5 8.1 %copy-start.4 = (bf16[2,104,1408]{2,1,0:T(8,128)(2,1)}, bf16[2,104,1408]{2,1,0:T(8,128)(2,1)S(1)}, u32[]{:S(2)}) copy-start(bf16[2,104,1408]{2,1,0:T(8,128)(2,1)S(1)} %collective-permute-done.9.refs_9_) | copy-start | bytes 1757188
  104.5 6.1 %copy-start.5 = (bf16[2,104,1408]{2,1,0:T(8,128)(2,1)}, bf16[2,104,1408]{2,1,0:T(8,128)(2,1)S(1)}, u32[]{:S(2)}) copy-start(bf16[2,104,1408]{2,1,0:T(8,128)(2,1)S(1)} %collective-permute-done.8.refs_8_) | copy-start | bytes 1757188
  110.6 5.0 %collective-permute-start.11 = (bf16[256,1408]{1,0:T(8,128)(2,1)}, bf16[256,1408]{1,0:T(8,128)(2,1)S(1)}, u32[]{:S(2)}, u32[]{:S(2)}) collective-permute-start(bf16[256,1408]{1,0:T(8,128)(2,1)} %get-tuple-element.51.refs_0_), channel_id=1, source_target_pairs={{0,1},{1,0},{2,3},{3,2},{4,5},{5,4},{6,7},{7,6},{8,9},{9,8},{10,11... | collective-permute-start | bytes 2162696 | tf_op jit(solution)/shard_map/ppermute | solution.py:410
  130.8 5.0 %collective-permute-start.14 = (bf16[256,1408]{1,0:T(8,128)(2,1)}, bf16[256,1408]{1,0:T(8,128)(2,1)S(1)}, u32[]{:S(2)}, u32[]{:S(2)}) collective-permute-start(bf16[256,1408]{1,0:T(8,128)(2,1)} %get-tuple-element.56), channel_id=1, source_target_pairs={{0,1},{1,0},{2,3},{3,2},{4,5},{5,4},{6,7},{7,6},{8,9},{9,8},{10,11... | collective-permute-start | bytes 2162696 | tf_op jit(solution)/shard_map/ppermute | solution.py:410
  139.1 26.1 %copy-start.1 = (bf16[32,5760]{1,0:T(8,128)(2,1)S(1)}, bf16[32,5760]{1,0:T(8,128)(2,1)}, u32[]{:S(2)}) copy-start(bf16[32,5760]{1,0:T(8,128)(2,1)} %get-tuple-element.57.refs_0_) | copy-start | bytes 1105924
  139.1 26.1 %copy-start.2 = (bf16[32,5760]{1,0:T(8,128)(2,1)S(1)}, bf16[32,5760]{1,0:T(8,128)(2,1)}, u32[]{:S(2)}) copy-start(bf16[32,5760]{1,0:T(8,128)(2,1)} %get-tuple-element.58.refs_5_) | copy-start | bytes 1105924
  139.1 11.2 %collective-permute-start.16 = (bf16[32,5760]{1,0:T(8,128)(2,1)}, bf16[32,5760]{1,0:T(8,128)(2,1)S(1)}, u32[]{:S(2)}, u32[]{:S(2)}) collective-permute-start(bf16[32,5760]{1,0:T(8,128)(2,1)} %get-tuple-element.57.refs_0_), channel_id=1, source_target_pairs={{0,32},{32,64},{64,96},{96,0},{1,33},{33,65},{65,97},{97,1},{2,34}... | collective-permute-start | bytes 1105928 | tf_op jit(solution)/shard_map/ppermute | solution.py:415
  139.1 11.3 %collective-permute-start.15 = (bf16[32,5760]{1,0:T(8,128)(2,1)}, bf16[32,5760]{1,0:T(8,128)(2,1)S(1)}, u32[]{:S(2)}, u32[]{:S(2)}) collective-permute-start(bf16[32,5760]{1,0:T(8,128)(2,1)} %get-tuple-element.57.refs_0_), channel_id=1, source_target_pairs={{0,96},{32,0},{64,32},{96,64},{1,97},{33,1},{65,33},{97,65},{2,98}... | collective-permute-start | bytes 1105928 | tf_op jit(solution)/shard_map/ppermute | solution.py:415
  141.7 16.4 %collective-permute-start.20 = (bf16[32,5760]{1,0:T(8,128)(2,1)}, bf16[32,5760]{1,0:T(8,128)(2,1)S(1)}, u32[]{:S(2)}, u32[]{:S(2)}) collective-permute-start(bf16[32,5760]{1,0:T(8,128)(2,1)} %get-tuple-element.58.refs_5_), channel_id=1, source_target_pairs={{0,32},{32,64},{64,96},{96,0},{1,33},{33,65},{65,97},{97,1},{2,34}... | collective-permute-start | bytes 1105928 | tf_op jit(solution)/shard_map/ppermute | solution.py:415
  141.7 16.5 %collective-permute-start.19 = (bf16[32,5760]{1,0:T(8,128)(2,1)}, bf16[32,5760]{1,0:T(8,128)(2,1)S(1)}, u32[]{:S(2)}, u32[]{:S(2)}) collective-permute-start(bf16[32,5760]{1,0:T(8,128)(2,1)} %get-tuple-element.58.refs_5_), channel_id=1, source_target_pairs={{0,96},{32,0},{64,32},{96,64},{1,97},{33,1},{65,33},{97,65},{2,98}... | collective-permute-start | bytes 1105928 | tf_op jit(solution)/shard_map/ppermute | solution.py:415
  150.3 11.8 %collective-permute-start.17 = (bf16[16,5760]{1,0:T(8,128)(2,1)S(1)}, bf16[16,5760]{1,0:T(8,128)(2,1)S(1)}, u32[]{:S(2)}, u32[]{:S(2)}) collective-permute-start(bf16[16,5760]{1,0:T(8,128)(2,1)S(1)} %slice.32), channel_id=1, source_target_pairs={{0,32},{32,64},{64,96},{96,0},{1,33},{33,65},{65,97},{97,1},{2,34}... | collective-permute-start | bytes 552968 | tf_op jit(solution)/shard_map/ppermute | solution.py:415
  150.4 11.7 %collective-permute-start.18 = (bf16[16,5760]{1,0:T(8,128)(2,1)S(1)}, bf16[16,5760]{1,0:T(8,128)(2,1)S(1)}, u32[]{:S(2)}, u32[]{:S(2)}) collective-permute-start(bf16[16,5760]{1,0:T(8,128)(2,1)S(1)} %slice.33), channel_id=1, source_target_pairs={{0,96},{32,0},{64,32},{96,64},{1,97},{33,1},{65,33},{97,65},{2,98}... | collective-permute-start | bytes 552968 | tf_op jit(solution)/shard_map/ppermute | solution.py:415
  158.2 6.9 %collective-permute-start.21 = (bf16[16,5760]{1,0:T(8,128)(2,1)S(1)}, bf16[16,5760]{1,0:T(8,128)(2,1)S(1)}, u32[]{:S(2)}, u32[]{:S(2)}) collective-permute-start(bf16[16,5760]{1,0:T(8,128)(2,1)S(1)} %slice.34), channel_id=1, source_target_pairs={{0,32},{32,64},{64,96},{96,0},{1,33},{33,65},{65,97},{97,1},{2,34}... | collective-permute-start | bytes 552968 | tf_op jit(solution)/shard_map/ppermute | solution.py:415
  158.3 6.8 %collective-permute-start.22 = (bf16[16,5760]{1,0:T(8,128)(2,1)S(1)}, bf16[16,5760]{1,0:T(8,128)(2,1)S(1)}, u32[]{:S(2)}, u32[]{:S(2)}) collective-permute-start(bf16[16,5760]{1,0:T(8,128)(2,1)S(1)} %slice.35), channel_id=1, source_target_pairs={{0,96},{32,0},{64,32},{96,64},{1,97},{33,1},{65,33},{97,65},{2,98}... | collective-permute-start | bytes 552968 | tf_op jit(solution)/shard_map/ppermute | solution.py:415

commit v8 on v7

--- a/solution.py
+++ b/solution.py
@@ -48,7 +48,7 @@
 
 
 def qkv_kernel(x_ref, seg_ref, w_hbm, out_ref, w_ref, sems):
-    group = HEADS // 2 * HD
+    group = HEADS * HD
     count = w_ref.shape[0] // group
     copies = []
     for number in range(count):
@@ -68,17 +68,15 @@
         copies[number].wait()
         part = dot(w_ref[number * group : (number + 1) * group, :], normed, NT)
         part = part.astype(BF16).astype(F32)
-        kind = number // 2
-        for i in range(HEADS // 2):
-            head = number % 2 * (HEADS // 2) + i
-            rows = part[i * HD : (i + 1) * HD]
-            if kind == 2:
+        for head in range(HEADS):
+            rows = part[head * HD : (head + 1) * HD]
+            if number == 2:
                 out_ref[head, HD : 2 * HD + EXT] = jnp.concatenate([extra, rows], axis=0).astype(
                     BF16
                 )
                 continue
             norm = lax.rsqrt(jnp.mean(rows * rows, axis=0, keepdims=True) + NORM_EPS)
-            if kind == 0:
+            if number == 0:
                 out_ref[head, :HD] = (rows * (norm * scale)).astype(BF16)
             else:
                 out_ref[head, 2 * HD + EXT :] = (rows * norm).astype(BF16)
@@ -97,7 +95,7 @@
         out_specs=pl.BlockSpec(memory_space=pltpu.VMEM),
         scratch_shapes=[
             pltpu.VMEM((w_qkv.shape[1], width), BF16),
-            pltpu.SemaphoreType.DMA((6,)),
+            pltpu.SemaphoreType.DMA((3,)),
         ],
         compiler_params=cparams(),
         cost_estimate=cost(2 * rows * width * w_qkv.shape[1], 8 << 20),
@@ -498,7 +496,7 @@
     row = [far] + [turn(far, ("xh", "xl"), by) for by in (1, 2, 3)]
     one, two = turn(near, "grp", 1), turn(near, "grp", -1)
     heads = qkv(tokens, seg_ids, w_qkv)
-    row, heads = lax.optimization_barrier((row, heads))
+    row[1], row[3], heads = lax.optimization_barrier((row[1], row[3], heads))
     mine = lax.all_to_all(heads, ("y", "xh"), 0, 0, tiled=True)
     row, mine = lax.optimization_barrier((jnp.stack(row), mine))
     below, above = turn(row, "y", 1), turn(row, "y", -1)

time: 192 us -> 192 us (level)
  starting transfers between devices: 41.3 us -> 49.3 us
  waiting for transfers between devices: 60.6 us -> 53.8 us
    all_to_all x1, waiting for transfers between devices: 16.1 us -> 0.01 us  [local(): mine = lax.all_to_all(heads, ('y', 'xh'), 0, 0, tiled=True)]
    ppermute x18, waiting for transfers between devices: 33.1 us -> 43.9 us  [turn(): lax.ppermute(value, axis, [(i, (i + by) % size) for i in range(size)])]
    ppermute x18, starting transfers between devices: 24.9 us -> 28.6 us  [turn(): lax.ppermute(value, axis, [(i, (i + by) % size) for i in range(size)])]
    ppermute x5, starting transfers between devices: 7.91 us -> 10.6 us  [flip(): return lax.ppermute(value, axis, [(0, 1), (1, 0)])]
  transfers between devices with their start and end apart: 25 -> 25, of which waited for: 15 -> 13; matrix products, arithmetic and copies ran while one was open for 2% -> 2% of each run, Pallas kernels for 20% -> 20%
where the time goes in v8:
time: 192 us; the launch traced here: 191 us
  Pallas kernels  63.7 us (33%)
  waiting for transfers between devices  53.8 us (28%)
  starting transfers between devices  49.3 us (26%)
  blocking collectives  19.2 us (10%)
  local copies, waits for them, and re-layouts  3.65 us (2%)
    ppermute x18, waiting for transfers between devices, turn(): lax.ppermute(value, axis, [(i, (i + by) % size) for i in range(size)])  43.9 us
    ppermute x18, starting transfers between devices, turn(): lax.ppermute(value, axis, [(i, (i + by) % size) for i in range(size)])  28.6 us
    pallas_call x3, Pallas kernels, attend(): pl.pallas_call(lambda *refs: attend_kernel(*refs, sets=len(sets), first=f...  21.7 us
    all_to_all x1, blocking collectives, local(): lax.all_to_all(outgoing, ('y', 'xh', 'xl', 'c'), 0, 0, tiled=True)  19.2 us
    pallas_call x1, Pallas kernels, mlp(): pl.pallas_call(lambda *refs: mlp_kernel(*refs, near_count=len(near), far_...  15.2 us
    ppermute x5, starting transfers between devices, flip(): return lax.ppermute(value, axis, [(0, 1), (1, 0)])  10.6 us
    ppermute x5, waiting for transfers between devices, flip(): return lax.ppermute(value, axis, [(0, 1), (1, 0)])  7.63 us
    pallas_call x1, Pallas kernels, qkv(): pl.pallas_call(qkv_kernel, out_shape=jax.ShapeDtypeStruct((HEADS, 3 * HD...  7.11 us
  transfers between devices with their start and end apart: 25, of which 13 were waited for; matrix products, arithmetic and copies ran while one was open for 2% of the time, Pallas kernels for 20%

profile of v8, /device:TPU:1, one launch (start us, length us, event | category | flops | bytes accessed | tf_op | source)
XLA Modules:
  0.0 191.1 jit_solution(7563082264592997195)
XLA Ops:
  0.0 2.4 %pack.2 = bf16[104,1408]{1,0:T(8,128)(2,1)} custom-call(bf16[1536,1408]{1,0:T(8,128)(2,1)} %refs_0_.3, bf16[1536]{0:T(1024)(128)(2,1)} %refs_1_.4, bf16[1536,1408]{1,0:T(8,128)(2,1)} %refs_2_.4), custom_call_target="tpu_custom_call" | custom-call | bytes 540672 | tf_op jit(solution)/shard_map/pack/pallas_call | solution.py:462
  2.4 4.5 %collective-permute-start = (bf16[104,1408]{1,0:T(8,128)(2,1)}, bf16[104,1408]{1,0:T(8,128)(2,1)S(1)}, u32[]{:S(2)}, u32[]{:S(2)}) collective-permute-start(bf16[104,1408]{1,0:T(8,128)(2,1)} %pack.2), channel_id=1, source_target_pairs={{0,64},{32,96},{64,0},{96,32},{1,65},{33,97},{65,1},{97,33},{2,66}... | collective-permute-start | bytes 878600 | tf_op jit(solution)/shard_map/ppermute | solution.py:413
  6.9 4.4 %pack.3.refs_2_ = bf16[1552,1408]{1,0:T(8,128)(2,1)} custom-call(bf16[1536,1408]{1,0:T(8,128)(2,1)} %refs_0_.3, bf16[1536]{0:T(1024)(128)(2,1)} %refs_1_.4, bf16[1536,1408]{1,0:T(8,128)(2,1)} %refs_2_.4), custom_call_target="tpu_custom_call" | custom-call | bytes 8650752 | tf_op jit(solution)/shard_map/pack/pallas_call | solution.py:462
  11.3 2.5 %collective-permute-done = bf16[104,1408]{1,0:T(8,128)(2,1)S(1)} collective-permute-done((bf16[104,1408]{1,0:T(8,128)(2,1)}, bf16[104,1408]{1,0:T(8,128)(2,1)S(1)}, u32[]{:S(2)}, u32[]{:S(2)}) %collective-permute-start) | collective-permute-done | bytes 292896 | tf_op jit(solution)/shard_map/ppermute | solution.py:413
  13.8 2.5 %collective-permute-start.2 = (bf16[104,1408]{1,0:T(8,128)(2,1)S(1)}, bf16[104,1408]{1,0:T(8,128)(2,1)S(1)}, u32[]{:S(2)}, u32[]{:S(2)}) collective-permute-start(bf16[104,1408]{1,0:T(8,128)(2,1)S(1)} %collective-permute-done), channel_id=1, source_target_pairs={{0,6},{2,0},{4,2},{6,4},{1,7},{3,1},{5,3},{7,5},{8,14},{10,8},{12,... | collective-permute-start | bytes 878600 | tf_op jit(solution)/shard_map/ppermute | solution.py:413
  16.3 0.0 collective-permute-start.1
  16.3 2.8 %collective-permute-start.13 = (bf16[1552,1408]{1,0:T(8,128)(2,1)}, bf16[1552,1408]{1,0:T(8,128)(2,1)}, u32[]{:S(2)}, u32[]{:S(2)}) collective-permute-start(bf16[1552,1408]{1,0:T(8,128)(2,1)} %pack.3.refs_2_), channel_id=1, source_target_pairs={{0,96},{32,0},{64,32},{96,64},{1,97},{33,1},{65,33},{97,65},{2,98}... | collective-permute-start | bytes 13111304 | tf_op jit(solution)/shard_map/ppermute | solution.py:413
  19.1 0.0 collective-permute-start.12
  19.1 7.1 %qkv.1 = bf16[8,272,256]{2,1,0:T(8,128)(2,1)} custom-call(bf16[256,1408]{1,0:T(8,128)(2,1)} %x_ref.3, s32[1,256]{1,0:T(1,128)} %bitcast.19, bf16[2112,1408]{1,0:T(8,128)(2,1)} %bitcast.12), custom_call_target="tpu_custom_call" | custom-call | flops 1522532352 | bytes 8388608 | tf_op jit(solution)/shard_map/qkv/pallas_call | solution.py:87
  26.2 0.0 collective-permute-done.2
  26.2 0.0 collective-permute-done.1
  26.2 5.6 %all-to-all-start = ((bf16[8,272,256]{2,1,0:T(8,128)(2,1)}), bf16[8,272,256]{2,1,0:T(8,128)(2,1)S(1)}, u32[]{:S(2)}, u32[]{:S(2)}) async-start(bf16[8,272,256]{2,1,0:T(8,128)(2,1)} %qkv.1), calls=%async_computation | async-start | bytes 2228224 | tf_op jit(solution)/shard_map/all_to_all | solution.py:500
  31.9 3.0 %collective-permute-start.3 = (bf16[104,1408]{1,0:T(8,128)(2,1)S(1)}, bf16[104,1408]{1,0:T(8,128)(2,1)S(1)}, u32[]{:S(2)}, u32[]{:S(2)}) collective-permute-start(bf16[104,1408]{1,0:T(8,128)(2,1)S(1)} %collective-permute-done), channel_id=1, source_target_pairs={{0,4},{2,6},{4,0},{6,2},{1,5},{3,7},{5,1},{7,3},{8,12},{10,14},{12... | collective-permute-start | bytes 878600 | tf_op jit(solution)/shard_map/ppermute | solution.py:413
  34.8 16.5 %collective-permute-done.3 = bf16[104,1408]{1,0:T(8,128)(2,1)S(1)} collective-permute-done((bf16[104,1408]{1,0:T(8,128)(2,1)S(1)}, bf16[104,1408]{1,0:T(8,128)(2,1)S(1)}, u32[]{:S(2)}, u32[]{:S(2)}) %collective-permute-start.3) | collective-permute-done | bytes 292896 | tf_op jit(solution)/shard_map/ppermute | solution.py:413
  51.3 1.2 pad_maximum_fusion.refs_5_
  52.5 0.0 all-to-all-done
  52.5 3.7 %collective-permute-start.6 = (bf16[8,184,256]{2,1,0:T(8,128)(2,1)S(1)}, bf16[8,184,256]{2,1,0:T(8,128)(2,1)S(1)}, u32[]{:S(2)}, u32[]{:S(2)}) collective-permute-start(bf16[8,184,256]{2,1,0:T(8,128)(2,1)S(1)} %slice.25.refs_1_), channel_id=1, source_target_pairs={{0,1},{1,0},{2,3},{3,2},{4,5},{5,4},{6,7},{7,6},{8,9},{9,8},{10,11... | collective-permute-start | bytes 2261000 | tf_op jit(solution)/shard_map/ppermute | solution.py:408
  56.2 2.4 %collective-permute-start.5 = (bf16[4,104,1408]{2,1,0:T(8,128)(2,1)}, bf16[4,104,1408]{2,1,0:T(8,128)(2,1)}, u32[]{:S(2)}, u32[]{:S(2)}) collective-permute-start(bf16[4,104,1408]{2,1,0:T(8,128)(2,1)} %pad_maximum_fusion.refs_5_), channel_id=1, source_target_pairs={{0,24},{8,0},{16,8},{24,16},{1,25},{9,1},{17,9},{25,17},{2,26},{10... | collective-permute-start | bytes 3514376 | tf_op jit(solution)/shard_map/ppermute | solution.py:413
  58.6 0.0 collective-permute-start.4
  58.7 0.0 collective-permute-done.6.refs_1_.refs_2_
  58.7 1.8 collective-permute-start.7
  60.5 5.5 %attend.3.refs_2_ = f32[96,2048]{1,0:T(8,128)} custom-call(bf16[8,96,256]{2,1,0:T(8,128)(2,1)S(1)} %slice.24.refs_0_, bf16[8,184,256]{2,1,0:T(8,128)(2,1)S(1)} %slice.25.refs_1_), custom_call_target="tpu_custom_call" | custom-call | flops 2147483648 | bytes 3145728 | tf_op jit(solution)/shard_map/attend/pallas_call | solution.py:171
  66.0 3.6 %collective-permute-done.7.refs_0_ = bf16[8,96,256]{2,1,0:T(8,128)(2,1)S(1)} collective-permute-done((bf16[8,96,256]{2,1,0:T(8,128)(2,1)S(1)}, bf16[8,96,256]{2,1,0:T(8,128)(2,1)S(1)}, u32[]{:S(2)}, u32[]{:S(2)}) %collective-permute-start.7) | collective-permute-done | bytes 393248 | tf_op jit(solution)/shard_map/ppermute | solution.py:408
  69.6 10.6 %attend.5 = bf16[8,96,256]{2,1,0:T(8,128)(2,1)} custom-call(bf16[8,96,256]{2,1,0:T(8,128)(2,1)S(1)} %collective-permute-done.7.refs_0_, bf16[8,184,256]{2,1,0:T(8,128)(2,1)S(1)} %slice.25.refs_1_, bf16[8,184,256]{2,1,0:T(8,128)(2,1)S(1)} %collective-permute-done.6.refs_1_.refs_2_), custom_call_target="tpu_custom_call" | custom-call | flops 4294967296 | bytes 3145728 | tf_op jit(solution)/shard_map/attend/pallas_call | solution.py:171
  80.2 1.3 collective-permute-start.10
  81.5 5.6 %attend.4.acc_ref = f32[96,2048]{1,0:T(8,128)} custom-call(bf16[8,96,256]{2,1,0:T(8,128)(2,1)S(1)} %slice.24.refs_0_, bf16[8,184,256]{2,1,0:T(8,128)(2,1)S(1)} %collective-permute-done.6.refs_1_.refs_2_, f32[96,2048]{1,0:T(8,128)S(1)} %copy-done.3), custom_call_target="tpu_custom_call" | custom-call | flops 2147483648 | bytes 3145728 | tf_op jit(solution)/shard_map/attend/pallas_call | solution.py:171
  87.1 0.0 collective-permute-done.5.refs_7_
  87.1 0.1 collective-permute-done.4.refs_6_
  87.2 1.2 slice.26
  88.3 1.1 slice.27
  89.5 2.4 %collective-permute-start.9 = (bf16[2,104,1408]{2,1,0:T(8,128)(2,1)S(1)}, bf16[2,104,1408]{2,1,0:T(8,128)(2,1)S(1)}, u32[]{:S(2)}, u32[]{:S(2)}) collective-permute-start(bf16[2,104,1408]{2,1,0:T(8,128)(2,1)S(1)} %slice.27), channel_id=1, source_target_pairs={{0,24},{8,0},{16,8},{24,16},{1,25},{9,1},{17,9},{25,17},{2,26},{10... | collective-permute-start | bytes 1757192 | tf_op jit(solution)/shard_map/ppermute | solution.py:413
  91.8 0.0 collective-permute-start.8
  91.8 0.0 collective-permute-done.10.sent_ref
  91.8 0.9 combine.1
  92.7 4.6 %all-to-all-start.1 = ((bf16[8,88,256]{2,1,0:T(8,128)(2,1)}), bf16[8,88,256]{2,1,0:T(8,128)(2,1)S(1)}, u32[]{:S(2)}, u32[]{:S(2)}) async-start(bf16[8,88,256]{2,1,0:T(8,128)(2,1)} %combine.1), calls=%async_computation.1 | async-start | bytes 720896 | tf_op jit(solution)/shard_map/all_to_all | solution.py:515
  97.2 6.3 %collective-permute-done.9.refs_9_ = bf16[2,104,1408]{2,1,0:T(8,128)(2,1)S(1)} collective-permute-done((bf16[2,104,1408]{2,1,0:T(8,128)(2,1)S(1)}, bf16[2,104,1408]{2,1,0:T(8,128)(2,1)S(1)}, u32[]{:S(2)}, u32[]{:S(2)}) %collective-permute-start.9) | collective-permute-done | bytes 585760 | tf_op jit(solution)/shard_map/ppermute | solution.py:413
  103.5 3.5 %collective-permute-done.8.refs_8_ = bf16[2,104,1408]{2,1,0:T(8,128)(2,1)S(1)} collective-permute-done((bf16[2,104,1408]{2,1,0:T(8,128)(2,1)S(1)}, bf16[2,104,1408]{2,1,0:T(8,128)(2,1)S(1)}, u32[]{:S(2)}, u32[]{:S(2)}) %collective-permute-start.8) | collective-permute-done | bytes 585760 | tf_op jit(solution)/shard_map/ppermute | solution.py:413
  107.0 2.3 %all-to-all-done.1.att_ref = bf16[8,88,256]{2,1,0:T(8,128)(2,1)S(1)} async-done(((bf16[8,88,256]{2,1,0:T(8,128)(2,1)}), bf16[8,88,256]{2,1,0:T(8,128)(2,1)S(1)}, u32[]{:S(2)}, u32[]{:S(2)}) %all-to-all-start.1) | async-done | bytes 360480 | tf_op jit(solution)/shard_map/all_to_all | solution.py:515
  109.3 3.8 %project.1 = (bf16[256,1408]{1,0:T(8,128)(2,1)}, bf16[256,1408]{1,0:T(8,128)(2,1)}) custom-call(bf16[8,88,256]{2,1,0:T(8,128)(2,1)S(1)} %all-to-all-done.1.att_ref, bf16[256,1408]{1,0:T(8,128)(2,1)} %x_ref.3, bf16[704,1408]{1,0:T(8,128)(2,1)} %w_ref.1), custom_call_target="tpu_custom_call" | custom-call | flops 507510784 | bytes 4194304 | tf_op jit(solution)/shard_map/project/pallas_call | solution.py:221
  113.1 3.3 %collective-permute-start.11 = (bf16[256,1408]{1,0:T(8,128)(2,1)}, bf16[256,1408]{1,0:T(8,128)(2,1)S(1)}, u32[]{:S(2)}, u32[]{:S(2)}) collective-permute-start(bf16[256,1408]{1,0:T(8,128)(2,1)} %get-tuple-element.47.refs_0_), channel_id=1, source_target_pairs={{0,1},{1,0},{2,3},{3,2},{4,5},{5,4},{6,7},{7,6},{8,9},{9,8},{10,11... | collective-permute-start | bytes 2162696 | tf_op jit(solution)/shard_map/ppermute | solution.py:408
  116.4 2.0 %collective-permute-done.11.refs_1_ = bf16[256,1408]{1,0:T(8,128)(2,1)S(1)} collective-permute-done((bf16[256,1408]{1,0:T(8,128)(2,1)}, bf16[256,1408]{1,0:T(8,128)(2,1)S(1)}, u32[]{:S(2)}, u32[]{:S(2)}) %collective-permute-start.11) | collective-permute-done | bytes 720928 | tf_op jit(solution)/shard_map/ppermute | solution.py:408
  118.4 15.2 %mlp.1 = (bf16[256,1408]{1,0:T(8,128)(2,1)}, bf16[256,1408]{1,0:T(8,128)(2,1)}) custom-call(bf16[256,1408]{1,0:T(8,128)(2,1)} %get-tuple-element.47.refs_0_, bf16[256,1408]{1,0:T(8,128)(2,1)S(1)} %collective-permute-done.11.refs_1_, bf16[1552,1408]{1,0:T(8,128)(2,1)} %pack.3.refs_2_, bf16[1552,1408]{1,0:T(8,128)(2,1)} %collective-permute-done.12.refs_3_, ...), custom_call_target="tpu_custom_call" | custom-call | flops 8858370048 | bytes 20971520 | tf_op jit(solution)/shard_map/mlp/pallas_call | solution.py:288
  133.6 0.5 collective-permute-start.14
  134.0 2.0 %collective-permute-done.14.refs_6_ = bf16[256,1408]{1,0:T(8,128)(2,1)S(1)} collective-permute-done((bf16[256,1408]{1,0:T(8,128)(2,1)}, bf16[256,1408]{1,0:T(8,128)(2,1)S(1)}, u32[]{:S(2)}, u32[]{:S(2)}) %collective-permute-start.14) | collective-permute-done | bytes 720928 | tf_op jit(solution)/shard_map/ppermute | solution.py:408
  136.1 3.3 %merge.1 = (bf16[32,5760]{1,0:T(8,128)(2,1)}, bf16[32,5760]{1,0:T(8,128)(2,1)}) custom-call(bf16[256,1408]{1,0:T(8,128)(2,1)} %get-tuple-element.46.refs_0_, f32[1408]{0:T(1024)} %refs_1_.5, f32[1408]{0:T(1024)} %refs_2_.5, s32[1,256]{1,0:T(1,128)} %bitcast.20, s32[1,64]{1,0:T(1,128)} %bitcast.21, bf16[256,1408]{1,0:T(8,128)(2,1)} %get-tuple-element.51.refs_5_, ...), custom_call_target="tpu_custom_call" | custom-call | flops 184549376 | bytes 4194304 | tf_op jit(solution)/shard_map/merge/pallas_call | solution.py:343
  139.3 0.0 collective-permute-start.16
  139.4 2.8 %collective-permute-start.15 = (bf16[32,5760]{1,0:T(8,128)(2,1)}, bf16[32,5760]{1,0:T(8,128)(2,1)S(1)}, u32[]{:S(2)}, u32[]{:S(2)}) collective-permute-start(bf16[32,5760]{1,0:T(8,128)(2,1)} %get-tuple-element.53.refs_0_), channel_id=1, source_target_pairs={{0,96},{32,0},{64,32},{96,64},{1,97},{33,1},{65,33},{97,65},{2,98}... | collective-permute-start | bytes 1105928 | tf_op jit(solution)/shard_map/ppermute | solution.py:413
  142.1 0.0 collective-permute-start.20
  142.1 2.7 %collective-permute-start.19 = (bf16[32,5760]{1,0:T(8,128)(2,1)}, bf16[32,5760]{1,0:T(8,128)(2,1)S(1)}, u32[]{:S(2)}, u32[]{:S(2)}) collective-permute-start(bf16[32,5760]{1,0:T(8,128)(2,1)} %get-tuple-element.54.refs_5_), channel_id=1, source_target_pairs={{0,96},{32,0},{64,32},{96,64},{1,97},{33,1},{65,33},{97,65},{2,98}... | collective-permute-start | bytes 1105928 | tf_op jit(solution)/shard_map/ppermute | solution.py:413
  144.8 5.9 %collective-permute-done.16.refs_4_ = bf16[32,5760]{1,0:T(8,128)(2,1)S(1)} collective-permute-done((bf16[32,5760]{1,0:T(8,128)(2,1)}, bf16[32,5760]{1,0:T(8,128)(2,1)S(1)}, u32[]{:S(2)}, u32[]{:S(2)}) %collective-permute-start.16) | collective-permute-done | bytes 368672 | tf_op jit(solution)/shard_map/ppermute | solution.py:413
  150.7 0.1 collective-permute-start.17
  150.8 0.0 collective-permute-done.15.refs_1_
  150.8 2.7 %collective-permute-start.18 = (bf16[16,5760]{1,0:T(8,128)(2,1)S(1)}, bf16[16,5760]{1,0:T(8,128)(2,1)S(1)}, u32[]{:S(2)}, u32[]{:S(2)}) collective-permute-start(bf16[16,5760]{1,0:T(8,128)(2,1)S(1)} %slice.33), channel_id=1, source_target_pairs={{0,96},{32,0},{64,32},{96,64},{1,97},{33,1},{65,33},{97,65},{2,98}... | collective-permute-start | bytes 552968 | tf_op jit(solution)/shard_map/ppermute | solution.py:413
  153.6 5.0 %collective-permute-done.20.refs_9_ = bf16[32,5760]{1,0:T(8,128)(2,1)S(1)} collective-permute-done((bf16[32,5760]{1,0:T(8,128)(2,1)}, bf16[32,5760]{1,0:T(8,128)(2,1)S(1)}, u32[]{:S(2)}, u32[]{:S(2)}) %collective-permute-start.20) | collective-permute-done | bytes 368672 | tf_op jit(solution)/shard_map/ppermute | solution.py:413
  158.6 0.1 collective-permute-start.21
  158.7 2.7 %collective-permute-start.22 = (bf16[16,5760]{1,0:T(8,128)(2,1)S(1)}, bf16[16,5760]{1,0:T(8,128)(2,1)S(1)}, u32[]{:S(2)}, u32[]{:S(2)}) collective-permute-start(bf16[16,5760]{1,0:T(8,128)(2,1)S(1)} %slice.35), channel_id=1, source_target_pairs={{0,96},{32,0},{64,32},{96,64},{1,97},{33,1},{65,33},{97,65},{2,98}... | collective-permute-start | bytes 552968 | tf_op jit(solution)/shard_map/ppermute | solution.py:413
  161.5 1.1 collective-permute-done.17.refs_2_
  162.6 3.0 %collective-permute-done.21.refs_7_ = bf16[16,5760]{1,0:T(8,128)(2,1)S(1)} collective-permute-done((bf16[16,5760]{1,0:T(8,128)(2,1)S(1)}, bf16[16,5760]{1,0:T(8,128)(2,1)S(1)}, u32[]{:S(2)}, u32[]{:S(2)}) %collective-permute-start.21) | collective-permute-done | bytes 184352 | tf_op jit(solution)/shard_map/ppermute | solution.py:413
  165.5 0.0 collective-permute-done.22.refs_8_
  165.6 5.1 %embed.1 = bf16[512,512]{1,0:T(8,128)(2,1)} custom-call(bf16[32,5760]{1,0:T(8,128)(2,1)S(1)} %copy-done.1, bf16[32,5760]{1,0:T(8,128)(2,1)S(1)} %collective-permute-done.15.refs_1_, bf16[16,5760]{1,0:T(8,128)(2,1)S(1)} %collective-permute-done.17.refs_2_, bf16[16,5760]{1,0:T(8,128)(2,1)S(1)} %collective-permute-done.18.refs_3_, ...), custom_call_target="tpu_custom_call" | custom-call | flops 1476395008 | bytes 10485760 | tf_op jit(solution)/shard_map/embed/pallas_call | solution.py:390
  170.7 19.2 %all_to_all.19 = bf16[32,16,512]{2,1,0:T(8,128)(2,1)S(1)} all-to-all(bf16[32,16,512]{2,1,0:T(8,128)(2,1)} %bitcast.13), channel_id=1, replica_groups=mesh['grp'=4,'y'=4,'xh'=2,'xl'=2,'c'=2] {'y','xh','xl','c'}, dimensions={0} | all-to-all | bytes 1048576 | tf_op jit(solution)/shard_map/all_to_all | solution.py:541
  189.8 0.1 reshape.21
  190.0 0.2 copy.16
  190.2 0.9 reshape.22
  (22 shorter events, 0.2 us)
Async XLA Ops:
  2.4 11.4 %collective-permute-start = (bf16[104,1408]{1,0:T(8,128)(2,1)}, bf16[104,1408]{1,0:T(8,128)(2,1)S(1)}, u32[]{:S(2)}, u32[]{:S(2)}) collective-permute-start(bf16[104,1408]{1,0:T(8,128)(2,1)} %pack.2), channel_id=1, source_target_pairs={{0,64},{32,96},{64,0},{96,32},{1,65},{33,97},{65,1},{97,33},{2,66}... | collective-permute-start | bytes 878600 | tf_op jit(solution)/shard_map/ppermute | solution.py:413
  13.8 12.4 %collective-permute-start.2 = (bf16[104,1408]{1,0:T(8,128)(2,1)S(1)}, bf16[104,1408]{1,0:T(8,128)(2,1)S(1)}, u32[]{:S(2)}, u32[]{:S(2)}) collective-permute-start(bf16[104,1408]{1,0:T(8,128)(2,1)S(1)} %collective-permute-done), channel_id=1, source_target_pairs={{0,6},{2,0},{4,2},{6,4},{1,7},{3,1},{5,3},{7,5},{8,14},{10,8},{12,... | collective-permute-start | bytes 878600 | tf_op jit(solution)/shard_map/ppermute | solution.py:413
  16.3 9.9 %collective-permute-start.1 = (bf16[104,1408]{1,0:T(8,128)(2,1)S(1)}, bf16[104,1408]{1,0:T(8,128)(2,1)S(1)}, u32[]{:S(2)}, u32[]{:S(2)}) collective-permute-start(bf16[104,1408]{1,0:T(8,128)(2,1)S(1)} %collective-permute-done), channel_id=1, source_target_pairs={{0,2},{2,4},{4,6},{6,0},{1,3},{3,5},{5,7},{7,1},{8,10},{10,12},{12... | collective-permute-start | bytes 878600 | tf_op jit(solution)/shard_map/ppermute | solution.py:413
  16.3 102.1 %collective-permute-start.13 = (bf16[1552,1408]{1,0:T(8,128)(2,1)}, bf16[1552,1408]{1,0:T(8,128)(2,1)}, u32[]{:S(2)}, u32[]{:S(2)}) collective-permute-start(bf16[1552,1408]{1,0:T(8,128)(2,1)} %pack.3.refs_2_), channel_id=1, source_target_pairs={{0,96},{32,0},{64,32},{96,64},{1,97},{33,1},{65,33},{97,65},{2,98}... | collective-permute-start | bytes 13111304 | tf_op jit(solution)/shard_map/ppermute | solution.py:413
  19.1 99.3 %collective-permute-start.12 = (bf16[1552,1408]{1,0:T(8,128)(2,1)}, bf16[1552,1408]{1,0:T(8,128)(2,1)}, u32[]{:S(2)}, u32[]{:S(2)}) collective-permute-start(bf16[1552,1408]{1,0:T(8,128)(2,1)} %pack.3.refs_2_), channel_id=1, source_target_pairs={{0,32},{32,64},{64,96},{96,0},{1,33},{33,65},{65,97},{97,1},{2,34}... | collective-permute-start | bytes 13111304 | tf_op jit(solution)/shard_map/ppermute | solution.py:413
  26.2 26.3 %all-to-all-start = ((bf16[8,272,256]{2,1,0:T(8,128)(2,1)}), bf16[8,272,256]{2,1,0:T(8,128)(2,1)S(1)}, u32[]{:S(2)}, u32[]{:S(2)}) async-start(bf16[8,272,256]{2,1,0:T(8,128)(2,1)} %qkv.1), calls=%async_computation | async-start | bytes 2228224 | tf_op jit(solution)/shard_map/all_to_all | solution.py:500
  31.9 19.4 %collective-permute-start.3 = (bf16[104,1408]{1,0:T(8,128)(2,1)S(1)}, bf16[104,1408]{1,0:T(8,128)(2,1)S(1)}, u32[]{:S(2)}, u32[]{:S(2)}) collective-permute-start(bf16[104,1408]{1,0:T(8,128)(2,1)S(1)} %collective-permute-done), channel_id=1, source_target_pairs={{0,4},{2,6},{4,0},{6,2},{1,5},{3,7},{5,1},{7,3},{8,12},{10,14},{12... | collective-permute-start | bytes 878600 | tf_op jit(solution)/shard_map/ppermute | solution.py:413
  52.5 6.1 %collective-permute-start.6 = (bf16[8,184,256]{2,1,0:T(8,128)(2,1)S(1)}, bf16[8,184,256]{2,1,0:T(8,128)(2,1)S(1)}, u32[]{:S(2)}, u32[]{:S(2)}) collective-permute-start(bf16[8,184,256]{2,1,0:T(8,128)(2,1)S(1)} %slice.25.refs_1_), channel_id=1, source_target_pairs={{0,1},{1,0},{2,3},{3,2},{4,5},{5,4},{6,7},{7,6},{8,9},{9,8},{10,11... | collective-permute-start | bytes 2261000 | tf_op jit(solution)/shard_map/ppermute | solution.py:408
  56.2 30.9 %collective-permute-start.5 = (bf16[4,104,1408]{2,1,0:T(8,128)(2,1)}, bf16[4,104,1408]{2,1,0:T(8,128)(2,1)}, u32[]{:S(2)}, u32[]{:S(2)}) collective-permute-start(bf16[4,104,1408]{2,1,0:T(8,128)(2,1)} %pad_maximum_fusion.refs_5_), channel_id=1, source_target_pairs={{0,24},{8,0},{16,8},{24,16},{1,25},{9,1},{17,9},{25,17},{2,26},{10... | collective-permute-start | bytes 3514376 | tf_op jit(solution)/shard_map/ppermute | solution.py:413
  58.6 28.6 %collective-permute-start.4 = (bf16[4,104,1408]{2,1,0:T(8,128)(2,1)}, bf16[4,104,1408]{2,1,0:T(8,128)(2,1)}, u32[]{:S(2)}, u32[]{:S(2)}) collective-permute-start(bf16[4,104,1408]{2,1,0:T(8,128)(2,1)} %pad_maximum_fusion.refs_5_), channel_id=1, source_target_pairs={{0,8},{8,16},{16,24},{24,0},{1,9},{9,17},{17,25},{25,1},{2,10},{10... | collective-permute-start | bytes 3514376 | tf_op jit(solution)/shard_map/ppermute | solution.py:413
  58.7 11.0 %collective-permute-start.7 = (bf16[8,96,256]{2,1,0:T(8,128)(2,1)S(1)}, bf16[8,96,256]{2,1,0:T(8,128)(2,1)S(1)}, u32[]{:S(2)}, u32[]{:S(2)}) collective-permute-start(bf16[8,96,256]{2,1,0:T(8,128)(2,1)S(1)} %slice.24.refs_0_), channel_id=1, source_target_pairs={{0,2},{2,0},{1,3},{3,1},{4,6},{6,4},{5,7},{7,5},{8,10},{10,8},{9,1... | collective-permute-start | bytes 1179656 | tf_op jit(solution)/shard_map/ppermute | solution.py:408
  66.0 15.5 %copy-start.3 = (f32[96,2048]{1,0:T(8,128)S(1)}, f32[96,2048]{1,0:T(8,128)}, u32[]{:S(2)}) copy-start(f32[96,2048]{1,0:T(8,128)} %attend.3.refs_2_) | copy-start | bytes 2359300
  80.2 11.6 %collective-permute-start.10 = (bf16[8,96,256]{2,1,0:T(8,128)(2,1)}, bf16[8,96,256]{2,1,0:T(8,128)(2,1)S(1)}, u32[]{:S(2)}, u32[]{:S(2)}) collective-permute-start(bf16[8,96,256]{2,1,0:T(8,128)(2,1)} %attend.5), channel_id=1, source_target_pairs={{0,2},{2,0},{1,3},{3,1},{4,6},{6,4},{5,7},{7,5},{8,10},{10,8},{9,1... | collective-permute-start | bytes 1179656 | tf_op jit(solution)/shard_map/ppermute | solution.py:408
  87.1 4.7 %copy-start = (f32[96,2048]{1,0:T(8,128)S(1)}, f32[96,2048]{1,0:T(8,128)}, u32[]{:S(2)}) copy-start(f32[96,2048]{1,0:T(8,128)} %attend.4.acc_ref) | copy-start | bytes 2359300
  89.5 14.0 %collective-permute-start.9 = (bf16[2,104,1408]{2,1,0:T(8,128)(2,1)S(1)}, bf16[2,104,1408]{2,1,0:T(8,128)(2,1)S(1)}, u32[]{:S(2)}, u32[]{:S(2)}) collective-permute-start(bf16[2,104,1408]{2,1,0:T(8,128)(2,1)S(1)} %slice.27), channel_id=1, source_target_pairs={{0,24},{8,0},{16,8},{24,16},{1,25},{9,1},{17,9},{25,17},{2,26},{10... | collective-permute-start | bytes 1757192 | tf_op jit(solution)/shard_map/ppermute | solution.py:413
  91.8 15.2 %collective-permute-start.8 = (bf16[2,104,1408]{2,1,0:T(8,128)(2,1)S(1)}, bf16[2,104,1408]{2,1,0:T(8,128)(2,1)S(1)}, u32[]{:S(2)}, u32[]{:S(2)}) collective-permute-start(bf16[2,104,1408]{2,1,0:T(8,128)(2,1)S(1)} %slice.26), channel_id=1, source_target_pairs={{0,8},{8,16},{16,24},{24,0},{1,9},{9,17},{17,25},{25,1},{2,10},{10... | collective-permute-start | bytes 1757192 | tf_op jit(solution)/shard_map/ppermute | solution.py:413
  92.7 16.6 %all-to-all-start.1 = ((bf16[8,88,256]{2,1,0:T(8,128)(2,1)}), bf16[8,88,256]{2,1,0:T(8,128)(2,1)S(1)}, u32[]{:S(2)}, u32[]{:S(2)}) async-start(bf16[8,88,256]{2,1,0:T(8,128)(2,1)} %combine.1), calls=%async_computation.1 | async-start | bytes 720896 | tf_op jit(solution)/shard_map/all_to_all | solution.py:515
  103.5 9.6 %copy-start.4 = (bf16[2,104,1408]{2,1,0:T(8,128)(2,1)}, bf16[2,104,1408]{2,1,0:T(8,128)(2,1)S(1)}, u32[]{:S(2)}) copy-start(bf16[2,104,1408]{2,1,0:T(8,128)(2,1)S(1)} %collective-permute-done.9.refs_9_) | copy-start | bytes 1757188
  107.0 6.1 %copy-start.5 = (bf16[2,104,1408]{2,1,0:T(8,128)(2,1)}, bf16[2,104,1408]{2,1,0:T(8,128)(2,1)S(1)}, u32[]{:S(2)}) copy-start(bf16[2,104,1408]{2,1,0:T(8,128)(2,1)S(1)} %collective-permute-done.8.refs_8_) | copy-start | bytes 1757188
  113.1 5.3 %collective-permute-start.11 = (bf16[256,1408]{1,0:T(8,128)(2,1)}, bf16[256,1408]{1,0:T(8,128)(2,1)S(1)}, u32[]{:S(2)}, u32[]{:S(2)}) collective-permute-start(bf16[256,1408]{1,0:T(8,128)(2,1)} %get-tuple-element.47.refs_0_), channel_id=1, source_target_pairs={{0,1},{1,0},{2,3},{3,2},{4,5},{5,4},{6,7},{7,6},{8,9},{9,8},{10,11... | collective-permute-start | bytes 2162696 | tf_op jit(solution)/shard_map/ppermute | solution.py:408
  133.6 2.5 %collective-permute-start.14 = (bf16[256,1408]{1,0:T(8,128)(2,1)}, bf16[256,1408]{1,0:T(8,128)(2,1)S(1)}, u32[]{:S(2)}, u32[]{:S(2)}) collective-permute-start(bf16[256,1408]{1,0:T(8,128)(2,1)} %get-tuple-element.52), channel_id=1, source_target_pairs={{0,1},{1,0},{2,3},{3,2},{4,5},{5,4},{6,7},{7,6},{8,9},{9,8},{10,11... | collective-permute-start | bytes 2162696 | tf_op jit(solution)/shard_map/ppermute | solution.py:408
  139.3 26.2 %copy-start.1 = (bf16[32,5760]{1,0:T(8,128)(2,1)S(1)}, bf16[32,5760]{1,0:T(8,128)(2,1)}, u32[]{:S(2)}) copy-start(bf16[32,5760]{1,0:T(8,128)(2,1)} %get-tuple-element.53.refs_0_) | copy-start | bytes 1105924
  139.3 26.2 %copy-start.2 = (bf16[32,5760]{1,0:T(8,128)(2,1)S(1)}, bf16[32,5760]{1,0:T(8,128)(2,1)}, u32[]{:S(2)}) copy-start(bf16[32,5760]{1,0:T(8,128)(2,1)} %get-tuple-element.54.refs_5_) | copy-start | bytes 1105924
  139.3 11.4 %collective-permute-start.16 = (bf16[32,5760]{1,0:T(8,128)(2,1)}, bf16[32,5760]{1,0:T(8,128)(2,1)S(1)}, u32[]{:S(2)}, u32[]{:S(2)}) collective-permute-start(bf16[32,5760]{1,0:T(8,128)(2,1)} %get-tuple-element.53.refs_0_), channel_id=1, source_target_pairs={{0,32},{32,64},{64,96},{96,0},{1,33},{33,65},{65,97},{97,1},{2,34}... | collective-permute-start | bytes 1105928 | tf_op jit(solution)/shard_map/ppermute | solution.py:413
  139.4 11.5 %collective-permute-start.15 = (bf16[32,5760]{1,0:T(8,128)(2,1)}, bf16[32,5760]{1,0:T(8,128)(2,1)S(1)}, u32[]{:S(2)}, u32[]{:S(2)}) collective-permute-start(bf16[32,5760]{1,0:T(8,128)(2,1)} %get-tuple-element.53.refs_0_), channel_id=1, source_target_pairs={{0,96},{32,0},{64,32},{96,64},{1,97},{33,1},{65,33},{97,65},{2,98}... | collective-permute-start | bytes 1105928 | tf_op jit(solution)/shard_map/ppermute | solution.py:413
  142.1 16.5 %collective-permute-start.20 = (bf16[32,5760]{1,0:T(8,128)(2,1)}, bf16[32,5760]{1,0:T(8,128)(2,1)S(1)}, u32[]{:S(2)}, u32[]{:S(2)}) collective-permute-start(bf16[32,5760]{1,0:T(8,128)(2,1)} %get-tuple-element.54.refs_5_), channel_id=1, source_target_pairs={{0,32},{32,64},{64,96},{96,0},{1,33},{33,65},{65,97},{97,1},{2,34}... | collective-permute-start | bytes 1105928 | tf_op jit(solution)/shard_map/ppermute | solution.py:413
  142.1 16.6 %collective-permute-start.19 = (bf16[32,5760]{1,0:T(8,128)(2,1)}, bf16[32,5760]{1,0:T(8,128)(2,1)S(1)}, u32[]{:S(2)}, u32[]{:S(2)}) collective-permute-start(bf16[32,5760]{1,0:T(8,128)(2,1)} %get-tuple-element.54.refs_5_), channel_id=1, source_target_pairs={{0,96},{32,0},{64,32},{96,64},{1,97},{33,1},{65,33},{97,65},{2,98}... | collective-permute-start | bytes 1105928 | tf_op jit(solution)/shard_map/ppermute | solution.py:413
  150.7 11.8 %collective-permute-start.17 = (bf16[16,5760]{1,0:T(8,128)(2,1)S(1)}, bf16[16,5760]{1,0:T(8,128)(2,1)S(1)}, u32[]{:S(2)}, u32[]{:S(2)}) collective-permute-start(bf16[16,5760]{1,0:T(8,128)(2,1)S(1)} %slice.32), channel_id=1, source_target_pairs={{0,32},{32,64},{64,96},{96,0},{1,33},{33,65},{65,97},{97,1},{2,34}... | collective-permute-start | bytes 552968 | tf_op jit(solution)/shard_map/ppermute | solution.py:413
  150.8 11.7 %collective-permute-start.18 = (bf16[16,5760]{1,0:T(8,128)(2,1)S(1)}, bf16[16,5760]{1,0:T(8,128)(2,1)S(1)}, u32[]{:S(2)}, u32[]{:S(2)}) collective-permute-start(bf16[16,5760]{1,0:T(8,128)(2,1)S(1)} %slice.33), channel_id=1, source_target_pairs={{0,96},{32,0},{64,32},{96,64},{1,97},{33,1},{65,33},{97,65},{2,98}... | collective-permute-start | bytes 552968 | tf_op jit(solution)/shard_map/ppermute | solution.py:413
  158.6 6.9 %collective-permute-start.21 = (bf16[16,5760]{1,0:T(8,128)(2,1)S(1)}, bf16[16,5760]{1,0:T(8,128)(2,1)S(1)}, u32[]{:S(2)}, u32[]{:S(2)}) collective-permute-start(bf16[16,5760]{1,0:T(8,128)(2,1)S(1)} %slice.34), channel_id=1, source_target_pairs={{0,32},{32,64},{64,96},{96,0},{1,33},{33,65},{65,97},{97,1},{2,34}... | collective-permute-start | bytes 552968 | tf_op jit(solution)/shard_map/ppermute | solution.py:413
  158.7 6.8 %collective-permute-start.22 = (bf16[16,5760]{1,0:T(8,128)(2,1)S(1)}, bf16[16,5760]{1,0:T(8,128)(2,1)S(1)}, u32[]{:S(2)}, u32[]{:S(2)}) collective-permute-start(bf16[16,5760]{1,0:T(8,128)(2,1)S(1)} %slice.35), channel_id=1, source_target_pairs={{0,96},{32,0},{64,32},{96,64},{1,97},{33,1},{65,33},{97,65},{2,98}... | collective-permute-start | bytes 552968 | tf_op jit(solution)/shard_map/ppermute | solution.py:413

commit v9 on v7

--- a/solution.py
+++ b/solution.py
@@ -508,7 +508,7 @@
     away = flip(queries, "xl")
     acc = attend(queries, [kv])
     away, acc = lax.optimization_barrier((away, acc))
-    sent = flip(attend(away, [kv, kv_c], send=True), "xl")
+    sent = flip(attend(away, [kv, kv_c], send=True, key_block=1024), "xl")
     acc = attend(queries, [kv_c], acc)
     below, above, acc = lax.optimization_barrier((below, above, acc))
     far_a, far_b = turn(below[:2], "y", 1), turn(above[2:], "y", -1)

time: 192 us -> 192 us (level)
    ppermute x18, waiting for transfers between devices: 33.1 us -> 35.6 us  [turn(): lax.ppermute(value, axis, [(i, (i + by) % size) for i in range(size)])]
  transfers between devices with their start and end apart: 25 -> 25, of which waited for: 15 -> 16; matrix products, arithmetic and copies ran while one was open for 2% -> 2% of each run, Pallas kernels for 20% -> 19%
where the time goes in v9:
time: 192 us
  Pallas kernels  63.2 us (33%)
  waiting for transfers between devices  62.1 us (32%)
  starting transfers between devices  41.2 us (21%)
  blocking collectives  20.1 us (10%)
  local copies, waits for them, and re-layouts  3.59 us (2%)
    ppermute x18, waiting for transfers between devices, turn(): lax.ppermute(value, axis, [(i, (i + by) % size) for i in range(size)])  35.6 us
    ppermute x18, starting transfers between devices, turn(): lax.ppermute(value, axis, [(i, (i + by) % size) for i in range(size)])  25.1 us
    pallas_call x3, Pallas kernels, attend(): pl.pallas_call(lambda *refs: attend_kernel(*refs, sets=len(sets), first=f...  20.3 us
    all_to_all x1, blocking collectives, local(): lax.all_to_all(outgoing, ('y', 'xh', 'xl', 'c'), 0, 0, tiled=True)  20.1 us
    all_to_all x1, waiting for transfers between devices, local(): mine = lax.all_to_all(heads, ('y', 'xh'), 0, 0, tiled=True)  16.1 us
    pallas_call x1, Pallas kernels, mlp(): pl.pallas_call(lambda *refs: mlp_kernel(*refs, near_count=len(near), far_...  15.2 us
    ppermute x5, waiting for transfers between devices, flip(): return lax.ppermute(value, axis, [(0, 1), (1, 0)])  9.09 us
    ppermute x5, starting transfers between devices, flip(): return lax.ppermute(value, axis, [(0, 1), (1, 0)])  8.21 us
  transfers between devices with their start and end apart: 25, of which 16 were waited for; matrix products, arithmetic and copies ran while one was open for 2% of the time, Pallas kernels for 19%

profile of v9, /device:TPU:1, one launch (start us, length us, event | category | flops | bytes accessed | tf_op | source)
XLA Modules:
  0.0 191.6 jit_solution(12088114121807235500)
XLA Ops:
  0.0 2.4 %pack.2 = bf16[104,1408]{1,0:T(8,128)(2,1)} custom-call(bf16[1536,1408]{1,0:T(8,128)(2,1)} %refs_0_.3, bf16[1536]{0:T(1024)(128)(2,1)} %refs_1_.4, bf16[1536,1408]{1,0:T(8,128)(2,1)} %refs_2_.4), custom_call_target="tpu_custom_call" | custom-call | bytes 540672 | tf_op jit(solution)/shard_map/pack/pallas_call | solution.py:464
  2.4 4.5 %collective-permute-start = (bf16[104,1408]{1,0:T(8,128)(2,1)}, bf16[104,1408]{1,0:T(8,128)(2,1)S(1)}, u32[]{:S(2)}, u32[]{:S(2)}) collective-permute-start(bf16[104,1408]{1,0:T(8,128)(2,1)} %pack.2), channel_id=1, source_target_pairs={{0,64},{32,96},{64,0},{96,32},{1,65},{33,97},{65,1},{97,33},{2,66}... | collective-permute-start | bytes 878600 | tf_op jit(solution)/shard_map/ppermute | solution.py:415
  6.9 4.4 %pack.3.refs_2_ = bf16[1552,1408]{1,0:T(8,128)(2,1)} custom-call(bf16[1536,1408]{1,0:T(8,128)(2,1)} %refs_0_.3, bf16[1536]{0:T(1024)(128)(2,1)} %refs_1_.4, bf16[1536,1408]{1,0:T(8,128)(2,1)} %refs_2_.4), custom_call_target="tpu_custom_call" | custom-call | bytes 8650752 | tf_op jit(solution)/shard_map/pack/pallas_call | solution.py:464
  11.3 2.5 %collective-permute-done = bf16[104,1408]{1,0:T(8,128)(2,1)S(1)} collective-permute-done((bf16[104,1408]{1,0:T(8,128)(2,1)}, bf16[104,1408]{1,0:T(8,128)(2,1)S(1)}, u32[]{:S(2)}, u32[]{:S(2)}) %collective-permute-start) | collective-permute-done | bytes 292896 | tf_op jit(solution)/shard_map/ppermute | solution.py:415
  13.8 2.5 %collective-permute-start.3 = (bf16[104,1408]{1,0:T(8,128)(2,1)S(1)}, bf16[104,1408]{1,0:T(8,128)(2,1)S(1)}, u32[]{:S(2)}, u32[]{:S(2)}) collective-permute-start(bf16[104,1408]{1,0:T(8,128)(2,1)S(1)} %collective-permute-done), channel_id=1, source_target_pairs={{0,6},{2,0},{4,2},{6,4},{1,7},{3,1},{5,3},{7,5},{8,14},{10,8},{12,... | collective-permute-start | bytes 878600 | tf_op jit(solution)/shard_map/ppermute | solution.py:415
  16.3 0.5 collective-permute-start.2
  16.8 0.6 collective-permute-start.1
  17.4 2.8 %collective-permute-start.13 = (bf16[1552,1408]{1,0:T(8,128)(2,1)}, bf16[1552,1408]{1,0:T(8,128)(2,1)}, u32[]{:S(2)}, u32[]{:S(2)}) collective-permute-start(bf16[1552,1408]{1,0:T(8,128)(2,1)} %pack.3.refs_2_), channel_id=1, source_target_pairs={{0,96},{32,0},{64,32},{96,64},{1,97},{33,1},{65,33},{97,65},{2,98}... | collective-permute-start | bytes 13111304 | tf_op jit(solution)/shard_map/ppermute | solution.py:415
  20.2 7.9 %qkv.1 = bf16[8,272,256]{2,1,0:T(8,128)(2,1)} custom-call(bf16[256,1408]{1,0:T(8,128)(2,1)} %x_ref.3, s32[1,256]{1,0:T(1,128)} %bitcast.19, bf16[2112,1408]{1,0:T(8,128)(2,1)} %bitcast.12), custom_call_target="tpu_custom_call" | custom-call | flops 1522532352 | bytes 8388608 | tf_op jit(solution)/shard_map/qkv/pallas_call | solution.py:89
  28.1 0.0 collective-permute-done.3
  28.1 0.0 collective-permute-done.2
  28.2 4.9 %collective-permute-done.1 = bf16[104,1408]{1,0:T(8,128)(2,1)S(1)} collective-permute-done((bf16[104,1408]{1,0:T(8,128)(2,1)S(1)}, bf16[104,1408]{1,0:T(8,128)(2,1)S(1)}, u32[]{:S(2)}, u32[]{:S(2)}) %collective-permute-start.1) | collective-permute-done | bytes 292896 | tf_op jit(solution)/shard_map/ppermute | solution.py:415
  33.0 4.4 %all-to-all-start = ((bf16[8,272,256]{2,1,0:T(8,128)(2,1)}), bf16[8,272,256]{2,1,0:T(8,128)(2,1)S(1)}, u32[]{:S(2)}, u32[]{:S(2)}) async-start(bf16[8,272,256]{2,1,0:T(8,128)(2,1)} %qkv.1), calls=%async_computation | async-start | bytes 2228224 | tf_op jit(solution)/shard_map/all_to_all | solution.py:502
  37.5 1.2 pad_maximum_fusion.refs_5_
  38.7 16.1 %all-to-all-done = bf16[8,272,256]{2,1,0:T(8,128)(2,1)S(1)} async-done(((bf16[8,272,256]{2,1,0:T(8,128)(2,1)}), bf16[8,272,256]{2,1,0:T(8,128)(2,1)S(1)}, u32[]{:S(2)}, u32[]{:S(2)}) %all-to-all-start) | async-done | bytes 1114144 | tf_op jit(solution)/shard_map/all_to_all | solution.py:502
  54.8 1.7 collective-permute-start.6
  56.5 0.5 collective-permute-start.5
  57.0 0.9 collective-permute-start.4
  58.0 0.4 collective-permute-done.6.refs_1_.refs_2_
  58.4 0.0 collective-permute-start.7
  58.4 5.6 %attend.3.refs_2_ = f32[96,2048]{1,0:T(8,128)} custom-call(bf16[8,96,256]{2,1,0:T(8,128)(2,1)S(1)} %slice.24.refs_0_, bf16[8,184,256]{2,1,0:T(8,128)(2,1)S(1)} %slice.25.refs_1_), custom_call_target="tpu_custom_call" | custom-call | flops 2147483648 | bytes 3145728 | tf_op jit(solution)/shard_map/attend/pallas_call | solution.py:173
  63.9 4.7 %collective-permute-done.7.refs_0_ = bf16[8,96,256]{2,1,0:T(8,128)(2,1)S(1)} collective-permute-done((bf16[8,96,256]{2,1,0:T(8,128)(2,1)S(1)}, bf16[8,96,256]{2,1,0:T(8,128)(2,1)S(1)}, u32[]{:S(2)}, u32[]{:S(2)}) %collective-permute-start.7) | collective-permute-done | bytes 393248 | tf_op jit(solution)/shard_map/ppermute | solution.py:410
  68.6 9.2 %attend.5 = bf16[8,96,256]{2,1,0:T(8,128)(2,1)} custom-call(bf16[8,96,256]{2,1,0:T(8,128)(2,1)S(1)} %collective-permute-done.7.refs_0_, bf16[8,184,256]{2,1,0:T(8,128)(2,1)S(1)} %slice.25.refs_1_, bf16[8,184,256]{2,1,0:T(8,128)(2,1)S(1)} %collective-permute-done.6.refs_1_.refs_2_), custom_call_target="tpu_custom_call" | custom-call | flops 4294967296 | bytes 3145728 | tf_op jit(solution)/shard_map/attend/pallas_call | solution.py:173
  77.8 0.3 collective-permute-start.10
  78.1 5.5 %attend.4.acc_ref = f32[96,2048]{1,0:T(8,128)} custom-call(bf16[8,96,256]{2,1,0:T(8,128)(2,1)S(1)} %slice.24.refs_0_, bf16[8,184,256]{2,1,0:T(8,128)(2,1)S(1)} %collective-permute-done.6.refs_1_.refs_2_, f32[96,2048]{1,0:T(8,128)S(1)} %copy-done.3), custom_call_target="tpu_custom_call" | custom-call | flops 2147483648 | bytes 3145728 | tf_op jit(solution)/shard_map/attend/pallas_call | solution.py:173
  83.6 0.5 collective-permute-done.5.refs_7_
  84.2 1.4 collective-permute-done.4.refs_6_
  85.6 1.1 slice.26
  86.7 1.1 slice.27
  87.8 0.4 collective-permute-start.9
  88.2 1.1 collective-permute-start.8
  89.4 0.0 collective-permute-done.10.sent_ref
  89.4 0.9 combine.1
  90.2 3.4 %all-to-all-start.1 = ((bf16[8,88,256]{2,1,0:T(8,128)(2,1)}), bf16[8,88,256]{2,1,0:T(8,128)(2,1)S(1)}, u32[]{:S(2)}, u32[]{:S(2)}) async-start(bf16[8,88,256]{2,1,0:T(8,128)(2,1)} %combine.1), calls=%async_computation.1 | async-start | bytes 720896 | tf_op jit(solution)/shard_map/all_to_all | solution.py:517
  93.7 9.8 %collective-permute-done.9.refs_9_ = bf16[2,104,1408]{2,1,0:T(8,128)(2,1)S(1)} collective-permute-done((bf16[2,104,1408]{2,1,0:T(8,128)(2,1)S(1)}, bf16[2,104,1408]{2,1,0:T(8,128)(2,1)S(1)}, u32[]{:S(2)}, u32[]{:S(2)}) %collective-permute-start.9) | collective-permute-done | bytes 585760 | tf_op jit(solution)/shard_map/ppermute | solution.py:415
  103.5 1.7 collective-permute-done.8.refs_8_
  105.2 1.3 all-to-all-done.1.att_ref
  106.5 3.8 %project.1 = (bf16[256,1408]{1,0:T(8,128)(2,1)}, bf16[256,1408]{1,0:T(8,128)(2,1)}) custom-call(bf16[8,88,256]{2,1,0:T(8,128)(2,1)S(1)} %all-to-all-done.1.att_ref, bf16[256,1408]{1,0:T(8,128)(2,1)} %x_ref.3, bf16[704,1408]{1,0:T(8,128)(2,1)} %w_ref.1), custom_call_target="tpu_custom_call" | custom-call | flops 507510784 | bytes 4194304 | tf_op jit(solution)/shard_map/project/pallas_call | solution.py:223
  110.3 2.6 %collective-permute-start.11 = (bf16[256,1408]{1,0:T(8,128)(2,1)}, bf16[256,1408]{1,0:T(8,128)(2,1)S(1)}, u32[]{:S(2)}, u32[]{:S(2)}) collective-permute-start(bf16[256,1408]{1,0:T(8,128)(2,1)} %get-tuple-element.51.refs_0_), channel_id=1, source_target_pairs={{0,1},{1,0},{2,3},{3,2},{4,5},{5,4},{6,7},{7,6},{8,9},{9,8},{10,11... | collective-permute-start | bytes 2162696 | tf_op jit(solution)/shard_map/ppermute | solution.py:410
  112.9 2.0 %collective-permute-done.11.refs_1_ = bf16[256,1408]{1,0:T(8,128)(2,1)S(1)} collective-permute-done((bf16[256,1408]{1,0:T(8,128)(2,1)}, bf16[256,1408]{1,0:T(8,128)(2,1)S(1)}, u32[]{:S(2)}, u32[]{:S(2)}) %collective-permute-start.11) | collective-permute-done | bytes 720928 | tf_op jit(solution)/shard_map/ppermute | solution.py:410
  114.9 0.0 collective-permute-done.13.refs_4_
  114.9 0.0 collective-permute-done.12.refs_3_
  114.9 15.2 %mlp.1 = (bf16[256,1408]{1,0:T(8,128)(2,1)}, bf16[256,1408]{1,0:T(8,128)(2,1)}) custom-call(bf16[256,1408]{1,0:T(8,128)(2,1)} %get-tuple-element.51.refs_0_, bf16[256,1408]{1,0:T(8,128)(2,1)S(1)} %collective-permute-done.11.refs_1_, bf16[1552,1408]{1,0:T(8,128)(2,1)} %pack.3.refs_2_, bf16[1552,1408]{1,0:T(8,128)(2,1)} %collective-permute-done.12.refs_3_, ...), custom_call_target="tpu_custom_call" | custom-call | flops 8858370048 | bytes 20971520 | tf_op jit(solution)/shard_map/mlp/pallas_call | solution.py:290
  130.1 3.6 %collective-permute-start.14 = (bf16[256,1408]{1,0:T(8,128)(2,1)}, bf16[256,1408]{1,0:T(8,128)(2,1)S(1)}, u32[]{:S(2)}, u32[]{:S(2)}) collective-permute-start(bf16[256,1408]{1,0:T(8,128)(2,1)} %get-tuple-element.56), channel_id=1, source_target_pairs={{0,1},{1,0},{2,3},{3,2},{4,5},{5,4},{6,7},{7,6},{8,9},{9,8},{10,11... | collective-permute-start | bytes 2162696 | tf_op jit(solution)/shard_map/ppermute | solution.py:410
  133.7 2.0 %collective-permute-done.14.refs_6_ = bf16[256,1408]{1,0:T(8,128)(2,1)S(1)} collective-permute-done((bf16[256,1408]{1,0:T(8,128)(2,1)}, bf16[256,1408]{1,0:T(8,128)(2,1)S(1)}, u32[]{:S(2)}, u32[]{:S(2)}) %collective-permute-start.14) | collective-permute-done | bytes 720928 | tf_op jit(solution)/shard_map/ppermute | solution.py:410
  135.8 3.3 %merge.1 = (bf16[32,5760]{1,0:T(8,128)(2,1)}, bf16[32,5760]{1,0:T(8,128)(2,1)}) custom-call(bf16[256,1408]{1,0:T(8,128)(2,1)} %get-tuple-element.50.refs_0_, f32[1408]{0:T(1024)} %refs_1_.5, f32[1408]{0:T(1024)} %refs_2_.5, s32[1,256]{1,0:T(1,128)} %bitcast.20, s32[1,64]{1,0:T(1,128)} %bitcast.21, bf16[256,1408]{1,0:T(8,128)(2,1)} %get-tuple-element.55.refs_5_, ...), custom_call_target="tpu_custom_call" | custom-call | flops 184549376 | bytes 4194304 | tf_op jit(solution)/shard_map/merge/pallas_call | solution.py:345
  139.1 0.0 collective-permute-start.16
  139.1 2.7 %collective-permute-start.15 = (bf16[32,5760]{1,0:T(8,128)(2,1)}, bf16[32,5760]{1,0:T(8,128)(2,1)S(1)}, u32[]{:S(2)}, u32[]{:S(2)}) collective-permute-start(bf16[32,5760]{1,0:T(8,128)(2,1)} %get-tuple-element.57.refs_0_), channel_id=1, source_target_pairs={{0,96},{32,0},{64,32},{96,64},{1,97},{33,1},{65,33},{97,65},{2,98}... | collective-permute-start | bytes 1105928 | tf_op jit(solution)/shard_map/ppermute | solution.py:415
  141.7 0.0 collective-permute-start.20
  141.7 2.7 %collective-permute-start.19 = (bf16[32,5760]{1,0:T(8,128)(2,1)}, bf16[32,5760]{1,0:T(8,128)(2,1)S(1)}, u32[]{:S(2)}, u32[]{:S(2)}) collective-permute-start(bf16[32,5760]{1,0:T(8,128)(2,1)} %get-tuple-element.58.refs_5_), channel_id=1, source_target_pairs={{0,96},{32,0},{64,32},{96,64},{1,97},{33,1},{65,33},{97,65},{2,98}... | collective-permute-start | bytes 1105928 | tf_op jit(solution)/shard_map/ppermute | solution.py:415
  144.4 5.9 %collective-permute-done.16.refs_4_ = bf16[32,5760]{1,0:T(8,128)(2,1)S(1)} collective-permute-done((bf16[32,5760]{1,0:T(8,128)(2,1)}, bf16[32,5760]{1,0:T(8,128)(2,1)S(1)}, u32[]{:S(2)}, u32[]{:S(2)}) %collective-permute-start.16) | collective-permute-done | bytes 368672 | tf_op jit(solution)/shard_map/ppermute | solution.py:415
  150.3 0.1 collective-permute-start.17
  150.4 0.0 collective-permute-done.15.refs_1_
  150.4 3.0 %collective-permute-start.18 = (bf16[16,5760]{1,0:T(8,128)(2,1)S(1)}, bf16[16,5760]{1,0:T(8,128)(2,1)S(1)}, u32[]{:S(2)}, u32[]{:S(2)}) collective-permute-start(bf16[16,5760]{1,0:T(8,128)(2,1)S(1)} %slice.33), channel_id=1, source_target_pairs={{0,96},{32,0},{64,32},{96,64},{1,97},{33,1},{65,33},{97,65},{2,98}... | collective-permute-start | bytes 552968 | tf_op jit(solution)/shard_map/ppermute | solution.py:415
  153.4 4.8 %collective-permute-done.20.refs_9_ = bf16[32,5760]{1,0:T(8,128)(2,1)S(1)} collective-permute-done((bf16[32,5760]{1,0:T(8,128)(2,1)}, bf16[32,5760]{1,0:T(8,128)(2,1)S(1)}, u32[]{:S(2)}, u32[]{:S(2)}) %collective-permute-start.20) | collective-permute-done | bytes 368672 | tf_op jit(solution)/shard_map/ppermute | solution.py:415
  158.2 0.1 collective-permute-start.21
  158.3 2.7 %collective-permute-start.22 = (bf16[16,5760]{1,0:T(8,128)(2,1)S(1)}, bf16[16,5760]{1,0:T(8,128)(2,1)S(1)}, u32[]{:S(2)}, u32[]{:S(2)}) collective-permute-start(bf16[16,5760]{1,0:T(8,128)(2,1)S(1)} %slice.35), channel_id=1, source_target_pairs={{0,96},{32,0},{64,32},{96,64},{1,97},{33,1},{65,33},{97,65},{2,98}... | collective-permute-start | bytes 552968 | tf_op jit(solution)/shard_map/ppermute | solution.py:415
  161.0 1.1 collective-permute-done.17.refs_2_
  162.1 3.0 %collective-permute-done.21.refs_7_ = bf16[16,5760]{1,0:T(8,128)(2,1)S(1)} collective-permute-done((bf16[16,5760]{1,0:T(8,128)(2,1)S(1)}, bf16[16,5760]{1,0:T(8,128)(2,1)S(1)}, u32[]{:S(2)}, u32[]{:S(2)}) %collective-permute-start.21) | collective-permute-done | bytes 184352 | tf_op jit(solution)/shard_map/ppermute | solution.py:415
  165.1 5.1 %embed.1 = bf16[512,512]{1,0:T(8,128)(2,1)} custom-call(bf16[32,5760]{1,0:T(8,128)(2,1)S(1)} %copy-done.1, bf16[32,5760]{1,0:T(8,128)(2,1)S(1)} %collective-permute-done.15.refs_1_, bf16[16,5760]{1,0:T(8,128)(2,1)S(1)} %collective-permute-done.17.refs_2_, bf16[16,5760]{1,0:T(8,128)(2,1)S(1)} %collective-permute-done.18.refs_3_, ...), custom_call_target="tpu_custom_call" | custom-call | flops 1476395008 | bytes 10485760 | tf_op jit(solution)/shard_map/embed/pallas_call | solution.py:392
  170.2 20.1 %all_to_all.19 = bf16[32,16,512]{2,1,0:T(8,128)(2,1)S(1)} all-to-all(bf16[32,16,512]{2,1,0:T(8,128)(2,1)} %bitcast.13), channel_id=1, replica_groups=mesh['grp'=4,'y'=4,'xh'=2,'xl'=2,'c'=2] {'y','xh','xl','c'}, dimensions={0} | all-to-all | bytes 1048576 | tf_op jit(solution)/shard_map/all_to_all | solution.py:543
  190.4 0.1 reshape.21
  190.5 0.2 copy.16
  190.7 0.9 reshape.22
  (22 shorter events, 0.2 us)
Async XLA Ops:
  2.4 11.4 %collective-permute-start = (bf16[104,1408]{1,0:T(8,128)(2,1)}, bf16[104,1408]{1,0:T(8,128)(2,1)S(1)}, u32[]{:S(2)}, u32[]{:S(2)}) collective-permute-start(bf16[104,1408]{1,0:T(8,128)(2,1)} %pack.2), channel_id=1, source_target_pairs={{0,64},{32,96},{64,0},{96,32},{1,65},{33,97},{65,1},{97,33},{2,66}... | collective-permute-start | bytes 878600 | tf_op jit(solution)/shard_map/ppermute | solution.py:415
  13.8 14.3 %collective-permute-start.3 = (bf16[104,1408]{1,0:T(8,128)(2,1)S(1)}, bf16[104,1408]{1,0:T(8,128)(2,1)S(1)}, u32[]{:S(2)}, u32[]{:S(2)}) collective-permute-start(bf16[104,1408]{1,0:T(8,128)(2,1)S(1)} %collective-permute-done), channel_id=1, source_target_pairs={{0,6},{2,0},{4,2},{6,4},{1,7},{3,1},{5,3},{7,5},{8,14},{10,8},{12,... | collective-permute-start | bytes 878600 | tf_op jit(solution)/shard_map/ppermute | solution.py:415
  16.3 11.9 %collective-permute-start.2 = (bf16[104,1408]{1,0:T(8,128)(2,1)S(1)}, bf16[104,1408]{1,0:T(8,128)(2,1)S(1)}, u32[]{:S(2)}, u32[]{:S(2)}) collective-permute-start(bf16[104,1408]{1,0:T(8,128)(2,1)S(1)} %collective-permute-done), channel_id=1, source_target_pairs={{0,4},{2,6},{4,0},{6,2},{1,5},{3,7},{5,1},{7,3},{8,12},{10,14},{12... | collective-permute-start | bytes 878600 | tf_op jit(solution)/shard_map/ppermute | solution.py:415
  16.8 16.3 %collective-permute-start.1 = (bf16[104,1408]{1,0:T(8,128)(2,1)S(1)}, bf16[104,1408]{1,0:T(8,128)(2,1)S(1)}, u32[]{:S(2)}, u32[]{:S(2)}) collective-permute-start(bf16[104,1408]{1,0:T(8,128)(2,1)S(1)} %collective-permute-done), channel_id=1, source_target_pairs={{0,2},{2,4},{4,6},{6,0},{1,3},{3,5},{5,7},{7,1},{8,10},{10,12},{12... | collective-permute-start | bytes 878600 | tf_op jit(solution)/shard_map/ppermute | solution.py:415
  17.4 97.5 %collective-permute-start.13 = (bf16[1552,1408]{1,0:T(8,128)(2,1)}, bf16[1552,1408]{1,0:T(8,128)(2,1)}, u32[]{:S(2)}, u32[]{:S(2)}) collective-permute-start(bf16[1552,1408]{1,0:T(8,128)(2,1)} %pack.3.refs_2_), channel_id=1, source_target_pairs={{0,96},{32,0},{64,32},{96,64},{1,97},{33,1},{65,33},{97,65},{2,98}... | collective-permute-start | bytes 13111304 | tf_op jit(solution)/shard_map/ppermute | solution.py:415
  20.2 94.7 %collective-permute-start.12 = (bf16[1552,1408]{1,0:T(8,128)(2,1)}, bf16[1552,1408]{1,0:T(8,128)(2,1)}, u32[]{:S(2)}, u32[]{:S(2)}) collective-permute-start(bf16[1552,1408]{1,0:T(8,128)(2,1)} %pack.3.refs_2_), channel_id=1, source_target_pairs={{0,32},{32,64},{64,96},{96,0},{1,33},{33,65},{65,97},{97,1},{2,34}... | collective-permute-start | bytes 13111304 | tf_op jit(solution)/shard_map/ppermute | solution.py:415
  33.0 21.7 %all-to-all-start = ((bf16[8,272,256]{2,1,0:T(8,128)(2,1)}), bf16[8,272,256]{2,1,0:T(8,128)(2,1)S(1)}, u32[]{:S(2)}, u32[]{:S(2)}) async-start(bf16[8,272,256]{2,1,0:T(8,128)(2,1)} %qkv.1), calls=%async_computation | async-start | bytes 2228224 | tf_op jit(solution)/shard_map/all_to_all | solution.py:502
  54.8 3.5 %collective-permute-start.6 = (bf16[8,184,256]{2,1,0:T(8,128)(2,1)S(1)}, bf16[8,184,256]{2,1,0:T(8,128)(2,1)S(1)}, u32[]{:S(2)}, u32[]{:S(2)}) collective-permute-start(bf16[8,184,256]{2,1,0:T(8,128)(2,1)S(1)} %slice.25.refs_1_), channel_id=1, source_target_pairs={{0,1},{1,0},{2,3},{3,2},{4,5},{5,4},{6,7},{7,6},{8,9},{9,8},{10,11... | collective-permute-start | bytes 2261000 | tf_op jit(solution)/shard_map/ppermute | solution.py:410
  56.5 27.7 %collective-permute-start.5 = (bf16[4,104,1408]{2,1,0:T(8,128)(2,1)}, bf16[4,104,1408]{2,1,0:T(8,128)(2,1)}, u32[]{:S(2)}, u32[]{:S(2)}) collective-permute-start(bf16[4,104,1408]{2,1,0:T(8,128)(2,1)} %pad_maximum_fusion.refs_5_), channel_id=1, source_target_pairs={{0,24},{8,0},{16,8},{24,16},{1,25},{9,1},{17,9},{25,17},{2,26},{10... | collective-permute-start | bytes 3514376 | tf_op jit(solution)/shard_map/ppermute | solution.py:415
  57.0 28.6 %collective-permute-start.4 = (bf16[4,104,1408]{2,1,0:T(8,128)(2,1)}, bf16[4,104,1408]{2,1,0:T(8,128)(2,1)}, u32[]{:S(2)}, u32[]{:S(2)}) collective-permute-start(bf16[4,104,1408]{2,1,0:T(8,128)(2,1)} %pad_maximum_fusion.refs_5_), channel_id=1, source_target_pairs={{0,8},{8,16},{16,24},{24,0},{1,9},{9,17},{17,25},{25,1},{2,10},{10... | collective-permute-start | bytes 3514376 | tf_op jit(solution)/shard_map/ppermute | solution.py:415
  58.4 10.2 %collective-permute-start.7 = (bf16[8,96,256]{2,1,0:T(8,128)(2,1)S(1)}, bf16[8,96,256]{2,1,0:T(8,128)(2,1)S(1)}, u32[]{:S(2)}, u32[]{:S(2)}) collective-permute-start(bf16[8,96,256]{2,1,0:T(8,128)(2,1)S(1)} %slice.24.refs_0_), channel_id=1, source_target_pairs={{0,2},{2,0},{1,3},{3,1},{4,6},{6,4},{5,7},{7,5},{8,10},{10,8},{9,1... | collective-permute-start | bytes 1179656 | tf_op jit(solution)/shard_map/ppermute | solution.py:410
  63.9 14.2 %copy-start.3 = (f32[96,2048]{1,0:T(8,128)S(1)}, f32[96,2048]{1,0:T(8,128)}, u32[]{:S(2)}) copy-start(f32[96,2048]{1,0:T(8,128)} %attend.3.refs_2_) | copy-start | bytes 2359300
  77.8 11.6 %collective-permute-start.10 = (bf16[8,96,256]{2,1,0:T(8,128)(2,1)}, bf16[8,96,256]{2,1,0:T(8,128)(2,1)S(1)}, u32[]{:S(2)}, u32[]{:S(2)}) collective-permute-start(bf16[8,96,256]{2,1,0:T(8,128)(2,1)} %attend.5), channel_id=1, source_target_pairs={{0,2},{2,0},{1,3},{3,1},{4,6},{6,4},{5,7},{7,5},{8,10},{10,8},{9,1... | collective-permute-start | bytes 1179656 | tf_op jit(solution)/shard_map/ppermute | solution.py:410
  83.6 5.7 %copy-start = (f32[96,2048]{1,0:T(8,128)S(1)}, f32[96,2048]{1,0:T(8,128)}, u32[]{:S(2)}) copy-start(f32[96,2048]{1,0:T(8,128)} %attend.4.acc_ref) | copy-start | bytes 2359300
  87.8 15.7 %collective-permute-start.9 = (bf16[2,104,1408]{2,1,0:T(8,128)(2,1)S(1)}, bf16[2,104,1408]{2,1,0:T(8,128)(2,1)S(1)}, u32[]{:S(2)}, u32[]{:S(2)}) collective-permute-start(bf16[2,104,1408]{2,1,0:T(8,128)(2,1)S(1)} %slice.27), channel_id=1, source_target_pairs={{0,24},{8,0},{16,8},{24,16},{1,25},{9,1},{17,9},{25,17},{2,26},{10... | collective-permute-start | bytes 1757192 | tf_op jit(solution)/shard_map/ppermute | solution.py:415
  88.2 16.9 %collective-permute-start.8 = (bf16[2,104,1408]{2,1,0:T(8,128)(2,1)S(1)}, bf16[2,104,1408]{2,1,0:T(8,128)(2,1)S(1)}, u32[]{:S(2)}, u32[]{:S(2)}) collective-permute-start(bf16[2,104,1408]{2,1,0:T(8,128)(2,1)S(1)} %slice.26), channel_id=1, source_target_pairs={{0,8},{8,16},{16,24},{24,0},{1,9},{9,17},{17,25},{25,1},{2,10},{10... | collective-permute-start | bytes 1757192 | tf_op jit(solution)/shard_map/ppermute | solution.py:415
  90.2 16.3 %all-to-all-start.1 = ((bf16[8,88,256]{2,1,0:T(8,128)(2,1)}), bf16[8,88,256]{2,1,0:T(8,128)(2,1)S(1)}, u32[]{:S(2)}, u32[]{:S(2)}) async-start(bf16[8,88,256]{2,1,0:T(8,128)(2,1)} %combine.1), calls=%async_computation.1 | async-start | bytes 720896 | tf_op jit(solution)/shard_map/all_to_all | solution.py:517
  103.5 6.8 %copy-start.4 = (bf16[2,104,1408]{2,1,0:T(8,128)(2,1)}, bf16[2,104,1408]{2,1,0:T(8,128)(2,1)S(1)}, u32[]{:S(2)}) copy-start(bf16[2,104,1408]{2,1,0:T(8,128)(2,1)S(1)} %collective-permute-done.9.refs_9_) | copy-start | bytes 1757188
  105.2 5.1 %copy-start.5 = (bf16[2,104,1408]{2,1,0:T(8,128)(2,1)}, bf16[2,104,1408]{2,1,0:T(8,128)(2,1)S(1)}, u32[]{:S(2)}) copy-start(bf16[2,104,1408]{2,1,0:T(8,128)(2,1)S(1)} %collective-permute-done.8.refs_8_) | copy-start | bytes 1757188
  110.3 4.6 %collective-permute-start.11 = (bf16[256,1408]{1,0:T(8,128)(2,1)}, bf16[256,1408]{1,0:T(8,128)(2,1)S(1)}, u32[]{:S(2)}, u32[]{:S(2)}) collective-permute-start(bf16[256,1408]{1,0:T(8,128)(2,1)} %get-tuple-element.51.refs_0_), channel_id=1, source_target_pairs={{0,1},{1,0},{2,3},{3,2},{4,5},{5,4},{6,7},{7,6},{8,9},{9,8},{10,11... | collective-permute-start | bytes 2162696 | tf_op jit(solution)/shard_map/ppermute | solution.py:410
  130.1 5.7 %collective-permute-start.14 = (bf16[256,1408]{1,0:T(8,128)(2,1)}, bf16[256,1408]{1,0:T(8,128)(2,1)S(1)}, u32[]{:S(2)}, u32[]{:S(2)}) collective-permute-start(bf16[256,1408]{1,0:T(8,128)(2,1)} %get-tuple-element.56), channel_id=1, source_target_pairs={{0,1},{1,0},{2,3},{3,2},{4,5},{5,4},{6,7},{7,6},{8,9},{9,8},{10,11... | collective-permute-start | bytes 2162696 | tf_op jit(solution)/shard_map/ppermute | solution.py:410
  139.1 26.1 %copy-start.1 = (bf16[32,5760]{1,0:T(8,128)(2,1)S(1)}, bf16[32,5760]{1,0:T(8,128)(2,1)}, u32[]{:S(2)}) copy-start(bf16[32,5760]{1,0:T(8,128)(2,1)} %get-tuple-element.57.refs_0_) | copy-start | bytes 1105924
  139.1 26.1 %copy-start.2 = (bf16[32,5760]{1,0:T(8,128)(2,1)S(1)}, bf16[32,5760]{1,0:T(8,128)(2,1)}, u32[]{:S(2)}) copy-start(bf16[32,5760]{1,0:T(8,128)(2,1)} %get-tuple-element.58.refs_5_) | copy-start | bytes 1105924
  139.1 11.2 %collective-permute-start.16 = (bf16[32,5760]{1,0:T(8,128)(2,1)}, bf16[32,5760]{1,0:T(8,128)(2,1)S(1)}, u32[]{:S(2)}, u32[]{:S(2)}) collective-permute-start(bf16[32,5760]{1,0:T(8,128)(2,1)} %get-tuple-element.57.refs_0_), channel_id=1, source_target_pairs={{0,32},{32,64},{64,96},{96,0},{1,33},{33,65},{65,97},{97,1},{2,34}... | collective-permute-start | bytes 1105928 | tf_op jit(solution)/shard_map/ppermute | solution.py:415
  139.1 11.3 %collective-permute-start.15 = (bf16[32,5760]{1,0:T(8,128)(2,1)}, bf16[32,5760]{1,0:T(8,128)(2,1)S(1)}, u32[]{:S(2)}, u32[]{:S(2)}) collective-permute-start(bf16[32,5760]{1,0:T(8,128)(2,1)} %get-tuple-element.57.refs_0_), channel_id=1, source_target_pairs={{0,96},{32,0},{64,32},{96,64},{1,97},{33,1},{65,33},{97,65},{2,98}... | collective-permute-start | bytes 1105928 | tf_op jit(solution)/shard_map/ppermute | solution.py:415
  141.7 16.4 %collective-permute-start.20 = (bf16[32,5760]{1,0:T(8,128)(2,1)}, bf16[32,5760]{1,0:T(8,128)(2,1)S(1)}, u32[]{:S(2)}, u32[]{:S(2)}) collective-permute-start(bf16[32,5760]{1,0:T(8,128)(2,1)} %get-tuple-element.58.refs_5_), channel_id=1, source_target_pairs={{0,32},{32,64},{64,96},{96,0},{1,33},{33,65},{65,97},{97,1},{2,34}... | collective-permute-start | bytes 1105928 | tf_op jit(solution)/shard_map/ppermute | solution.py:415
  141.7 16.5 %collective-permute-start.19 = (bf16[32,5760]{1,0:T(8,128)(2,1)}, bf16[32,5760]{1,0:T(8,128)(2,1)S(1)}, u32[]{:S(2)}, u32[]{:S(2)}) collective-permute-start(bf16[32,5760]{1,0:T(8,128)(2,1)} %get-tuple-element.58.refs_5_), channel_id=1, source_target_pairs={{0,96},{32,0},{64,32},{96,64},{1,97},{33,1},{65,33},{97,65},{2,98}... | collective-permute-start | bytes 1105928 | tf_op jit(solution)/shard_map/ppermute | solution.py:415
  150.3 11.8 %collective-permute-start.17 = (bf16[16,5760]{1,0:T(8,128)(2,1)S(1)}, bf16[16,5760]{1,0:T(8,128)(2,1)S(1)}, u32[]{:S(2)}, u32[]{:S(2)}) collective-permute-start(bf16[16,5760]{1,0:T(8,128)(2,1)S(1)} %slice.32), channel_id=1, source_target_pairs={{0,32},{32,64},{64,96},{96,0},{1,33},{33,65},{65,97},{97,1},{2,34}... | collective-permute-start | bytes 552968 | tf_op jit(solution)/shard_map/ppermute | solution.py:415
  150.4 11.7 %collective-permute-start.18 = (bf16[16,5760]{1,0:T(8,128)(2,1)S(1)}, bf16[16,5760]{1,0:T(8,128)(2,1)S(1)}, u32[]{:S(2)}, u32[]{:S(2)}) collective-permute-start(bf16[16,5760]{1,0:T(8,128)(2,1)S(1)} %slice.33), channel_id=1, source_target_pairs={{0,96},{32,0},{64,32},{96,64},{1,97},{33,1},{65,33},{97,65},{2,98}... | collective-permute-start | bytes 552968 | tf_op jit(solution)/shard_map/ppermute | solution.py:415
  158.2 6.9 %collective-permute-start.21 = (bf16[16,5760]{1,0:T(8,128)(2,1)S(1)}, bf16[16,5760]{1,0:T(8,128)(2,1)S(1)}, u32[]{:S(2)}, u32[]{:S(2)}) collective-permute-start(bf16[16,5760]{1,0:T(8,128)(2,1)S(1)} %slice.34), channel_id=1, source_target_pairs={{0,32},{32,64},{64,96},{96,0},{1,33},{33,65},{65,97},{97,1},{2,34}... | collective-permute-start | bytes 552968 | tf_op jit(solution)/shard_map/ppermute | solution.py:415
  158.3 6.8 %collective-permute-start.22 = (bf16[16,5760]{1,0:T(8,128)(2,1)S(1)}, bf16[16,5760]{1,0:T(8,128)(2,1)S(1)}, u32[]{:S(2)}, u32[]{:S(2)}) collective-permute-start(bf16[16,5760]{1,0:T(8,128)(2,1)S(1)} %slice.35), channel_id=1, source_target_pairs={{0,96},{32,0},{64,32},{96,64},{1,97},{33,1},{65,33},{97,65},{2,98}... | collective-permute-start | bytes 552968 | tf_op jit(solution)/shard_map/ppermute | solution.py:415
